TPU v7x, 128 devices: a whole 4x4x4 slice. The times are simulated.
128 devices in a mesh: node: 16 (over x, y), head: 8 (over z, core).
Axes of the slice: x: 4, y: 4, z: 4, core: 2. Of those that a mesh axis runs over, the one named last changes fastest.
Arguments:
- features: bfloat16 [131072, 768], P(('node', 'head'))
- w_query: bfloat16 [768, 768], replicated
- w_key: bfloat16 [768, 768], replicated
- w_value: bfloat16 [768, 768], replicated, may hold values from -0.86328125 to 0.86328125
- w_out: bfloat16 [768, 768], replicated, may hold values from -0.21875 to 0.21875
- w_up: bfloat16 [768, 1536], replicated, may hold values from -0.21875 to 0.21875
- w_down: bfloat16 [1536, 768], replicated, may hold values from -0.21875 to 0.21875
- gain_attn: float32 [768], replicated, may hold values from 0.25 to 1.75
- gain_ffn: float32 [768], replicated, may hold values from 0.25 to 1.75
- send_list: int32 [16, 16, 16], P('node'), may hold values from 0 to 127
- edge_owner: int32 [2048, 8], P('node'), may hold values from 0 to 15
- edge_slot: int32 [2048, 8], P('node'), may hold values from 0 to 15
- edge_count: int32 [2048], P('node'), may hold values from 1 to 8, as said below
Outputs:
- layer_out: bfloat16 [131072, 768], P(('node', 'head'))
Inputs may be any that keep to these rules, and one draw needn't show every extreme that they name: `edge_count`: at least one query block uses 1 entry; every query block of every fourth node group (0, 4, 8, ...) uses all 8.
All inputs are finite; a program needn't handle non-finite values.
Results may differ from a plain program's by a relative error of at most 0.0076.
Values may be sent and summed in bfloat16 or wider, within the bound.
No kernel may reach another device: no remote copies, remote signals or barrier semaphores. Data moves between devices by JAX's collectives and lax.ppermute only.
A program may use at most 128 MiB of HBM per device.

v0:
```python
import math

import jax
import jax.numpy as jnp
from jax import lax
from jax.sharding import PartitionSpec as P

HDIM = 64
BLOCK = 64
MAXK = 8
CAP = 16


def normed(values, gain):
    center = values - jnp.mean(values, axis=-1, keepdims=True)
    spread = jnp.mean(center * center, axis=-1, keepdims=True)
    return center * lax.rsqrt(spread + 1e-05) * gain


def per_device(
    features,
    w_query,
    w_key,
    w_value,
    w_out,
    w_up,
    w_down,
    gain_attn,
    gain_ffn,
    send_list,
    edge_owner,
    edge_slot,
    edge_count,
):
    head_devs = lax.axis_size("head")
    head_index = lax.axis_index("head")
    local_rows, width = features.shape
    head_groups = math.gcd(width // HDIM, head_devs)
    node_parts = head_devs // head_groups
    group_index = head_index % head_groups
    part_index = head_index // head_groups
    head_cols = width // head_groups
    heads_here = head_cols // HDIM
    part_rows = local_rows // node_parts
    mine = [
        lax.dynamic_slice_in_dim(matrix, group_index * head_cols, head_cols, 1)
        for matrix in (w_query, w_key, w_value)
    ]
    w_heads = jnp.concatenate(mine, axis=1)
    projected = jnp.dot(
        lax.all_gather(features, "head", axis=0, tiled=True),
        w_heads,
        preferred_element_type=jnp.float32,
    ).astype(jnp.bfloat16)
    group_rows = projected.shape[0]
    blocks_here = group_rows // BLOCK
    pair_blocks = projected[:, head_cols:].reshape(blocks_here, BLOCK, 2 * head_cols)
    outgoing = jnp.take(pair_blocks, send_list.reshape(-1), axis=0)
    outgoing = outgoing.reshape(send_list.shape[1], send_list.shape[2], BLOCK, 2 * head_cols)
    incoming = lax.all_to_all(outgoing, "node", split_axis=0, concat_axis=0, tiled=True)
    incoming_flat = incoming.reshape(-1, BLOCK, 2 * head_cols)

    def select_part(array):
        rest = array.shape[1:]
        shaped = array.reshape((head_devs, node_parts, -1) + rest)
        picked = lax.dynamic_index_in_dim(shaped, part_index, 1, keepdims=False)
        return picked.reshape((-1,) + rest)

    query_blocks = select_part(projected[:, :head_cols].reshape(blocks_here, BLOCK, head_cols))
    own_blocks = select_part(pair_blocks)
    owner_part = select_part(edge_owner)
    slot_part = select_part(edge_slot)
    count_part = select_part(edge_count)
    my_blocks = query_blocks.shape[0]
    group_size = math.gcd(8, my_blocks)
    steps_count = my_blocks // group_size
    query_groups = query_blocks.reshape(steps_count, group_size, BLOCK, heads_here, HDIM)
    slot_ids = (owner_part * CAP + slot_part).reshape(steps_count, group_size, MAXK)
    count_groups = count_part.reshape(steps_count, group_size)
    own_groups = own_blocks.reshape(steps_count, group_size, BLOCK, 2 * head_cols)
    list_ids = jnp.arange(MAXK, dtype=jnp.int32)

    def attend(args):
        query_rows, slot_rows, count_rows, own_rows = args
        remote = jnp.take(incoming_flat, slot_rows.reshape(-1), axis=0)
        remote = remote.reshape(group_size, MAXK * BLOCK, 2 * head_cols)
        remote_keys = remote[:, :, :head_cols].reshape(group_size, -1, heads_here, HDIM)
        remote_values = remote[:, :, head_cols:].reshape(group_size, -1, heads_here, HDIM)
        own_keys = own_rows[:, :, :head_cols].reshape(group_size, BLOCK, heads_here, HDIM)
        own_values = own_rows[:, :, head_cols:].reshape(group_size, BLOCK, heads_here, HDIM)
        own_scores = jnp.einsum(
            "gqhd,gkhd->ghqk", query_rows, own_keys, preferred_element_type=jnp.float32
        ) / math.sqrt(HDIM)
        far_scores = jnp.einsum(
            "gqhd,gkhd->ghqk", query_rows, remote_keys, preferred_element_type=jnp.float32
        ) / math.sqrt(HDIM)
        valid = list_ids[None, :] < count_rows[:, None]
        valid = jnp.repeat(valid, BLOCK, axis=1)
        far_scores = jnp.where(valid[:, None, None, :], far_scores, -1e30)
        top = jnp.maximum(
            jnp.max(own_scores, axis=-1, keepdims=True), jnp.max(far_scores, axis=-1, keepdims=True)
        )
        own_weights = jnp.exp(own_scores - top)
        far_weights = jnp.exp(far_scores - top)
        total = jnp.sum(own_weights, axis=-1, keepdims=True) + jnp.sum(
            far_weights, axis=-1, keepdims=True
        )
        own_probs = (own_weights / total).astype(jnp.bfloat16)
        far_probs = (far_weights / total).astype(jnp.bfloat16)
        result = jnp.einsum(
            "ghqk,gkhd->gqhd", own_probs, own_values, preferred_element_type=jnp.float32
        )
        result = result + jnp.einsum(
            "ghqk,gkhd->gqhd", far_probs, remote_values, preferred_element_type=jnp.float32
        )
        return result.astype(jnp.bfloat16).reshape(group_size * BLOCK, head_cols)

    attended = lax.map(attend, (query_groups, slot_ids, count_groups, own_groups)).reshape(
        my_blocks * BLOCK, head_cols
    )
    spread_out = attended.reshape(head_devs, part_rows, head_cols)
    back = lax.all_to_all(spread_out, "head", split_axis=0, concat_axis=0, tiled=True)
    back = back.reshape(node_parts, head_groups, part_rows, head_cols)
    w_split = w_out.reshape(head_groups, head_cols, width)
    mixed = jnp.einsum("pgrc,gcd->prd", back, w_split, preferred_element_type=jnp.float32).reshape(
        local_rows, width
    )
    first = normed(features.astype(jnp.float32) + mixed, gain_attn).astype(jnp.bfloat16)
    hidden = jnp.maximum(jnp.dot(first, w_up, preferred_element_type=jnp.float32), 0.0).astype(
        jnp.bfloat16
    )
    total = first.astype(jnp.float32) + jnp.dot(hidden, w_down, preferred_element_type=jnp.float32)
    return normed(total, gain_ffn).astype(jnp.bfloat16)


def solution(mesh):
    return jax.shard_map(
        per_device,
        mesh=mesh,
        in_specs=(
            P(("node", "head"), None),
            P(),
            P(),
            P(),
            P(),
            P(),
            P(),
            P(),
            P(),
            P("node", None, None),
            P("node", None),
            P("node", None),
            P("node"),
        ),
        out_specs=P(("node", "head"), None),
        check_vma=False,
    )
```

profile of v0, /device:TPU:20, one launch (start us, length us, event | category | flops | bytes accessed | tf_op | source)
XLA Modules:
  0.0 660.5 jit_solution(7683124207177126961)
XLA Ops:
  10.9 67.8 %all-gather.2.cloned.1.call-done = bf16[8192,768]{1,0:T(8,128)(2,1)} async-done(((bf16[1024,768]{1,0:T(8,128)(2,1)}), bf16[8192,768]{1,0:T(8,128)(2,1)}) %all-gather.2.cloned.1.call-update) | async-done | bytes 12582928 | tf_op jit(solution)/shard_map/all_gather | solution.py:51
  78.7 14.2 %fusion.21 = bf16[8192,576]{0,1:T(8,128)(2,1)} fusion(bf16[8192,768]{1,0:T(8,128)(2,1)} %all-gather.2.cloned.1.call-done, bf16[768,192]{1,0:T(8,128)(2,1)S(1)} %get-tuple-element.104, bf16[768,192]{1,0:T(8,128)(2,1)S(1)} %get-tuple-element.105, bf16[768,192]{1,0:T(8,128)(2,1)S(1)} %constant_dynamic-slice_fusion.7), kind=kOutput, calls=%fused_computation.41 | convolution fusion | flops 7255130112 | bytes 22904832 | tf_op jit(solution)/shard_map/dot_general | solution.py:50
  92.9 6.1 slice.32
  99.0 8.6 %copy.39 = bf16[8192,384]{1,0:T(8,128)(2,1)} copy(bf16[8192,384]{0,1:T(8,128)(2,1)} %slice.32) | data formatting | bytes 12582912 | tf_op jit(solution)/shard_map/slice | solution.py:57
  107.6 13.8 %gather_fusion.1 = bf16[256,64,384]{2,1,0:T(8,128)(2,1)} fusion(bf16[128,64,384]{2,1,0:T(8,128)(2,1)} %bitcast.105, s32[1024]{0:T(1024)S(1)} %pad_clamp_fusion.1), kind=kCustom, calls=%fused_computation.1 | custom fusion | bytes 25166848 | tf_op jit(solution)/shard_map/jit(_take)/gather | solution.py:58
  121.4 10.9 %broadcast_select_fusion.1 = bf16[16,16,64,384]{3,2,1,0:T(8,128)(2,1)} fusion(bf16[16,16,64,384]{3,2,1,0:T(8,128)(2,1)} %bitcast.107, pred[16,16]{1,0:T(8,128)(4,1)S(1)} %compare_and_fusion.1), kind=kLoop, calls=%fused_computation.39 | loop fusion | flops 6291456 | bytes 25166080 | tf_op jit(solution)/shard_map/jit(_take)/select_n | solution.py:58
  132.3 7.4 %all-to-all-start = ((bf16[16,16,64,384]{3,2,1,0:T(8,128)(2,1)}), bf16[16,16,64,384]{3,2,1,0:T(8,128)(2,1)}, u32[]{:S(2)}, u32[]{:S(2)}) async-start(bf16[16,16,64,384]{3,2,1,0:T(8,128)(2,1)} %broadcast_select_fusion.1), calls=%async_computation | async-start | bytes 25165824 | tf_op jit(solution)/shard_map/all_to_all | solution.py:60
  141.3 3.9 slice.33
  145.2 5.9 copy.40
  151.1 3.2 constant_dynamic-slice_fusion.4
  154.3 4.5 copy.41
  158.8 4.0 dynamic-slice_bitcast_fusion
  162.8 197.5 %all-to-all-done = bf16[16,16,64,384]{3,2,1,0:T(8,128)(2,1)} async-done(((bf16[16,16,64,384]{3,2,1,0:T(8,128)(2,1)}), bf16[16,16,64,384]{3,2,1,0:T(8,128)(2,1)}, u32[]{:S(2)}, u32[]{:S(2)}) %all-to-all-start) | async-done | bytes 12582944 | tf_op jit(solution)/shard_map/all_to_all | solution.py:60
  360.3 236.2 %while.11 = (s32[]{:T(128)}, bf16[8,512,192]{1,2,0:T(8,128)(2,1)}, bf16[8,8,64,384]{3,2,1,0:T(8,128)(2,1)}, bf16[8,8,64,3,64]{2,4,3,1,0:T(8,128)(2,1)}, s32[8,8]...) while((s32[]{:T(128)}, bf16[8,512,192]{1,2,0:T(8,128)(2,1)}, ...), condition=%wide.region_5.6_spmd.clone, body=%wide.region_0.0_spmd.clone.sunk | while | flops 238385792 | bytes 63683908 | solution.py:118
  361.2 7.2 %gather_fusion = bf16[64,64,384]{2,1,0:T(8,128)(2,1)} fusion(bf16[256,64,384]{2,1,0:T(8,128)(2,1)} %get-tuple-element.187, s32[1024]{0:T(1024)S(1)} %pad_clamp_fusion.3), kind=kCustom, calls=%fused_computation.clone.clone.1 | custom fusion | bytes 6291712 | tf_op jit(solution)/shard_map/while/body/eval_jaxpr/jit(_take)/gather | solution.py:85
  368.4 4.7 copy.60
  378.4 3.8 fusion.64
  390.8 7.2 %gather_fusion = bf16[64,64,384]{2,1,0:T(8,128)(2,1)} fusion(bf16[256,64,384]{2,1,0:T(8,128)(2,1)} %get-tuple-element.187, s32[1024]{0:T(1024)S(1)} %pad_clamp_fusion.3), kind=kCustom, calls=%fused_computation.clone.clone.1 | custom fusion | bytes 6291712 | tf_op jit(solution)/shard_map/while/body/eval_jaxpr/jit(_take)/gather | solution.py:85
  398.0 4.7 copy.60
  402.8 2.2 broadcast_select_fusion.3
  407.9 3.8 fusion.64
  420.3 7.2 %gather_fusion = bf16[64,64,384]{2,1,0:T(8,128)(2,1)} fusion(bf16[256,64,384]{2,1,0:T(8,128)(2,1)} %get-tuple-element.187, s32[1024]{0:T(1024)S(1)} %pad_clamp_fusion.3), kind=kCustom, calls=%fused_computation.clone.clone.1 | custom fusion | bytes 6291712 | tf_op jit(solution)/shard_map/while/body/eval_jaxpr/jit(_take)/gather | solution.py:85
  427.5 4.7 copy.60
  437.4 3.8 fusion.64
  449.8 7.2 %gather_fusion = bf16[64,64,384]{2,1,0:T(8,128)(2,1)} fusion(bf16[256,64,384]{2,1,0:T(8,128)(2,1)} %get-tuple-element.187, s32[1024]{0:T(1024)S(1)} %pad_clamp_fusion.3), kind=kCustom, calls=%fused_computation.clone.clone.1 | custom fusion | bytes 6291712 | tf_op jit(solution)/shard_map/while/body/eval_jaxpr/jit(_take)/gather | solution.py:85
  457.0 4.7 copy.60
  466.9 3.8 fusion.64
  479.3 7.2 %gather_fusion = bf16[64,64,384]{2,1,0:T(8,128)(2,1)} fusion(bf16[256,64,384]{2,1,0:T(8,128)(2,1)} %get-tuple-element.187, s32[1024]{0:T(1024)S(1)} %pad_clamp_fusion.3), kind=kCustom, calls=%fused_computation.clone.clone.1 | custom fusion | bytes 6291712 | tf_op jit(solution)/shard_map/while/body/eval_jaxpr/jit(_take)/gather | solution.py:85
  486.5 4.7 copy.60
  496.5 3.8 fusion.64
  508.9 7.2 %gather_fusion = bf16[64,64,384]{2,1,0:T(8,128)(2,1)} fusion(bf16[256,64,384]{2,1,0:T(8,128)(2,1)} %get-tuple-element.187, s32[1024]{0:T(1024)S(1)} %pad_clamp_fusion.3), kind=kCustom, calls=%fused_computation.clone.clone.1 | custom fusion | bytes 6291712 | tf_op jit(solution)/shard_map/while/body/eval_jaxpr/jit(_take)/gather | solution.py:85
  516.1 4.7 copy.60
  526.0 3.8 fusion.64
  538.4 7.2 %gather_fusion = bf16[64,64,384]{2,1,0:T(8,128)(2,1)} fusion(bf16[256,64,384]{2,1,0:T(8,128)(2,1)} %get-tuple-element.187, s32[1024]{0:T(1024)S(1)} %pad_clamp_fusion.3), kind=kCustom, calls=%fused_computation.clone.clone.1 | custom fusion | bytes 6291712 | tf_op jit(solution)/shard_map/while/body/eval_jaxpr/jit(_take)/gather | solution.py:85
  545.6 4.7 copy.60
  555.5 3.8 fusion.64
  567.9 7.2 %gather_fusion = bf16[64,64,384]{2,1,0:T(8,128)(2,1)} fusion(bf16[256,64,384]{2,1,0:T(8,128)(2,1)} %get-tuple-element.187, s32[1024]{0:T(1024)S(1)} %pad_clamp_fusion.3), kind=kCustom, calls=%fused_computation.clone.clone.1 | custom fusion | bytes 6291712 | tf_op jit(solution)/shard_map/while/body/eval_jaxpr/jit(_take)/gather | solution.py:85
  575.1 4.7 copy.60
  585.0 3.8 fusion.64
  596.5 4.5 all-to-all-start.1
  601.0 2.6 copy.38
  603.6 18.7 %all-to-all-done.1 = bf16[8,512,192]{1,2,0:T(8,128)(2,1)} async-done(((bf16[8,512,192]{1,2,0:T(8,128)(2,1)}), bf16[8,512,192]{1,2,0:T(8,128)(2,1)}, u32[]{:S(2)}, u32[]{:S(2)}) %all-to-all-start.1) | async-done | bytes 1572896 | tf_op jit(solution)/shard_map/all_to_all | solution.py:122
  622.4 4.3 copy.54
  626.6 3.8 dot_general.30
  630.4 3.4 fusion.32
  635.9 10.8 %fusion.33 = (f32[1024]{0:T(1024)S(1)}, f32[1024,768]{0,1:T(8,128)}) fusion(bf16[1536,768]{1,0:T(8,128)(2,1)S(1)} %copy-done, bf16[768,1536]{1,0:T(8,128)(2,1)} %param.20, f32[1024,768]{0,1:T(8,128)} %copy-done.4, f32[768]{0:T(1024)S(1)} %copy-done.13, f32[1024]{0:T(1024)S(1)} %add_rsqrt_fusion.1, f32[1024]{0:T(1024)S(1)} %broadcast_multiply_fusion.1), kind=kOutput, calls=%fused_computation.76 | convolution fusion | flops 4843633664 | bytes 11025408 | tf_op jit(solution)/shard_map/dot_general | solution.py:132
  646.7 2.4 multiply_reduce_fusion
  651.1 2.6 copy.47
  (319 shorter events, 117.7 us)
Async XLA Ops:
  6.5 629.4 %copy-start = (bf16[1536,768]{1,0:T(8,128)(2,1)S(1)}, bf16[1536,768]{1,0:T(8,128)(2,1)}, u32[]{:S(2)}) copy-start(bf16[1536,768]{1,0:T(8,128)(2,1)} %param.21) | copy-start | bytes 7077892
  6.5 4.4 copy-start.7
  6.5 72.2 %all-gather.2.cloned.1.call-start = ((), (), s32[]{:S(2)}) async-start(), calls=%async_computation.2 | async-start | bytes 14155776 | tf_op jit(solution)/shard_map/all_gather | solution.py:51
  132.2 7.4 %copy-start.11 = (s32[128]{0:T(128)S(1)}, s32[128]{0:T(128)}, u32[]{:S(2)}) copy-start(s32[128]{0:T(128)} %param.27) | copy-start | bytes 1540
  132.2 7.5 %copy-start.8 = (s32[128,8]{0,1:T(8,128)S(1)}, s32[128,8]{0,1:T(8,128)}, u32[]{:S(2)}) copy-start(s32[128,8]{0,1:T(8,128)} %param.26) | copy-start | bytes 12292
  132.2 7.7 %copy-start.9 = (s32[128,8]{0,1:T(8,128)S(1)}, s32[128,8]{0,1:T(8,128)}, u32[]{:S(2)}) copy-start(s32[128,8]{0,1:T(8,128)} %param.25) | copy-start | bytes 12292
  132.3 228.1 %all-to-all-start = ((bf16[16,16,64,384]{3,2,1,0:T(8,128)(2,1)}), bf16[16,16,64,384]{3,2,1,0:T(8,128)(2,1)}, u32[]{:S(2)}, u32[]{:S(2)}) async-start(bf16[16,16,64,384]{3,2,1,0:T(8,128)(2,1)} %broadcast_select_fusion.1), calls=%async_computation | async-start | bytes 25165824 | tf_op jit(solution)/shard_map/all_to_all | solution.py:60
  378.4 3.8 copy-start.5
  383.6 2.0 copy-start.1
  383.6 2.0 copy-start.6
  383.7 2.9 copy-start.2
  407.9 3.8 copy-start.5
  413.1 2.0 copy-start.1
  413.1 2.0 copy-start.6
  413.2 2.9 copy-start.2
  437.4 3.8 copy-start.5
  442.7 2.0 copy-start.1
  442.7 2.0 copy-start.6
  442.7 2.9 copy-start.2
  466.9 3.8 copy-start.5
  472.2 2.0 copy-start.1
  472.2 2.0 copy-start.6
  472.3 2.9 copy-start.2
  496.5 3.8 copy-start.5
  501.7 2.0 copy-start.1
  501.7 2.0 copy-start.6
  501.8 2.9 copy-start.2
  526.0 3.8 copy-start.5
  531.2 2.0 copy-start.1
  531.2 2.0 copy-start.6
  531.3 2.9 copy-start.2
  555.5 3.8 copy-start.5
  560.8 2.0 copy-start.1
  560.8 2.0 copy-start.6
  560.8 2.9 copy-start.2
  585.0 3.8 copy-start.5
  590.3 2.0 copy-start.1
  590.3 2.0 copy-start.6
  590.4 2.9 copy-start.2
  596.5 25.9 %all-to-all-start.1 = ((bf16[8,512,192]{1,2,0:T(8,128)(2,1)}), bf16[8,512,192]{1,2,0:T(8,128)(2,1)}, u32[]{:S(2)}, u32[]{:S(2)}) async-start(bf16[8,512,192]{1,2,0:T(8,128)(2,1)} %get-tuple-element.47), calls=%async_computation.1 | async-start | bytes 3145728 | tf_op jit(solution)/shard_map/all_to_all | solution.py:122
  622.4 8.1 %copy-start.12 = (bf16[768,768]{1,0:T(8,128)(2,1)S(1)}, bf16[768,768]{1,0:T(8,128)(2,1)}, u32[]{:S(2)}) copy-start(bf16[768,768]{1,0:T(8,128)(2,1)} %param.19) | copy-start | bytes 3538948
  633.9 1.7 copy-start.4
  633.9 2.1 copy-start.13
  646.7 2.8 copy-start.3
  646.7 2.8 copy-start.10
Sparse Core Ops, SparseCore 0:
  9.0 69.6 all-gather.1
where the time goes:
time: 664 us; the launch traced here: 660 us
  waiting for transfers between devices  285 us (43%)
  local copies, waits for them, and re-layouts  220 us (33%)
  matrix products  86.2 us (13%)
  other arithmetic  43.8 us (7%)
  between operations  13.6 us (2%)
  starting transfers between devices  11.9 us (2%)
    all_to_all x1, waiting for transfers between devices, per_device(): lax.all_to_all(outgoing, 'node', split_axis=0, concat_axis=0, tiled=True)  197 us
    gather x16, local copies, waits for them, and re-layouts, attend(): remote = jnp.take(incoming_flat, slot_rows.reshape(-1), axis=0)  94.9 us
    all_gather x1, waiting for transfers between devices, per_device(): lax.all_gather(features, 'head', axis=0, tiled=True)  67.8 us
    dot_general x8, matrix products, attend(): jnp.einsum('gqhd,gkhd->ghqk', query_rows, remote_keys, preferred_element_...  30.5 us
    all_to_all x1, waiting for transfers between devices, per_device(): lax.all_to_all(spread_out, 'head', split_axis=0, concat_axis=0, tiled=True)  18.7 us
    dynamic_slice x32, local copies, waits for them, and re-layouts, per_device(): lax.map(attend, (query_groups, slot_ids, count_groups, own_groups))  18 us
    select_n x16, other arithmetic, attend(): remote = jnp.take(incoming_flat, slot_rows.reshape(-1), axis=0)  17.7 us
    slice x8, local copies, waits for them, and re-layouts, attend(): remote[:, :, :head_cols].reshape(group_size, -1, heads_here, HDIM)  15.4 us
  transfers between devices with their start and end apart: 3, of which 3 were waited for; matrix products, arithmetic and copies ran while one was open for 4% of the time, Pallas kernels for 0%

commit v1 on v0

v1 whole, which is shorter than its diff:
```python
import functools
import math

import jax
import jax.numpy as jnp
from jax import lax
from jax.experimental import pallas as pl
from jax.experimental.pallas import tpu as pltpu
from jax.sharding import PartitionSpec as P

HDIM = 64
BLOCK = 64
MAXK = 8
CAP = 16
HALF = BLOCK // 2
LANES = 2 * HDIM
CHUNKS = 3
QUADS = 4
LOG2E = 1.4426950408889634
F32 = jnp.float32
BF16 = jnp.bfloat16
VMEM = pl.BlockSpec(memory_space=pltpu.VMEM)
SMEM = pl.BlockSpec(memory_space=pltpu.SMEM)
ANY = pl.BlockSpec(memory_space=pl.ANY)
LIMIT = 60 * 1024 * 1024


def low_lanes(rows):
    return lax.broadcasted_iota(jnp.int32, (rows, LANES), 1) < HDIM


def pack_pair(both):
    blocks = both.shape[0] // BLOCK
    split = both.reshape(blocks, 2, HALF, LANES)
    first = split[:, 0].reshape(blocks * HALF, LANES)
    second = split[:, 1].reshape(blocks * HALF, LANES)
    low = low_lanes(blocks * HALF)
    even = jnp.where(low, first, pltpu.roll(second, HDIM, 1))
    odd = jnp.where(low, pltpu.roll(first, HDIM, 1), second)
    return even.reshape(blocks, HALF, LANES), odd.reshape(blocks, HALF, LANES)


def unpack_pair(even, odd):
    blocks = even.shape[0]
    even = even.reshape(blocks * HALF, LANES).astype(F32)
    odd = odd.reshape(blocks * HALF, LANES).astype(F32)
    low = low_lanes(blocks * HALF)
    first = jnp.where(low, even, pltpu.roll(odd, HDIM, 1)).reshape(blocks, 1, HALF, LANES)
    second = jnp.where(low, pltpu.roll(even, HDIM, 1), odd).reshape(blocks, 1, HALF, LANES)
    return jnp.concatenate([first, second], axis=1).reshape(blocks * BLOCK, LANES)


def keys_values_kernel(feat_ref, key_ref, value_ref, out_ref):
    for half in range(2):
        rows = feat_ref[half * 512 : half * 512 + 512, :]
        for kind, w_ref in enumerate((key_ref, value_ref)):
            made = jnp.dot(rows, w_ref[...], preferred_element_type=F32)
            for pair in range(2):
                packed = pack_pair(made[:, pair * LANES : (pair + 1) * LANES])
                for side in range(2):
                    dest = 2 * (2 * pair + side) + kind
                    out_ref[dest, half * 8 : half * 8 + 8] = packed[side].astype(BF16)


def queries_kernel(feat_ref, query_ref, out_ref):
    for half in range(2):
        rows = feat_ref[half * 512 : half * 512 + 512, :]
        made = jnp.dot(rows, query_ref[...], preferred_element_type=F32)
        for pair in range(2):
            packed = pack_pair(made[:, pair * LANES : (pair + 1) * LANES])
            for side in range(2):
                out_ref[2 * (2 * pair + side) + half] = packed[side].astype(BF16)


def project_keys_values(features, w_key, w_value, chunk):
    rows, width = features.shape
    cols = QUADS * HDIM
    return pl.pallas_call(
        keys_values_kernel,
        grid=(1,),
        in_specs=[
            pl.BlockSpec((rows, width), lambda i: (0, 0)),
            pl.BlockSpec((width, cols), lambda i: (0, chunk)),
            pl.BlockSpec((width, cols), lambda i: (0, chunk)),
        ],
        out_specs=pl.BlockSpec((8, 16, HALF, LANES), lambda i: (0, 0, 0, 0)),
        out_shape=jax.ShapeDtypeStruct((8, 16, HALF, LANES), BF16),
        compiler_params=pltpu.CompilerParams(vmem_limit_bytes=LIMIT),
        cost_estimate=pl.CostEstimate(flops=4 * rows * width * cols, bytes_accessed=5 << 20, transcendentals=0),
        name="keys_values",
    )(features, w_key, w_value)


def project_queries(features, w_query, chunk):
    rows, width = features.shape
    cols = QUADS * HDIM
    return pl.pallas_call(
        queries_kernel,
        grid=(1,),
        in_specs=[
            pl.BlockSpec((rows, width), lambda i: (0, 0)),
            pl.BlockSpec((width, cols), lambda i: (0, chunk)),
        ],
        out_specs=pl.BlockSpec((8, 8, HALF, LANES), lambda i: (0, 0, 0, 0)),
        out_shape=jax.ShapeDtypeStruct((8, 8, HALF, LANES), BF16),
        compiler_params=pltpu.CompilerParams(vmem_limit_bytes=LIMIT),
        cost_estimate=pl.CostEstimate(flops=2 * rows * width * cols, bytes_accessed=3 << 20, transcendentals=0),
        name="queries",
    )(features, w_query)


def collect_kernel(list_ref, core_ref, held_ref, out_ref, swap_ref):
    def body(step, carry):
        for extra in range(8):
            slot = step * 8 + extra
            out_ref[slot] = held_ref[list_ref[slot]]
        return carry

    lax.fori_loop(0, out_ref.shape[0] // 8, body, 0)
    other = 1 - core_ref[0]
    for source in range(8):
        swap_ref[source] = held_ref[pl.ds(source * 16 + other * 8, 8)]


def collect(held, flat_list, core):
    slots = flat_list.shape[0]
    return pl.pallas_call(
        collect_kernel,
        in_specs=[SMEM, SMEM, VMEM],
        out_specs=[VMEM, VMEM],
        out_shape=[
            jax.ShapeDtypeStruct((slots, HALF, LANES), BF16),
            jax.ShapeDtypeStruct((8, 8, HALF, LANES), BF16),
        ],
        compiler_params=pltpu.CompilerParams(vmem_limit_bytes=LIMIT),
        cost_estimate=pl.CostEstimate(flops=0, bytes_accessed=4 << 20, transcendentals=0),
        name="collect",
    )(flat_list, core, held)


def attend_kernel(
    id_ref, count_ref, core_ref, query_ref, held_ref, swap_ref, mine_ref, other_ref,
    out_ref, keys, values, own_keys, own_values, sems,
):
    core = core_ref[0]

    def fetch(which, near, near_own, far, far_own):
        copies = [
            pltpu.make_async_copy(held_ref.at[:, which], near_own, sems.at[0]),
            pltpu.make_async_copy(swap_ref, far_own, sems.at[1]),
            pltpu.make_async_copy(mine_ref, near, sems.at[2]),
            pltpu.make_async_copy(other_ref, far, sems.at[3]),
        ]
        for copy in copies:
            copy.start()
        for copy in copies:
            copy.wait()

    @pl.when(core == 0)
    def _():
        fetch(0, keys, own_keys, values, own_values)

    @pl.when(core == 1)
    def _():
        fetch(1, values, own_values, keys, own_keys)

    low = low_lanes(HALF)
    lane = lax.broadcasted_iota(jnp.int32, (1, MAXK * HALF), 1)
    dims = (((1,), (1,)), ((), ()))

    def unit(source, place):
        block = source * 16 + core * 8 + place
        query = query_ref[source, place].astype(F32)
        turned = pltpu.roll(query, HDIM, 1)
        zero = jnp.zeros_like(query)
        left = jnp.concatenate(
            [
                jnp.where(low, query, zero),
                jnp.where(low, turned, zero),
                jnp.where(low, zero, turned),
                jnp.where(low, zero, query),
            ],
            axis=0,
        ).astype(BF16)
        slots = [id_ref[block * MAXK + entry] for entry in range(MAXK)]
        far_keys = jnp.concatenate([keys[slot] for slot in slots], axis=0)
        far = lax.dot_general(left, far_keys, dims, preferred_element_type=F32)
        near = lax.dot_general(left, own_keys[source, place], dims, preferred_element_type=F32)
        far = jnp.where(lane < count_ref[block] * HALF, far, -8e30)
        top = jnp.maximum(
            jnp.max(far, axis=1, keepdims=True), jnp.max(near, axis=1, keepdims=True)
        )
        top = jnp.maximum(top[:BLOCK], top[BLOCK:])
        top = jnp.concatenate([top, top], axis=0)
        scale = LOG2E / math.sqrt(HDIM)
        far = jnp.exp2((far - top) * scale)
        near = jnp.exp2((near - top) * scale)
        total = jnp.sum(far, axis=1, keepdims=True) + jnp.sum(near, axis=1, keepdims=True)
        total = total[:BLOCK] + total[BLOCK:]
        far_values = jnp.concatenate([values[slot] for slot in slots], axis=0)
        summed = jnp.dot(far.astype(BF16), far_values, preferred_element_type=F32)
        summed = summed + jnp.dot(
            near.astype(BF16), own_values[source, place], preferred_element_type=F32
        )
        straight = jnp.where(low, summed[:HALF], summed[3 * HALF :])
        crossed = jnp.where(low, summed[HALF : 2 * HALF], summed[2 * HALF : 3 * HALF])
        result = straight + pltpu.roll(crossed, HDIM, 1)
        share = 1.0 / total
        share = jnp.where(low, share[:HALF], share[HALF:])
        out_ref[source, place] = (result * share).astype(BF16)

    def body(step, carry):
        for extra in range(2):
            at = step * 2 + extra
            unit(at // 8, at % 8)
        return carry

    lax.fori_loop(0, 32, body, 0)


def attend(ids, counts, core, queries, held, swapped, mine, other):
    slots = mine.shape[0]
    return pl.pallas_call(
        attend_kernel,
        in_specs=[SMEM, SMEM, SMEM, VMEM, ANY, ANY, ANY, ANY],
        out_specs=VMEM,
        out_shape=jax.ShapeDtypeStruct((8, 8, HALF, LANES), BF16),
        scratch_shapes=[
            pltpu.VMEM((slots, HALF, LANES), BF16),
            pltpu.VMEM((slots, HALF, LANES), BF16),
            pltpu.VMEM((8, 8, HALF, LANES), BF16),
            pltpu.VMEM((8, 8, HALF, LANES), BF16),
            pltpu.SemaphoreType.DMA((4,)),
        ],
        compiler_params=pltpu.CompilerParams(vmem_limit_bytes=LIMIT),
        cost_estimate=pl.CostEstimate(
            flops=64 * 4 * 128 * 128 * 288, bytes_accessed=6 << 20, transcendentals=64 * 128 * 288
        ),
        name="attend",
    )(ids, counts, core, queries, held.reshape(8, 2, 8, HALF, LANES), swapped, mine, other)


def normed(values, gain):
    center = values - jnp.mean(values, axis=-1, keepdims=True)
    spread = jnp.mean(center * center, axis=-1, keepdims=True)
    return center * lax.rsqrt(spread + 1e-05) * gain


def finish_kernel(feat_ref, *refs):
    backs = refs[:CHUNKS]
    out_w_ref, up_ref, down_ref, gain_a_ref, gain_f_ref, result_ref = refs[CHUNKS:]
    mixed = feat_ref[...].astype(F32)
    for chunk, back in enumerate(backs):
        pieces = [unpack_pair(back[2 * pair, 0], back[2 * pair + 1, 0]) for pair in range(2)]
        attended = jnp.concatenate(pieces, axis=1).astype(BF16)
        mixed = mixed + jnp.dot(
            attended,
            out_w_ref[chunk * QUADS * HDIM : (chunk + 1) * QUADS * HDIM, :],
            preferred_element_type=F32,
        )
    first = normed(mixed, gain_a_ref[...]).astype(BF16)
    hidden = jnp.maximum(jnp.dot(first, up_ref[...], preferred_element_type=F32), 0.0).astype(BF16)
    total = first.astype(F32) + jnp.dot(hidden, down_ref[...], preferred_element_type=F32)
    result_ref[...] = normed(total, gain_f_ref[...]).astype(BF16)


def finish(features, backs, w_out, w_up, w_down, gain_attn, gain_ffn):
    rows, width = features.shape
    tile = rows // 2

    def once(shape):
        return pl.BlockSpec(shape, lambda i: (0,) * len(shape), pipeline_mode=pl.Buffered(1))

    return pl.pallas_call(
        finish_kernel,
        grid=(2,),
        in_specs=[pl.BlockSpec((tile, width), lambda i: (i, 0))]
        + [pl.BlockSpec((4, 1, 8, HALF, LANES), lambda i: (0, i, 0, 0, 0))] * CHUNKS
        + [
            once(w_out.shape),
            once(w_up.shape),
            once(w_down.shape),
            once((1, width)),
            once((1, width)),
        ],
        out_specs=pl.BlockSpec((tile, width), lambda i: (i, 0)),
        out_shape=jax.ShapeDtypeStruct((rows, width), BF16),
        compiler_params=pltpu.CompilerParams(vmem_limit_bytes=LIMIT),
        name="finish",
    )(
        features,
        *[back.reshape(4, 2, 8, HALF, LANES) for back in backs],
        w_out,
        w_up,
        w_down,
        gain_attn.reshape(1, width),
        gain_ffn.reshape(1, width),
    )


def per_device(
    features, w_query, w_key, w_value, w_out, w_up, w_down, gain_attn, gain_ffn,
    send_list, edge_owner, edge_slot, edge_count,
):
    core = (lax.axis_index("head") % 2).astype(jnp.int32).reshape(1)
    flat_list = send_list.reshape(-1)
    ids = (edge_owner * CAP + edge_slot).reshape(-1)
    across = functools.partial(lax.all_to_all, split_axis=0, concat_axis=0, tiled=True)
    swap = functools.partial(lax.ppermute, axis_name="head", perm=[(i, i ^ 1) for i in range(8)])
    helds = [across(project_keys_values(features, w_key, w_value, c), "head") for c in range(CHUNKS)]
    collected = [collect(held.reshape(128, HALF, LANES), flat_list, core) for held in helds]
    mines = [
        across(out.reshape(16, 16, HALF, LANES), "node").reshape(256, HALF, LANES)
        for out, _ in collected
    ]
    queries = [across(project_queries(features, w_query, c), "head") for c in range(CHUNKS)]
    backs = []
    for c in range(CHUNKS):
        swapped = swap(collected[c][1])
        other = swap(mines[c])
        done = attend(ids, edge_count, core, queries[c], helds[c], swapped, mines[c], other)
        backs.append(across(done, "head"))
    return finish(features, backs, w_out, w_up, w_down, gain_attn, gain_ffn)


def solution(mesh):
    return jax.shard_map(
        per_device,
        mesh=mesh,
        in_specs=(
            P(("node", "head"), None),
            P(), P(), P(), P(), P(), P(), P(), P(),
            P("node", None, None),
            P("node", None),
            P("node", None),
            P("node"),
        ),
        out_specs=P(("node", "head"), None),
        check_vma=False,
    )
```

time: 664 us -> 348 us (0.52)
  local copies, waits for them, and re-layouts: 220 us -> 5.82 us
  waiting for transfers between devices: 285 us -> 126 us
  Pallas kernels: 0 us -> 151 us
  matrix products: 86.2 us -> 0 us
  starting transfers between devices: 11.9 us -> 60.5 us
  other arithmetic: 43.8 us -> 0.01 us
  between operations: 13.6 us -> 0.24 us
    pallas_call x0 -> x13, Pallas kernels: none -> 151 us  [the longest x3 108 us: attend(): pl.pallas_call(attend_kernel, in_specs=[SMEM, SMEM, SMEM, VMEM, ANY, ANY,...]
    gather x17 -> x0, local copies, waits for them, and re-layouts: 109 us -> none  [the longest x16 94.9 us: attend(): remote = jnp.take(incoming_flat, slot_rows.reshape(-1), axis=0)]
    all_to_all x2 -> x12, waiting for transfers between devices: 216 us -> 126 us  [the longest x3 66.3 us: per_device(): across(out.reshape(16, 16, HALF, LANES), 'node').reshape(256, HALF, LANES)]
    dot_general x35 -> x0, matrix products: 86.2 us -> none  [the longest x8 30.5 us: attend(): jnp.einsum('gqhd,gkhd->ghqk', query_rows, remote_keys, preferred_element_...]
    all_gather x1 -> x0, waiting for transfers between devices: 67.8 us -> none  [per_device(): lax.all_gather(features, 'head', axis=0, tiled=True)]
    all_to_all x2 -> x12, starting transfers between devices: 11.9 us -> 58.3 us  [the longest x3 21.7 us: per_device(): across(out.reshape(16, 16, HALF, LANES), 'node').reshape(256, HALF, LANES)]
    slice x20 -> x0, local copies, waits for them, and re-layouts: 40.3 us -> none  [the longest x8 15.4 us: attend(): remote[:, :, :head_cols].reshape(group_size, -1, heads_here, HDIM)]
    dynamic_slice x37 -> x0, local copies, waits for them, and re-layouts: 29.2 us -> none  [the longest x32 18 us: per_device(): lax.map(attend, (query_groups, slot_ids, count_groups, own_groups))]
  transfers between devices with their start and end apart: 3 -> 18, of which waited for: 3 -> 9; matrix products, arithmetic and copies ran while one was open for 4% -> 1% of each run, Pallas kernels for 0% -> 39%
where the time goes in v1:
time: 348 us; the launch traced here: 343 us
  Pallas kernels  151 us (43%)
  waiting for transfers between devices  126 us (36%)
  starting transfers between devices  60.5 us (17%)
  local copies, waits for them, and re-layouts  5.82 us (2%)
    pallas_call x3, Pallas kernels, attend(): pl.pallas_call(attend_kernel, in_specs=[SMEM, SMEM, SMEM, VMEM, ANY, ANY,...  108 us
    all_to_all x3, waiting for transfers between devices, per_device(): across(out.reshape(16, 16, HALF, LANES), 'node').reshape(256, HALF, LANES)  66.3 us
    all_to_all x3, waiting for transfers between devices, per_device(): across(project_keys_values(features, w_key, w_value, c), 'head')  36.5 us
    all_to_all x3, starting transfers between devices, per_device(): across(out.reshape(16, 16, HALF, LANES), 'node').reshape(256, HALF, LANES)  21.7 us
    all_to_all x3, waiting for transfers between devices, per_device(): across(project_queries(features, w_query, c), 'head')  13.8 us
    all_to_all x3, starting transfers between devices, per_device(): backs.append(across(done, 'head'))  13.7 us
    pallas_call x1, Pallas kernels, finish(): pl.pallas_call(finish_kernel, grid=(2,), in_specs=[pl.BlockSpec((tile, wi...  13.7 us
    all_to_all x3, starting transfers between devices, per_device(): across(project_keys_values(features, w_key, w_value, c), 'head')  12.4 us
  transfers between devices with their start and end apart: 18, of which 9 were waited for; matrix products, arithmetic and copies ran while one was open for 1% of the time, Pallas kernels for 39%

profile of v1, /device:TPU:20, one launch (start us, length us, event | category | flops | bytes accessed | tf_op | source)
XLA Modules:
  0.0 342.9 jit_solution(4501244136871789424)
XLA Ops:
  0.0 3.6 %keys_values.3 = bf16[8,16,32,128]{3,2,1,0:T(8,128)(2,1)} custom-call(bf16[1024,768]{1,0:T(8,128)(2,1)} %feat_ref.13, bf16[768,768]{1,0:T(8,128)(2,1)} %key_ref.5, bf16[768,768]{1,0:T(8,128)(2,1)} %value_ref.5), custom_call_target="tpu_custom_call" | custom-call | flops 805306368 | bytes 5242880 | tf_op jit(solution)/shard_map/keys_values/pallas_call | solution.py:78
  3.6 5.3 %all-to-all-start.1 = ((bf16[8,16,32,128]{3,2,1,0:T(8,128)(2,1)}), bf16[8,16,32,128]{3,2,1,0:T(8,128)(2,1)S(1)}, u32[]{:S(2)}, u32[]{:S(2)}) async-start(bf16[8,16,32,128]{3,2,1,0:T(8,128)(2,1)} %keys_values.3), calls=%async_computation.1 | async-start | bytes 2097152 | tf_op jit(solution)/shard_map/all_to_all | solution.py:310
  8.9 3.7 %keys_values.4 = bf16[8,16,32,128]{3,2,1,0:T(8,128)(2,1)} custom-call(bf16[1024,768]{1,0:T(8,128)(2,1)} %feat_ref.13, bf16[768,768]{1,0:T(8,128)(2,1)} %key_ref.5, bf16[768,768]{1,0:T(8,128)(2,1)} %value_ref.5), custom_call_target="tpu_custom_call" | custom-call | flops 805306368 | bytes 5242880 | tf_op jit(solution)/shard_map/keys_values/pallas_call | solution.py:78
  12.6 12.3 %all-to-all-done.1 = bf16[8,16,32,128]{3,2,1,0:T(8,128)(2,1)S(1)} async-done(((bf16[8,16,32,128]{3,2,1,0:T(8,128)(2,1)}), bf16[8,16,32,128]{3,2,1,0:T(8,128)(2,1)S(1)}, u32[]{:S(2)}, u32[]{:S(2)}) %all-to-all-start.1) | async-done | bytes 1048608 | tf_op jit(solution)/shard_map/all_to_all | solution.py:310
  24.9 3.6 %all-to-all-start.5 = ((bf16[8,16,32,128]{3,2,1,0:T(8,128)(2,1)}), bf16[8,16,32,128]{3,2,1,0:T(8,128)(2,1)S(1)}, u32[]{:S(2)}, u32[]{:S(2)}) async-start(bf16[8,16,32,128]{3,2,1,0:T(8,128)(2,1)} %keys_values.4), calls=%async_computation.5 | async-start | bytes 2097152 | tf_op jit(solution)/shard_map/all_to_all | solution.py:310
  28.4 3.6 %keys_values.5 = bf16[8,16,32,128]{3,2,1,0:T(8,128)(2,1)} custom-call(bf16[1024,768]{1,0:T(8,128)(2,1)} %feat_ref.13, bf16[768,768]{1,0:T(8,128)(2,1)} %key_ref.5, bf16[768,768]{1,0:T(8,128)(2,1)} %value_ref.5), custom_call_target="tpu_custom_call" | custom-call | flops 805306368 | bytes 5242880 | tf_op jit(solution)/shard_map/keys_values/pallas_call | solution.py:78
  32.1 12.2 %all-to-all-done.5 = bf16[8,16,32,128]{3,2,1,0:T(8,128)(2,1)S(1)} async-done(((bf16[8,16,32,128]{3,2,1,0:T(8,128)(2,1)}), bf16[8,16,32,128]{3,2,1,0:T(8,128)(2,1)S(1)}, u32[]{:S(2)}, u32[]{:S(2)}) %all-to-all-start.5) | async-done | bytes 1048608 | tf_op jit(solution)/shard_map/all_to_all | solution.py:310
  44.3 3.6 %all-to-all-start.9 = ((bf16[8,16,32,128]{3,2,1,0:T(8,128)(2,1)}), bf16[8,16,32,128]{3,2,1,0:T(8,128)(2,1)S(1)}, u32[]{:S(2)}, u32[]{:S(2)}) async-start(bf16[8,16,32,128]{3,2,1,0:T(8,128)(2,1)} %keys_values.5), calls=%async_computation.9 | async-start | bytes 2097152 | tf_op jit(solution)/shard_map/all_to_all | solution.py:310
  47.9 0.6 reshape.63.list_ref
  48.5 3.2 collect.3
  51.8 12.0 %all-to-all-done.9 = bf16[8,16,32,128]{3,2,1,0:T(8,128)(2,1)S(1)} async-done(((bf16[8,16,32,128]{3,2,1,0:T(8,128)(2,1)}), bf16[8,16,32,128]{3,2,1,0:T(8,128)(2,1)S(1)}, u32[]{:S(2)}, u32[]{:S(2)}) %all-to-all-start.9) | async-done | bytes 1048608 | tf_op jit(solution)/shard_map/all_to_all | solution.py:310
  63.7 1.0 copy-done
  64.7 7.2 %all-to-all-start.2 = ((bf16[16,16,32,128]{3,2,1,0:T(8,128)(2,1)}), bf16[16,16,32,128]{3,2,1,0:T(8,128)(2,1)}, u32[]{:S(2)}, u32[]{:S(2)}) async-start(bf16[16,16,32,128]{3,2,1,0:T(8,128)(2,1)} %bitcast.28), calls=%async_computation.2 | async-start | bytes 4194304 | tf_op jit(solution)/shard_map/all_to_all | solution.py:313
  71.9 3.2 collect.4
  75.2 23.3 %all-to-all-done.2 = bf16[16,16,32,128]{3,2,1,0:T(8,128)(2,1)} async-done(((bf16[16,16,32,128]{3,2,1,0:T(8,128)(2,1)}), bf16[16,16,32,128]{3,2,1,0:T(8,128)(2,1)}, u32[]{:S(2)}, u32[]{:S(2)}) %all-to-all-start.2) | async-done | bytes 2097184 | tf_op jit(solution)/shard_map/all_to_all | solution.py:313
  98.5 7.2 %all-to-all-start.6 = ((bf16[16,16,32,128]{3,2,1,0:T(8,128)(2,1)}), bf16[16,16,32,128]{3,2,1,0:T(8,128)(2,1)S(1)}, u32[]{:S(2)}, u32[]{:S(2)}) async-start(bf16[16,16,32,128]{3,2,1,0:T(8,128)(2,1)} %bitcast.27), calls=%async_computation.6 | async-start | bytes 4194304 | tf_op jit(solution)/shard_map/all_to_all | solution.py:313
  105.7 3.2 collect.5
  108.9 21.6 %all-to-all-done.6 = bf16[16,16,32,128]{3,2,1,0:T(8,128)(2,1)S(1)} async-done(((bf16[16,16,32,128]{3,2,1,0:T(8,128)(2,1)}), bf16[16,16,32,128]{3,2,1,0:T(8,128)(2,1)S(1)}, u32[]{:S(2)}, u32[]{:S(2)}) %all-to-all-start.6) | async-done | bytes 2097184 | tf_op jit(solution)/shard_map/all_to_all | solution.py:313
  130.5 1.4 copy-done.4
  131.9 7.2 %all-to-all-start.10 = ((bf16[16,16,32,128]{3,2,1,0:T(8,128)(2,1)}), bf16[16,16,32,128]{3,2,1,0:T(8,128)(2,1)S(1)}, u32[]{:S(2)}, u32[]{:S(2)}) async-start(bf16[16,16,32,128]{3,2,1,0:T(8,128)(2,1)} %bitcast.26), calls=%async_computation.10 | async-start | bytes 4194304 | tf_op jit(solution)/shard_map/all_to_all | solution.py:313
  139.1 0.5 collective-permute-start.3
  139.6 2.9 queries.3
  142.5 21.4 %all-to-all-done.10 = bf16[16,16,32,128]{3,2,1,0:T(8,128)(2,1)S(1)} async-done(((bf16[16,16,32,128]{3,2,1,0:T(8,128)(2,1)}), bf16[16,16,32,128]{3,2,1,0:T(8,128)(2,1)S(1)}, u32[]{:S(2)}, u32[]{:S(2)}) %all-to-all-start.10) | async-done | bytes 2097184 | tf_op jit(solution)/shard_map/all_to_all | solution.py:313
  163.9 3.5 %all-to-all-start = ((bf16[8,8,32,128]{3,2,1,0:T(8,128)(2,1)}), bf16[8,8,32,128]{3,2,1,0:T(8,128)(2,1)S(1)}, u32[]{:S(2)}, u32[]{:S(2)}) async-start(bf16[8,8,32,128]{3,2,1,0:T(8,128)(2,1)} %queries.3), calls=%async_computation | async-start | bytes 1048576 | tf_op jit(solution)/shard_map/all_to_all | solution.py:316
  167.4 0.4 collective-permute-start.5
  167.8 2.9 queries.4
  170.7 6.9 %all-to-all-done.query_ref = bf16[8,8,32,128]{3,2,1,0:T(8,128)(2,1)S(1)} async-done(((bf16[8,8,32,128]{3,2,1,0:T(8,128)(2,1)}), bf16[8,8,32,128]{3,2,1,0:T(8,128)(2,1)S(1)}, u32[]{:S(2)}, u32[]{:S(2)}) %all-to-all-start) | async-done | bytes 524320 | tf_op jit(solution)/shard_map/all_to_all | solution.py:316
  177.6 3.5 %all-to-all-start.4 = ((bf16[8,8,32,128]{3,2,1,0:T(8,128)(2,1)}), bf16[8,8,32,128]{3,2,1,0:T(8,128)(2,1)S(1)}, u32[]{:S(2)}, u32[]{:S(2)}) async-start(bf16[8,8,32,128]{3,2,1,0:T(8,128)(2,1)} %queries.4), calls=%async_computation.4 | async-start | bytes 1048576 | tf_op jit(solution)/shard_map/all_to_all | solution.py:316
  181.1 0.0 copy-start.13
  181.2 0.4 collective-permute-start
  181.5 2.9 queries.5
  184.5 6.9 %all-to-all-done.4.query_ref = bf16[8,8,32,128]{3,2,1,0:T(8,128)(2,1)S(1)} async-done(((bf16[8,8,32,128]{3,2,1,0:T(8,128)(2,1)}), bf16[8,8,32,128]{3,2,1,0:T(8,128)(2,1)S(1)}, u32[]{:S(2)}, u32[]{:S(2)}) %all-to-all-start.4) | async-done | bytes 524320 | tf_op jit(solution)/shard_map/all_to_all | solution.py:316
  191.4 3.5 %all-to-all-start.8 = ((bf16[8,8,32,128]{3,2,1,0:T(8,128)(2,1)}), bf16[8,8,32,128]{3,2,1,0:T(8,128)(2,1)S(1)}, u32[]{:S(2)}, u32[]{:S(2)}) async-start(bf16[8,8,32,128]{3,2,1,0:T(8,128)(2,1)} %queries.5), calls=%async_computation.8 | async-start | bytes 1048576 | tf_op jit(solution)/shard_map/all_to_all | solution.py:316
  194.9 0.4 collective-permute-start.2
  195.3 0.1 copy.14
  195.4 0.7 reshape.60.id_ref
  196.1 35.9 %attend.3 = bf16[8,8,32,128]{3,2,1,0:T(8,128)(2,1)} custom-call(s32[1024]{0:T(1024)} %reshape.60.id_ref, s32[128]{0:T(128)} %count_ref.5, s32[1]{0:T(128)} %bitcast.core_ref, bf16[8,8,32,128]{3,2,1,0:T(8,128)(2,1)} %copy-done.7, bf16[8,2,8,32,128]{4,3,2,1,0:T(8,128)(2,1)} %bitcast.21, bf16[8,8,32,128]{3,2,1,0:T(8,128)(2,1)} %collective-permute-done.swap_ref, ...), custom_call_target="tpu_custom_call" | custom-call | flops 1207959552 | bytes 6291456 | tf_op jit(solution)/shard_map/attend/pallas_call | solution.py:223
  232.0 4.5 %all-to-all-start.3 = ((bf16[8,8,32,128]{3,2,1,0:T(8,128)(2,1)}), bf16[8,8,32,128]{3,2,1,0:T(8,128)(2,1)S(1)}, u32[]{:S(2)}, u32[]{:S(2)}) async-start(bf16[8,8,32,128]{3,2,1,0:T(8,128)(2,1)} %attend.3), calls=%async_computation.3 | async-start | bytes 1048576 | tf_op jit(solution)/shard_map/all_to_all | solution.py:322
  236.5 0.5 collective-permute-start.4
  237.0 35.9 %attend.4 = bf16[8,8,32,128]{3,2,1,0:T(8,128)(2,1)} custom-call(s32[1024]{0:T(1024)} %reshape.60.id_ref, s32[128]{0:T(128)} %count_ref.5, s32[1]{0:T(128)} %bitcast.core_ref, bf16[8,8,32,128]{3,2,1,0:T(8,128)(2,1)} %copy-done.6, bf16[8,2,8,32,128]{4,3,2,1,0:T(8,128)(2,1)} %bitcast.19, bf16[8,8,32,128]{3,2,1,0:T(8,128)(2,1)} %collective-permute-done.2.swap_ref, ...), custom_call_target="tpu_custom_call" | custom-call | flops 1207959552 | bytes 6291456 | tf_op jit(solution)/shard_map/attend/pallas_call | solution.py:223
  272.9 4.4 %all-to-all-start.7 = ((bf16[8,8,32,128]{3,2,1,0:T(8,128)(2,1)}), bf16[8,8,32,128]{3,2,1,0:T(8,128)(2,1)S(1)}, u32[]{:S(2)}, u32[]{:S(2)}) async-start(bf16[8,8,32,128]{3,2,1,0:T(8,128)(2,1)} %attend.4), calls=%async_computation.7 | async-start | bytes 1048576 | tf_op jit(solution)/shard_map/all_to_all | solution.py:322
  277.4 35.9 %attend.5 = bf16[8,8,32,128]{3,2,1,0:T(8,128)(2,1)} custom-call(s32[1024]{0:T(1024)} %reshape.60.id_ref, s32[128]{0:T(128)} %count_ref.5, s32[1]{0:T(128)} %bitcast.core_ref, bf16[8,8,32,128]{3,2,1,0:T(8,128)(2,1)} %copy-done.5, bf16[8,2,8,32,128]{4,3,2,1,0:T(8,128)(2,1)} %bitcast.17, bf16[8,8,32,128]{3,2,1,0:T(8,128)(2,1)} %collective-permute-done.4.swap_ref, ...), custom_call_target="tpu_custom_call" | custom-call | flops 1207959552 | bytes 6291456 | tf_op jit(solution)/shard_map/attend/pallas_call | solution.py:223
  313.3 4.8 %all-to-all-start.11 = ((bf16[8,8,32,128]{3,2,1,0:T(8,128)(2,1)}), bf16[8,8,32,128]{3,2,1,0:T(8,128)(2,1)S(1)}, u32[]{:S(2)}, u32[]{:S(2)}) async-start(bf16[8,8,32,128]{3,2,1,0:T(8,128)(2,1)} %attend.5), calls=%async_computation.11 | async-start | bytes 1048576 | tf_op jit(solution)/shard_map/all_to_all | solution.py:322
  318.1 0.6 reshape.78.refs_6_
  318.7 0.6 reshape.79.refs_7_
  319.3 9.1 %all-to-all-done.11 = bf16[8,8,32,128]{3,2,1,0:T(8,128)(2,1)S(1)} async-done(((bf16[8,8,32,128]{3,2,1,0:T(8,128)(2,1)}), bf16[8,8,32,128]{3,2,1,0:T(8,128)(2,1)S(1)}, u32[]{:S(2)}, u32[]{:S(2)}) %all-to-all-start.11) | async-done | bytes 524320 | tf_op jit(solution)/shard_map/all_to_all | solution.py:322
  328.4 0.8 copy-done.10
  329.2 13.7 %finish.1 = bf16[1024,768]{1,0:T(8,128)(2,1)} custom-call(bf16[1024,768]{1,0:T(8,128)(2,1)} %feat_ref.13, bf16[4,2,8,32,128]{4,3,2,1,0:T(8,128)(2,1)} %bitcast.29, bf16[4,2,8,32,128]{4,3,2,1,0:T(8,128)(2,1)} %bitcast.30, bf16[4,2,8,32,128]{4,3,2,1,0:T(8,128)(2,1)} %bitcast.31, bf16[768,768]{1,0:T(8,128)(2,1)} %refs_3_.1, bf16[768,1536]{1,0:T(8,128)(2,1)} %refs_4_.1, ...), custom_call_target="tpu_custom_call" | custom-call | tf_op jit(solution)/shard_map/finish/pallas_call | solution.py:274
  (39 shorter events, 0.1 us)
Async XLA Ops:
  3.6 21.2 %all-to-all-start.1 = ((bf16[8,16,32,128]{3,2,1,0:T(8,128)(2,1)}), bf16[8,16,32,128]{3,2,1,0:T(8,128)(2,1)S(1)}, u32[]{:S(2)}, u32[]{:S(2)}) async-start(bf16[8,16,32,128]{3,2,1,0:T(8,128)(2,1)} %keys_values.3), calls=%async_computation.1 | async-start | bytes 2097152 | tf_op jit(solution)/shard_map/all_to_all | solution.py:310
  24.9 7.2 %copy-start.2 = (bf16[8,16,32,128]{3,2,1,0:T(8,128)(2,1)}, bf16[8,16,32,128]{3,2,1,0:T(8,128)(2,1)S(1)}, u32[]{:S(2)}) copy-start(bf16[8,16,32,128]{3,2,1,0:T(8,128)(2,1)S(1)} %all-to-all-done.1) | copy-start | bytes 3145732
  24.9 19.4 %all-to-all-start.5 = ((bf16[8,16,32,128]{3,2,1,0:T(8,128)(2,1)}), bf16[8,16,32,128]{3,2,1,0:T(8,128)(2,1)S(1)}, u32[]{:S(2)}, u32[]{:S(2)}) async-start(bf16[8,16,32,128]{3,2,1,0:T(8,128)(2,1)} %keys_values.4), calls=%async_computation.5 | async-start | bytes 2097152 | tf_op jit(solution)/shard_map/all_to_all | solution.py:310
  32.1 15.8 %copy-start.11 = (s32[1,16,16]{2,1,0:T(8,128)S(1)}, s32[1,16,16]{2,1,0:T(8,128)}, u32[]{:S(2)}) copy-start(s32[1,16,16]{2,1,0:T(8,128)} %param.22) | copy-start | bytes 3076
  44.3 19.4 %copy-start.1 = (bf16[8,16,32,128]{3,2,1,0:T(8,128)(2,1)}, bf16[8,16,32,128]{3,2,1,0:T(8,128)(2,1)S(1)}, u32[]{:S(2)}) copy-start(bf16[8,16,32,128]{3,2,1,0:T(8,128)(2,1)S(1)} %all-to-all-done.5) | copy-start | bytes 3145732
  44.3 19.4 %all-to-all-start.9 = ((bf16[8,16,32,128]{3,2,1,0:T(8,128)(2,1)}), bf16[8,16,32,128]{3,2,1,0:T(8,128)(2,1)S(1)}, u32[]{:S(2)}, u32[]{:S(2)}) async-start(bf16[8,16,32,128]{3,2,1,0:T(8,128)(2,1)} %keys_values.5), calls=%async_computation.9 | async-start | bytes 2097152 | tf_op jit(solution)/shard_map/all_to_all | solution.py:310
  63.7 1.0 copy-start
  64.7 33.8 %all-to-all-start.2 = ((bf16[16,16,32,128]{3,2,1,0:T(8,128)(2,1)}), bf16[16,16,32,128]{3,2,1,0:T(8,128)(2,1)}, u32[]{:S(2)}, u32[]{:S(2)}) async-start(bf16[16,16,32,128]{3,2,1,0:T(8,128)(2,1)} %bitcast.28), calls=%async_computation.2 | async-start | bytes 4194304 | tf_op jit(solution)/shard_map/all_to_all | solution.py:313
  98.5 32.0 %all-to-all-start.6 = ((bf16[16,16,32,128]{3,2,1,0:T(8,128)(2,1)}), bf16[16,16,32,128]{3,2,1,0:T(8,128)(2,1)S(1)}, u32[]{:S(2)}, u32[]{:S(2)}) async-start(bf16[16,16,32,128]{3,2,1,0:T(8,128)(2,1)} %bitcast.27), calls=%async_computation.6 | async-start | bytes 4194304 | tf_op jit(solution)/shard_map/all_to_all | solution.py:313
  130.5 1.4 copy-start.4
  131.9 32.0 %all-to-all-start.10 = ((bf16[16,16,32,128]{3,2,1,0:T(8,128)(2,1)}), bf16[16,16,32,128]{3,2,1,0:T(8,128)(2,1)S(1)}, u32[]{:S(2)}, u32[]{:S(2)}) async-start(bf16[16,16,32,128]{3,2,1,0:T(8,128)(2,1)} %bitcast.26), calls=%async_computation.10 | async-start | bytes 4194304 | tf_op jit(solution)/shard_map/all_to_all | solution.py:313
  139.1 57.0 %collective-permute-start.1 = (bf16[256,32,128]{2,1,0:T(8,128)(2,1)}, bf16[256,32,128]{2,1,0:T(8,128)(2,1)}, u32[]{:S(2)}, u32[]{:S(2)}) collective-permute-start(bf16[256,32,128]{2,1,0:T(8,128)(2,1)} %bitcast.4.mine_ref), channel_id=1, source_target_pairs={{0,1},{1,0},{2,3},{3,2},{4,5},{5,4},{6,7},{7,6},{8,9},{9,8},{10,11... | collective-permute-start | bytes 6291464 | tf_op jit(solution)/shard_map/ppermute | solution.py:320
  139.1 97.9 %collective-permute-start.3 = (bf16[256,32,128]{2,1,0:T(8,128)(2,1)}, bf16[256,32,128]{2,1,0:T(8,128)(2,1)}, u32[]{:S(2)}, u32[]{:S(2)}) collective-permute-start(bf16[256,32,128]{2,1,0:T(8,128)(2,1)} %bitcast.24), channel_id=1, source_target_pairs={{0,1},{1,0},{2,3},{3,2},{4,5},{5,4},{6,7},{7,6},{8,9},{9,8},{10,11... | collective-permute-start | bytes 6291464 | tf_op jit(solution)/shard_map/ppermute | solution.py:320
  163.9 6.8 %copy-start.3 = (bf16[16,16,32,128]{3,2,1,0:T(8,128)(2,1)}, bf16[16,16,32,128]{3,2,1,0:T(8,128)(2,1)S(1)}, u32[]{:S(2)}) copy-start(bf16[16,16,32,128]{3,2,1,0:T(8,128)(2,1)S(1)} %all-to-all-done.10) | copy-start | bytes 6291460
  163.9 13.7 %all-to-all-start = ((bf16[8,8,32,128]{3,2,1,0:T(8,128)(2,1)}), bf16[8,8,32,128]{3,2,1,0:T(8,128)(2,1)S(1)}, u32[]{:S(2)}, u32[]{:S(2)}) async-start(bf16[8,8,32,128]{3,2,1,0:T(8,128)(2,1)} %queries.3), calls=%async_computation | async-start | bytes 1048576 | tf_op jit(solution)/shard_map/all_to_all | solution.py:316
  167.4 109.9 %collective-permute-start.5 = (bf16[256,32,128]{2,1,0:T(8,128)(2,1)S(1)}, bf16[256,32,128]{2,1,0:T(8,128)(2,1)}, u32[]{:S(2)}, u32[]{:S(2)}) collective-permute-start(bf16[256,32,128]{2,1,0:T(8,128)(2,1)S(1)} %bitcast.22), channel_id=1, source_target_pairs={{0,1},{1,0},{2,3},{3,2},{4,5},{5,4},{6,7},{7,6},{8,9},{9,8},{10,11... | collective-permute-start | bytes 6291464 | tf_op jit(solution)/shard_map/ppermute | solution.py:320
  177.6 6.9 %copy-start.7 = (bf16[8,8,32,128]{3,2,1,0:T(8,128)(2,1)}, bf16[8,8,32,128]{3,2,1,0:T(8,128)(2,1)S(1)}, u32[]{:S(2)}) copy-start(bf16[8,8,32,128]{3,2,1,0:T(8,128)(2,1)S(1)} %all-to-all-done.query_ref) | copy-start | bytes 1572868
  177.6 13.7 %all-to-all-start.4 = ((bf16[8,8,32,128]{3,2,1,0:T(8,128)(2,1)}), bf16[8,8,32,128]{3,2,1,0:T(8,128)(2,1)S(1)}, u32[]{:S(2)}, u32[]{:S(2)}) async-start(bf16[8,8,32,128]{3,2,1,0:T(8,128)(2,1)} %queries.4), calls=%async_computation.4 | async-start | bytes 1048576 | tf_op jit(solution)/shard_map/all_to_all | solution.py:316
  181.1 14.1 %copy-start.12 = (s32[128,8]{0,1:T(8,128)S(1)}, s32[128,8]{0,1:T(8,128)}, u32[]{:S(2)}) copy-start(s32[128,8]{0,1:T(8,128)} %param.24) | copy-start | bytes 12292
  181.1 14.1 %copy-start.13 = (s32[128,8]{0,1:T(8,128)S(1)}, s32[128,8]{0,1:T(8,128)}, u32[]{:S(2)}) copy-start(s32[128,8]{0,1:T(8,128)} %param.23) | copy-start | bytes 12292
  181.2 14.9 %collective-permute-start = (bf16[8,8,32,128]{3,2,1,0:T(8,128)(2,1)}, bf16[8,8,32,128]{3,2,1,0:T(8,128)(2,1)}, u32[]{:S(2)}, u32[]{:S(2)}) collective-permute-start(bf16[8,8,32,128]{3,2,1,0:T(8,128)(2,1)} %get-tuple-element.11), channel_id=1, source_target_pairs={{0,1},{1,0},{2,3},{3,2},{4,5},{5,4},{6,7},{7,6},{8,9},{9,8},{10,11... | collective-permute-start | bytes 1572872 | tf_op jit(solution)/shard_map/ppermute | solution.py:319
  191.4 40.6 %copy-start.6 = (bf16[8,8,32,128]{3,2,1,0:T(8,128)(2,1)}, bf16[8,8,32,128]{3,2,1,0:T(8,128)(2,1)S(1)}, u32[]{:S(2)}) copy-start(bf16[8,8,32,128]{3,2,1,0:T(8,128)(2,1)S(1)} %all-to-all-done.4.query_ref) | copy-start | bytes 1572868
  191.4 40.6 %all-to-all-start.8 = ((bf16[8,8,32,128]{3,2,1,0:T(8,128)(2,1)}), bf16[8,8,32,128]{3,2,1,0:T(8,128)(2,1)S(1)}, u32[]{:S(2)}, u32[]{:S(2)}) async-start(bf16[8,8,32,128]{3,2,1,0:T(8,128)(2,1)} %queries.5), calls=%async_computation.8 | async-start | bytes 1048576 | tf_op jit(solution)/shard_map/all_to_all | solution.py:316
  194.9 42.1 %collective-permute-start.2 = (bf16[8,8,32,128]{3,2,1,0:T(8,128)(2,1)}, bf16[8,8,32,128]{3,2,1,0:T(8,128)(2,1)}, u32[]{:S(2)}, u32[]{:S(2)}) collective-permute-start(bf16[8,8,32,128]{3,2,1,0:T(8,128)(2,1)} %get-tuple-element.13), channel_id=1, source_target_pairs={{0,1},{1,0},{2,3},{3,2},{4,5},{5,4},{6,7},{7,6},{8,9},{9,8},{10,11... | collective-permute-start | bytes 1572872 | tf_op jit(solution)/shard_map/ppermute | solution.py:319
  232.0 40.9 %copy-start.5 = (bf16[8,8,32,128]{3,2,1,0:T(8,128)(2,1)}, bf16[8,8,32,128]{3,2,1,0:T(8,128)(2,1)S(1)}, u32[]{:S(2)}) copy-start(bf16[8,8,32,128]{3,2,1,0:T(8,128)(2,1)S(1)} %all-to-all-done.8.query_ref) | copy-start | bytes 1572868
  232.0 40.9 %all-to-all-start.3 = ((bf16[8,8,32,128]{3,2,1,0:T(8,128)(2,1)}), bf16[8,8,32,128]{3,2,1,0:T(8,128)(2,1)S(1)}, u32[]{:S(2)}, u32[]{:S(2)}) async-start(bf16[8,8,32,128]{3,2,1,0:T(8,128)(2,1)} %attend.3), calls=%async_computation.3 | async-start | bytes 1048576 | tf_op jit(solution)/shard_map/all_to_all | solution.py:322
  236.5 40.8 %collective-permute-start.4 = (bf16[8,8,32,128]{3,2,1,0:T(8,128)(2,1)}, bf16[8,8,32,128]{3,2,1,0:T(8,128)(2,1)}, u32[]{:S(2)}, u32[]{:S(2)}) collective-permute-start(bf16[8,8,32,128]{3,2,1,0:T(8,128)(2,1)} %get-tuple-element.15), channel_id=1, source_target_pairs={{0,1},{1,0},{2,3},{3,2},{4,5},{5,4},{6,7},{7,6},{8,9},{9,8},{10,11... | collective-permute-start | bytes 1572872 | tf_op jit(solution)/shard_map/ppermute | solution.py:319
  272.9 40.4 %copy-start.8 = (bf16[8,8,32,128]{3,2,1,0:T(8,128)(2,1)}, bf16[8,8,32,128]{3,2,1,0:T(8,128)(2,1)S(1)}, u32[]{:S(2)}) copy-start(bf16[8,8,32,128]{3,2,1,0:T(8,128)(2,1)S(1)} %all-to-all-done.3) | copy-start | bytes 1572868
  272.9 40.4 %all-to-all-start.7 = ((bf16[8,8,32,128]{3,2,1,0:T(8,128)(2,1)}), bf16[8,8,32,128]{3,2,1,0:T(8,128)(2,1)S(1)}, u32[]{:S(2)}, u32[]{:S(2)}) async-start(bf16[8,8,32,128]{3,2,1,0:T(8,128)(2,1)} %attend.4), calls=%async_computation.7 | async-start | bytes 1048576 | tf_op jit(solution)/shard_map/all_to_all | solution.py:322
  277.3 40.8 %copy-start.14 = (f32[768]{0:T(1024)S(1)}, f32[768]{0:T(1024)}, u32[]{:S(2)}) copy-start(f32[768]{0:T(1024)} %param.20) | copy-start | bytes 9220
  277.3 41.3 %copy-start.15 = (f32[768]{0:T(1024)S(1)}, f32[768]{0:T(1024)}, u32[]{:S(2)}) copy-start(f32[768]{0:T(1024)} %param.21) | copy-start | bytes 9220
  313.3 15.1 %copy-start.9 = (bf16[8,8,32,128]{3,2,1,0:T(8,128)(2,1)}, bf16[8,8,32,128]{3,2,1,0:T(8,128)(2,1)S(1)}, u32[]{:S(2)}) copy-start(bf16[8,8,32,128]{3,2,1,0:T(8,128)(2,1)S(1)} %all-to-all-done.7) | copy-start | bytes 1572868
  313.3 15.1 %all-to-all-start.11 = ((bf16[8,8,32,128]{3,2,1,0:T(8,128)(2,1)}), bf16[8,8,32,128]{3,2,1,0:T(8,128)(2,1)S(1)}, u32[]{:S(2)}, u32[]{:S(2)}) async-start(bf16[8,8,32,128]{3,2,1,0:T(8,128)(2,1)} %attend.5), calls=%async_computation.11 | async-start | bytes 1048576 | tf_op jit(solution)/shard_map/all_to_all | solution.py:322
  328.4 0.8 copy-start.10

commit v2 on v1

v2 whole, which is shorter than its diff:
```python
import functools
import math

import jax
import jax.numpy as jnp
from jax import lax
from jax.experimental import pallas as pl
from jax.experimental.pallas import tpu as pltpu
from jax.sharding import PartitionSpec as P


HDIM = 64
BLOCK = 64
MAXK = 8
CAP = 16
HALF = BLOCK // 2
LANES = 2 * HDIM
CHUNKS = 3
CHIPS = 4
COLS = CHIPS * HDIM
OWN = 16
SCALE = 1.4426950408889634 / math.sqrt(HDIM)
MASKED = -8e30
F32 = jnp.float32
BF16 = jnp.bfloat16
VMEM = pl.BlockSpec(memory_space=pltpu.VMEM)
SMEM = pl.BlockSpec(memory_space=pltpu.SMEM)
ANY = pl.BlockSpec(memory_space=pl.ANY)
LIMIT = 60 * 1024 * 1024
TILE = (HALF, LANES)


def low_lanes(rows):
    return lax.broadcasted_iota(jnp.int32, (rows, LANES), 1) < HDIM


def pack_pair(both):
    blocks = both.shape[0] // BLOCK
    split = both.reshape(blocks, 2, HALF, LANES)
    first = split[:, 0].reshape(blocks * HALF, LANES)
    second = split[:, 1].reshape(blocks * HALF, LANES)
    low = low_lanes(blocks * HALF)
    even = jnp.where(low, first, pltpu.roll(second, HDIM, 1))
    odd = jnp.where(low, pltpu.roll(first, HDIM, 1), second)
    return [part.reshape(blocks, HALF, LANES).astype(BF16) for part in (even, odd)]


def unpack_pair(even, odd):
    blocks = even.shape[0]
    even = even.reshape(blocks * HALF, LANES).astype(F32)
    odd = odd.reshape(blocks * HALF, LANES).astype(F32)
    low = low_lanes(blocks * HALF)
    first = jnp.where(low, even, pltpu.roll(odd, HDIM, 1)).reshape(blocks, 1, HALF, LANES)
    second = jnp.where(low, pltpu.roll(even, HDIM, 1), odd).reshape(blocks, 1, HALF, LANES)
    return jnp.concatenate([first, second], axis=1).reshape(blocks * BLOCK, LANES).astype(BF16)


def params():
    return pltpu.CompilerParams(vmem_limit_bytes=LIMIT)


def keys_values_kernel(chunk, place_ref, near_ref, far_ref, key_ref, value_ref, *refs):
    outs, (weight, packed, sem) = refs[:CHIPS], refs[CHIPS:]
    z, core = place_ref[0], place_ref[1]

    def fetch(source):
        copy = pltpu.make_async_copy(source.at[:, chunk * COLS : (chunk + 1) * COLS], weight, sem)
        copy.start()
        copy.wait()

    @pl.when(core == 0)
    def _():
        fetch(key_ref)

    @pl.when(core == 1)
    def _():
        fetch(value_ref)

    for owner, feat_ref in ((core, near_ref), (1 - core, far_ref)):
        for half in range(2):
            made = jnp.dot(
                feat_ref[half * 512 : half * 512 + 512, :], weight[...], preferred_element_type=F32
            )
            for pair in range(2):
                both = pack_pair(made[:, pair * LANES : (pair + 1) * LANES])
                for side in range(2):
                    packed[2 * pair + side, pl.ds(owner * OWN + half * 8, 8)] = both[side]
    for step in range(CHIPS):
        outs[step][...] = packed[lax.rem(z + step, CHIPS)]


def project_keys_values(place, near, far, w_key, w_value, chunk):
    rows, width = near.shape
    return pl.pallas_call(
        functools.partial(keys_values_kernel, chunk),
        in_specs=[SMEM, VMEM, VMEM, ANY, ANY],
        out_specs=[VMEM] * CHIPS,
        out_shape=[jax.ShapeDtypeStruct((2 * OWN,) + TILE, BF16)] * CHIPS,
        scratch_shapes=[
            pltpu.VMEM((width, COLS), BF16),
            pltpu.VMEM((CHIPS, 2 * OWN) + TILE, BF16),
            pltpu.SemaphoreType.DMA,
        ],
        compiler_params=params(),
        cost_estimate=pl.CostEstimate(
            flops=4 * rows * width * COLS, bytes_accessed=5 << 20, transcendentals=0
        ),
        name="keys_values",
    )(place, near, far, w_key, w_value)


def queries_kernel(place_ref, feat_ref, query_ref, *refs):
    outs, (packed,) = refs[:CHIPS], refs[CHIPS:]
    z = place_ref[0]
    for chunk in range(CHUNKS):
        for half in range(2):
            made = jnp.dot(
                feat_ref[half * 512 : half * 512 + 512, :],
                query_ref[:, chunk * COLS : (chunk + 1) * COLS],
                preferred_element_type=F32,
            )
            for pair in range(2):
                both = pack_pair(made[:, pair * LANES : (pair + 1) * LANES])
                for side in range(2):
                    packed[2 * pair + side, chunk, half * 8 : half * 8 + 8] = both[side]
    for step in range(CHIPS):
        outs[step][...] = packed[lax.rem(z + step, CHIPS)]


def project_queries(place, features, w_query):
    rows, width = features.shape
    return pl.pallas_call(
        queries_kernel,
        in_specs=[SMEM, VMEM, VMEM],
        out_specs=[VMEM] * CHIPS,
        out_shape=[jax.ShapeDtypeStruct((CHUNKS, OWN) + TILE, BF16)] * CHIPS,
        scratch_shapes=[pltpu.VMEM((CHIPS, CHUNKS, OWN) + TILE, BF16)],
        compiler_params=params(),
        cost_estimate=pl.CostEstimate(
            flops=2 * rows * width * width, bytes_accessed=5 << 20, transcendentals=0
        ),
        name="queries",
    )(place, features, w_query)


def collect_kernel(list_ref, place_ref, *refs):
    parts, (out_ref, own_ref, swap_ref, held) = refs[:CHIPS], refs[CHIPS:]
    z, core = place_ref[0], place_ref[1]
    for step in range(CHIPS):
        source = lax.rem(z + CHIPS - step, CHIPS)
        held[pl.ds(source * 2 * OWN, 2 * OWN)] = parts[step][...]

    def body(step, carry):
        for extra in range(8):
            slot = step * 8 + extra
            out_ref[slot] = held[list_ref[slot]]
        return carry

    lax.fori_loop(0, out_ref.shape[0] // 8, body, 0)
    for source in range(CHIPS):
        own_ref[source] = held[pl.ds(source * 2 * OWN + core * OWN, OWN)]
        swap_ref[source] = held[pl.ds(source * 2 * OWN + (1 - core) * OWN, OWN)]


def collect(flat_list, place, parts):
    slots = flat_list.shape[0]
    own = jax.ShapeDtypeStruct((CHIPS, OWN) + TILE, BF16)
    return pl.pallas_call(
        collect_kernel,
        in_specs=[SMEM, SMEM] + [VMEM] * CHIPS,
        out_specs=[VMEM] * 3,
        out_shape=[jax.ShapeDtypeStruct((slots,) + TILE, BF16), own, own],
        scratch_shapes=[pltpu.VMEM((CHIPS * 2 * OWN,) + TILE, BF16)],
        compiler_params=params(),
        cost_estimate=pl.CostEstimate(flops=0, bytes_accessed=5 << 20, transcendentals=0),
        name="collect",
    )(flat_list, place, *parts)


def attend_kernel(id_ref, count_ref, place_ref, *refs):
    parts, (own_ref, swap_ref, mine_ref, other_ref) = refs[:CHIPS], refs[CHIPS : CHIPS + 4]
    outs = refs[CHIPS + 4 : 2 * CHIPS + 4]
    queries, made, keys, values, own_keys, own_values, sems = refs[2 * CHIPS + 4 :]
    z, core = place_ref[0], place_ref[1]

    def fetch(near, near_own, far, far_own):
        copies = [
            pltpu.make_async_copy(own_ref, near_own, sems.at[0]),
            pltpu.make_async_copy(swap_ref, far_own, sems.at[1]),
            pltpu.make_async_copy(mine_ref, near, sems.at[2]),
            pltpu.make_async_copy(other_ref, far, sems.at[3]),
        ]
        for copy in copies:
            copy.start()
        for copy in copies:
            copy.wait()

    @pl.when(core == 0)
    def _():
        fetch(keys, own_keys, values, own_values)

    @pl.when(core == 1)
    def _():
        fetch(values, own_values, keys, own_keys)

    for step in range(CHIPS):
        queries[lax.rem(z + CHIPS - step, CHIPS)] = parts[step][0]

    low = low_lanes(HALF)
    lane = lax.broadcasted_iota(jnp.int32, (1, LANES), 1)
    dims = (((1,), (1,)), ((), ()))
    rows = 2 * BLOCK
    group = 8

    def attend_group(at, carry):
        source, first = at // 2, (at % 2) * group
        blocks = [source * 2 * OWN + core * OWN + first + k for k in range(group)]
        slots = [[id_ref[block * MAXK + entry] for entry in range(MAXK)] for block in blocks]
        left = []
        for k in range(group):
            query = queries[source, first + k].astype(F32)
            turned = pltpu.roll(query, HDIM, 1)
            zero = jnp.zeros_like(query)
            left.append(
                jnp.concatenate(
                    [
                        jnp.where(low, query, zero),
                        jnp.where(low, turned, zero),
                        jnp.where(low, zero, turned),
                        jnp.where(low, zero, query),
                    ],
                    axis=0,
                ).astype(BF16)
            )
        near = []
        for quad in range(group // 4):
            four = own_keys[source, pl.ds(first + 4 * quad, 4)].reshape(LANES, LANES)
            scores = lax.dot_general(
                jnp.concatenate(left[4 * quad : 4 * quad + 4], axis=0),
                four,
                dims,
                preferred_element_type=F32,
            )
            for j in range(4):
                near.append(
                    jnp.where(lane // HALF == j, scores[j * rows : (j + 1) * rows], MASKED)
                )
        far = []
        for k in range(group):
            far_keys = jnp.concatenate([keys[slot] for slot in slots[k]], axis=0)
            scores = lax.dot_general(left[k], far_keys, dims, preferred_element_type=F32)
            limit = count_ref[blocks[k]] * HALF
            far.append(
                [
                    jnp.where(lane < limit, scores[:, :LANES], MASKED),
                    jnp.where(lane + LANES < limit, scores[:, LANES:], MASKED),
                ]
            )
        tops = []
        for k in range(group):
            top = jnp.maximum(jnp.maximum(far[k][0], far[k][1]), near[k])
            top = jnp.max(jnp.maximum(top[:BLOCK], top[BLOCK:]), axis=1, keepdims=True)
            tops.append(jnp.concatenate([top, top], axis=0))
        far = [[jnp.exp2((part - tops[k]) * SCALE) for part in far[k]] for k in range(group)]
        near = [jnp.exp2((near[k] - tops[k]) * SCALE) for k in range(group)]
        summed = []
        for quad in range(group // 4):
            four = own_values[source, pl.ds(first + 4 * quad, 4)].reshape(LANES, LANES)
            weights = [near[4 * quad + j].astype(BF16) for j in range(4)]
            product = jnp.dot(
                jnp.concatenate(weights, axis=0), four, preferred_element_type=F32
            )
            summed += [product[j * rows : (j + 1) * rows] for j in range(4)]
        for k in range(group):
            far_values = jnp.concatenate([values[slot] for slot in slots[k]], axis=0)
            weights = jnp.concatenate([part.astype(BF16) for part in far[k]], axis=1)
            summed[k] = summed[k] + jnp.dot(weights, far_values, preferred_element_type=F32)
        for k in range(group):
            total = far[k][0] + far[k][1] + near[k]
            total = jnp.sum(total[:BLOCK] + total[BLOCK:], axis=1, keepdims=True)
            share = 1.0 / total
            share = jnp.where(low, share[:HALF], share[HALF:])
            straight = jnp.where(low, summed[k][:HALF], summed[k][3 * HALF :])
            crossed = jnp.where(low, summed[k][HALF : 2 * HALF], summed[k][2 * HALF : 3 * HALF])
            result = (straight + pltpu.roll(crossed, HDIM, 1)) * share
            made[source, first + k] = result.astype(BF16)
        return carry

    lax.fori_loop(0, CHIPS * OWN // group, attend_group, 0)
    for step in range(CHIPS):
        outs[step][...] = made[lax.rem(z + step, CHIPS)]


def attend(ids, counts, place, queries, own, swapped, mine, other, chunk):
    slots = mine.shape[0]
    blocks = pltpu.VMEM((CHIPS, OWN) + TILE, BF16)
    return pl.pallas_call(
        attend_kernel,
        grid=(1,),
        in_specs=[SMEM, SMEM, SMEM]
        + [pl.BlockSpec((1, OWN) + TILE, lambda i: (chunk, 0, 0, 0))] * CHIPS
        + [ANY] * 4,
        out_specs=[VMEM] * CHIPS,
        out_shape=[jax.ShapeDtypeStruct((OWN,) + TILE, BF16)] * CHIPS,
        scratch_shapes=[
            blocks,
            blocks,
            pltpu.VMEM((slots,) + TILE, BF16),
            pltpu.VMEM((slots,) + TILE, BF16),
            blocks,
            blocks,
            pltpu.SemaphoreType.DMA((4,)),
        ],
        compiler_params=params(),
        cost_estimate=pl.CostEstimate(
            flops=64 * 4 * 128 * 128 * 384, bytes_accessed=8 << 20, transcendentals=64 * 128 * 384
        ),
        name="attend",
    )(ids, counts, place, *queries, own, swapped, mine, other)


def normed(values, gain):
    center = values - jnp.mean(values, axis=-1, keepdims=True)
    spread = jnp.mean(center * center, axis=-1, keepdims=True)
    return center * lax.rsqrt(spread + 1e-05) * gain


def finish_kernel(place_ref, feat_ref, *refs):
    backs = refs[: CHUNKS * CHIPS]
    out_w_ref, up_ref, down_ref, gain_a_ref, gain_f_ref, result_ref = refs[CHUNKS * CHIPS :][:6]
    attended, out_w, up, down, sems = refs[CHUNKS * CHIPS + 6 :]
    copies = [
        pltpu.make_async_copy(out_w_ref, out_w, sems.at[0]),
        pltpu.make_async_copy(up_ref, up, sems.at[1]),
        pltpu.make_async_copy(down_ref, down, sems.at[2]),
    ]
    for copy in copies:
        copy.start()
    z = place_ref[0]
    for chunk in range(CHUNKS):
        for step in range(CHIPS):
            source = lax.rem(z + CHIPS - step, CHIPS)
            attended[chunk, source] = backs[chunk * CHIPS + step][...]
    rows = feat_ref.shape[0] // 2
    firsts = []
    copies[0].wait()
    for half in range(2):
        at = slice(half * rows, (half + 1) * rows)
        mixed = feat_ref[at, :].astype(F32)
        for chunk in range(CHUNKS):
            pieces = [
                unpack_pair(
                    attended[chunk, 2 * pair, half * 8 : half * 8 + 8],
                    attended[chunk, 2 * pair + 1, half * 8 : half * 8 + 8],
                )
                for pair in range(2)
            ]
            mixed = mixed + jnp.dot(
                jnp.concatenate(pieces, axis=1),
                out_w[chunk * COLS : (chunk + 1) * COLS, :],
                preferred_element_type=F32,
            )
        firsts.append(normed(mixed, gain_a_ref[...]).astype(BF16))
    copies[1].wait()
    copies[2].wait()
    for half in range(2):
        at = slice(half * rows, (half + 1) * rows)
        first = firsts[half]
        hidden = jnp.maximum(jnp.dot(first, up[...], preferred_element_type=F32), 0.0).astype(BF16)
        total = first.astype(F32) + jnp.dot(hidden, down[...], preferred_element_type=F32)
        result_ref[at, :] = normed(total, gain_f_ref[...]).astype(BF16)


def finish(place, features, backs, w_out, w_up, w_down, gain_attn, gain_ffn):
    rows, width = features.shape
    return pl.pallas_call(
        finish_kernel,
        in_specs=[SMEM, VMEM] + [VMEM] * (CHUNKS * CHIPS) + [ANY] * 3 + [VMEM] * 2,
        out_specs=VMEM,
        out_shape=jax.ShapeDtypeStruct((rows, width), BF16),
        scratch_shapes=[
            pltpu.VMEM((CHUNKS, CHIPS, OWN) + TILE, BF16),
            pltpu.VMEM(w_out.shape, BF16),
            pltpu.VMEM(w_up.shape, BF16),
            pltpu.VMEM(w_down.shape, BF16),
            pltpu.SemaphoreType.DMA((3,)),
        ],
        compiler_params=params(),
        name="finish",
    )(
        place,
        features,
        *[part for back in backs for part in back],
        w_out,
        w_up,
        w_down,
        gain_attn.reshape(1, width),
        gain_ffn.reshape(1, width),
    )


def swap(array):
    return lax.ppermute(array, "head", [(i, i ^ 1) for i in range(2 * CHIPS)])


def along_z(parts):
    moved = [parts[0]]
    for step in range(1, CHIPS):
        moved.append(
            lax.ppermute(
                parts[step], "head", [(i, (i + 2 * step) % (2 * CHIPS)) for i in range(2 * CHIPS)]
            )
        )
    return moved


def per_device(
    features, w_query, w_key, w_value, w_out, w_up, w_down, gain_attn, gain_ffn,
    send_list, edge_owner, edge_slot, edge_count,
):
    head = lax.axis_index("head").astype(jnp.int32)
    place = jnp.stack([head // 2, head % 2])
    groups = send_list.shape[1]
    flat_list = send_list.reshape(-1)
    ids = (edge_owner * CAP + edge_slot).reshape(-1)
    far = swap(features)
    collected = []
    for c in range(CHUNKS):
        parts = project_keys_values(place, features, far, w_key, w_value, c)
        parts = along_z(parts)
        collected.append(collect(flat_list, place, parts))
    queries = along_z(project_queries(place, features, w_query))
    mines = []
    for c in range(CHUNKS):
        sent = collected[c][0].reshape((groups, CAP) + TILE)
        got = lax.all_to_all(sent, "node", split_axis=0, concat_axis=0, tiled=True)
        mines.append(got.reshape((groups * CAP,) + TILE))
    backs = []
    for c in range(CHUNKS):
        swapped = swap(collected[c][2])
        other = swap(mines[c])
        done = attend(ids, edge_count, place, queries, collected[c][1], swapped, mines[c], other, c)
        backs.append(along_z(done))
    return finish(place, features, backs, w_out, w_up, w_down, gain_attn, gain_ffn)


def solution(mesh):
    return jax.shard_map(
        per_device,
        mesh=mesh,
        in_specs=(
            P(("node", "head"), None),
            P(), P(), P(), P(), P(), P(), P(), P(),
            P("node", None, None),
            P("node", None),
            P("node", None),
            P("node"),
        ),
        out_specs=P(("node", "head"), None),
        check_vma=False,
    )
```

time: 348 us -> 237 us (0.68)
  Pallas kernels: 151 us -> 84.1 us
  waiting for transfers between devices: 126 us -> 81.8 us
    all_to_all x12 -> x3, waiting for transfers between devices: 126 us -> 26.6 us  [per_device(): got = lax.all_to_all(sent, 'node', split_axis=0, concat_axis=0, tiled=True)]
    pallas_call x13 -> x11, Pallas kernels: 151 us -> 84.1 us  [the longest x3 40.6 us: attend(): pl.pallas_call(attend_kernel, grid=(1,), in_specs=[SMEM, SMEM, SMEM] + [p...]
    ppermute x6 -> x28, waiting for transfers between devices: 0.02 us -> 55.2 us  [the longest x21 51.7 us: along_z(): lax.ppermute(parts[step], 'head', [(i, (i + 2 * step) % (2 * CHIPS)) for...]
    all_to_all x12 -> x3, starting transfers between devices: 58.3 us -> 22 us  [per_device(): got = lax.all_to_all(sent, 'node', split_axis=0, concat_axis=0, tiled=True)]
    ppermute x6 -> x28, starting transfers between devices: 2.2 us -> 38.3 us  [the longest x21 37.6 us: along_z(): lax.ppermute(parts[step], 'head', [(i, (i + 2 * step) % (2 * CHIPS)) for...]
  transfers between devices with their start and end apart: 18 -> 31, of which waited for: 9 -> 16; matrix products, arithmetic and copies ran while one was open for 1% -> 1% of each run, Pallas kernels for 39% -> 27%
where the time goes in v2:
time: 237 us; the launch traced here: 234 us
  Pallas kernels  84.1 us (35%)
  waiting for transfers between devices  81.8 us (35%)
  starting transfers between devices  60.4 us (25%)
  local copies, waits for them, and re-layouts  6.7 us (3%)
    ppermute x21, waiting for transfers between devices, along_z(): lax.ppermute(parts[step], 'head', [(i, (i + 2 * step) % (2 * CHIPS)) for...  51.7 us
    pallas_call x3, Pallas kernels, attend(): pl.pallas_call(attend_kernel, grid=(1,), in_specs=[SMEM, SMEM, SMEM] + [p...  40.6 us
    ppermute x21, starting transfers between devices, along_z(): lax.ppermute(parts[step], 'head', [(i, (i + 2 * step) % (2 * CHIPS)) for...  37.6 us
    all_to_all x3, waiting for transfers between devices, per_device(): got = lax.all_to_all(sent, 'node', split_axis=0, concat_axis=0, tiled=True)  26.6 us
    all_to_all x3, starting transfers between devices, per_device(): got = lax.all_to_all(sent, 'node', split_axis=0, concat_axis=0, tiled=True)  22 us
    pallas_call x3, Pallas kernels, project_keys_values(): pl.pallas_call(functools.partial(keys_values_kernel, chunk), in_specs=[SM...  14.8 us
    pallas_call x1, Pallas kernels, finish(): pl.pallas_call(finish_kernel, in_specs=[SMEM, VMEM] + [VMEM] * (CHUNKS *...  13.5 us
    pallas_call x3, Pallas kernels, collect(): pl.pallas_call(collect_kernel, in_specs=[SMEM, SMEM] + [VMEM] * CHIPS, ou...  10.4 us
  transfers between devices with their start and end apart: 31, of which 16 were waited for; matrix products, arithmetic and copies ran while one was open for 1% of the time, Pallas kernels for 27%

profile of v2, /device:TPU:20, one launch (start us, length us, event | category | flops | bytes accessed | tf_op | source)
XLA Modules:
  0.0 234.1 jit_solution(14521099682556153144)
XLA Ops:
  0.7 3.0 %collective-permute-done.3.far_ref = bf16[1024,768]{1,0:T(8,128)(2,1)S(1)} collective-permute-done((bf16[1024,768]{1,0:T(8,128)(2,1)}, bf16[1024,768]{1,0:T(8,128)(2,1)S(1)}, u32[]{:S(2)}, u32[]{:S(2)}) %collective-permute-start.3) | collective-permute-done | bytes 1572896 | tf_op jit(solution)/shard_map/ppermute | solution.py:403
  3.6 1.1 copy-done
  4.8 5.0 %keys_values.3 = (bf16[32,32,128]{2,1,0:T(8,128)(2,1)}, bf16[32,32,128]{2,1,0:T(8,128)(2,1)}, bf16[32,32,128]{2,1,0:T(8,128)(2,1)}, bf16[32,32,128]{2,1,0:T(8,128)(2,1)}) custom-call(s32[2]{0:T(128)} %pad_add_fusion.place_ref, bf16[1024,768]{1,0:T(8,128)(2,1)} %feat_ref.3, bf16[1024,768]{1,0:T(8,128)(2,1)} %copy-done, bf16[768,768]{1,0:T(8,128)(2,1)} %key_ref.5, ...), custom_call_target="tpu_custom_call" | custom-call | flops 805306368 | bytes 5242880 | tf_op jit(solution)/shard_map/keys_values/pallas_call | solution.py:94
  9.8 2.0 collective-permute-start.4
  11.7 3.6 %collective-permute-start.5 = (bf16[32,32,128]{2,1,0:T(8,128)(2,1)}, bf16[32,32,128]{2,1,0:T(8,128)(2,1)S(1)}, u32[]{:S(2)}, u32[]{:S(2)}) collective-permute-start(bf16[32,32,128]{2,1,0:T(8,128)(2,1)} %get-tuple-element.48), channel_id=1, source_target_pairs={{0,4},{1,5},{2,6},{3,7},{4,0},{5,1},{6,2},{7,3},{8,12},{9,13},{10,... | collective-permute-start | bytes 786440 | tf_op jit(solution)/shard_map/ppermute | solution.py:410
  15.3 1.0 collective-permute-start.6
  16.9 3.7 %collective-permute-done.4.refs_1_ = bf16[32,32,128]{2,1,0:T(8,128)(2,1)S(1)} collective-permute-done((bf16[32,32,128]{2,1,0:T(8,128)(2,1)}, bf16[32,32,128]{2,1,0:T(8,128)(2,1)S(1)}, u32[]{:S(2)}, u32[]{:S(2)}) %collective-permute-start.4) | collective-permute-done | bytes 262176 | tf_op jit(solution)/shard_map/ppermute | solution.py:410
  20.7 6.8 %collective-permute-done.5.refs_2_ = bf16[32,32,128]{2,1,0:T(8,128)(2,1)S(1)} collective-permute-done((bf16[32,32,128]{2,1,0:T(8,128)(2,1)}, bf16[32,32,128]{2,1,0:T(8,128)(2,1)S(1)}, u32[]{:S(2)}, u32[]{:S(2)}) %collective-permute-start.5) | collective-permute-done | bytes 262176 | tf_op jit(solution)/shard_map/ppermute | solution.py:410
  27.5 0.7 copy-done.8
  28.3 3.5 %collect.3 = (bf16[256,32,128]{2,1,0:T(8,128)(2,1)}, bf16[4,16,32,128]{3,2,1,0:T(8,128)(2,1)}, bf16[4,16,32,128]{3,2,1,0:T(8,128)(2,1)}) custom-call(s32[256]{0:T(256)} %reshape.31.list_ref, s32[2]{0:T(128)} %pad_add_fusion.place_ref, bf16[32,32,128]{2,1,0:T(8,128)(2,1)} %get-tuple-element.46.refs_0_, bf16[32,32,128]{2,1,0:T(8,128)(2,1)} %copy-done.5, ...), custom_call_target="tpu_custom_call" | custom-call | bytes 5242880 | tf_op jit(solution)/shard_map/collect/pallas_call | solution.py:168
  31.8 7.2 %all-to-all-start = ((bf16[16,16,32,128]{3,2,1,0:T(8,128)(2,1)}), bf16[16,16,32,128]{3,2,1,0:T(8,128)(2,1)S(1)}, u32[]{:S(2)}, u32[]{:S(2)}) async-start(bf16[16,16,32,128]{3,2,1,0:T(8,128)(2,1)} %bitcast.11), calls=%async_computation | async-start | bytes 4194304 | tf_op jit(solution)/shard_map/all_to_all | solution.py:436
  39.0 4.9 %keys_values.4 = (bf16[32,32,128]{2,1,0:T(8,128)(2,1)}, bf16[32,32,128]{2,1,0:T(8,128)(2,1)}, bf16[32,32,128]{2,1,0:T(8,128)(2,1)}, bf16[32,32,128]{2,1,0:T(8,128)(2,1)}) custom-call(s32[2]{0:T(128)} %pad_add_fusion.place_ref, bf16[1024,768]{1,0:T(8,128)(2,1)} %feat_ref.3, bf16[1024,768]{1,0:T(8,128)(2,1)} %copy-done, bf16[768,768]{1,0:T(8,128)(2,1)} %key_ref.5, ...), custom_call_target="tpu_custom_call" | custom-call | flops 805306368 | bytes 5242880 | tf_op jit(solution)/shard_map/keys_values/pallas_call | solution.py:94
  43.9 1.2 collective-permute-start.12
  45.1 2.4 %collective-permute-start.13 = (bf16[32,32,128]{2,1,0:T(8,128)(2,1)}, bf16[32,32,128]{2,1,0:T(8,128)(2,1)S(1)}, u32[]{:S(2)}, u32[]{:S(2)}) collective-permute-start(bf16[32,32,128]{2,1,0:T(8,128)(2,1)} %get-tuple-element.59), channel_id=1, source_target_pairs={{0,4},{1,5},{2,6},{3,7},{4,0},{5,1},{6,2},{7,3},{8,12},{9,13},{10,... | collective-permute-start | bytes 786440 | tf_op jit(solution)/shard_map/ppermute | solution.py:410
  47.5 1.2 collective-permute-start.14
  48.8 4.1 %collective-permute-done.12.refs_1_ = bf16[32,32,128]{2,1,0:T(8,128)(2,1)S(1)} collective-permute-done((bf16[32,32,128]{2,1,0:T(8,128)(2,1)}, bf16[32,32,128]{2,1,0:T(8,128)(2,1)S(1)}, u32[]{:S(2)}, u32[]{:S(2)}) %collective-permute-start.12) | collective-permute-done | bytes 262176 | tf_op jit(solution)/shard_map/ppermute | solution.py:410
  52.8 6.1 %collective-permute-done.13.refs_2_ = bf16[32,32,128]{2,1,0:T(8,128)(2,1)S(1)} collective-permute-done((bf16[32,32,128]{2,1,0:T(8,128)(2,1)}, bf16[32,32,128]{2,1,0:T(8,128)(2,1)S(1)}, u32[]{:S(2)}, u32[]{:S(2)}) %collective-permute-start.13) | collective-permute-done | bytes 262176 | tf_op jit(solution)/shard_map/ppermute | solution.py:410
  59.0 0.7 copy-done.10
  59.8 3.5 %collect.4 = (bf16[256,32,128]{2,1,0:T(8,128)(2,1)}, bf16[4,16,32,128]{3,2,1,0:T(8,128)(2,1)}, bf16[4,16,32,128]{3,2,1,0:T(8,128)(2,1)}) custom-call(s32[256]{0:T(256)} %reshape.31.list_ref, s32[2]{0:T(128)} %pad_add_fusion.place_ref, bf16[32,32,128]{2,1,0:T(8,128)(2,1)} %get-tuple-element.57.refs_0_, bf16[32,32,128]{2,1,0:T(8,128)(2,1)} %copy-done.7, ...), custom_call_target="tpu_custom_call" | custom-call | bytes 5242880 | tf_op jit(solution)/shard_map/collect/pallas_call | solution.py:168
  63.2 1.8 all-to-all-done
  65.1 7.6 %all-to-all-start.1 = ((bf16[16,16,32,128]{3,2,1,0:T(8,128)(2,1)}), bf16[16,16,32,128]{3,2,1,0:T(8,128)(2,1)}, u32[]{:S(2)}, u32[]{:S(2)}) async-start(bf16[16,16,32,128]{3,2,1,0:T(8,128)(2,1)} %bitcast.10), calls=%async_computation.1 | async-start | bytes 4194304 | tf_op jit(solution)/shard_map/all_to_all | solution.py:436
  72.7 4.9 %keys_values.5 = (bf16[32,32,128]{2,1,0:T(8,128)(2,1)}, bf16[32,32,128]{2,1,0:T(8,128)(2,1)}, bf16[32,32,128]{2,1,0:T(8,128)(2,1)}, bf16[32,32,128]{2,1,0:T(8,128)(2,1)}) custom-call(s32[2]{0:T(128)} %pad_add_fusion.place_ref, bf16[1024,768]{1,0:T(8,128)(2,1)} %feat_ref.3, bf16[1024,768]{1,0:T(8,128)(2,1)} %copy-done, bf16[768,768]{1,0:T(8,128)(2,1)} %key_ref.5, ...), custom_call_target="tpu_custom_call" | custom-call | flops 805306368 | bytes 5242880 | tf_op jit(solution)/shard_map/keys_values/pallas_call | solution.py:94
  77.6 2.0 collective-permute-start.20
  79.5 3.1 %collective-permute-start.21 = (bf16[32,32,128]{2,1,0:T(8,128)(2,1)}, bf16[32,32,128]{2,1,0:T(8,128)(2,1)S(1)}, u32[]{:S(2)}, u32[]{:S(2)}) collective-permute-start(bf16[32,32,128]{2,1,0:T(8,128)(2,1)} %get-tuple-element.70), channel_id=1, source_target_pairs={{0,4},{1,5},{2,6},{3,7},{4,0},{5,1},{6,2},{7,3},{8,12},{9,13},{10,... | collective-permute-start | bytes 786440 | tf_op jit(solution)/shard_map/ppermute | solution.py:410
  82.6 5.3 %collective-permute-done.20.refs_1_ = bf16[32,32,128]{2,1,0:T(8,128)(2,1)S(1)} collective-permute-done((bf16[32,32,128]{2,1,0:T(8,128)(2,1)}, bf16[32,32,128]{2,1,0:T(8,128)(2,1)S(1)}, u32[]{:S(2)}, u32[]{:S(2)}) %collective-permute-start.20) | collective-permute-done | bytes 262176 | tf_op jit(solution)/shard_map/ppermute | solution.py:410
  87.9 4.4 %collective-permute-done.21.refs_2_ = bf16[32,32,128]{2,1,0:T(8,128)(2,1)S(1)} collective-permute-done((bf16[32,32,128]{2,1,0:T(8,128)(2,1)}, bf16[32,32,128]{2,1,0:T(8,128)(2,1)S(1)}, u32[]{:S(2)}, u32[]{:S(2)}) %collective-permute-start.21) | collective-permute-done | bytes 262176 | tf_op jit(solution)/shard_map/ppermute | solution.py:410
  92.4 0.7 copy-done.9
  93.1 3.5 %collect.5 = (bf16[256,32,128]{2,1,0:T(8,128)(2,1)}, bf16[4,16,32,128]{3,2,1,0:T(8,128)(2,1)}, bf16[4,16,32,128]{3,2,1,0:T(8,128)(2,1)}) custom-call(s32[256]{0:T(256)} %reshape.31.list_ref, s32[2]{0:T(128)} %pad_add_fusion.place_ref, bf16[32,32,128]{2,1,0:T(8,128)(2,1)} %get-tuple-element.68.refs_0_, bf16[32,32,128]{2,1,0:T(8,128)(2,1)} %copy-done.6, ...), custom_call_target="tpu_custom_call" | custom-call | bytes 5242880 | tf_op jit(solution)/shard_map/collect/pallas_call | solution.py:168
  96.6 0.8 all-to-all-done.1
  97.4 7.2 %all-to-all-start.2 = ((bf16[16,16,32,128]{3,2,1,0:T(8,128)(2,1)}), bf16[16,16,32,128]{3,2,1,0:T(8,128)(2,1)}, u32[]{:S(2)}, u32[]{:S(2)}) async-start(bf16[16,16,32,128]{3,2,1,0:T(8,128)(2,1)} %bitcast.12), calls=%async_computation.2 | async-start | bytes 4194304 | tf_op jit(solution)/shard_map/all_to_all | solution.py:436
  105.2 24.0 %all-to-all-done.2 = bf16[16,16,32,128]{3,2,1,0:T(8,128)(2,1)} async-done(((bf16[16,16,32,128]{3,2,1,0:T(8,128)(2,1)}), bf16[16,16,32,128]{3,2,1,0:T(8,128)(2,1)}, u32[]{:S(2)}, u32[]{:S(2)}) %all-to-all-start.2) | async-done | bytes 2097184 | tf_op jit(solution)/shard_map/all_to_all | solution.py:436
  129.2 4.8 %queries.1 = (bf16[3,16,32,128]{3,2,1,0:T(8,128)(2,1)}, bf16[3,16,32,128]{3,2,1,0:T(8,128)(2,1)}, bf16[3,16,32,128]{3,2,1,0:T(8,128)(2,1)}, bf16[3,16,32,128]{3,2,1,0:T(8,128)(2,1)}) custom-call(s32[2]{0:T(128)} %pad_add_fusion.place_ref, bf16[1024,768]{1,0:T(8,128)(2,1)} %feat_ref.3, bf16[768,768]{1,0:T(8,128)(2,1)} %query_ref.1), custom_call_target="tpu_custom_call" | custom-call | flops 1207959552 | bytes 5242880 | tf_op jit(solution)/shard_map/queries/pallas_call | solution.py:132
  134.0 6.0 %collective-permute-start.1 = (bf16[3,16,32,128]{3,2,1,0:T(8,128)(2,1)}, bf16[3,16,32,128]{3,2,1,0:T(8,128)(2,1)S(1)}, u32[]{:S(2)}, u32[]{:S(2)}) collective-permute-start(bf16[3,16,32,128]{3,2,1,0:T(8,128)(2,1)} %get-tuple-element.44), channel_id=1, source_target_pairs={{0,4},{1,5},{2,6},{3,7},{4,0},{5,1},{6,2},{7,3},{8,12},{9,13},{10,... | collective-permute-start | bytes 1179656 | tf_op jit(solution)/shard_map/ppermute | solution.py:410
  139.9 8.5 %collective-permute-done.refs_1_ = bf16[3,16,32,128]{3,2,1,0:T(8,128)(2,1)S(1)} collective-permute-done((bf16[3,16,32,128]{3,2,1,0:T(8,128)(2,1)}, bf16[3,16,32,128]{3,2,1,0:T(8,128)(2,1)S(1)}, u32[]{:S(2)}, u32[]{:S(2)}) %collective-permute-start) | collective-permute-done | bytes 393248 | tf_op jit(solution)/shard_map/ppermute | solution.py:410
  148.4 2.3 collective-permute-start.2
  150.7 7.3 %collective-permute-done.1.refs_2_ = bf16[3,16,32,128]{3,2,1,0:T(8,128)(2,1)S(1)} collective-permute-done((bf16[3,16,32,128]{3,2,1,0:T(8,128)(2,1)}, bf16[3,16,32,128]{3,2,1,0:T(8,128)(2,1)S(1)}, u32[]{:S(2)}, u32[]{:S(2)}) %collective-permute-start.1) | collective-permute-done | bytes 393248 | tf_op jit(solution)/shard_map/ppermute | solution.py:410
  158.0 1.5 collective-permute-done.2.refs_3_
  160.3 0.7 reshape.30.id_ref
  161.0 13.5 %attend.3 = (bf16[16,32,128]{2,1,0:T(8,128)(2,1)}, bf16[16,32,128]{2,1,0:T(8,128)(2,1)}, bf16[16,32,128]{2,1,0:T(8,128)(2,1)}, bf16[16,32,128]{2,1,0:T(8,128)(2,1)}) custom-call(s32[1024]{0:T(1024)} %reshape.30.id_ref, s32[128]{0:T(128)} %count_ref.5, s32[2]{0:T(128)} %pad_add_fusion.place_ref, bf16[3,16,32,128]{3,2,1,0:T(8,128)(2,1)} %get-tuple-element.42.refs_0_, ...), custom_call_target="tpu_custom_call" | custom-call | flops 1610612736 | bytes 8388608 | tf_op jit(solution)/shard_map/attend/pallas_call | solution.py:297
  174.6 3.9 %collective-permute-start.10 = (bf16[16,32,128]{2,1,0:T(8,128)(2,1)}, bf16[16,32,128]{2,1,0:T(8,128)(2,1)S(1)}, u32[]{:S(2)}, u32[]{:S(2)}) collective-permute-start(bf16[16,32,128]{2,1,0:T(8,128)(2,1)} %get-tuple-element.55), channel_id=1, source_target_pairs={{0,4},{1,5},{2,6},{3,7},{4,0},{5,1},{6,2},{7,3},{8,12},{9,13},{10,... | collective-permute-start | bytes 393224 | tf_op jit(solution)/shard_map/ppermute | solution.py:410
  178.6 13.5 %attend.4 = (bf16[16,32,128]{2,1,0:T(8,128)(2,1)}, bf16[16,32,128]{2,1,0:T(8,128)(2,1)}, bf16[16,32,128]{2,1,0:T(8,128)(2,1)}, bf16[16,32,128]{2,1,0:T(8,128)(2,1)}) custom-call(s32[1024]{0:T(1024)} %reshape.30.id_ref, s32[128]{0:T(128)} %count_ref.5, s32[2]{0:T(128)} %pad_add_fusion.place_ref, bf16[3,16,32,128]{3,2,1,0:T(8,128)(2,1)} %get-tuple-element.42.refs_0_, ...), custom_call_target="tpu_custom_call" | custom-call | flops 1610612736 | bytes 8388608 | tf_op jit(solution)/shard_map/attend/pallas_call | solution.py:297
  192.1 2.1 collective-permute-start.17
  194.5 13.5 %attend.5 = (bf16[16,32,128]{2,1,0:T(8,128)(2,1)}, bf16[16,32,128]{2,1,0:T(8,128)(2,1)}, bf16[16,32,128]{2,1,0:T(8,128)(2,1)}, bf16[16,32,128]{2,1,0:T(8,128)(2,1)}) custom-call(s32[1024]{0:T(1024)} %reshape.30.id_ref, s32[128]{0:T(128)} %count_ref.5, s32[2]{0:T(128)} %pad_add_fusion.place_ref, bf16[3,16,32,128]{3,2,1,0:T(8,128)(2,1)} %get-tuple-element.42.refs_0_, ...), custom_call_target="tpu_custom_call" | custom-call | flops 1610612736 | bytes 8388608 | tf_op jit(solution)/shard_map/attend/pallas_call | solution.py:297
  208.1 2.6 %collective-permute-start.19 = (bf16[16,32,128]{2,1,0:T(8,128)(2,1)S(1)}, bf16[16,32,128]{2,1,0:T(8,128)(2,1)S(1)}, u32[]{:S(2)}, u32[]{:S(2)}) collective-permute-start(bf16[16,32,128]{2,1,0:T(8,128)(2,1)S(1)} %copy-done.29), channel_id=1, source_target_pairs={{0,6},{1,7},{2,0},{3,1},{4,2},{5,3},{6,4},{7,5},{8,14},{9,15},{10,... | collective-permute-start | bytes 393224 | tf_op jit(solution)/shard_map/ppermute | solution.py:410
  210.7 2.7 %collective-permute-start.26 = (bf16[16,32,128]{2,1,0:T(8,128)(2,1)}, bf16[16,32,128]{2,1,0:T(8,128)(2,1)S(1)}, u32[]{:S(2)}, u32[]{:S(2)}) collective-permute-start(bf16[16,32,128]{2,1,0:T(8,128)(2,1)} %get-tuple-element.77), channel_id=1, source_target_pairs={{0,4},{1,5},{2,6},{3,7},{4,0},{5,1},{6,2},{7,3},{8,12},{9,13},{10,... | collective-permute-start | bytes 393224 | tf_op jit(solution)/shard_map/ppermute | solution.py:410
  213.4 1.2 collective-permute-start.27
  215.8 3.3 %collective-permute-done.25.refs_9_ = bf16[16,32,128]{2,1,0:T(8,128)(2,1)S(1)} collective-permute-done((bf16[16,32,128]{2,1,0:T(8,128)(2,1)}, bf16[16,32,128]{2,1,0:T(8,128)(2,1)S(1)}, u32[]{:S(2)}, u32[]{:S(2)}) %collective-permute-start.25) | collective-permute-done | bytes 131104 | tf_op jit(solution)/shard_map/ppermute | solution.py:410
  220.4 13.5 %finish.1 = bf16[1024,768]{1,0:T(8,128)(2,1)} custom-call(s32[2]{0:T(128)} %pad_add_fusion.place_ref, bf16[1024,768]{1,0:T(8,128)(2,1)} %feat_ref.3, bf16[16,32,128]{2,1,0:T(8,128)(2,1)} %get-tuple-element.53.refs_0_, bf16[16,32,128]{2,1,0:T(8,128)(2,1)} %copy-done.14, bf16[16,32,128]{2,1,0:T(8,128)(2,1)} %copy-done.15, bf16[16,32,128]{2,1,0:T(8,128)(2,1)} %copy-done.16, ...), custom_call_target="tpu_custom_call" | custom-call | tf_op jit(solution)/shard_map/finish/pallas_call | solution.py:376
  (92 shorter events, 5.8 us)
Async XLA Ops:
  0.0 3.6 %collective-permute-start.3 = (bf16[1024,768]{1,0:T(8,128)(2,1)}, bf16[1024,768]{1,0:T(8,128)(2,1)S(1)}, u32[]{:S(2)}, u32[]{:S(2)}) collective-permute-start(bf16[1024,768]{1,0:T(8,128)(2,1)} %feat_ref.3), channel_id=1, source_target_pairs={{0,1},{1,0},{2,3},{3,2},{4,5},{5,4},{6,7},{7,6},{8,9},{9,8},{10,11... | collective-permute-start | bytes 4718600 | tf_op jit(solution)/shard_map/ppermute | solution.py:403
  0.7 15.7 %copy-start.23 = (s32[1,16,16]{2,1,0:T(8,128)S(1)}, s32[1,16,16]{2,1,0:T(8,128)}, u32[]{:S(2)}) copy-start(s32[1,16,16]{2,1,0:T(8,128)} %param.22) | copy-start | bytes 3076
  9.8 10.9 %collective-permute-start.4 = (bf16[32,32,128]{2,1,0:T(8,128)(2,1)}, bf16[32,32,128]{2,1,0:T(8,128)(2,1)S(1)}, u32[]{:S(2)}, u32[]{:S(2)}) collective-permute-start(bf16[32,32,128]{2,1,0:T(8,128)(2,1)} %get-tuple-element.47), channel_id=1, source_target_pairs={{0,2},{1,3},{2,4},{3,5},{4,6},{5,7},{6,0},{7,1},{8,10},{9,11},{10,... | collective-permute-start | bytes 786440 | tf_op jit(solution)/shard_map/ppermute | solution.py:410
  11.7 15.7 %collective-permute-start.5 = (bf16[32,32,128]{2,1,0:T(8,128)(2,1)}, bf16[32,32,128]{2,1,0:T(8,128)(2,1)S(1)}, u32[]{:S(2)}, u32[]{:S(2)}) collective-permute-start(bf16[32,32,128]{2,1,0:T(8,128)(2,1)} %get-tuple-element.48), channel_id=1, source_target_pairs={{0,4},{1,5},{2,6},{3,7},{4,0},{5,1},{6,2},{7,3},{8,12},{9,13},{10,... | collective-permute-start | bytes 786440 | tf_op jit(solution)/shard_map/ppermute | solution.py:410
  15.3 12.2 %collective-permute-start.6 = (bf16[32,32,128]{2,1,0:T(8,128)(2,1)}, bf16[32,32,128]{2,1,0:T(8,128)(2,1)S(1)}, u32[]{:S(2)}, u32[]{:S(2)}) collective-permute-start(bf16[32,32,128]{2,1,0:T(8,128)(2,1)} %get-tuple-element.49), channel_id=1, source_target_pairs={{0,6},{1,7},{2,0},{3,1},{4,2},{5,3},{6,4},{7,5},{8,14},{9,15},{10,... | collective-permute-start | bytes 786440 | tf_op jit(solution)/shard_map/ppermute | solution.py:410
  20.7 6.8 %copy-start.5 = (bf16[32,32,128]{2,1,0:T(8,128)(2,1)}, bf16[32,32,128]{2,1,0:T(8,128)(2,1)S(1)}, u32[]{:S(2)}) copy-start(bf16[32,32,128]{2,1,0:T(8,128)(2,1)S(1)} %collective-permute-done.4.refs_1_) | copy-start | bytes 786436
  31.8 33.3 %all-to-all-start = ((bf16[16,16,32,128]{3,2,1,0:T(8,128)(2,1)}), bf16[16,16,32,128]{3,2,1,0:T(8,128)(2,1)S(1)}, u32[]{:S(2)}, u32[]{:S(2)}) async-start(bf16[16,16,32,128]{3,2,1,0:T(8,128)(2,1)} %bitcast.11), calls=%async_computation | async-start | bytes 4194304 | tf_op jit(solution)/shard_map/all_to_all | solution.py:436
  43.9 8.9 %collective-permute-start.12 = (bf16[32,32,128]{2,1,0:T(8,128)(2,1)}, bf16[32,32,128]{2,1,0:T(8,128)(2,1)S(1)}, u32[]{:S(2)}, u32[]{:S(2)}) collective-permute-start(bf16[32,32,128]{2,1,0:T(8,128)(2,1)} %get-tuple-element.58), channel_id=1, source_target_pairs={{0,2},{1,3},{2,4},{3,5},{4,6},{5,7},{6,0},{7,1},{8,10},{9,11},{10,... | collective-permute-start | bytes 786440 | tf_op jit(solution)/shard_map/ppermute | solution.py:410
  45.1 13.9 %collective-permute-start.13 = (bf16[32,32,128]{2,1,0:T(8,128)(2,1)}, bf16[32,32,128]{2,1,0:T(8,128)(2,1)S(1)}, u32[]{:S(2)}, u32[]{:S(2)}) collective-permute-start(bf16[32,32,128]{2,1,0:T(8,128)(2,1)} %get-tuple-element.59), channel_id=1, source_target_pairs={{0,4},{1,5},{2,6},{3,7},{4,0},{5,1},{6,2},{7,3},{8,12},{9,13},{10,... | collective-permute-start | bytes 786440 | tf_op jit(solution)/shard_map/ppermute | solution.py:410
  47.5 11.5 %collective-permute-start.14 = (bf16[32,32,128]{2,1,0:T(8,128)(2,1)}, bf16[32,32,128]{2,1,0:T(8,128)(2,1)S(1)}, u32[]{:S(2)}, u32[]{:S(2)}) collective-permute-start(bf16[32,32,128]{2,1,0:T(8,128)(2,1)} %get-tuple-element.60), channel_id=1, source_target_pairs={{0,6},{1,7},{2,0},{3,1},{4,2},{5,3},{6,4},{7,5},{8,14},{9,15},{10,... | collective-permute-start | bytes 786440 | tf_op jit(solution)/shard_map/ppermute | solution.py:410
  52.8 6.2 %copy-start.7 = (bf16[32,32,128]{2,1,0:T(8,128)(2,1)}, bf16[32,32,128]{2,1,0:T(8,128)(2,1)S(1)}, u32[]{:S(2)}) copy-start(bf16[32,32,128]{2,1,0:T(8,128)(2,1)S(1)} %collective-permute-done.12.refs_1_) | copy-start | bytes 786436
  65.0 39.6 %copy-start.1 = (bf16[16,16,32,128]{3,2,1,0:T(8,128)(2,1)}, bf16[16,16,32,128]{3,2,1,0:T(8,128)(2,1)S(1)}, u32[]{:S(2)}) copy-start(bf16[16,16,32,128]{3,2,1,0:T(8,128)(2,1)S(1)} %all-to-all-done) | copy-start | bytes 6291460
  65.1 32.3 %all-to-all-start.1 = ((bf16[16,16,32,128]{3,2,1,0:T(8,128)(2,1)}), bf16[16,16,32,128]{3,2,1,0:T(8,128)(2,1)}, u32[]{:S(2)}, u32[]{:S(2)}) async-start(bf16[16,16,32,128]{3,2,1,0:T(8,128)(2,1)} %bitcast.10), calls=%async_computation.1 | async-start | bytes 4194304 | tf_op jit(solution)/shard_map/all_to_all | solution.py:436
  77.6 10.4 %collective-permute-start.20 = (bf16[32,32,128]{2,1,0:T(8,128)(2,1)}, bf16[32,32,128]{2,1,0:T(8,128)(2,1)S(1)}, u32[]{:S(2)}, u32[]{:S(2)}) collective-permute-start(bf16[32,32,128]{2,1,0:T(8,128)(2,1)} %get-tuple-element.69), channel_id=1, source_target_pairs={{0,2},{1,3},{2,4},{3,5},{4,6},{5,7},{6,0},{7,1},{8,10},{9,11},{10,... | collective-permute-start | bytes 786440 | tf_op jit(solution)/shard_map/ppermute | solution.py:410
  79.5 12.8 %collective-permute-start.21 = (bf16[32,32,128]{2,1,0:T(8,128)(2,1)}, bf16[32,32,128]{2,1,0:T(8,128)(2,1)S(1)}, u32[]{:S(2)}, u32[]{:S(2)}) collective-permute-start(bf16[32,32,128]{2,1,0:T(8,128)(2,1)} %get-tuple-element.70), channel_id=1, source_target_pairs={{0,4},{1,5},{2,6},{3,7},{4,0},{5,1},{6,2},{7,3},{8,12},{9,13},{10,... | collective-permute-start | bytes 786440 | tf_op jit(solution)/shard_map/ppermute | solution.py:410
  82.6 9.7 %collective-permute-start.22 = (bf16[32,32,128]{2,1,0:T(8,128)(2,1)}, bf16[32,32,128]{2,1,0:T(8,128)(2,1)S(1)}, u32[]{:S(2)}, u32[]{:S(2)}) collective-permute-start(bf16[32,32,128]{2,1,0:T(8,128)(2,1)} %get-tuple-element.71), channel_id=1, source_target_pairs={{0,6},{1,7},{2,0},{3,1},{4,2},{5,3},{6,4},{7,5},{8,14},{9,15},{10,... | collective-permute-start | bytes 786440 | tf_op jit(solution)/shard_map/ppermute | solution.py:410
  87.9 4.4 %copy-start.6 = (bf16[32,32,128]{2,1,0:T(8,128)(2,1)}, bf16[32,32,128]{2,1,0:T(8,128)(2,1)S(1)}, u32[]{:S(2)}) copy-start(bf16[32,32,128]{2,1,0:T(8,128)(2,1)S(1)} %collective-permute-done.20.refs_1_) | copy-start | bytes 786436
  97.4 31.8 %all-to-all-start.2 = ((bf16[16,16,32,128]{3,2,1,0:T(8,128)(2,1)}), bf16[16,16,32,128]{3,2,1,0:T(8,128)(2,1)}, u32[]{:S(2)}, u32[]{:S(2)}) async-start(bf16[16,16,32,128]{3,2,1,0:T(8,128)(2,1)} %bitcast.12), calls=%async_computation.2 | async-start | bytes 4194304 | tf_op jit(solution)/shard_map/all_to_all | solution.py:436
  104.6 56.4 %collective-permute-start.8 = (bf16[256,32,128]{2,1,0:T(8,128)(2,1)S(1)}, bf16[256,32,128]{2,1,0:T(8,128)(2,1)}, u32[]{:S(2)}, u32[]{:S(2)}) collective-permute-start(bf16[256,32,128]{2,1,0:T(8,128)(2,1)S(1)} %bitcast.8), channel_id=1, source_target_pairs={{0,1},{1,0},{2,3},{3,2},{4,5},{5,4},{6,7},{7,6},{8,9},{9,8},{10,11... | collective-permute-start | bytes 6291464 | tf_op jit(solution)/shard_map/ppermute | solution.py:403
  104.7 73.8 %collective-permute-start.16 = (bf16[256,32,128]{2,1,0:T(8,128)(2,1)}, bf16[256,32,128]{2,1,0:T(8,128)(2,1)}, u32[]{:S(2)}, u32[]{:S(2)}) collective-permute-start(bf16[256,32,128]{2,1,0:T(8,128)(2,1)} %bitcast.5.refs_6_), channel_id=1, source_target_pairs={{0,1},{1,0},{2,3},{3,2},{4,5},{5,4},{6,7},{7,6},{8,9},{9,8},{10,11... | collective-permute-start | bytes 6291464 | tf_op jit(solution)/shard_map/ppermute | solution.py:403
  129.2 28.8 %copy-start.28 = (bf16[4,16,32,128]{3,2,1,0:T(8,128)(2,1)S(1)}, bf16[4,16,32,128]{3,2,1,0:T(8,128)(2,1)}, u32[]{:S(2)}) copy-start(bf16[4,16,32,128]{3,2,1,0:T(8,128)(2,1)} %get-tuple-element.51) | copy-start | bytes 1572868
  129.2 31.0 %copy-start.24 = (s32[128,8]{0,1:T(8,128)S(1)}, s32[128,8]{0,1:T(8,128)}, u32[]{:S(2)}) copy-start(s32[128,8]{0,1:T(8,128)} %param.24) | copy-start | bytes 12292
  129.2 31.0 %copy-start.25 = (s32[128,8]{0,1:T(8,128)S(1)}, s32[128,8]{0,1:T(8,128)}, u32[]{:S(2)}) copy-start(s32[128,8]{0,1:T(8,128)} %param.23) | copy-start | bytes 12292
  129.2 65.0 %collective-permute-start.24 = (bf16[256,32,128]{2,1,0:T(8,128)(2,1)}, bf16[256,32,128]{2,1,0:T(8,128)(2,1)}, u32[]{:S(2)}, u32[]{:S(2)}) collective-permute-start(bf16[256,32,128]{2,1,0:T(8,128)(2,1)} %bitcast.7.refs_6_), channel_id=1, source_target_pairs={{0,1},{1,0},{2,3},{3,2},{4,5},{5,4},{6,7},{7,6},{8,9},{9,8},{10,11... | collective-permute-start | bytes 6291464 | tf_op jit(solution)/shard_map/ppermute | solution.py:403
  134.0 14.4 %collective-permute-start = (bf16[3,16,32,128]{3,2,1,0:T(8,128)(2,1)}, bf16[3,16,32,128]{3,2,1,0:T(8,128)(2,1)S(1)}, u32[]{:S(2)}, u32[]{:S(2)}) collective-permute-start(bf16[3,16,32,128]{3,2,1,0:T(8,128)(2,1)} %get-tuple-element.43), channel_id=1, source_target_pairs={{0,2},{1,3},{2,4},{3,5},{4,6},{5,7},{6,0},{7,1},{8,10},{9,11},{10,... | collective-permute-start | bytes 1179656 | tf_op jit(solution)/shard_map/ppermute | solution.py:410
  134.0 24.0 %collective-permute-start.1 = (bf16[3,16,32,128]{3,2,1,0:T(8,128)(2,1)}, bf16[3,16,32,128]{3,2,1,0:T(8,128)(2,1)S(1)}, u32[]{:S(2)}, u32[]{:S(2)}) collective-permute-start(bf16[3,16,32,128]{3,2,1,0:T(8,128)(2,1)} %get-tuple-element.44), channel_id=1, source_target_pairs={{0,4},{1,5},{2,6},{3,7},{4,0},{5,1},{6,2},{7,3},{8,12},{9,13},{10,... | collective-permute-start | bytes 1179656 | tf_op jit(solution)/shard_map/ppermute | solution.py:410
  148.4 12.6 %copy-start.2 = (bf16[3,16,32,128]{3,2,1,0:T(8,128)(2,1)}, bf16[3,16,32,128]{3,2,1,0:T(8,128)(2,1)S(1)}, u32[]{:S(2)}) copy-start(bf16[3,16,32,128]{3,2,1,0:T(8,128)(2,1)S(1)} %collective-permute-done.refs_1_) | copy-start | bytes 1179652
  148.4 11.1 %collective-permute-start.2 = (bf16[3,16,32,128]{3,2,1,0:T(8,128)(2,1)}, bf16[3,16,32,128]{3,2,1,0:T(8,128)(2,1)S(1)}, u32[]{:S(2)}, u32[]{:S(2)}) collective-permute-start(bf16[3,16,32,128]{3,2,1,0:T(8,128)(2,1)} %get-tuple-element.45), channel_id=1, source_target_pairs={{0,6},{1,7},{2,0},{3,1},{4,2},{5,3},{6,4},{7,5},{8,14},{9,15},{10,... | collective-permute-start | bytes 1179656 | tf_op jit(solution)/shard_map/ppermute | solution.py:410
  158.0 2.0 collective-permute-start.7
  159.5 15.1 %collective-permute-start.15 = (bf16[4,16,32,128]{3,2,1,0:T(8,128)(2,1)}, bf16[4,16,32,128]{3,2,1,0:T(8,128)(2,1)}, u32[]{:S(2)}, u32[]{:S(2)}) collective-permute-start(bf16[4,16,32,128]{3,2,1,0:T(8,128)(2,1)} %get-tuple-element.62), channel_id=1, source_target_pairs={{0,1},{1,0},{2,3},{3,2},{4,5},{5,4},{6,7},{7,6},{8,9},{9,8},{10,11... | collective-permute-start | bytes 1572872 | tf_op jit(solution)/shard_map/ppermute | solution.py:403
  160.1 32.0 %collective-permute-start.23 = (bf16[4,16,32,128]{3,2,1,0:T(8,128)(2,1)}, bf16[4,16,32,128]{3,2,1,0:T(8,128)(2,1)}, u32[]{:S(2)}, u32[]{:S(2)}) collective-permute-start(bf16[4,16,32,128]{3,2,1,0:T(8,128)(2,1)} %get-tuple-element.73), channel_id=1, source_target_pairs={{0,1},{1,0},{2,3},{3,2},{4,5},{5,4},{6,7},{7,6},{8,9},{9,8},{10,11... | collective-permute-start | bytes 1572872 | tf_op jit(solution)/shard_map/ppermute | solution.py:403
  174.5 33.5 %collective-permute-start.9 = (bf16[16,32,128]{2,1,0:T(8,128)(2,1)}, bf16[16,32,128]{2,1,0:T(8,128)(2,1)S(1)}, u32[]{:S(2)}, u32[]{:S(2)}) collective-permute-start(bf16[16,32,128]{2,1,0:T(8,128)(2,1)} %get-tuple-element.54), channel_id=1, source_target_pairs={{0,2},{1,3},{2,4},{3,5},{4,6},{5,7},{6,0},{7,1},{8,10},{9,11},{10,... | collective-permute-start | bytes 393224 | tf_op jit(solution)/shard_map/ppermute | solution.py:410
  174.6 36.0 %collective-permute-start.10 = (bf16[16,32,128]{2,1,0:T(8,128)(2,1)}, bf16[16,32,128]{2,1,0:T(8,128)(2,1)S(1)}, u32[]{:S(2)}, u32[]{:S(2)}) collective-permute-start(bf16[16,32,128]{2,1,0:T(8,128)(2,1)} %get-tuple-element.55), channel_id=1, source_target_pairs={{0,4},{1,5},{2,6},{3,7},{4,0},{5,1},{6,2},{7,3},{8,12},{9,13},{10,... | collective-permute-start | bytes 393224 | tf_op jit(solution)/shard_map/ppermute | solution.py:410
  178.6 32.1 %collective-permute-start.11 = (bf16[16,32,128]{2,1,0:T(8,128)(2,1)}, bf16[16,32,128]{2,1,0:T(8,128)(2,1)S(1)}, u32[]{:S(2)}, u32[]{:S(2)}) collective-permute-start(bf16[16,32,128]{2,1,0:T(8,128)(2,1)} %get-tuple-element.56), channel_id=1, source_target_pairs={{0,6},{1,7},{2,0},{3,1},{4,2},{5,3},{6,4},{7,5},{8,14},{9,15},{10,... | collective-permute-start | bytes 393224 | tf_op jit(solution)/shard_map/ppermute | solution.py:410
  192.1 21.3 %collective-permute-start.17 = (bf16[16,32,128]{2,1,0:T(8,128)(2,1)}, bf16[16,32,128]{2,1,0:T(8,128)(2,1)S(1)}, u32[]{:S(2)}, u32[]{:S(2)}) collective-permute-start(bf16[16,32,128]{2,1,0:T(8,128)(2,1)} %get-tuple-element.65), channel_id=1, source_target_pairs={{0,2},{1,3},{2,4},{3,5},{4,6},{5,7},{6,0},{7,1},{8,10},{9,11},{10,... | collective-permute-start | bytes 393224 | tf_op jit(solution)/shard_map/ppermute | solution.py:410
  194.2 21.6 %collective-permute-start.18 = (bf16[16,32,128]{2,1,0:T(8,128)(2,1)}, bf16[16,32,128]{2,1,0:T(8,128)(2,1)S(1)}, u32[]{:S(2)}, u32[]{:S(2)}) collective-permute-start(bf16[16,32,128]{2,1,0:T(8,128)(2,1)} %get-tuple-element.66), channel_id=1, source_target_pairs={{0,4},{1,5},{2,6},{3,7},{4,0},{5,1},{6,2},{7,3},{8,12},{9,13},{10,... | collective-permute-start | bytes 393224 | tf_op jit(solution)/shard_map/ppermute | solution.py:410
  194.5 13.6 %copy-start.29 = (bf16[16,32,128]{2,1,0:T(8,128)(2,1)S(1)}, bf16[16,32,128]{2,1,0:T(8,128)(2,1)}, u32[]{:S(2)}) copy-start(bf16[16,32,128]{2,1,0:T(8,128)(2,1)} %get-tuple-element.67) | copy-start | bytes 393220
  194.5 20.1 %copy-start.26 = (f32[768]{0:T(1024)S(1)}, f32[768]{0:T(1024)}, u32[]{:S(2)}) copy-start(f32[768]{0:T(1024)} %param.20) | copy-start | bytes 9220
  194.5 20.7 %copy-start.27 = (f32[768]{0:T(1024)S(1)}, f32[768]{0:T(1024)}, u32[]{:S(2)}) copy-start(f32[768]{0:T(1024)} %param.21) | copy-start | bytes 9220
  208.0 11.7 %copy-start.14 = (bf16[16,32,128]{2,1,0:T(8,128)(2,1)}, bf16[16,32,128]{2,1,0:T(8,128)(2,1)S(1)}, u32[]{:S(2)}) copy-start(bf16[16,32,128]{2,1,0:T(8,128)(2,1)S(1)} %collective-permute-done.9.refs_1_) | copy-start | bytes 393220
  208.1 7.7 %collective-permute-start.19 = (bf16[16,32,128]{2,1,0:T(8,128)(2,1)S(1)}, bf16[16,32,128]{2,1,0:T(8,128)(2,1)S(1)}, u32[]{:S(2)}, u32[]{:S(2)}) collective-permute-start(bf16[16,32,128]{2,1,0:T(8,128)(2,1)S(1)} %copy-done.29), channel_id=1, source_target_pairs={{0,6},{1,7},{2,0},{3,1},{4,2},{5,3},{6,4},{7,5},{8,14},{9,15},{10,... | collective-permute-start | bytes 393224 | tf_op jit(solution)/shard_map/ppermute | solution.py:410
  210.7 9.1 %copy-start.15 = (bf16[16,32,128]{2,1,0:T(8,128)(2,1)}, bf16[16,32,128]{2,1,0:T(8,128)(2,1)S(1)}, u32[]{:S(2)}) copy-start(bf16[16,32,128]{2,1,0:T(8,128)(2,1)S(1)} %collective-permute-done.10.refs_2_) | copy-start | bytes 393220
  210.7 8.5 %collective-permute-start.25 = (bf16[16,32,128]{2,1,0:T(8,128)(2,1)}, bf16[16,32,128]{2,1,0:T(8,128)(2,1)S(1)}, u32[]{:S(2)}, u32[]{:S(2)}) collective-permute-start(bf16[16,32,128]{2,1,0:T(8,128)(2,1)} %get-tuple-element.76), channel_id=1, source_target_pairs={{0,2},{1,3},{2,4},{3,5},{4,6},{5,7},{6,0},{7,1},{8,10},{9,11},{10,... | collective-permute-start | bytes 393224 | tf_op jit(solution)/shard_map/ppermute | solution.py:410
  210.7 9.1 %copy-start.16 = (bf16[16,32,128]{2,1,0:T(8,128)(2,1)}, bf16[16,32,128]{2,1,0:T(8,128)(2,1)S(1)}, u32[]{:S(2)}) copy-start(bf16[16,32,128]{2,1,0:T(8,128)(2,1)S(1)} %collective-permute-done.11.refs_3_) | copy-start | bytes 393220
  210.7 8.4 %collective-permute-start.26 = (bf16[16,32,128]{2,1,0:T(8,128)(2,1)}, bf16[16,32,128]{2,1,0:T(8,128)(2,1)S(1)}, u32[]{:S(2)}, u32[]{:S(2)}) collective-permute-start(bf16[16,32,128]{2,1,0:T(8,128)(2,1)} %get-tuple-element.77), channel_id=1, source_target_pairs={{0,4},{1,5},{2,6},{3,7},{4,0},{5,1},{6,2},{7,3},{8,12},{9,13},{10,... | collective-permute-start | bytes 393224 | tf_op jit(solution)/shard_map/ppermute | solution.py:410
  213.4 6.4 %copy-start.17 = (bf16[16,32,128]{2,1,0:T(8,128)(2,1)}, bf16[16,32,128]{2,1,0:T(8,128)(2,1)S(1)}, u32[]{:S(2)}) copy-start(bf16[16,32,128]{2,1,0:T(8,128)(2,1)S(1)} %collective-permute-done.17.refs_5_) | copy-start | bytes 393220
  213.4 6.3 %collective-permute-start.27 = (bf16[16,32,128]{2,1,0:T(8,128)(2,1)}, bf16[16,32,128]{2,1,0:T(8,128)(2,1)S(1)}, u32[]{:S(2)}, u32[]{:S(2)}) collective-permute-start(bf16[16,32,128]{2,1,0:T(8,128)(2,1)} %get-tuple-element.78), channel_id=1, source_target_pairs={{0,6},{1,7},{2,0},{3,1},{4,2},{5,3},{6,4},{7,5},{8,14},{9,15},{10,... | collective-permute-start | bytes 393224 | tf_op jit(solution)/shard_map/ppermute | solution.py:410
  215.8 4.0 %copy-start.19 = (bf16[16,32,128]{2,1,0:T(8,128)(2,1)}, bf16[16,32,128]{2,1,0:T(8,128)(2,1)S(1)}, u32[]{:S(2)}) copy-start(bf16[16,32,128]{2,1,0:T(8,128)(2,1)S(1)} %collective-permute-done.19.refs_7_) | copy-start | bytes 393220
  (13 other events, 16.1 us)

commit v3 on v2

--- a/solution.py
+++ b/solution.py
@@ -26,7 +26,6 @@
 VMEM = pl.BlockSpec(memory_space=pltpu.VMEM)
 SMEM = pl.BlockSpec(memory_space=pltpu.SMEM)
 ANY = pl.BlockSpec(memory_space=pl.ANY)
-LIMIT = 60 * 1024 * 1024
 TILE = (HALF, LANES)
 
 
@@ -55,8 +54,8 @@
     return jnp.concatenate([first, second], axis=1).reshape(blocks * BLOCK, LANES).astype(BF16)
 
 
-def params():
-    return pltpu.CompilerParams(vmem_limit_bytes=LIMIT)
+def params(mebibytes):
+    return pltpu.CompilerParams(vmem_limit_bytes=mebibytes << 20)
 
 
 def keys_values_kernel(chunk, place_ref, near_ref, far_ref, key_ref, value_ref, *refs):
@@ -101,7 +100,7 @@
             pltpu.VMEM((CHIPS, 2 * OWN) + TILE, BF16),
             pltpu.SemaphoreType.DMA,
         ],
-        compiler_params=params(),
+        compiler_params=params(24),
         cost_estimate=pl.CostEstimate(
             flops=4 * rows * width * COLS, bytes_accessed=5 << 20, transcendentals=0
         ),
@@ -135,7 +134,7 @@
         out_specs=[VMEM] * CHIPS,
         out_shape=[jax.ShapeDtypeStruct((CHUNKS, OWN) + TILE, BF16)] * CHIPS,
         scratch_shapes=[pltpu.VMEM((CHIPS, CHUNKS, OWN) + TILE, BF16)],
-        compiler_params=params(),
+        compiler_params=params(24),
         cost_estimate=pl.CostEstimate(
             flops=2 * rows * width * width, bytes_accessed=5 << 20, transcendentals=0
         ),
@@ -151,19 +150,18 @@
         held[pl.ds(source * 2 * OWN, 2 * OWN)] = parts[step][...]
 
     def body(step, carry):
-        for extra in range(8):
-            slot = step * 8 + extra
-            out_ref[slot] = held[list_ref[slot]]
+        for extra in range(CAP):
+            out_ref[step * CAP + extra] = held[list_ref[0, step, extra]]
         return carry
 
-    lax.fori_loop(0, out_ref.shape[0] // 8, body, 0)
+    lax.fori_loop(0, out_ref.shape[0] // CAP, body, 0)
     for source in range(CHIPS):
         own_ref[source] = held[pl.ds(source * 2 * OWN + core * OWN, OWN)]
         swap_ref[source] = held[pl.ds(source * 2 * OWN + (1 - core) * OWN, OWN)]
 
 
-def collect(flat_list, place, parts):
-    slots = flat_list.shape[0]
+def collect(send_list, place, parts):
+    slots = send_list.shape[1] * send_list.shape[2]
     own = jax.ShapeDtypeStruct((CHIPS, OWN) + TILE, BF16)
     return pl.pallas_call(
         collect_kernel,
@@ -171,40 +169,39 @@
         out_specs=[VMEM] * 3,
         out_shape=[jax.ShapeDtypeStruct((slots,) + TILE, BF16), own, own],
         scratch_shapes=[pltpu.VMEM((CHIPS * 2 * OWN,) + TILE, BF16)],
-        compiler_params=params(),
+        compiler_params=params(24),
         cost_estimate=pl.CostEstimate(flops=0, bytes_accessed=5 << 20, transcendentals=0),
         name="collect",
-    )(flat_list, place, *parts)
-
-
-def attend_kernel(id_ref, count_ref, place_ref, *refs):
+    )(send_list, place, *parts)
+
+
+def attend_kernel(chunk, owner_ref, slot_ref, count_ref, place_ref, *refs):
     parts, (own_ref, swap_ref, mine_ref, other_ref) = refs[:CHIPS], refs[CHIPS : CHIPS + 4]
     outs = refs[CHIPS + 4 : 2 * CHIPS + 4]
-    queries, made, keys, values, own_keys, own_values, sems = refs[2 * CHIPS + 4 :]
+    queries, made, keys, values, own_keys, own_values = refs[2 * CHIPS + 4 :]
     z, core = place_ref[0], place_ref[1]
 
-    def fetch(near, near_own, far, far_own):
-        copies = [
-            pltpu.make_async_copy(own_ref, near_own, sems.at[0]),
-            pltpu.make_async_copy(swap_ref, far_own, sems.at[1]),
-            pltpu.make_async_copy(mine_ref, near, sems.at[2]),
-            pltpu.make_async_copy(other_ref, far, sems.at[3]),
-        ]
-        for copy in copies:
-            copy.start()
-        for copy in copies:
-            copy.wait()
+    def place_in(near, near_own, far, far_own):
+        def body(step, carry):
+            at = pl.ds(step * 8, 8)
+            near[at] = mine_ref[at]
+            far[at] = other_ref[at]
+            return carry
+
+        lax.fori_loop(0, mine_ref.shape[0] // 8, body, 0)
+        near_own[...] = own_ref[...]
+        far_own[...] = swap_ref[...]
 
     @pl.when(core == 0)
     def _():
-        fetch(keys, own_keys, values, own_values)
+        place_in(keys, own_keys, values, own_values)
 
     @pl.when(core == 1)
     def _():
-        fetch(values, own_values, keys, own_keys)
-
-    for step in range(CHIPS):
-        queries[lax.rem(z + CHIPS - step, CHIPS)] = parts[step][0]
+        place_in(values, own_values, keys, own_keys)
+
+    for step in range(CHIPS):
+        queries[lax.rem(z + CHIPS - step, CHIPS)] = parts[step][chunk]
 
     low = low_lanes(HALF)
     lane = lax.broadcasted_iota(jnp.int32, (1, LANES), 1)
@@ -215,7 +212,10 @@
     def attend_group(at, carry):
         source, first = at // 2, (at % 2) * group
         blocks = [source * 2 * OWN + core * OWN + first + k for k in range(group)]
-        slots = [[id_ref[block * MAXK + entry] for entry in range(MAXK)] for block in blocks]
+        slots = [
+            [owner_ref[entry, block] * CAP + slot_ref[entry, block] for entry in range(MAXK)]
+            for block in blocks
+        ]
         left = []
         for k in range(group):
             query = queries[source, first + k].astype(F32)
@@ -291,15 +291,12 @@
         outs[step][...] = made[lax.rem(z + step, CHIPS)]
 
 
-def attend(ids, counts, place, queries, own, swapped, mine, other, chunk):
+def attend(tables, place, queries, own, swapped, mine, other, chunk):
     slots = mine.shape[0]
     blocks = pltpu.VMEM((CHIPS, OWN) + TILE, BF16)
     return pl.pallas_call(
-        attend_kernel,
-        grid=(1,),
-        in_specs=[SMEM, SMEM, SMEM]
-        + [pl.BlockSpec((1, OWN) + TILE, lambda i: (chunk, 0, 0, 0))] * CHIPS
-        + [ANY] * 4,
+        functools.partial(attend_kernel, chunk),
+        in_specs=[SMEM] * 4 + [VMEM] * (CHIPS + 4),
         out_specs=[VMEM] * CHIPS,
         out_shape=[jax.ShapeDtypeStruct((OWN,) + TILE, BF16)] * CHIPS,
         scratch_shapes=[
@@ -309,14 +306,13 @@
             pltpu.VMEM((slots,) + TILE, BF16),
             blocks,
             blocks,
-            pltpu.SemaphoreType.DMA((4,)),
         ],
-        compiler_params=params(),
+        compiler_params=params(28),
         cost_estimate=pl.CostEstimate(
             flops=64 * 4 * 128 * 128 * 384, bytes_accessed=8 << 20, transcendentals=64 * 128 * 384
         ),
         name="attend",
-    )(ids, counts, place, *queries, own, swapped, mine, other)
+    )(*tables, place, *queries, own, swapped, mine, other)
 
 
 def normed(values, gain):
@@ -325,44 +321,67 @@
     return center * lax.rsqrt(spread + 1e-05) * gain
 
 
-def finish_kernel(place_ref, feat_ref, *refs):
-    backs = refs[: CHUNKS * CHIPS]
-    out_w_ref, up_ref, down_ref, gain_a_ref, gain_f_ref, result_ref = refs[CHUNKS * CHIPS :][:6]
-    attended, out_w, up, down, sems = refs[CHUNKS * CHIPS + 6 :]
+def mixed_rows(held, half, weight):
+    at = slice(half * 8, half * 8 + 8)
+    pieces = [unpack_pair(held[2 * pair, at], held[2 * pair + 1, at]) for pair in range(2)]
+    return jnp.dot(jnp.concatenate(pieces, axis=1), weight, preferred_element_type=F32)
+
+
+def gather_parts(place_ref, parts, held):
+    z = place_ref[0]
+    for step in range(CHIPS):
+        held[lax.rem(z + CHIPS - step, CHIPS)] = parts[step][...]
+
+
+def mix_kernel(place_ref, feat_ref, *refs):
+    parts, (weight_ref, out_ref, held) = refs[: 2 * CHIPS], refs[2 * CHIPS :]
+    rows = feat_ref.shape[0] // 2
+    for chunk in range(2):
+        gather_parts(place_ref, parts[chunk * CHIPS : (chunk + 1) * CHIPS], held.at[chunk])
+    for half in range(2):
+        at = slice(half * rows, (half + 1) * rows)
+        mixed = feat_ref[at, :].astype(F32)
+        for chunk in range(2):
+            weight = weight_ref[chunk * COLS : (chunk + 1) * COLS, :]
+            mixed = mixed + mixed_rows(held.at[chunk], half, weight)
+        out_ref[at, :] = mixed
+
+
+def mix(place, features, backs, w_out):
+    rows, width = features.shape
+    return pl.pallas_call(
+        mix_kernel,
+        in_specs=[SMEM, VMEM] + [VMEM] * (2 * CHIPS + 1),
+        out_specs=VMEM,
+        out_shape=jax.ShapeDtypeStruct((rows, width), F32),
+        scratch_shapes=[pltpu.VMEM((2, CHIPS, OWN) + TILE, BF16)],
+        compiler_params=params(24),
+        cost_estimate=pl.CostEstimate(
+            flops=4 * rows * COLS * width, bytes_accessed=7 << 20, transcendentals=0
+        ),
+        name="mix",
+    )(place, features, *[part for back in backs for part in back], w_out)
+
+
+def finish_kernel(place_ref, mixed_ref, *refs):
+    parts, refs = refs[:CHIPS], refs[CHIPS:]
+    out_w_ref, up_ref, down_ref, gain_a_ref, gain_f_ref, result_ref, held, up, down, sems = refs
     copies = [
-        pltpu.make_async_copy(out_w_ref, out_w, sems.at[0]),
-        pltpu.make_async_copy(up_ref, up, sems.at[1]),
-        pltpu.make_async_copy(down_ref, down, sems.at[2]),
+        pltpu.make_async_copy(up_ref, up, sems.at[0]),
+        pltpu.make_async_copy(down_ref, down, sems.at[1]),
     ]
     for copy in copies:
         copy.start()
-    z = place_ref[0]
-    for chunk in range(CHUNKS):
-        for step in range(CHIPS):
-            source = lax.rem(z + CHIPS - step, CHIPS)
-            attended[chunk, source] = backs[chunk * CHIPS + step][...]
-    rows = feat_ref.shape[0] // 2
+    gather_parts(place_ref, parts, held)
+    rows = mixed_ref.shape[0] // 2
+    last = (CHUNKS - 1) * COLS
     firsts = []
-    copies[0].wait()
     for half in range(2):
         at = slice(half * rows, (half + 1) * rows)
-        mixed = feat_ref[at, :].astype(F32)
-        for chunk in range(CHUNKS):
-            pieces = [
-                unpack_pair(
-                    attended[chunk, 2 * pair, half * 8 : half * 8 + 8],
-                    attended[chunk, 2 * pair + 1, half * 8 : half * 8 + 8],
-                )
-                for pair in range(2)
-            ]
-            mixed = mixed + jnp.dot(
-                jnp.concatenate(pieces, axis=1),
-                out_w[chunk * COLS : (chunk + 1) * COLS, :],
-                preferred_element_type=F32,
-            )
+        mixed = mixed_ref[at, :] + mixed_rows(held, half, out_w_ref[last : last + COLS, :])
         firsts.append(normed(mixed, gain_a_ref[...]).astype(BF16))
-    copies[1].wait()
-    copies[2].wait()
+    for copy in copies:
+        copy.wait()
     for half in range(2):
         at = slice(half * rows, (half + 1) * rows)
         first = firsts[half]
@@ -371,26 +390,25 @@
         result_ref[at, :] = normed(total, gain_f_ref[...]).astype(BF16)
 
 
-def finish(place, features, backs, w_out, w_up, w_down, gain_attn, gain_ffn):
-    rows, width = features.shape
+def finish(place, mixed, back, w_out, w_up, w_down, gain_attn, gain_ffn):
+    rows, width = mixed.shape
     return pl.pallas_call(
         finish_kernel,
-        in_specs=[SMEM, VMEM] + [VMEM] * (CHUNKS * CHIPS) + [ANY] * 3 + [VMEM] * 2,
+        in_specs=[SMEM, VMEM] + [VMEM] * CHIPS + [VMEM, ANY, ANY, VMEM, VMEM],
         out_specs=VMEM,
         out_shape=jax.ShapeDtypeStruct((rows, width), BF16),
         scratch_shapes=[
-            pltpu.VMEM((CHUNKS, CHIPS, OWN) + TILE, BF16),
-            pltpu.VMEM(w_out.shape, BF16),
+            pltpu.VMEM((CHIPS, OWN) + TILE, BF16),
             pltpu.VMEM(w_up.shape, BF16),
             pltpu.VMEM(w_down.shape, BF16),
-            pltpu.SemaphoreType.DMA((3,)),
+            pltpu.SemaphoreType.DMA((2,)),
         ],
-        compiler_params=params(),
+        compiler_params=params(40),
         name="finish",
     )(
         place,
-        features,
-        *[part for back in backs for part in back],
+        mixed,
+        *back,
         w_out,
         w_up,
         w_down,
@@ -421,14 +439,13 @@
     head = lax.axis_index("head").astype(jnp.int32)
     place = jnp.stack([head // 2, head % 2])
     groups = send_list.shape[1]
-    flat_list = send_list.reshape(-1)
-    ids = (edge_owner * CAP + edge_slot).reshape(-1)
+    owners, slots = edge_owner.T, edge_slot.T
     far = swap(features)
     collected = []
     for c in range(CHUNKS):
         parts = project_keys_values(place, features, far, w_key, w_value, c)
         parts = along_z(parts)
-        collected.append(collect(flat_list, place, parts))
+        collected.append(collect(send_list, place, parts))
     queries = along_z(project_queries(place, features, w_query))
     mines = []
     for c in range(CHUNKS):
@@ -439,9 +456,13 @@
     for c in range(CHUNKS):
         swapped = swap(collected[c][2])
         other = swap(mines[c])
-        done = attend(ids, edge_count, place, queries, collected[c][1], swapped, mines[c], other, c)
+        tables = (owners, slots, edge_count)
+        done = attend(
+            tables, place, queries, collected[c][1], swapped, mines[c], other, c
+        )
         backs.append(along_z(done))
-    return finish(place, features, backs, w_out, w_up, w_down, gain_attn, gain_ffn)
+    mixed = mix(place, features, backs[:2], w_out)
+    return finish(place, mixed, backs[2], w_out, w_up, w_down, gain_attn, gain_ffn)
 
 
 def solution(mesh):

time: 237 us -> 224 us (0.945)
  Pallas kernels: 84.1 us -> 56.8 us
  local copies, waits for them, and re-layouts: 6.7 us -> 17.7 us
  starting transfers between devices: 60.4 us -> 64.1 us
    unnamed x60 -> x58, local copies, waits for them, and re-layouts: 4.15 us -> 17.7 us
    pallas_call x3, Pallas kernels: 14.8 us -> 5.15 us  [project_keys_values(): pl.pallas_call(functools.partial(keys_values_kernel, chunk), in_specs=[SM...]
    pallas_call x4 -> x5, Pallas kernels: 54.1 us -> 45.8 us  [the longest x3 34.5 us: attend(): pl.pallas_call(functools.partial(attend_kernel, chunk), in_specs=[SMEM] *...]
    pallas_call x3, Pallas kernels: 10.4 us -> 3.49 us  [collect(): pl.pallas_call(collect_kernel, in_specs=[SMEM, SMEM] + [VMEM] * CHIPS, ou...]
    ppermute x21, starting transfers between devices: 37.6 us -> 41.2 us  [along_z(): lax.ppermute(parts[step], 'head', [(i, (i + 2 * step) % (2 * CHIPS)) for...]
    pallas_call x1, Pallas kernels: 4.75 us -> 2.31 us  [project_queries(): pl.pallas_call(queries_kernel, in_specs=[SMEM, VMEM, VMEM], out_specs=[VM...]
  transfers between devices with their start and end apart: 31 -> 31, of which waited for: 16 -> 17; matrix products, arithmetic and copies ran while one was open for 1% -> 0% of each run, Pallas kernels for 27% -> 20%
where the time goes in v3:
time: 224 us; the launch traced here: 221 us
  waiting for transfers between devices  82.1 us (37%)
  starting transfers between devices  64.1 us (29%)
  Pallas kernels  56.8 us (25%)
  local copies, waits for them, and re-layouts  17.7 us (8%)
    ppermute x21, waiting for transfers between devices, along_z(): lax.ppermute(parts[step], 'head', [(i, (i + 2 * step) % (2 * CHIPS)) for...  50.5 us
    ppermute x21, starting transfers between devices, along_z(): lax.ppermute(parts[step], 'head', [(i, (i + 2 * step) % (2 * CHIPS)) for...  41.2 us
    pallas_call x3, Pallas kernels, attend(): pl.pallas_call(functools.partial(attend_kernel, chunk), in_specs=[SMEM] *...  34.5 us
    all_to_all x3, waiting for transfers between devices, per_device(): got = lax.all_to_all(sent, 'node', split_axis=0, concat_axis=0, tiled=True)  27.4 us
    all_to_all x3, starting transfers between devices, per_device(): got = lax.all_to_all(sent, 'node', split_axis=0, concat_axis=0, tiled=True)  22.2 us
    unnamed x58, local copies, waits for them, and re-layouts  17.7 us
    pallas_call x1, Pallas kernels, finish(): pl.pallas_call(finish_kernel, in_specs=[SMEM, VMEM] + [VMEM] * CHIPS + [V...  9.65 us
    pallas_call x3, Pallas kernels, project_keys_values(): pl.pallas_call(functools.partial(keys_values_kernel, chunk), in_specs=[SM...  5.15 us
  transfers between devices with their start and end apart: 31, of which 17 were waited for; matrix products, arithmetic and copies ran while one was open for 0% of the time, Pallas kernels for 20%

profile of v3, /device:TPU:20, one launch (start us, length us, event | category | flops | bytes accessed | tf_op | source)
XLA Modules:
  0.0 221.2 jit_solution(13731032117218984052)
XLA Ops:
  0.1 3.5 %collective-permute-done.3.far_ref = bf16[1024,768]{1,0:T(8,128)(2,1)S(1)} collective-permute-done((bf16[1024,768]{1,0:T(8,128)(2,1)}, bf16[1024,768]{1,0:T(8,128)(2,1)S(1)}, u32[]{:S(2)}, u32[]{:S(2)}) %collective-permute-start.3) | collective-permute-done | bytes 1572896 | tf_op jit(solution)/shard_map/ppermute | solution.py:421
  3.6 1.4 copy-done
  5.0 1.3 copy-done.2
  6.3 1.3 copy-done.5
  7.6 1.7 keys_values.4
  9.3 2.0 collective-permute-start.12
  11.3 3.6 %collective-permute-start.13 = (bf16[32,32,128]{2,1,0:T(8,128)(2,1)S(1)}, bf16[32,32,128]{2,1,0:T(8,128)(2,1)S(1)}, u32[]{:S(2)}, u32[]{:S(2)}) collective-permute-start(bf16[32,32,128]{2,1,0:T(8,128)(2,1)S(1)} %get-tuple-element.59), channel_id=1, source_target_pairs={{0,4},{1,5},{2,6},{3,7},{4,0},{5,1},{6,2},{7,3},{8,12},{9,13},{10,... | collective-permute-start | bytes 786440 | tf_op jit(solution)/shard_map/ppermute | solution.py:428
  15.9 4.1 %collective-permute-done.12.refs_1_ = bf16[32,32,128]{2,1,0:T(8,128)(2,1)S(1)} collective-permute-done((bf16[32,32,128]{2,1,0:T(8,128)(2,1)S(1)}, bf16[32,32,128]{2,1,0:T(8,128)(2,1)S(1)}, u32[]{:S(2)}, u32[]{:S(2)}) %collective-permute-start.12) | collective-permute-done | bytes 262176 | tf_op jit(solution)/shard_map/ppermute | solution.py:428
  20.0 6.8 %collective-permute-done.13.refs_2_ = bf16[32,32,128]{2,1,0:T(8,128)(2,1)S(1)} collective-permute-done((bf16[32,32,128]{2,1,0:T(8,128)(2,1)S(1)}, bf16[32,32,128]{2,1,0:T(8,128)(2,1)S(1)}, u32[]{:S(2)}, u32[]{:S(2)}) %collective-permute-start.13) | collective-permute-done | bytes 262176 | tf_op jit(solution)/shard_map/ppermute | solution.py:428
  28.0 1.3 copy-done.12
  30.9 7.4 %all-to-all-start.1 = ((bf16[16,16,32,128]{3,2,1,0:T(8,128)(2,1)}), bf16[16,16,32,128]{3,2,1,0:T(8,128)(2,1)}, u32[]{:S(2)}, u32[]{:S(2)}) async-start(bf16[16,16,32,128]{3,2,1,0:T(8,128)(2,1)} %bitcast.11), calls=%async_computation.1 | async-start | bytes 4194304 | tf_op jit(solution)/shard_map/all_to_all | solution.py:453
  39.5 1.3 copy-done.6
  40.8 1.7 keys_values.3
  42.5 1.3 collective-permute-start.4
  43.8 2.4 %collective-permute-start.5 = (bf16[32,32,128]{2,1,0:T(8,128)(2,1)S(1)}, bf16[32,32,128]{2,1,0:T(8,128)(2,1)S(1)}, u32[]{:S(2)}, u32[]{:S(2)}) collective-permute-start(bf16[32,32,128]{2,1,0:T(8,128)(2,1)S(1)} %get-tuple-element.48), channel_id=1, source_target_pairs={{0,4},{1,5},{2,6},{3,7},{4,0},{5,1},{6,2},{7,3},{8,12},{9,13},{10,... | collective-permute-start | bytes 786440 | tf_op jit(solution)/shard_map/ppermute | solution.py:428
  47.5 3.7 %collective-permute-done.4.refs_1_ = bf16[32,32,128]{2,1,0:T(8,128)(2,1)S(1)} collective-permute-done((bf16[32,32,128]{2,1,0:T(8,128)(2,1)S(1)}, bf16[32,32,128]{2,1,0:T(8,128)(2,1)S(1)}, u32[]{:S(2)}, u32[]{:S(2)}) %collective-permute-start.4) | collective-permute-done | bytes 262176 | tf_op jit(solution)/shard_map/ppermute | solution.py:428
  51.1 6.3 %collective-permute-done.5.refs_2_ = bf16[32,32,128]{2,1,0:T(8,128)(2,1)S(1)} collective-permute-done((bf16[32,32,128]{2,1,0:T(8,128)(2,1)S(1)}, bf16[32,32,128]{2,1,0:T(8,128)(2,1)S(1)}, u32[]{:S(2)}, u32[]{:S(2)}) %collective-permute-start.5) | collective-permute-done | bytes 262176 | tf_op jit(solution)/shard_map/ppermute | solution.py:428
  58.7 1.3 copy-done.11
  61.6 2.8 %all-to-all-done.1 = bf16[16,16,32,128]{3,2,1,0:T(8,128)(2,1)} async-done(((bf16[16,16,32,128]{3,2,1,0:T(8,128)(2,1)}), bf16[16,16,32,128]{3,2,1,0:T(8,128)(2,1)}, u32[]{:S(2)}, u32[]{:S(2)}) %all-to-all-start.1) | async-done | bytes 2097184 | tf_op jit(solution)/shard_map/all_to_all | solution.py:453
  64.4 7.6 %all-to-all-start = ((bf16[16,16,32,128]{3,2,1,0:T(8,128)(2,1)}), bf16[16,16,32,128]{3,2,1,0:T(8,128)(2,1)}, u32[]{:S(2)}, u32[]{:S(2)}) async-start(bf16[16,16,32,128]{3,2,1,0:T(8,128)(2,1)} %bitcast.10), calls=%async_computation | async-start | bytes 4194304 | tf_op jit(solution)/shard_map/all_to_all | solution.py:453
  73.3 1.3 copy-done.7
  74.6 1.7 keys_values.5
  76.3 2.1 collective-permute-start.20
  78.4 3.1 %collective-permute-start.21 = (bf16[32,32,128]{2,1,0:T(8,128)(2,1)S(1)}, bf16[32,32,128]{2,1,0:T(8,128)(2,1)S(1)}, u32[]{:S(2)}, u32[]{:S(2)}) collective-permute-start(bf16[32,32,128]{2,1,0:T(8,128)(2,1)S(1)} %get-tuple-element.70), channel_id=1, source_target_pairs={{0,4},{1,5},{2,6},{3,7},{4,0},{5,1},{6,2},{7,3},{8,12},{9,13},{10,... | collective-permute-start | bytes 786440 | tf_op jit(solution)/shard_map/ppermute | solution.py:428
  81.4 5.1 %collective-permute-done.20.refs_1_ = bf16[32,32,128]{2,1,0:T(8,128)(2,1)S(1)} collective-permute-done((bf16[32,32,128]{2,1,0:T(8,128)(2,1)S(1)}, bf16[32,32,128]{2,1,0:T(8,128)(2,1)S(1)}, u32[]{:S(2)}, u32[]{:S(2)}) %collective-permute-start.20) | collective-permute-done | bytes 262176 | tf_op jit(solution)/shard_map/ppermute | solution.py:428
  86.5 4.4 %collective-permute-done.21.refs_2_ = bf16[32,32,128]{2,1,0:T(8,128)(2,1)S(1)} collective-permute-done((bf16[32,32,128]{2,1,0:T(8,128)(2,1)S(1)}, bf16[32,32,128]{2,1,0:T(8,128)(2,1)S(1)}, u32[]{:S(2)}, u32[]{:S(2)}) %collective-permute-start.21) | collective-permute-done | bytes 262176 | tf_op jit(solution)/shard_map/ppermute | solution.py:428
  92.1 1.4 copy-done.13
  93.5 3.2 %all-to-all-done = bf16[16,16,32,128]{3,2,1,0:T(8,128)(2,1)} async-done(((bf16[16,16,32,128]{3,2,1,0:T(8,128)(2,1)}), bf16[16,16,32,128]{3,2,1,0:T(8,128)(2,1)}, u32[]{:S(2)}, u32[]{:S(2)}) %all-to-all-start) | async-done | bytes 2097184 | tf_op jit(solution)/shard_map/all_to_all | solution.py:453
  96.8 7.2 %all-to-all-start.2 = ((bf16[16,16,32,128]{3,2,1,0:T(8,128)(2,1)}), bf16[16,16,32,128]{3,2,1,0:T(8,128)(2,1)}, u32[]{:S(2)}, u32[]{:S(2)}) async-start(bf16[16,16,32,128]{3,2,1,0:T(8,128)(2,1)} %bitcast.12), calls=%async_computation.2 | async-start | bytes 4194304 | tf_op jit(solution)/shard_map/all_to_all | solution.py:453
  104.5 21.3 %all-to-all-done.2 = bf16[16,16,32,128]{3,2,1,0:T(8,128)(2,1)} async-done(((bf16[16,16,32,128]{3,2,1,0:T(8,128)(2,1)}), bf16[16,16,32,128]{3,2,1,0:T(8,128)(2,1)}, u32[]{:S(2)}, u32[]{:S(2)}) %all-to-all-start.2) | async-done | bytes 2097184 | tf_op jit(solution)/shard_map/all_to_all | solution.py:453
  126.0 1.3 copy-done.22
  127.3 2.3 %queries.1 = (bf16[3,16,32,128]{3,2,1,0:T(8,128)(2,1)S(1)}, bf16[3,16,32,128]{3,2,1,0:T(8,128)(2,1)S(1)}, bf16[3,16,32,128]{3,2,1,0:T(8,128)(2,1)S(1)}, bf16[3,16,32,128]{3,2,1,0:T(8,128)(2,1)S(1)}) custom-call(s32[2]{0:T(128)S(1)} %pad_add_fusion.place_ref, bf16[1024,768]{1,0:T(8,128)(2,1)S(1)} %copy-done.1, bf16[768,768]{1,0:T(8,128)(2,1)S(1)} %copy-done.22), custom_call_target="tpu_custom_call" | custom-call | flops 1207959552 | bytes 5242880 | tf_op jit(solution)/shard_map/queries/pallas_call | solution.py:131
  129.6 2.3 %collective-permute-start = (bf16[3,16,32,128]{3,2,1,0:T(8,128)(2,1)S(1)}, bf16[3,16,32,128]{3,2,1,0:T(8,128)(2,1)S(1)}, u32[]{:S(2)}, u32[]{:S(2)}) collective-permute-start(bf16[3,16,32,128]{3,2,1,0:T(8,128)(2,1)S(1)} %get-tuple-element.43), channel_id=1, source_target_pairs={{0,2},{1,3},{2,4},{3,5},{4,6},{5,7},{6,0},{7,1},{8,10},{9,11},{10,... | collective-permute-start | bytes 1179656 | tf_op jit(solution)/shard_map/ppermute | solution.py:428
  131.9 6.5 %collective-permute-start.1 = (bf16[3,16,32,128]{3,2,1,0:T(8,128)(2,1)S(1)}, bf16[3,16,32,128]{3,2,1,0:T(8,128)(2,1)S(1)}, u32[]{:S(2)}, u32[]{:S(2)}) collective-permute-start(bf16[3,16,32,128]{3,2,1,0:T(8,128)(2,1)S(1)} %get-tuple-element.44), channel_id=1, source_target_pairs={{0,4},{1,5},{2,6},{3,7},{4,0},{5,1},{6,2},{7,3},{8,12},{9,13},{10,... | collective-permute-start | bytes 1179656 | tf_op jit(solution)/shard_map/ppermute | solution.py:428
  138.4 8.3 %collective-permute-done.refs_1_ = bf16[3,16,32,128]{3,2,1,0:T(8,128)(2,1)S(1)} collective-permute-done((bf16[3,16,32,128]{3,2,1,0:T(8,128)(2,1)S(1)}, bf16[3,16,32,128]{3,2,1,0:T(8,128)(2,1)S(1)}, u32[]{:S(2)}, u32[]{:S(2)}) %collective-permute-start) | collective-permute-done | bytes 393248 | tf_op jit(solution)/shard_map/ppermute | solution.py:428
  146.7 2.3 %collective-permute-start.2 = (bf16[3,16,32,128]{3,2,1,0:T(8,128)(2,1)S(1)}, bf16[3,16,32,128]{3,2,1,0:T(8,128)(2,1)S(1)}, u32[]{:S(2)}, u32[]{:S(2)}) collective-permute-start(bf16[3,16,32,128]{3,2,1,0:T(8,128)(2,1)S(1)} %get-tuple-element.45), channel_id=1, source_target_pairs={{0,6},{1,7},{2,0},{3,1},{4,2},{5,3},{6,4},{7,5},{8,14},{9,15},{10,... | collective-permute-start | bytes 1179656 | tf_op jit(solution)/shard_map/ppermute | solution.py:428
  149.0 7.3 %collective-permute-done.1.refs_2_ = bf16[3,16,32,128]{3,2,1,0:T(8,128)(2,1)S(1)} collective-permute-done((bf16[3,16,32,128]{3,2,1,0:T(8,128)(2,1)S(1)}, bf16[3,16,32,128]{3,2,1,0:T(8,128)(2,1)S(1)}, u32[]{:S(2)}, u32[]{:S(2)}) %collective-permute-start.1) | collective-permute-done | bytes 393248 | tf_op jit(solution)/shard_map/ppermute | solution.py:428
  156.3 1.3 collective-permute-done.2.refs_3_
  158.4 11.8 %attend.4 = (bf16[16,32,128]{2,1,0:T(8,128)(2,1)S(1)}, bf16[16,32,128]{2,1,0:T(8,128)(2,1)S(1)}, bf16[16,32,128]{2,1,0:T(8,128)(2,1)S(1)}, bf16[16,32,128]{2,1,0:T(8,128)(2,1)S(1)}) custom-call(s32[8,128]{1,0:T(8,128)S(1)} %bitcast.13, s32[8,128]{1,0:T(8,128)S(1)} %bitcast.16, s32[128]{0:T(128)S(1)} %copy-done.21, s32[2]{0:T(128)S(1)} %pad_add_fusion.place_ref, ...), custom_call_target="tpu_custom_call" | custom-call | flops 1610612736 | bytes 8388608 | tf_op jit(solution)/shard_map/attend/pallas_call | solution.py:297
  170.3 3.9 %collective-permute-start.18 = (bf16[16,32,128]{2,1,0:T(8,128)(2,1)S(1)}, bf16[16,32,128]{2,1,0:T(8,128)(2,1)S(1)}, u32[]{:S(2)}, u32[]{:S(2)}) collective-permute-start(bf16[16,32,128]{2,1,0:T(8,128)(2,1)S(1)} %get-tuple-element.66), channel_id=1, source_target_pairs={{0,4},{1,5},{2,6},{3,7},{4,0},{5,1},{6,2},{7,3},{8,12},{9,13},{10,... | collective-permute-start | bytes 393224 | tf_op jit(solution)/shard_map/ppermute | solution.py:428
  174.2 11.6 %attend.3 = (bf16[16,32,128]{2,1,0:T(8,128)(2,1)S(1)}, bf16[16,32,128]{2,1,0:T(8,128)(2,1)S(1)}, bf16[16,32,128]{2,1,0:T(8,128)(2,1)S(1)}, bf16[16,32,128]{2,1,0:T(8,128)(2,1)S(1)}) custom-call(s32[8,128]{1,0:T(8,128)S(1)} %bitcast.14, s32[8,128]{1,0:T(8,128)S(1)} %bitcast.17, s32[128]{0:T(128)S(1)} %copy-done.21, s32[2]{0:T(128)S(1)} %pad_add_fusion.place_ref, ...), custom_call_target="tpu_custom_call" | custom-call | flops 1610612736 | bytes 8388608 | tf_op jit(solution)/shard_map/attend/pallas_call | solution.py:297
  185.8 2.3 %collective-permute-start.10 = (bf16[16,32,128]{2,1,0:T(8,128)(2,1)S(1)}, bf16[16,32,128]{2,1,0:T(8,128)(2,1)S(1)}, u32[]{:S(2)}, u32[]{:S(2)}) collective-permute-start(bf16[16,32,128]{2,1,0:T(8,128)(2,1)S(1)} %get-tuple-element.55), channel_id=1, source_target_pairs={{0,4},{1,5},{2,6},{3,7},{4,0},{5,1},{6,2},{7,3},{8,12},{9,13},{10,... | collective-permute-start | bytes 393224 | tf_op jit(solution)/shard_map/ppermute | solution.py:428
  188.2 2.4 %collective-permute-start.11 = (bf16[16,32,128]{2,1,0:T(8,128)(2,1)S(1)}, bf16[16,32,128]{2,1,0:T(8,128)(2,1)S(1)}, u32[]{:S(2)}, u32[]{:S(2)}) collective-permute-start(bf16[16,32,128]{2,1,0:T(8,128)(2,1)S(1)} %get-tuple-element.56), channel_id=1, source_target_pairs={{0,6},{1,7},{2,0},{3,1},{4,2},{5,3},{6,4},{7,5},{8,14},{9,15},{10,... | collective-permute-start | bytes 393224 | tf_op jit(solution)/shard_map/ppermute | solution.py:428
  190.6 11.1 %attend.5 = (bf16[16,32,128]{2,1,0:T(8,128)(2,1)S(1)}, bf16[16,32,128]{2,1,0:T(8,128)(2,1)S(1)}, bf16[16,32,128]{2,1,0:T(8,128)(2,1)S(1)}, bf16[16,32,128]{2,1,0:T(8,128)(2,1)S(1)}) custom-call(s32[8,128]{1,0:T(8,128)S(1)} %bitcast.15, s32[8,128]{1,0:T(8,128)S(1)} %bitcast.18, s32[128]{0:T(128)S(1)} %copy-done.21, s32[2]{0:T(128)S(1)} %pad_add_fusion.place_ref, ...), custom_call_target="tpu_custom_call" | custom-call | flops 1610612736 | bytes 8388608 | tf_op jit(solution)/shard_map/attend/pallas_call | solution.py:297
  201.8 4.6 %collective-permute-start.26 = (bf16[16,32,128]{2,1,0:T(8,128)(2,1)S(1)}, bf16[16,32,128]{2,1,0:T(8,128)(2,1)S(1)}, u32[]{:S(2)}, u32[]{:S(2)}) collective-permute-start(bf16[16,32,128]{2,1,0:T(8,128)(2,1)S(1)} %get-tuple-element.77), channel_id=1, source_target_pairs={{0,4},{1,5},{2,6},{3,7},{4,0},{5,1},{6,2},{7,3},{8,12},{9,13},{10,... | collective-permute-start | bytes 393224 | tf_op jit(solution)/shard_map/ppermute | solution.py:428
  206.5 1.7 mix.1.mixed_ref
  209.3 1.7 collective-permute-done.26.refs_2_
  211.4 9.7 %finish.1 = bf16[1024,768]{1,0:T(8,128)(2,1)} custom-call(s32[2]{0:T(128)S(1)} %pad_add_fusion.place_ref, f32[1024,768]{1,0:T(8,128)S(1)} %mix.1.mixed_ref, bf16[16,32,128]{2,1,0:T(8,128)(2,1)S(1)} %get-tuple-element.75.refs_0_, bf16[16,32,128]{2,1,0:T(8,128)(2,1)S(1)} %collective-permute-done.25.refs_1_, ...), custom_call_target="tpu_custom_call" | custom-call | tf_op jit(solution)/shard_map/finish/pallas_call | solution.py:395
  (87 shorter events, 14.6 us)
Async XLA Ops:
  0.0 3.6 %collective-permute-start.3 = (bf16[1024,768]{1,0:T(8,128)(2,1)}, bf16[1024,768]{1,0:T(8,128)(2,1)S(1)}, u32[]{:S(2)}, u32[]{:S(2)}) collective-permute-start(bf16[1024,768]{1,0:T(8,128)(2,1)} %near_ref.5), channel_id=1, source_target_pairs={{0,1},{1,0},{2,3},{3,2},{4,5},{5,4},{6,7},{7,6},{8,9},{9,8},{10,11... | collective-permute-start | bytes 4718600 | tf_op jit(solution)/shard_map/ppermute | solution.py:421
  3.6 1.4 copy-start
  7.6 19.2 %copy-start.18 = (s32[1,16,16]{2,1,0:T(8,128)S(1)}, s32[1,16,16]{2,1,0:T(8,128)}, u32[]{:S(2)}) copy-start(s32[1,16,16]{2,1,0:T(8,128)} %list_ref.5) | copy-start | bytes 3076
  9.3 10.7 %collective-permute-start.12 = (bf16[32,32,128]{2,1,0:T(8,128)(2,1)S(1)}, bf16[32,32,128]{2,1,0:T(8,128)(2,1)S(1)}, u32[]{:S(2)}, u32[]{:S(2)}) collective-permute-start(bf16[32,32,128]{2,1,0:T(8,128)(2,1)S(1)} %get-tuple-element.58), channel_id=1, source_target_pairs={{0,2},{1,3},{2,4},{3,5},{4,6},{5,7},{6,0},{7,1},{8,10},{9,11},{10,... | collective-permute-start | bytes 786440 | tf_op jit(solution)/shard_map/ppermute | solution.py:428
  11.3 15.5 %collective-permute-start.13 = (bf16[32,32,128]{2,1,0:T(8,128)(2,1)S(1)}, bf16[32,32,128]{2,1,0:T(8,128)(2,1)S(1)}, u32[]{:S(2)}, u32[]{:S(2)}) collective-permute-start(bf16[32,32,128]{2,1,0:T(8,128)(2,1)S(1)} %get-tuple-element.59), channel_id=1, source_target_pairs={{0,4},{1,5},{2,6},{3,7},{4,0},{5,1},{6,2},{7,3},{8,12},{9,13},{10,... | collective-permute-start | bytes 786440 | tf_op jit(solution)/shard_map/ppermute | solution.py:428
  14.9 11.9 %collective-permute-start.14 = (bf16[32,32,128]{2,1,0:T(8,128)(2,1)S(1)}, bf16[32,32,128]{2,1,0:T(8,128)(2,1)S(1)}, u32[]{:S(2)}, u32[]{:S(2)}) collective-permute-start(bf16[32,32,128]{2,1,0:T(8,128)(2,1)S(1)} %get-tuple-element.60), channel_id=1, source_target_pairs={{0,6},{1,7},{2,0},{3,1},{4,2},{5,3},{6,4},{7,5},{8,14},{9,15},{10,... | collective-permute-start | bytes 786440 | tf_op jit(solution)/shard_map/ppermute | solution.py:428
  30.9 7.4 %copy-start.1 = (bf16[1024,768]{1,0:T(8,128)(2,1)S(1)}, bf16[1024,768]{1,0:T(8,128)(2,1)}, u32[]{:S(2)}) copy-start(bf16[1024,768]{1,0:T(8,128)(2,1)} %near_ref.5) | copy-start | bytes 4718596
  30.9 33.5 %all-to-all-start.1 = ((bf16[16,16,32,128]{3,2,1,0:T(8,128)(2,1)}), bf16[16,16,32,128]{3,2,1,0:T(8,128)(2,1)}, u32[]{:S(2)}, u32[]{:S(2)}) async-start(bf16[16,16,32,128]{3,2,1,0:T(8,128)(2,1)} %bitcast.11), calls=%async_computation.1 | async-start | bytes 4194304 | tf_op jit(solution)/shard_map/all_to_all | solution.py:453
  42.5 8.6 %collective-permute-start.4 = (bf16[32,32,128]{2,1,0:T(8,128)(2,1)S(1)}, bf16[32,32,128]{2,1,0:T(8,128)(2,1)S(1)}, u32[]{:S(2)}, u32[]{:S(2)}) collective-permute-start(bf16[32,32,128]{2,1,0:T(8,128)(2,1)S(1)} %get-tuple-element.47), channel_id=1, source_target_pairs={{0,2},{1,3},{2,4},{3,5},{4,6},{5,7},{6,0},{7,1},{8,10},{9,11},{10,... | collective-permute-start | bytes 786440 | tf_op jit(solution)/shard_map/ppermute | solution.py:428
  43.8 13.6 %collective-permute-start.5 = (bf16[32,32,128]{2,1,0:T(8,128)(2,1)S(1)}, bf16[32,32,128]{2,1,0:T(8,128)(2,1)S(1)}, u32[]{:S(2)}, u32[]{:S(2)}) collective-permute-start(bf16[32,32,128]{2,1,0:T(8,128)(2,1)S(1)} %get-tuple-element.48), channel_id=1, source_target_pairs={{0,4},{1,5},{2,6},{3,7},{4,0},{5,1},{6,2},{7,3},{8,12},{9,13},{10,... | collective-permute-start | bytes 786440 | tf_op jit(solution)/shard_map/ppermute | solution.py:428
  46.2 11.3 %collective-permute-start.6 = (bf16[32,32,128]{2,1,0:T(8,128)(2,1)S(1)}, bf16[32,32,128]{2,1,0:T(8,128)(2,1)S(1)}, u32[]{:S(2)}, u32[]{:S(2)}) collective-permute-start(bf16[32,32,128]{2,1,0:T(8,128)(2,1)S(1)} %get-tuple-element.49), channel_id=1, source_target_pairs={{0,6},{1,7},{2,0},{3,1},{4,2},{5,3},{6,4},{7,5},{8,14},{9,15},{10,... | collective-permute-start | bytes 786440 | tf_op jit(solution)/shard_map/ppermute | solution.py:428
  58.7 1.4 copy-start.11
  64.4 32.3 %all-to-all-start = ((bf16[16,16,32,128]{3,2,1,0:T(8,128)(2,1)}), bf16[16,16,32,128]{3,2,1,0:T(8,128)(2,1)}, u32[]{:S(2)}, u32[]{:S(2)}) async-start(bf16[16,16,32,128]{3,2,1,0:T(8,128)(2,1)} %bitcast.10), calls=%async_computation | async-start | bytes 4194304 | tf_op jit(solution)/shard_map/all_to_all | solution.py:453
  76.3 10.2 %collective-permute-start.20 = (bf16[32,32,128]{2,1,0:T(8,128)(2,1)S(1)}, bf16[32,32,128]{2,1,0:T(8,128)(2,1)S(1)}, u32[]{:S(2)}, u32[]{:S(2)}) collective-permute-start(bf16[32,32,128]{2,1,0:T(8,128)(2,1)S(1)} %get-tuple-element.69), channel_id=1, source_target_pairs={{0,2},{1,3},{2,4},{3,5},{4,6},{5,7},{6,0},{7,1},{8,10},{9,11},{10,... | collective-permute-start | bytes 786440 | tf_op jit(solution)/shard_map/ppermute | solution.py:428
  78.4 12.6 %collective-permute-start.21 = (bf16[32,32,128]{2,1,0:T(8,128)(2,1)S(1)}, bf16[32,32,128]{2,1,0:T(8,128)(2,1)S(1)}, u32[]{:S(2)}, u32[]{:S(2)}) collective-permute-start(bf16[32,32,128]{2,1,0:T(8,128)(2,1)S(1)} %get-tuple-element.70), channel_id=1, source_target_pairs={{0,4},{1,5},{2,6},{3,7},{4,0},{5,1},{6,2},{7,3},{8,12},{9,13},{10,... | collective-permute-start | bytes 786440 | tf_op jit(solution)/shard_map/ppermute | solution.py:428
  81.4 9.5 %collective-permute-start.22 = (bf16[32,32,128]{2,1,0:T(8,128)(2,1)S(1)}, bf16[32,32,128]{2,1,0:T(8,128)(2,1)S(1)}, u32[]{:S(2)}, u32[]{:S(2)}) collective-permute-start(bf16[32,32,128]{2,1,0:T(8,128)(2,1)S(1)} %get-tuple-element.71), channel_id=1, source_target_pairs={{0,6},{1,7},{2,0},{3,1},{4,2},{5,3},{6,4},{7,5},{8,14},{9,15},{10,... | collective-permute-start | bytes 786440 | tf_op jit(solution)/shard_map/ppermute | solution.py:428
  92.1 1.4 copy-start.13
  96.8 29.1 %all-to-all-start.2 = ((bf16[16,16,32,128]{3,2,1,0:T(8,128)(2,1)}), bf16[16,16,32,128]{3,2,1,0:T(8,128)(2,1)}, u32[]{:S(2)}, u32[]{:S(2)}) async-start(bf16[16,16,32,128]{3,2,1,0:T(8,128)(2,1)} %bitcast.12), calls=%async_computation.2 | async-start | bytes 4194304 | tf_op jit(solution)/shard_map/all_to_all | solution.py:453
  104.0 54.4 %collective-permute-start.16 = (bf16[256,32,128]{2,1,0:T(8,128)(2,1)}, bf16[256,32,128]{2,1,0:T(8,128)(2,1)}, u32[]{:S(2)}, u32[]{:S(2)}) collective-permute-start(bf16[256,32,128]{2,1,0:T(8,128)(2,1)} %bitcast.7.refs_6_), channel_id=1, source_target_pairs={{0,1},{1,0},{2,3},{3,2},{4,5},{5,4},{6,7},{7,6},{8,9},{9,8},{10,11... | collective-permute-start | bytes 6291464 | tf_op jit(solution)/shard_map/ppermute | solution.py:421
  104.0 70.2 %collective-permute-start.8 = (bf16[256,32,128]{2,1,0:T(8,128)(2,1)}, bf16[256,32,128]{2,1,0:T(8,128)(2,1)}, u32[]{:S(2)}, u32[]{:S(2)}) collective-permute-start(bf16[256,32,128]{2,1,0:T(8,128)(2,1)} %bitcast.5.refs_6_), channel_id=1, source_target_pairs={{0,1},{1,0},{2,3},{3,2},{4,5},{5,4},{6,7},{7,6},{8,9},{9,8},{10,11... | collective-permute-start | bytes 6291464 | tf_op jit(solution)/shard_map/ppermute | solution.py:421
  125.8 32.5 %copy-start.15 = (bf16[4,16,32,128]{3,2,1,0:T(8,128)(2,1)S(1)}, bf16[4,16,32,128]{3,2,1,0:T(8,128)(2,1)}, u32[]{:S(2)}) copy-start(bf16[4,16,32,128]{3,2,1,0:T(8,128)(2,1)} %copy-done.14) | copy-start | bytes 1572868
  125.8 32.5 %copy-start.19 = (s32[128,8]{0,1:T(8,128)S(1)}, s32[128,8]{0,1:T(8,128)}, u32[]{:S(2)}) copy-start(s32[128,8]{0,1:T(8,128)} %param.23) | copy-start | bytes 12292
  125.9 32.5 %copy-start.20 = (s32[128,8]{0,1:T(8,128)S(1)}, s32[128,8]{0,1:T(8,128)}, u32[]{:S(2)}) copy-start(s32[128,8]{0,1:T(8,128)} %param.24) | copy-start | bytes 12292
  125.9 32.5 %copy-start.21 = (s32[128]{0:T(128)S(1)}, s32[128]{0:T(128)}, u32[]{:S(2)}) copy-start(s32[128]{0:T(128)} %count_ref.5) | copy-start | bytes 1540
  125.9 62.3 %collective-permute-start.24 = (bf16[256,32,128]{2,1,0:T(8,128)(2,1)}, bf16[256,32,128]{2,1,0:T(8,128)(2,1)S(1)}, u32[]{:S(2)}, u32[]{:S(2)}) collective-permute-start(bf16[256,32,128]{2,1,0:T(8,128)(2,1)} %bitcast.9.refs_6_), channel_id=1, source_target_pairs={{0,1},{1,0},{2,3},{3,2},{4,5},{5,4},{6,7},{7,6},{8,9},{9,8},{10,11... | collective-permute-start | bytes 6291464 | tf_op jit(solution)/shard_map/ppermute | solution.py:421
  127.3 29.0 %copy-start.24 = (bf16[4,16,32,128]{3,2,1,0:T(8,128)(2,1)S(1)}, bf16[4,16,32,128]{3,2,1,0:T(8,128)(2,1)}, u32[]{:S(2)}) copy-start(bf16[4,16,32,128]{3,2,1,0:T(8,128)(2,1)} %copy-done.23) | copy-start | bytes 1572868
  127.3 30.3 %copy-start.26 = (bf16[4,16,32,128]{3,2,1,0:T(8,128)(2,1)S(1)}, bf16[4,16,32,128]{3,2,1,0:T(8,128)(2,1)}, u32[]{:S(2)}) copy-start(bf16[4,16,32,128]{3,2,1,0:T(8,128)(2,1)} %copy-done.25) | copy-start | bytes 1572868
  129.6 17.1 %collective-permute-start = (bf16[3,16,32,128]{3,2,1,0:T(8,128)(2,1)S(1)}, bf16[3,16,32,128]{3,2,1,0:T(8,128)(2,1)S(1)}, u32[]{:S(2)}, u32[]{:S(2)}) collective-permute-start(bf16[3,16,32,128]{3,2,1,0:T(8,128)(2,1)S(1)} %get-tuple-element.43), channel_id=1, source_target_pairs={{0,2},{1,3},{2,4},{3,5},{4,6},{5,7},{6,0},{7,1},{8,10},{9,11},{10,... | collective-permute-start | bytes 1179656 | tf_op jit(solution)/shard_map/ppermute | solution.py:428
  131.9 24.4 %collective-permute-start.1 = (bf16[3,16,32,128]{3,2,1,0:T(8,128)(2,1)S(1)}, bf16[3,16,32,128]{3,2,1,0:T(8,128)(2,1)S(1)}, u32[]{:S(2)}, u32[]{:S(2)}) collective-permute-start(bf16[3,16,32,128]{3,2,1,0:T(8,128)(2,1)S(1)} %get-tuple-element.44), channel_id=1, source_target_pairs={{0,4},{1,5},{2,6},{3,7},{4,0},{5,1},{6,2},{7,3},{8,12},{9,13},{10,... | collective-permute-start | bytes 1179656 | tf_op jit(solution)/shard_map/ppermute | solution.py:428
  146.7 10.9 %collective-permute-start.2 = (bf16[3,16,32,128]{3,2,1,0:T(8,128)(2,1)S(1)}, bf16[3,16,32,128]{3,2,1,0:T(8,128)(2,1)S(1)}, u32[]{:S(2)}, u32[]{:S(2)}) collective-permute-start(bf16[3,16,32,128]{3,2,1,0:T(8,128)(2,1)S(1)} %get-tuple-element.45), channel_id=1, source_target_pairs={{0,6},{1,7},{2,0},{3,1},{4,2},{5,3},{6,4},{7,5},{8,14},{9,15},{10,... | collective-permute-start | bytes 1179656 | tf_op jit(solution)/shard_map/ppermute | solution.py:428
  156.3 1.9 collective-permute-start.15
  157.6 12.7 %collective-permute-start.7 = (bf16[4,16,32,128]{3,2,1,0:T(8,128)(2,1)S(1)}, bf16[4,16,32,128]{3,2,1,0:T(8,128)(2,1)S(1)}, u32[]{:S(2)}, u32[]{:S(2)}) collective-permute-start(bf16[4,16,32,128]{3,2,1,0:T(8,128)(2,1)S(1)} %copy-done.26), channel_id=1, source_target_pairs={{0,1},{1,0},{2,3},{3,2},{4,5},{5,4},{6,7},{7,6},{8,9},{9,8},{10,11... | collective-permute-start | bytes 1572872 | tf_op jit(solution)/shard_map/ppermute | solution.py:421
  158.2 27.6 %collective-permute-start.23 = (bf16[4,16,32,128]{3,2,1,0:T(8,128)(2,1)S(1)}, bf16[4,16,32,128]{3,2,1,0:T(8,128)(2,1)S(1)}, u32[]{:S(2)}, u32[]{:S(2)}) collective-permute-start(bf16[4,16,32,128]{3,2,1,0:T(8,128)(2,1)S(1)} %get-tuple-element.73), channel_id=1, source_target_pairs={{0,1},{1,0},{2,3},{3,2},{4,5},{5,4},{6,7},{7,6},{8,9},{9,8},{10,11... | collective-permute-start | bytes 1572872 | tf_op jit(solution)/shard_map/ppermute | solution.py:421
  158.4 15.8 %copy-start.17 = (bf16[4,16,32,128]{3,2,1,0:T(8,128)(2,1)S(1)}, bf16[4,16,32,128]{3,2,1,0:T(8,128)(2,1)}, u32[]{:S(2)}) copy-start(bf16[4,16,32,128]{3,2,1,0:T(8,128)(2,1)} %copy-done.16) | copy-start | bytes 1572868
  170.2 20.3 %collective-permute-start.17 = (bf16[16,32,128]{2,1,0:T(8,128)(2,1)S(1)}, bf16[16,32,128]{2,1,0:T(8,128)(2,1)S(1)}, u32[]{:S(2)}, u32[]{:S(2)}) collective-permute-start(bf16[16,32,128]{2,1,0:T(8,128)(2,1)S(1)} %get-tuple-element.65), channel_id=1, source_target_pairs={{0,2},{1,3},{2,4},{3,5},{4,6},{5,7},{6,0},{7,1},{8,10},{9,11},{10,... | collective-permute-start | bytes 393224 | tf_op jit(solution)/shard_map/ppermute | solution.py:428
  170.3 31.3 %collective-permute-start.18 = (bf16[16,32,128]{2,1,0:T(8,128)(2,1)S(1)}, bf16[16,32,128]{2,1,0:T(8,128)(2,1)S(1)}, u32[]{:S(2)}, u32[]{:S(2)}) collective-permute-start(bf16[16,32,128]{2,1,0:T(8,128)(2,1)S(1)} %get-tuple-element.66), channel_id=1, source_target_pairs={{0,4},{1,5},{2,6},{3,7},{4,0},{5,1},{6,2},{7,3},{8,12},{9,13},{10,... | collective-permute-start | bytes 393224 | tf_op jit(solution)/shard_map/ppermute | solution.py:428
  174.2 27.6 %collective-permute-start.19 = (bf16[16,32,128]{2,1,0:T(8,128)(2,1)S(1)}, bf16[16,32,128]{2,1,0:T(8,128)(2,1)S(1)}, u32[]{:S(2)}, u32[]{:S(2)}) collective-permute-start(bf16[16,32,128]{2,1,0:T(8,128)(2,1)S(1)} %get-tuple-element.67), channel_id=1, source_target_pairs={{0,6},{1,7},{2,0},{3,1},{4,2},{5,3},{6,4},{7,5},{8,14},{9,15},{10,... | collective-permute-start | bytes 393224 | tf_op jit(solution)/shard_map/ppermute | solution.py:428
  185.8 20.6 %collective-permute-start.10 = (bf16[16,32,128]{2,1,0:T(8,128)(2,1)S(1)}, bf16[16,32,128]{2,1,0:T(8,128)(2,1)S(1)}, u32[]{:S(2)}, u32[]{:S(2)}) collective-permute-start(bf16[16,32,128]{2,1,0:T(8,128)(2,1)S(1)} %get-tuple-element.55), channel_id=1, source_target_pairs={{0,4},{1,5},{2,6},{3,7},{4,0},{5,1},{6,2},{7,3},{8,12},{9,13},{10,... | collective-permute-start | bytes 393224 | tf_op jit(solution)/shard_map/ppermute | solution.py:428
  188.2 18.3 %collective-permute-start.11 = (bf16[16,32,128]{2,1,0:T(8,128)(2,1)S(1)}, bf16[16,32,128]{2,1,0:T(8,128)(2,1)S(1)}, u32[]{:S(2)}, u32[]{:S(2)}) collective-permute-start(bf16[16,32,128]{2,1,0:T(8,128)(2,1)S(1)} %get-tuple-element.56), channel_id=1, source_target_pairs={{0,6},{1,7},{2,0},{3,1},{4,2},{5,3},{6,4},{7,5},{8,14},{9,15},{10,... | collective-permute-start | bytes 393224 | tf_op jit(solution)/shard_map/ppermute | solution.py:428
  190.6 15.9 %collective-permute-start.9 = (bf16[16,32,128]{2,1,0:T(8,128)(2,1)S(1)}, bf16[16,32,128]{2,1,0:T(8,128)(2,1)S(1)}, u32[]{:S(2)}, u32[]{:S(2)}) collective-permute-start(bf16[16,32,128]{2,1,0:T(8,128)(2,1)S(1)} %get-tuple-element.54), channel_id=1, source_target_pairs={{0,2},{1,3},{2,4},{3,5},{4,6},{5,7},{6,0},{7,1},{8,10},{9,11},{10,... | collective-permute-start | bytes 393224 | tf_op jit(solution)/shard_map/ppermute | solution.py:428
  190.6 15.8 %copy-start.27 = (f32[768]{0:T(1024)S(1)}, f32[768]{0:T(1024)}, u32[]{:S(2)}) copy-start(f32[768]{0:T(1024)} %param.20) | copy-start | bytes 9220
  190.6 15.9 %copy-start.28 = (f32[768]{0:T(1024)S(1)}, f32[768]{0:T(1024)}, u32[]{:S(2)}) copy-start(f32[768]{0:T(1024)} %param.21) | copy-start | bytes 9220
  190.6 15.9 %copy-start.8 = (bf16[768,768]{1,0:T(8,128)(2,1)S(1)}, bf16[768,768]{1,0:T(8,128)(2,1)}, u32[]{:S(2)}) copy-start(bf16[768,768]{1,0:T(8,128)(2,1)} %refs_4_.1) | copy-start | bytes 3538948
  201.7 7.7 %collective-permute-start.25 = (bf16[16,32,128]{2,1,0:T(8,128)(2,1)S(1)}, bf16[16,32,128]{2,1,0:T(8,128)(2,1)S(1)}, u32[]{:S(2)}, u32[]{:S(2)}) collective-permute-start(bf16[16,32,128]{2,1,0:T(8,128)(2,1)S(1)} %get-tuple-element.76), channel_id=1, source_target_pairs={{0,2},{1,3},{2,4},{3,5},{4,6},{5,7},{6,0},{7,1},{8,10},{9,11},{10,... | collective-permute-start | bytes 393224 | tf_op jit(solution)/shard_map/ppermute | solution.py:428
  201.8 9.3 %collective-permute-start.26 = (bf16[16,32,128]{2,1,0:T(8,128)(2,1)S(1)}, bf16[16,32,128]{2,1,0:T(8,128)(2,1)S(1)}, u32[]{:S(2)}, u32[]{:S(2)}) collective-permute-start(bf16[16,32,128]{2,1,0:T(8,128)(2,1)S(1)} %get-tuple-element.77), channel_id=1, source_target_pairs={{0,4},{1,5},{2,6},{3,7},{4,0},{5,1},{6,2},{7,3},{8,12},{9,13},{10,... | collective-permute-start | bytes 393224 | tf_op jit(solution)/shard_map/ppermute | solution.py:428
  206.4 5.0 %collective-permute-start.27 = (bf16[16,32,128]{2,1,0:T(8,128)(2,1)S(1)}, bf16[16,32,128]{2,1,0:T(8,128)(2,1)S(1)}, u32[]{:S(2)}, u32[]{:S(2)}) collective-permute-start(bf16[16,32,128]{2,1,0:T(8,128)(2,1)S(1)} %get-tuple-element.78), channel_id=1, source_target_pairs={{0,6},{1,7},{2,0},{3,1},{4,2},{5,3},{6,4},{7,5},{8,14},{9,15},{10,... | collective-permute-start | bytes 393224 | tf_op jit(solution)/shard_map/ppermute | solution.py:428
  206.5 4.9 %copy-start.9 = (bf16[768,1536]{1,0:T(8,128)(2,1)S(1)}, bf16[768,1536]{1,0:T(8,128)(2,1)}, u32[]{:S(2)}) copy-start(bf16[768,1536]{1,0:T(8,128)(2,1)} %refs_5_.1) | copy-start | bytes 7077892
  206.5 4.9 %copy-start.10 = (bf16[1536,768]{1,0:T(8,128)(2,1)S(1)}, bf16[1536,768]{1,0:T(8,128)(2,1)}, u32[]{:S(2)}) copy-start(bf16[1536,768]{1,0:T(8,128)(2,1)} %refs_6_.1) | copy-start | bytes 7077892
  (12 other events, 13.5 us)

commit v4 on v3

--- a/solution.py
+++ b/solution.py
@@ -25,7 +25,7 @@
 BF16 = jnp.bfloat16
 VMEM = pl.BlockSpec(memory_space=pltpu.VMEM)
 SMEM = pl.BlockSpec(memory_space=pltpu.SMEM)
-ANY = pl.BlockSpec(memory_space=pl.ANY)
+HBM = pl.BlockSpec(memory_space=pltpu.HBM)
 TILE = (HALF, LANES)
 
 
@@ -54,14 +54,11 @@
     return jnp.concatenate([first, second], axis=1).reshape(blocks * BLOCK, LANES).astype(BF16)
 
 
-def params(mebibytes):
-    return pltpu.CompilerParams(vmem_limit_bytes=mebibytes << 20)
-
-
-def keys_values_kernel(chunk, place_ref, near_ref, far_ref, key_ref, value_ref, *refs):
-    outs, (weight, packed, sem) = refs[:CHIPS], refs[CHIPS:]
-    z, core = place_ref[0], place_ref[1]
-
+def params(room):
+    return pltpu.CompilerParams(vmem_limit_bytes=67_043_328 - room)
+
+
+def fetch_weight(chunk, core, key_ref, value_ref, weight, sem):
     def fetch(source):
         copy = pltpu.make_async_copy(source.at[:, chunk * COLS : (chunk + 1) * COLS], weight, sem)
         copy.start()
@@ -75,15 +72,74 @@
     def _():
         fetch(value_ref)
 
-    for owner, feat_ref in ((core, near_ref), (1 - core, far_ref)):
-        for half in range(2):
-            made = jnp.dot(
-                feat_ref[half * 512 : half * 512 + 512, :], weight[...], preferred_element_type=F32
-            )
-            for pair in range(2):
-                both = pack_pair(made[:, pair * LANES : (pair + 1) * LANES])
-                for side in range(2):
-                    packed[2 * pair + side, pl.ds(owner * OWN + half * 8, 8)] = both[side]
+
+def pack_rows(feat_ref, weight, packed, first):
+    for half in range(2):
+        made = jnp.dot(
+            feat_ref[half * 512 : half * 512 + 512, :], weight[...], preferred_element_type=F32
+        )
+        for pair in range(2):
+            both = pack_pair(made[:, pair * LANES : (pair + 1) * LANES])
+            for side in range(2):
+                packed[2 * pair + side, pl.ds(first + half * 8, 8)] = both[side]
+
+
+def near_kernel(place_ref, near_ref, key_ref, value_ref, weight, packed, sem):
+    fetch_weight(0, place_ref[1], key_ref, value_ref, weight, sem)
+    pack_rows(near_ref, weight, packed, 0)
+
+
+def project_near(place, near, w_key, w_value):
+    rows, width = near.shape
+    return pl.pallas_call(
+        near_kernel,
+        in_specs=[SMEM, VMEM, HBM, HBM],
+        out_specs=[VMEM] * 2,
+        out_shape=[
+            jax.ShapeDtypeStruct((width, COLS), BF16),
+            jax.ShapeDtypeStruct((CHIPS, OWN) + TILE, BF16),
+        ],
+        scratch_shapes=[pltpu.SemaphoreType.DMA],
+        compiler_params=params(0),
+        cost_estimate=pl.CostEstimate(
+            flops=2 * rows * width * COLS, bytes_accessed=3 << 20, transcendentals=0
+        ),
+        name="near_keys_values",
+    )(place, near, w_key, w_value)
+
+
+def far_kernel(place_ref, far_ref, weight, near_packed, *refs):
+    outs, (packed,) = refs[:CHIPS], refs[CHIPS:]
+    z, core = place_ref[0], place_ref[1]
+    pack_rows(far_ref, weight, packed, 0)
+    for step in range(CHIPS):
+        dest = lax.rem(z + step, CHIPS)
+        outs[step][pl.ds(core * OWN, OWN)] = near_packed[dest]
+        outs[step][pl.ds((1 - core) * OWN, OWN)] = packed[dest]
+
+
+def project_far(place, far, weight, near_packed):
+    rows, width = far.shape
+    return pl.pallas_call(
+        far_kernel,
+        in_specs=[SMEM] + [VMEM] * 3,
+        out_specs=[VMEM] * CHIPS,
+        out_shape=[jax.ShapeDtypeStruct((2 * OWN,) + TILE, BF16)] * CHIPS,
+        scratch_shapes=[pltpu.VMEM((CHIPS, OWN) + TILE, BF16)],
+        compiler_params=params(0),
+        cost_estimate=pl.CostEstimate(
+            flops=2 * rows * width * COLS, bytes_accessed=3 << 20, transcendentals=0
+        ),
+        name="far_keys_values",
+    )(place, far, weight, near_packed)
+
+
+def keys_values_kernel(chunk, place_ref, near_ref, far_ref, key_ref, value_ref, *refs):
+    outs, (weight, packed, sem) = refs[:CHIPS], refs[CHIPS:]
+    z, core = place_ref[0], place_ref[1]
+    fetch_weight(chunk, core, key_ref, value_ref, weight, sem)
+    pack_rows(near_ref, weight, packed, core * OWN)
+    pack_rows(far_ref, weight, packed, (1 - core) * OWN)
     for step in range(CHIPS):
         outs[step][...] = packed[lax.rem(z + step, CHIPS)]
 
@@ -92,7 +148,7 @@
     rows, width = near.shape
     return pl.pallas_call(
         functools.partial(keys_values_kernel, chunk),
-        in_specs=[SMEM, VMEM, VMEM, ANY, ANY],
+        in_specs=[SMEM, VMEM, VMEM, HBM, HBM],
         out_specs=[VMEM] * CHIPS,
         out_shape=[jax.ShapeDtypeStruct((2 * OWN,) + TILE, BF16)] * CHIPS,
         scratch_shapes=[
@@ -100,7 +156,7 @@
             pltpu.VMEM((CHIPS, 2 * OWN) + TILE, BF16),
             pltpu.SemaphoreType.DMA,
         ],
-        compiler_params=params(24),
+        compiler_params=params(0),
         cost_estimate=pl.CostEstimate(
             flops=4 * rows * width * COLS, bytes_accessed=5 << 20, transcendentals=0
         ),
@@ -134,7 +190,7 @@
         out_specs=[VMEM] * CHIPS,
         out_shape=[jax.ShapeDtypeStruct((CHUNKS, OWN) + TILE, BF16)] * CHIPS,
         scratch_shapes=[pltpu.VMEM((CHIPS, CHUNKS, OWN) + TILE, BF16)],
-        compiler_params=params(24),
+        compiler_params=params(0),
         cost_estimate=pl.CostEstimate(
             flops=2 * rows * width * width, bytes_accessed=5 << 20, transcendentals=0
         ),
@@ -143,21 +199,36 @@
 
 
 def collect_kernel(list_ref, place_ref, *refs):
-    parts, (out_ref, own_ref, swap_ref, held) = refs[:CHIPS], refs[CHIPS:]
+    parts, (out_ref, own_ref, swap_ref, held, picked, sems) = refs[:CHIPS], refs[CHIPS:]
     z, core = place_ref[0], place_ref[1]
     for step in range(CHIPS):
         source = lax.rem(z + CHIPS - step, CHIPS)
         held[pl.ds(source * 2 * OWN, 2 * OWN)] = parts[step][...]
+    quarter = picked.shape[0] // CAP // 4
 
     def body(step, carry):
         for extra in range(CAP):
-            out_ref[step * CAP + extra] = held[list_ref[0, step, extra]]
+            picked[step * CAP + extra] = held[list_ref[0, step, extra]]
         return carry
 
-    lax.fori_loop(0, out_ref.shape[0] // CAP, body, 0)
+    copies = []
+    for part in range(4):
+        lax.fori_loop(part * quarter, (part + 1) * quarter, body, 0)
+        at = pl.ds(part * quarter * CAP, quarter * CAP)
+        copies.append(pltpu.make_async_copy(picked.at[at], out_ref.at[at], sems.at[part]))
+        copies[-1].start()
     for source in range(CHIPS):
-        own_ref[source] = held[pl.ds(source * 2 * OWN + core * OWN, OWN)]
-        swap_ref[source] = held[pl.ds(source * 2 * OWN + (1 - core) * OWN, OWN)]
+        for which, target in enumerate((own_ref, swap_ref)):
+            side = core if which == 0 else 1 - core
+            at = pl.ds(source * 2 * OWN + side * OWN, OWN)
+            copies.append(
+                pltpu.make_async_copy(
+                    held.at[at], target.at[source], sems.at[4 + 2 * source + which]
+                )
+            )
+            copies[-1].start()
+    for copy in copies:
+        copy.wait()
 
 
 def collect(send_list, place, parts):
@@ -166,10 +237,14 @@
     return pl.pallas_call(
         collect_kernel,
         in_specs=[SMEM, SMEM] + [VMEM] * CHIPS,
-        out_specs=[VMEM] * 3,
+        out_specs=[HBM] * 3,
         out_shape=[jax.ShapeDtypeStruct((slots,) + TILE, BF16), own, own],
-        scratch_shapes=[pltpu.VMEM((CHIPS * 2 * OWN,) + TILE, BF16)],
-        compiler_params=params(24),
+        scratch_shapes=[
+            pltpu.VMEM((CHIPS * 2 * OWN,) + TILE, BF16),
+            pltpu.VMEM((slots,) + TILE, BF16),
+            pltpu.SemaphoreType.DMA((4 + 2 * CHIPS,)),
+        ],
+        compiler_params=params(0),
         cost_estimate=pl.CostEstimate(flops=0, bytes_accessed=5 << 20, transcendentals=0),
         name="collect",
     )(send_list, place, *parts)
@@ -178,19 +253,20 @@
 def attend_kernel(chunk, owner_ref, slot_ref, count_ref, place_ref, *refs):
     parts, (own_ref, swap_ref, mine_ref, other_ref) = refs[:CHIPS], refs[CHIPS : CHIPS + 4]
     outs = refs[CHIPS + 4 : 2 * CHIPS + 4]
-    queries, made, keys, values, own_keys, own_values = refs[2 * CHIPS + 4 :]
+    queries, made, keys, values, own_keys, own_values, sems = refs[2 * CHIPS + 4 :]
     z, core = place_ref[0], place_ref[1]
 
     def place_in(near, near_own, far, far_own):
-        def body(step, carry):
-            at = pl.ds(step * 8, 8)
-            near[at] = mine_ref[at]
-            far[at] = other_ref[at]
-            return carry
-
-        lax.fori_loop(0, mine_ref.shape[0] // 8, body, 0)
-        near_own[...] = own_ref[...]
-        far_own[...] = swap_ref[...]
+        copies = [
+            pltpu.make_async_copy(mine_ref, near, sems.at[0]),
+            pltpu.make_async_copy(other_ref, far, sems.at[1]),
+            pltpu.make_async_copy(own_ref, near_own, sems.at[2]),
+            pltpu.make_async_copy(swap_ref, far_own, sems.at[3]),
+        ]
+        for copy in copies:
+            copy.start()
+        for copy in copies:
+            copy.wait()
 
     @pl.when(core == 0)
     def _():
@@ -296,7 +372,7 @@
     blocks = pltpu.VMEM((CHIPS, OWN) + TILE, BF16)
     return pl.pallas_call(
         functools.partial(attend_kernel, chunk),
-        in_specs=[SMEM] * 4 + [VMEM] * (CHIPS + 4),
+        in_specs=[SMEM] * 4 + [VMEM] * CHIPS + [HBM] * 4,
         out_specs=[VMEM] * CHIPS,
         out_shape=[jax.ShapeDtypeStruct((OWN,) + TILE, BF16)] * CHIPS,
         scratch_shapes=[
@@ -306,8 +382,9 @@
             pltpu.VMEM((slots,) + TILE, BF16),
             blocks,
             blocks,
+            pltpu.SemaphoreType.DMA((4,)),
         ],
-        compiler_params=params(28),
+        compiler_params=params(0),
         cost_estimate=pl.CostEstimate(
             flops=64 * 4 * 128 * 128 * 384, bytes_accessed=8 << 20, transcendentals=64 * 128 * 384
         ),
@@ -334,7 +411,8 @@
 
 
 def mix_kernel(place_ref, feat_ref, *refs):
-    parts, (weight_ref, out_ref, held) = refs[: 2 * CHIPS], refs[2 * CHIPS :]
+    parts, (weight_ref, out_ref, held, made, sems) = refs[: 2 * CHIPS], refs[2 * CHIPS :]
+    copies = []
     rows = feat_ref.shape[0] // 2
     for chunk in range(2):
         gather_parts(place_ref, parts[chunk * CHIPS : (chunk + 1) * CHIPS], held.at[chunk])
@@ -344,7 +422,11 @@
         for chunk in range(2):
             weight = weight_ref[chunk * COLS : (chunk + 1) * COLS, :]
             mixed = mixed + mixed_rows(held.at[chunk], half, weight)
-        out_ref[at, :] = mixed
+        made[at, :] = mixed
+        copies.append(pltpu.make_async_copy(made.at[at], out_ref.at[at], sems.at[half]))
+        copies[-1].start()
+    for copy in copies:
+        copy.wait()
 
 
 def mix(place, features, backs, w_out):
@@ -352,10 +434,14 @@
     return pl.pallas_call(
         mix_kernel,
         in_specs=[SMEM, VMEM] + [VMEM] * (2 * CHIPS + 1),
-        out_specs=VMEM,
+        out_specs=HBM,
         out_shape=jax.ShapeDtypeStruct((rows, width), F32),
-        scratch_shapes=[pltpu.VMEM((2, CHIPS, OWN) + TILE, BF16)],
-        compiler_params=params(24),
+        scratch_shapes=[
+            pltpu.VMEM((2, CHIPS, OWN) + TILE, BF16),
+            pltpu.VMEM((rows, width), F32),
+            pltpu.SemaphoreType.DMA((2,)),
+        ],
+        compiler_params=params(0),
         cost_estimate=pl.CostEstimate(
             flops=4 * rows * COLS * width, bytes_accessed=7 << 20, transcendentals=0
         ),
@@ -365,27 +451,33 @@
 
 def finish_kernel(place_ref, mixed_ref, *refs):
     parts, refs = refs[:CHIPS], refs[CHIPS:]
-    out_w_ref, up_ref, down_ref, gain_a_ref, gain_f_ref, result_ref, held, up, down, sems = refs
+    out_w_ref, up_ref, down_ref, gain_a_ref, gain_f_ref, result_ref, *scratch = refs
+    held, early, out_w, up, down, sems = scratch
+    rows = mixed_ref.shape[0] // 2
+    halves = [slice(half * rows, (half + 1) * rows) for half in range(2)]
     copies = [
-        pltpu.make_async_copy(up_ref, up, sems.at[0]),
-        pltpu.make_async_copy(down_ref, down, sems.at[1]),
+        pltpu.make_async_copy(out_w_ref.at[(CHUNKS - 1) * COLS :], out_w, sems.at[0]),
+        pltpu.make_async_copy(mixed_ref.at[halves[0]], early.at[halves[0]], sems.at[1]),
+        pltpu.make_async_copy(mixed_ref.at[halves[1]], early.at[halves[1]], sems.at[2]),
+        pltpu.make_async_copy(up_ref, up, sems.at[3]),
+        pltpu.make_async_copy(down_ref, down, sems.at[4]),
     ]
     for copy in copies:
         copy.start()
     gather_parts(place_ref, parts, held)
-    rows = mixed_ref.shape[0] // 2
-    last = (CHUNKS - 1) * COLS
+    copies[0].wait()
     firsts = []
-    for half in range(2):
-        at = slice(half * rows, (half + 1) * rows)
-        mixed = mixed_ref[at, :] + mixed_rows(held, half, out_w_ref[last : last + COLS, :])
-        firsts.append(normed(mixed, gain_a_ref[...]).astype(BF16))
-    for copy in copies:
-        copy.wait()
-    for half in range(2):
-        at = slice(half * rows, (half + 1) * rows)
+    for half, at in enumerate(halves):
+        added = mixed_rows(held, half, out_w[...])
+        copies[1 + half].wait()
+        firsts.append(normed(early[at, :] + added, gain_a_ref[...]).astype(BF16))
+    for half, at in enumerate(halves):
         first = firsts[half]
+        if half == 0:
+            copies[3].wait()
         hidden = jnp.maximum(jnp.dot(first, up[...], preferred_element_type=F32), 0.0).astype(BF16)
+        if half == 0:
+            copies[4].wait()
         total = first.astype(F32) + jnp.dot(hidden, down[...], preferred_element_type=F32)
         result_ref[at, :] = normed(total, gain_f_ref[...]).astype(BF16)
 
@@ -394,16 +486,18 @@
     rows, width = mixed.shape
     return pl.pallas_call(
         finish_kernel,
-        in_specs=[SMEM, VMEM] + [VMEM] * CHIPS + [VMEM, ANY, ANY, VMEM, VMEM],
+        in_specs=[SMEM, HBM] + [VMEM] * CHIPS + [HBM, HBM, HBM, VMEM, VMEM],
         out_specs=VMEM,
         out_shape=jax.ShapeDtypeStruct((rows, width), BF16),
         scratch_shapes=[
             pltpu.VMEM((CHIPS, OWN) + TILE, BF16),
+            pltpu.VMEM((rows, width), F32),
+            pltpu.VMEM((COLS, width), BF16),
             pltpu.VMEM(w_up.shape, BF16),
             pltpu.VMEM(w_down.shape, BF16),
-            pltpu.SemaphoreType.DMA((2,)),
+            pltpu.SemaphoreType.DMA((5,)),
         ],
-        compiler_params=params(40),
+        compiler_params=params(0),
         name="finish",
     )(
         place,
@@ -422,12 +516,10 @@
 
 
 def along_z(parts):
-    moved = [parts[0]]
-    for step in range(1, CHIPS):
-        moved.append(
-            lax.ppermute(
-                parts[step], "head", [(i, (i + 2 * step) % (2 * CHIPS)) for i in range(2 * CHIPS)]
-            )
+    moved = list(parts)
+    for step in (2, 1, 3):
+        moved[step] = lax.ppermute(
+            parts[step], "head", [(i, (i + 2 * step) % (2 * CHIPS)) for i in range(2 * CHIPS)]
         )
     return moved
 
@@ -441,9 +533,13 @@
     groups = send_list.shape[1]
     owners, slots = edge_owner.T, edge_slot.T
     far = swap(features)
+    weight, near_packed = project_near(place, features, w_key, w_value)
     collected = []
     for c in range(CHUNKS):
-        parts = project_keys_values(place, features, far, w_key, w_value, c)
+        if c == 0:
+            parts = project_far(place, far, weight, near_packed)
+        else:
+            parts = project_keys_values(place, features, far, w_key, w_value, c)
         parts = along_z(parts)
         collected.append(collect(send_list, place, parts))
     queries = along_z(project_queries(place, features, w_query))

time: 224 us -> 235 us (1.049)
  Pallas kernels: 56.8 us -> 88.5 us
  local copies, waits for them, and re-layouts: 17.7 us -> 2.56 us
  starting transfers between devices: 64.1 us -> 60.7 us
  waiting for transfers between devices: 82.1 us -> 79.4 us
    unnamed x58 -> x0, local copies, waits for them, and re-layouts: 17.7 us -> none
    pallas_call x1 -> x3, Pallas kernels: 9.65 us -> 18.6 us  [the longest x1 11.3 us: finish(): pl.pallas_call(finish_kernel, in_specs=[SMEM, HBM] + [VMEM] * CHIPS + [HB...]
    pallas_call x3, Pallas kernels: 34.5 us -> 41 us  [attend(): pl.pallas_call(functools.partial(attend_kernel, chunk), in_specs=[SMEM] *...]
    pallas_call x3, Pallas kernels: 3.49 us -> 9.41 us  [collect(): pl.pallas_call(collect_kernel, in_specs=[SMEM, SMEM] + [VMEM] * CHIPS, ou...]
    pallas_call x3 -> x2, Pallas kernels: 5.15 us -> 9.99 us  [project_keys_values(): pl.pallas_call(functools.partial(keys_values_kernel, chunk), in_specs=[SM...]
    ppermute x21, starting transfers between devices: 41.2 us -> 37.8 us  [along_z(): lax.ppermute(parts[step], 'head', [(i, (i + 2 * step) % (2 * CHIPS)) for...]
    pallas_call x1, Pallas kernels: 1.72 us -> 4.75 us  [mix(): pl.pallas_call(mix_kernel, in_specs=[SMEM, VMEM] + [VMEM] * (2 * CHIPS +...]
    pallas_call x1, Pallas kernels: 2.31 us -> 4.76 us  [project_queries(): pl.pallas_call(queries_kernel, in_specs=[SMEM, VMEM, VMEM], out_specs=[VM...]
  transfers between devices with their start and end apart: 31 -> 31, of which waited for: 17 -> 14; matrix products, arithmetic and copies ran while one was open for 0% -> 1% of each run, Pallas kernels for 20% -> 30%
where the time goes in v4:
time: 235 us; the launch traced here: 232 us
  Pallas kernels  88.5 us (38%)
  waiting for transfers between devices  79.4 us (34%)
  starting transfers between devices  60.7 us (26%)
  local copies, waits for them, and re-layouts  2.56 us (1%)
    ppermute x21, waiting for transfers between devices, along_z(): lax.ppermute(parts[step], 'head', [(i, (i + 2 * step) % (2 * CHIPS)) for...  49.1 us
    pallas_call x3, Pallas kernels, attend(): pl.pallas_call(functools.partial(attend_kernel, chunk), in_specs=[SMEM] *...  41 us
    ppermute x21, starting transfers between devices, along_z(): lax.ppermute(parts[step], 'head', [(i, (i + 2 * step) % (2 * CHIPS)) for...  37.8 us
    all_to_all x3, waiting for transfers between devices, per_device(): got = lax.all_to_all(sent, 'node', split_axis=0, concat_axis=0, tiled=True)  26.5 us
    all_to_all x3, starting transfers between devices, per_device(): got = lax.all_to_all(sent, 'node', split_axis=0, concat_axis=0, tiled=True)  22.2 us
    pallas_call x1, Pallas kernels, finish(): pl.pallas_call(finish_kernel, in_specs=[SMEM, HBM] + [VMEM] * CHIPS + [HB...  11.3 us
    pallas_call x2, Pallas kernels, project_keys_values(): pl.pallas_call(functools.partial(keys_values_kernel, chunk), in_specs=[SM...  9.99 us
    pallas_call x3, Pallas kernels, collect(): pl.pallas_call(collect_kernel, in_specs=[SMEM, SMEM] + [VMEM] * CHIPS, ou...  9.41 us
  transfers between devices with their start and end apart: 31, of which 14 were waited for; matrix products, arithmetic and copies ran while one was open for 1% of the time, Pallas kernels for 30%

profile of v4, /device:TPU:20, one launch (start us, length us, event | category | flops | bytes accessed | tf_op | source)
XLA Modules:
  0.0 232.1 jit_solution(10339324282388239299)
XLA Ops:
  0.0 0.6 pad_add_fusion.place_ref
  0.7 3.1 %collective-permute-done.3.far_ref = bf16[1024,768]{1,0:T(8,128)(2,1)} collective-permute-done((bf16[1024,768]{1,0:T(8,128)(2,1)}, bf16[1024,768]{1,0:T(8,128)(2,1)}, u32[]{:S(2)}, u32[]{:S(2)}) %collective-permute-start.3) | collective-permute-done | bytes 1572896 | tf_op jit(solution)/shard_map/ppermute | solution.py:515
  3.8 5.0 %keys_values.2 = (bf16[32,32,128]{2,1,0:T(8,128)(2,1)}, bf16[32,32,128]{2,1,0:T(8,128)(2,1)}, bf16[32,32,128]{2,1,0:T(8,128)(2,1)}, bf16[32,32,128]{2,1,0:T(8,128)(2,1)}) custom-call(s32[2]{0:T(128)} %pad_add_fusion.place_ref, bf16[1024,768]{1,0:T(8,128)(2,1)} %near_ref.5, bf16[1024,768]{1,0:T(8,128)(2,1)} %collective-permute-done.3.far_ref, ...), custom_call_target="tpu_custom_call" | custom-call | flops 805306368 | bytes 5242880 | tf_op jit(solution)/shard_map/keys_values/pallas_call | solution.py:149
  8.7 2.0 collective-permute-start.12
  10.7 3.6 %collective-permute-start.13 = (bf16[32,32,128]{2,1,0:T(8,128)(2,1)}, bf16[32,32,128]{2,1,0:T(8,128)(2,1)}, u32[]{:S(2)}, u32[]{:S(2)}) collective-permute-start(bf16[32,32,128]{2,1,0:T(8,128)(2,1)} %get-tuple-element.63), channel_id=1, source_target_pairs={{0,4},{1,5},{2,6},{3,7},{4,0},{5,1},{6,2},{7,3},{8,12},{9,13},{10,... | collective-permute-start | bytes 786440 | tf_op jit(solution)/shard_map/ppermute | solution.py:521
  14.3 1.0 collective-permute-start.14
  15.3 4.5 %collective-permute-done.12.refs_1_ = bf16[32,32,128]{2,1,0:T(8,128)(2,1)} collective-permute-done((bf16[32,32,128]{2,1,0:T(8,128)(2,1)}, bf16[32,32,128]{2,1,0:T(8,128)(2,1)}, u32[]{:S(2)}, u32[]{:S(2)}) %collective-permute-start.12) | collective-permute-done | bytes 262176 | tf_op jit(solution)/shard_map/ppermute | solution.py:521
  19.8 6.8 %collective-permute-done.13.refs_2_ = bf16[32,32,128]{2,1,0:T(8,128)(2,1)} collective-permute-done((bf16[32,32,128]{2,1,0:T(8,128)(2,1)}, bf16[32,32,128]{2,1,0:T(8,128)(2,1)}, u32[]{:S(2)}, u32[]{:S(2)}) %collective-permute-start.13) | collective-permute-done | bytes 262176 | tf_op jit(solution)/shard_map/ppermute | solution.py:521
  26.6 3.1 %collect.4 = (bf16[256,32,128]{2,1,0:T(8,128)(2,1)}, bf16[4,16,32,128]{3,2,1,0:T(8,128)(2,1)}, bf16[4,16,32,128]{3,2,1,0:T(8,128)(2,1)}) custom-call(s32[1,16,16]{2,1,0:T(8,128)} %list_ref.5, s32[2]{0:T(128)} %pad_add_fusion.place_ref, bf16[32,32,128]{2,1,0:T(8,128)(2,1)} %get-tuple-element.61.refs_0_, bf16[32,32,128]{2,1,0:T(8,128)(2,1)} %collective-permute-done.12.refs_1_, ...), custom_call_target="tpu_custom_call" | custom-call | bytes 5242880 | tf_op jit(solution)/shard_map/collect/pallas_call | solution.py:237
  29.7 7.2 %all-to-all-start.1 = ((bf16[16,16,32,128]{3,2,1,0:T(8,128)(2,1)}), bf16[16,16,32,128]{3,2,1,0:T(8,128)(2,1)}, u32[]{:S(2)}, u32[]{:S(2)}) async-start(bf16[16,16,32,128]{3,2,1,0:T(8,128)(2,1)} %bitcast.10), calls=%async_computation.1 | async-start | bytes 4194304 | tf_op jit(solution)/shard_map/all_to_all | solution.py:549
  36.9 3.9 %near_keys_values.1 = (bf16[768,256]{1,0:T(8,128)(2,1)}, bf16[4,16,32,128]{3,2,1,0:T(8,128)(2,1)}) custom-call(s32[2]{0:T(128)} %pad_add_fusion.place_ref, bf16[1024,768]{1,0:T(8,128)(2,1)} %near_ref.5, bf16[768,768]{1,0:T(8,128)(2,1)} %key_ref.5, bf16[768,768]{1,0:T(8,128)(2,1)} %value_ref.5), custom_call_target="tpu_custom_call" | custom-call | flops 402653184 | bytes 3145728 | tf_op jit(solution)/shard_map/near_keys_values/pallas_call | solution.py:94
  40.8 3.4 %far_keys_values.1 = (bf16[32,32,128]{2,1,0:T(8,128)(2,1)}, bf16[32,32,128]{2,1,0:T(8,128)(2,1)}, bf16[32,32,128]{2,1,0:T(8,128)(2,1)}, bf16[32,32,128]{2,1,0:T(8,128)(2,1)}) custom-call(s32[2]{0:T(128)} %pad_add_fusion.place_ref, bf16[1024,768]{1,0:T(8,128)(2,1)} %collective-permute-done.3.far_ref, bf16[768,256]{1,0:T(8,128)(2,1)} %get-tuple-element.48.weight, ...), custom_call_target="tpu_custom_call" | custom-call | flops 402653184 | bytes 3145728 | tf_op jit(solution)/shard_map/far_keys_values/pallas_call | solution.py:123
  44.2 1.2 collective-permute-start.4
  45.4 2.4 %collective-permute-start.5 = (bf16[32,32,128]{2,1,0:T(8,128)(2,1)}, bf16[32,32,128]{2,1,0:T(8,128)(2,1)}, u32[]{:S(2)}, u32[]{:S(2)}) collective-permute-start(bf16[32,32,128]{2,1,0:T(8,128)(2,1)} %get-tuple-element.52), channel_id=1, source_target_pairs={{0,4},{1,5},{2,6},{3,7},{4,0},{5,1},{6,2},{7,3},{8,12},{9,13},{10,... | collective-permute-start | bytes 786440 | tf_op jit(solution)/shard_map/ppermute | solution.py:521
  47.8 1.2 collective-permute-start.6
  49.1 4.0 %collective-permute-done.4.refs_1_ = bf16[32,32,128]{2,1,0:T(8,128)(2,1)} collective-permute-done((bf16[32,32,128]{2,1,0:T(8,128)(2,1)}, bf16[32,32,128]{2,1,0:T(8,128)(2,1)}, u32[]{:S(2)}, u32[]{:S(2)}) %collective-permute-start.4) | collective-permute-done | bytes 262176 | tf_op jit(solution)/shard_map/ppermute | solution.py:521
  53.0 6.4 %collective-permute-done.5.refs_2_ = bf16[32,32,128]{2,1,0:T(8,128)(2,1)} collective-permute-done((bf16[32,32,128]{2,1,0:T(8,128)(2,1)}, bf16[32,32,128]{2,1,0:T(8,128)(2,1)}, u32[]{:S(2)}, u32[]{:S(2)}) %collective-permute-start.5) | collective-permute-done | bytes 262176 | tf_op jit(solution)/shard_map/ppermute | solution.py:521
  59.4 3.1 %collect.3 = (bf16[256,32,128]{2,1,0:T(8,128)(2,1)}, bf16[4,16,32,128]{3,2,1,0:T(8,128)(2,1)}, bf16[4,16,32,128]{3,2,1,0:T(8,128)(2,1)}) custom-call(s32[1,16,16]{2,1,0:T(8,128)} %list_ref.5, s32[2]{0:T(128)} %pad_add_fusion.place_ref, bf16[32,32,128]{2,1,0:T(8,128)(2,1)} %get-tuple-element.50.refs_0_, bf16[32,32,128]{2,1,0:T(8,128)(2,1)} %collective-permute-done.4.refs_1_, ...), custom_call_target="tpu_custom_call" | custom-call | bytes 5242880 | tf_op jit(solution)/shard_map/collect/pallas_call | solution.py:237
  62.5 0.5 all-to-all-done.1
  63.1 7.6 %all-to-all-start = ((bf16[16,16,32,128]{3,2,1,0:T(8,128)(2,1)}), bf16[16,16,32,128]{3,2,1,0:T(8,128)(2,1)}, u32[]{:S(2)}, u32[]{:S(2)}) async-start(bf16[16,16,32,128]{3,2,1,0:T(8,128)(2,1)} %bitcast.11), calls=%async_computation | async-start | bytes 4194304 | tf_op jit(solution)/shard_map/all_to_all | solution.py:549
  70.7 5.0 %keys_values.3 = (bf16[32,32,128]{2,1,0:T(8,128)(2,1)}, bf16[32,32,128]{2,1,0:T(8,128)(2,1)}, bf16[32,32,128]{2,1,0:T(8,128)(2,1)}, bf16[32,32,128]{2,1,0:T(8,128)(2,1)}) custom-call(s32[2]{0:T(128)} %pad_add_fusion.place_ref, bf16[1024,768]{1,0:T(8,128)(2,1)} %near_ref.5, bf16[1024,768]{1,0:T(8,128)(2,1)} %collective-permute-done.3.far_ref, ...), custom_call_target="tpu_custom_call" | custom-call | flops 805306368 | bytes 5242880 | tf_op jit(solution)/shard_map/keys_values/pallas_call | solution.py:149
  75.7 2.1 collective-permute-start.20
  77.7 3.1 %collective-permute-start.21 = (bf16[32,32,128]{2,1,0:T(8,128)(2,1)}, bf16[32,32,128]{2,1,0:T(8,128)(2,1)}, u32[]{:S(2)}, u32[]{:S(2)}) collective-permute-start(bf16[32,32,128]{2,1,0:T(8,128)(2,1)} %get-tuple-element.74), channel_id=1, source_target_pairs={{0,4},{1,5},{2,6},{3,7},{4,0},{5,1},{6,2},{7,3},{8,12},{9,13},{10,... | collective-permute-start | bytes 786440 | tf_op jit(solution)/shard_map/ppermute | solution.py:521
  80.8 5.4 %collective-permute-done.20.refs_1_ = bf16[32,32,128]{2,1,0:T(8,128)(2,1)} collective-permute-done((bf16[32,32,128]{2,1,0:T(8,128)(2,1)}, bf16[32,32,128]{2,1,0:T(8,128)(2,1)}, u32[]{:S(2)}, u32[]{:S(2)}) %collective-permute-start.20) | collective-permute-done | bytes 262176 | tf_op jit(solution)/shard_map/ppermute | solution.py:521
  86.2 4.4 %collective-permute-done.21.refs_2_ = bf16[32,32,128]{2,1,0:T(8,128)(2,1)} collective-permute-done((bf16[32,32,128]{2,1,0:T(8,128)(2,1)}, bf16[32,32,128]{2,1,0:T(8,128)(2,1)}, u32[]{:S(2)}, u32[]{:S(2)}) %collective-permute-start.21) | collective-permute-done | bytes 262176 | tf_op jit(solution)/shard_map/ppermute | solution.py:521
  90.6 3.2 %collect.5 = (bf16[256,32,128]{2,1,0:T(8,128)(2,1)}, bf16[4,16,32,128]{3,2,1,0:T(8,128)(2,1)}, bf16[4,16,32,128]{3,2,1,0:T(8,128)(2,1)}) custom-call(s32[1,16,16]{2,1,0:T(8,128)} %list_ref.5, s32[2]{0:T(128)} %pad_add_fusion.place_ref, bf16[32,32,128]{2,1,0:T(8,128)(2,1)} %get-tuple-element.72.refs_0_, bf16[32,32,128]{2,1,0:T(8,128)(2,1)} %collective-permute-done.20.refs_1_, ...), custom_call_target="tpu_custom_call" | custom-call | bytes 5242880 | tf_op jit(solution)/shard_map/collect/pallas_call | solution.py:237
  93.9 1.7 all-to-all-done
  95.5 7.4 %all-to-all-start.2 = ((bf16[16,16,32,128]{3,2,1,0:T(8,128)(2,1)}), bf16[16,16,32,128]{3,2,1,0:T(8,128)(2,1)}, u32[]{:S(2)}, u32[]{:S(2)}) async-start(bf16[16,16,32,128]{3,2,1,0:T(8,128)(2,1)} %bitcast.12), calls=%async_computation.2 | async-start | bytes 4194304 | tf_op jit(solution)/shard_map/all_to_all | solution.py:549
  103.4 24.3 %all-to-all-done.2 = bf16[16,16,32,128]{3,2,1,0:T(8,128)(2,1)} async-done(((bf16[16,16,32,128]{3,2,1,0:T(8,128)(2,1)}), bf16[16,16,32,128]{3,2,1,0:T(8,128)(2,1)}, u32[]{:S(2)}, u32[]{:S(2)}) %all-to-all-start.2) | async-done | bytes 2097184 | tf_op jit(solution)/shard_map/all_to_all | solution.py:549
  127.7 4.8 %queries.1 = (bf16[3,16,32,128]{3,2,1,0:T(8,128)(2,1)}, bf16[3,16,32,128]{3,2,1,0:T(8,128)(2,1)}, bf16[3,16,32,128]{3,2,1,0:T(8,128)(2,1)}, bf16[3,16,32,128]{3,2,1,0:T(8,128)(2,1)}) custom-call(s32[2]{0:T(128)} %pad_add_fusion.place_ref, bf16[1024,768]{1,0:T(8,128)(2,1)} %near_ref.5, bf16[768,768]{1,0:T(8,128)(2,1)} %query_ref.1), custom_call_target="tpu_custom_call" | custom-call | flops 1207959552 | bytes 5242880 | tf_op jit(solution)/shard_map/queries/pallas_call | solution.py:187
  132.5 2.0 collective-permute-start
  134.5 3.5 %collective-permute-start.1 = (bf16[3,16,32,128]{3,2,1,0:T(8,128)(2,1)}, bf16[3,16,32,128]{3,2,1,0:T(8,128)(2,1)}, u32[]{:S(2)}, u32[]{:S(2)}) collective-permute-start(bf16[3,16,32,128]{3,2,1,0:T(8,128)(2,1)} %get-tuple-element.46), channel_id=1, source_target_pairs={{0,4},{1,5},{2,6},{3,7},{4,0},{5,1},{6,2},{7,3},{8,12},{9,13},{10,... | collective-permute-start | bytes 1179656 | tf_op jit(solution)/shard_map/ppermute | solution.py:521
  138.0 8.6 %collective-permute-done.refs_1_ = bf16[3,16,32,128]{3,2,1,0:T(8,128)(2,1)} collective-permute-done((bf16[3,16,32,128]{3,2,1,0:T(8,128)(2,1)}, bf16[3,16,32,128]{3,2,1,0:T(8,128)(2,1)}, u32[]{:S(2)}, u32[]{:S(2)}) %collective-permute-start) | collective-permute-done | bytes 393248 | tf_op jit(solution)/shard_map/ppermute | solution.py:521
  146.7 2.2 collective-permute-start.2
  148.9 7.4 %collective-permute-done.1.refs_2_ = bf16[3,16,32,128]{3,2,1,0:T(8,128)(2,1)} collective-permute-done((bf16[3,16,32,128]{3,2,1,0:T(8,128)(2,1)}, bf16[3,16,32,128]{3,2,1,0:T(8,128)(2,1)}, u32[]{:S(2)}, u32[]{:S(2)}) %collective-permute-start.1) | collective-permute-done | bytes 393248 | tf_op jit(solution)/shard_map/ppermute | solution.py:521
  156.3 1.7 collective-permute-done.2.refs_3_
  157.9 0.6 collective-permute-done.15.refs_5_
  158.7 13.7 %attend.4 = (bf16[16,32,128]{2,1,0:T(8,128)(2,1)}, bf16[16,32,128]{2,1,0:T(8,128)(2,1)}, bf16[16,32,128]{2,1,0:T(8,128)(2,1)}, bf16[16,32,128]{2,1,0:T(8,128)(2,1)}) custom-call(s32[8,128]{1,0:T(8,128)} %bitcast.13, s32[8,128]{1,0:T(8,128)} %bitcast.16, s32[128]{0:T(128)} %count_ref.5, s32[2]{0:T(128)} %pad_add_fusion.place_ref, ...), custom_call_target="tpu_custom_call" | custom-call | flops 1610612736 | bytes 8388608 | tf_op jit(solution)/shard_map/attend/pallas_call | solution.py:373
  172.5 3.9 %collective-permute-start.18 = (bf16[16,32,128]{2,1,0:T(8,128)(2,1)}, bf16[16,32,128]{2,1,0:T(8,128)(2,1)}, u32[]{:S(2)}, u32[]{:S(2)}) collective-permute-start(bf16[16,32,128]{2,1,0:T(8,128)(2,1)} %get-tuple-element.70), channel_id=1, source_target_pairs={{0,4},{1,5},{2,6},{3,7},{4,0},{5,1},{6,2},{7,3},{8,12},{9,13},{10,... | collective-permute-start | bytes 393224 | tf_op jit(solution)/shard_map/ppermute | solution.py:521
  176.4 13.8 %attend.3 = (bf16[16,32,128]{2,1,0:T(8,128)(2,1)}, bf16[16,32,128]{2,1,0:T(8,128)(2,1)}, bf16[16,32,128]{2,1,0:T(8,128)(2,1)}, bf16[16,32,128]{2,1,0:T(8,128)(2,1)}) custom-call(s32[8,128]{1,0:T(8,128)} %bitcast.14, s32[8,128]{1,0:T(8,128)} %bitcast.17, s32[128]{0:T(128)} %count_ref.5, s32[2]{0:T(128)} %pad_add_fusion.place_ref, ...), custom_call_target="tpu_custom_call" | custom-call | flops 1610612736 | bytes 8388608 | tf_op jit(solution)/shard_map/attend/pallas_call | solution.py:373
  190.1 2.3 collective-permute-start.10
  192.4 2.5 %collective-permute-start.11 = (bf16[16,32,128]{2,1,0:T(8,128)(2,1)}, bf16[16,32,128]{2,1,0:T(8,128)(2,1)}, u32[]{:S(2)}, u32[]{:S(2)}) collective-permute-start(bf16[16,32,128]{2,1,0:T(8,128)(2,1)} %get-tuple-element.60), channel_id=1, source_target_pairs={{0,6},{1,7},{2,0},{3,1},{4,2},{5,3},{6,4},{7,5},{8,14},{9,15},{10,... | collective-permute-start | bytes 393224 | tf_op jit(solution)/shard_map/ppermute | solution.py:521
  194.9 13.6 %attend.5 = (bf16[16,32,128]{2,1,0:T(8,128)(2,1)}, bf16[16,32,128]{2,1,0:T(8,128)(2,1)}, bf16[16,32,128]{2,1,0:T(8,128)(2,1)}, bf16[16,32,128]{2,1,0:T(8,128)(2,1)}) custom-call(s32[8,128]{1,0:T(8,128)} %bitcast.15, s32[8,128]{1,0:T(8,128)} %bitcast.18, s32[128]{0:T(128)} %count_ref.5, s32[2]{0:T(128)} %pad_add_fusion.place_ref, ...), custom_call_target="tpu_custom_call" | custom-call | flops 1610612736 | bytes 8388608 | tf_op jit(solution)/shard_map/attend/pallas_call | solution.py:373
  208.6 4.7 %collective-permute-start.26 = (bf16[16,32,128]{2,1,0:T(8,128)(2,1)}, bf16[16,32,128]{2,1,0:T(8,128)(2,1)}, u32[]{:S(2)}, u32[]{:S(2)}) collective-permute-start(bf16[16,32,128]{2,1,0:T(8,128)(2,1)} %get-tuple-element.81), channel_id=1, source_target_pairs={{0,4},{1,5},{2,6},{3,7},{4,0},{5,1},{6,2},{7,3},{8,12},{9,13},{10,... | collective-permute-start | bytes 393224 | tf_op jit(solution)/shard_map/ppermute | solution.py:521
  213.3 1.3 reshape.30.refs_7_
  214.6 1.3 reshape.31.refs_8_
  215.9 4.8 %mix.1.mixed_ref = f32[1024,768]{1,0:T(8,128)} custom-call(s32[2]{0:T(128)} %pad_add_fusion.place_ref, bf16[1024,768]{1,0:T(8,128)(2,1)} %near_ref.5, bf16[16,32,128]{2,1,0:T(8,128)(2,1)} %get-tuple-element.57.refs_0_, bf16[16,32,128]{2,1,0:T(8,128)(2,1)} %collective-permute-done.9.refs_1_, bf16[16,32,128]{2,1,0:T(8,128)(2,1)} %collective-permute-done.10.refs_2_, ...), custom_call_target="tpu_custom_call" | custom-call | flops 805306368 | bytes 7340032 | tf_op jit(solution)/shard_map/mix/pallas_call | solution.py:434
  220.7 11.3 %finish.1 = bf16[1024,768]{1,0:T(8,128)(2,1)} custom-call(s32[2]{0:T(128)} %pad_add_fusion.place_ref, f32[1024,768]{1,0:T(8,128)} %mix.1.mixed_ref, bf16[16,32,128]{2,1,0:T(8,128)(2,1)} %get-tuple-element.79.refs_0_, bf16[16,32,128]{2,1,0:T(8,128)(2,1)} %collective-permute-done.25.refs_1_, bf16[16,32,128]{2,1,0:T(8,128)(2,1)} %collective-permute-done.26.refs_2_, ...), custom_call_target="tpu_custom_call" | custom-call | tf_op jit(solution)/shard_map/finish/pallas_call | solution.py:487
  (30 shorter events, 0.9 us)
Async XLA Ops:
  0.0 3.8 %collective-permute-start.3 = (bf16[1024,768]{1,0:T(8,128)(2,1)}, bf16[1024,768]{1,0:T(8,128)(2,1)}, u32[]{:S(2)}, u32[]{:S(2)}) collective-permute-start(bf16[1024,768]{1,0:T(8,128)(2,1)} %near_ref.5), channel_id=1, source_target_pairs={{0,1},{1,0},{2,3},{3,2},{4,5},{5,4},{6,7},{7,6},{8,9},{9,8},{10,11... | collective-permute-start | bytes 4718600 | tf_op jit(solution)/shard_map/ppermute | solution.py:515
  8.7 11.0 %collective-permute-start.12 = (bf16[32,32,128]{2,1,0:T(8,128)(2,1)}, bf16[32,32,128]{2,1,0:T(8,128)(2,1)}, u32[]{:S(2)}, u32[]{:S(2)}) collective-permute-start(bf16[32,32,128]{2,1,0:T(8,128)(2,1)} %get-tuple-element.62), channel_id=1, source_target_pairs={{0,2},{1,3},{2,4},{3,5},{4,6},{5,7},{6,0},{7,1},{8,10},{9,11},{10,... | collective-permute-start | bytes 786440 | tf_op jit(solution)/shard_map/ppermute | solution.py:521
  10.7 15.8 %collective-permute-start.13 = (bf16[32,32,128]{2,1,0:T(8,128)(2,1)}, bf16[32,32,128]{2,1,0:T(8,128)(2,1)}, u32[]{:S(2)}, u32[]{:S(2)}) collective-permute-start(bf16[32,32,128]{2,1,0:T(8,128)(2,1)} %get-tuple-element.63), channel_id=1, source_target_pairs={{0,4},{1,5},{2,6},{3,7},{4,0},{5,1},{6,2},{7,3},{8,12},{9,13},{10,... | collective-permute-start | bytes 786440 | tf_op jit(solution)/shard_map/ppermute | solution.py:521
  14.3 12.3 %collective-permute-start.14 = (bf16[32,32,128]{2,1,0:T(8,128)(2,1)}, bf16[32,32,128]{2,1,0:T(8,128)(2,1)}, u32[]{:S(2)}, u32[]{:S(2)}) collective-permute-start(bf16[32,32,128]{2,1,0:T(8,128)(2,1)} %get-tuple-element.64), channel_id=1, source_target_pairs={{0,6},{1,7},{2,0},{3,1},{4,2},{5,3},{6,4},{7,5},{8,14},{9,15},{10,... | collective-permute-start | bytes 786440 | tf_op jit(solution)/shard_map/ppermute | solution.py:521
  29.7 33.4 %all-to-all-start.1 = ((bf16[16,16,32,128]{3,2,1,0:T(8,128)(2,1)}), bf16[16,16,32,128]{3,2,1,0:T(8,128)(2,1)}, u32[]{:S(2)}, u32[]{:S(2)}) async-start(bf16[16,16,32,128]{3,2,1,0:T(8,128)(2,1)} %bitcast.10), calls=%async_computation.1 | async-start | bytes 4194304 | tf_op jit(solution)/shard_map/all_to_all | solution.py:549
  44.2 8.8 %collective-permute-start.4 = (bf16[32,32,128]{2,1,0:T(8,128)(2,1)}, bf16[32,32,128]{2,1,0:T(8,128)(2,1)}, u32[]{:S(2)}, u32[]{:S(2)}) collective-permute-start(bf16[32,32,128]{2,1,0:T(8,128)(2,1)} %get-tuple-element.51), channel_id=1, source_target_pairs={{0,2},{1,3},{2,4},{3,5},{4,6},{5,7},{6,0},{7,1},{8,10},{9,11},{10,... | collective-permute-start | bytes 786440 | tf_op jit(solution)/shard_map/ppermute | solution.py:521
  45.4 14.0 %collective-permute-start.5 = (bf16[32,32,128]{2,1,0:T(8,128)(2,1)}, bf16[32,32,128]{2,1,0:T(8,128)(2,1)}, u32[]{:S(2)}, u32[]{:S(2)}) collective-permute-start(bf16[32,32,128]{2,1,0:T(8,128)(2,1)} %get-tuple-element.52), channel_id=1, source_target_pairs={{0,4},{1,5},{2,6},{3,7},{4,0},{5,1},{6,2},{7,3},{8,12},{9,13},{10,... | collective-permute-start | bytes 786440 | tf_op jit(solution)/shard_map/ppermute | solution.py:521
  47.8 11.6 %collective-permute-start.6 = (bf16[32,32,128]{2,1,0:T(8,128)(2,1)}, bf16[32,32,128]{2,1,0:T(8,128)(2,1)}, u32[]{:S(2)}, u32[]{:S(2)}) collective-permute-start(bf16[32,32,128]{2,1,0:T(8,128)(2,1)} %get-tuple-element.53), channel_id=1, source_target_pairs={{0,6},{1,7},{2,0},{3,1},{4,2},{5,3},{6,4},{7,5},{8,14},{9,15},{10,... | collective-permute-start | bytes 786440 | tf_op jit(solution)/shard_map/ppermute | solution.py:521
  63.1 32.5 %all-to-all-start = ((bf16[16,16,32,128]{3,2,1,0:T(8,128)(2,1)}), bf16[16,16,32,128]{3,2,1,0:T(8,128)(2,1)}, u32[]{:S(2)}, u32[]{:S(2)}) async-start(bf16[16,16,32,128]{3,2,1,0:T(8,128)(2,1)} %bitcast.11), calls=%async_computation | async-start | bytes 4194304 | tf_op jit(solution)/shard_map/all_to_all | solution.py:549
  75.7 10.6 %collective-permute-start.20 = (bf16[32,32,128]{2,1,0:T(8,128)(2,1)}, bf16[32,32,128]{2,1,0:T(8,128)(2,1)}, u32[]{:S(2)}, u32[]{:S(2)}) collective-permute-start(bf16[32,32,128]{2,1,0:T(8,128)(2,1)} %get-tuple-element.73), channel_id=1, source_target_pairs={{0,2},{1,3},{2,4},{3,5},{4,6},{5,7},{6,0},{7,1},{8,10},{9,11},{10,... | collective-permute-start | bytes 786440 | tf_op jit(solution)/shard_map/ppermute | solution.py:521
  77.7 12.9 %collective-permute-start.21 = (bf16[32,32,128]{2,1,0:T(8,128)(2,1)}, bf16[32,32,128]{2,1,0:T(8,128)(2,1)}, u32[]{:S(2)}, u32[]{:S(2)}) collective-permute-start(bf16[32,32,128]{2,1,0:T(8,128)(2,1)} %get-tuple-element.74), channel_id=1, source_target_pairs={{0,4},{1,5},{2,6},{3,7},{4,0},{5,1},{6,2},{7,3},{8,12},{9,13},{10,... | collective-permute-start | bytes 786440 | tf_op jit(solution)/shard_map/ppermute | solution.py:521
  80.8 9.8 %collective-permute-start.22 = (bf16[32,32,128]{2,1,0:T(8,128)(2,1)}, bf16[32,32,128]{2,1,0:T(8,128)(2,1)}, u32[]{:S(2)}, u32[]{:S(2)}) collective-permute-start(bf16[32,32,128]{2,1,0:T(8,128)(2,1)} %get-tuple-element.75), channel_id=1, source_target_pairs={{0,6},{1,7},{2,0},{3,1},{4,2},{5,3},{6,4},{7,5},{8,14},{9,15},{10,... | collective-permute-start | bytes 786440 | tf_op jit(solution)/shard_map/ppermute | solution.py:521
  95.5 32.2 %all-to-all-start.2 = ((bf16[16,16,32,128]{3,2,1,0:T(8,128)(2,1)}), bf16[16,16,32,128]{3,2,1,0:T(8,128)(2,1)}, u32[]{:S(2)}, u32[]{:S(2)}) async-start(bf16[16,16,32,128]{3,2,1,0:T(8,128)(2,1)} %bitcast.12), calls=%async_computation.2 | async-start | bytes 4194304 | tf_op jit(solution)/shard_map/all_to_all | solution.py:549
  102.9 55.8 %collective-permute-start.16 = (bf16[256,32,128]{2,1,0:T(8,128)(2,1)}, bf16[256,32,128]{2,1,0:T(8,128)(2,1)}, u32[]{:S(2)}, u32[]{:S(2)}) collective-permute-start(bf16[256,32,128]{2,1,0:T(8,128)(2,1)} %bitcast.7.refs_6_), channel_id=1, source_target_pairs={{0,1},{1,0},{2,3},{3,2},{4,5},{5,4},{6,7},{7,6},{8,9},{9,8},{10,11... | collective-permute-start | bytes 6291464 | tf_op jit(solution)/shard_map/ppermute | solution.py:515
  102.9 73.4 %collective-permute-start.8 = (bf16[256,32,128]{2,1,0:T(8,128)(2,1)}, bf16[256,32,128]{2,1,0:T(8,128)(2,1)}, u32[]{:S(2)}, u32[]{:S(2)}) collective-permute-start(bf16[256,32,128]{2,1,0:T(8,128)(2,1)} %bitcast.5.refs_6_), channel_id=1, source_target_pairs={{0,1},{1,0},{2,3},{3,2},{4,5},{5,4},{6,7},{7,6},{8,9},{9,8},{10,11... | collective-permute-start | bytes 6291464 | tf_op jit(solution)/shard_map/ppermute | solution.py:515
  127.7 64.7 %collective-permute-start.24 = (bf16[256,32,128]{2,1,0:T(8,128)(2,1)}, bf16[256,32,128]{2,1,0:T(8,128)(2,1)}, u32[]{:S(2)}, u32[]{:S(2)}) collective-permute-start(bf16[256,32,128]{2,1,0:T(8,128)(2,1)} %bitcast.9.refs_6_), channel_id=1, source_target_pairs={{0,1},{1,0},{2,3},{3,2},{4,5},{5,4},{6,7},{7,6},{8,9},{9,8},{10,11... | collective-permute-start | bytes 6291464 | tf_op jit(solution)/shard_map/ppermute | solution.py:515
  132.5 14.2 %collective-permute-start = (bf16[3,16,32,128]{3,2,1,0:T(8,128)(2,1)}, bf16[3,16,32,128]{3,2,1,0:T(8,128)(2,1)}, u32[]{:S(2)}, u32[]{:S(2)}) collective-permute-start(bf16[3,16,32,128]{3,2,1,0:T(8,128)(2,1)} %get-tuple-element.45), channel_id=1, source_target_pairs={{0,2},{1,3},{2,4},{3,5},{4,6},{5,7},{6,0},{7,1},{8,10},{9,11},{10,... | collective-permute-start | bytes 1179656 | tf_op jit(solution)/shard_map/ppermute | solution.py:521
  134.5 21.7 %collective-permute-start.1 = (bf16[3,16,32,128]{3,2,1,0:T(8,128)(2,1)}, bf16[3,16,32,128]{3,2,1,0:T(8,128)(2,1)}, u32[]{:S(2)}, u32[]{:S(2)}) collective-permute-start(bf16[3,16,32,128]{3,2,1,0:T(8,128)(2,1)} %get-tuple-element.46), channel_id=1, source_target_pairs={{0,4},{1,5},{2,6},{3,7},{4,0},{5,1},{6,2},{7,3},{8,12},{9,13},{10,... | collective-permute-start | bytes 1179656 | tf_op jit(solution)/shard_map/ppermute | solution.py:521
  146.7 11.3 %collective-permute-start.2 = (bf16[3,16,32,128]{3,2,1,0:T(8,128)(2,1)}, bf16[3,16,32,128]{3,2,1,0:T(8,128)(2,1)}, u32[]{:S(2)}, u32[]{:S(2)}) collective-permute-start(bf16[3,16,32,128]{3,2,1,0:T(8,128)(2,1)} %get-tuple-element.47), channel_id=1, source_target_pairs={{0,6},{1,7},{2,0},{3,1},{4,2},{5,3},{6,4},{7,5},{8,14},{9,15},{10,... | collective-permute-start | bytes 1179656 | tf_op jit(solution)/shard_map/ppermute | solution.py:521
  156.3 2.3 collective-permute-start.15
  157.9 14.5 %collective-permute-start.7 = (bf16[4,16,32,128]{3,2,1,0:T(8,128)(2,1)}, bf16[4,16,32,128]{3,2,1,0:T(8,128)(2,1)}, u32[]{:S(2)}, u32[]{:S(2)}) collective-permute-start(bf16[4,16,32,128]{3,2,1,0:T(8,128)(2,1)} %get-tuple-element.55), channel_id=1, source_target_pairs={{0,1},{1,0},{2,3},{3,2},{4,5},{5,4},{6,7},{7,6},{8,9},{9,8},{10,11... | collective-permute-start | bytes 1572872 | tf_op jit(solution)/shard_map/ppermute | solution.py:515
  158.5 31.6 %collective-permute-start.23 = (bf16[4,16,32,128]{3,2,1,0:T(8,128)(2,1)}, bf16[4,16,32,128]{3,2,1,0:T(8,128)(2,1)}, u32[]{:S(2)}, u32[]{:S(2)}) collective-permute-start(bf16[4,16,32,128]{3,2,1,0:T(8,128)(2,1)} %get-tuple-element.77), channel_id=1, source_target_pairs={{0,1},{1,0},{2,3},{3,2},{4,5},{5,4},{6,7},{7,6},{8,9},{9,8},{10,11... | collective-permute-start | bytes 1572872 | tf_op jit(solution)/shard_map/ppermute | solution.py:515
  172.4 22.6 %collective-permute-start.17 = (bf16[16,32,128]{2,1,0:T(8,128)(2,1)}, bf16[16,32,128]{2,1,0:T(8,128)(2,1)}, u32[]{:S(2)}, u32[]{:S(2)}) collective-permute-start(bf16[16,32,128]{2,1,0:T(8,128)(2,1)} %get-tuple-element.69), channel_id=1, source_target_pairs={{0,2},{1,3},{2,4},{3,5},{4,6},{5,7},{6,0},{7,1},{8,10},{9,11},{10,... | collective-permute-start | bytes 393224 | tf_op jit(solution)/shard_map/ppermute | solution.py:521
  172.5 36.0 %collective-permute-start.18 = (bf16[16,32,128]{2,1,0:T(8,128)(2,1)}, bf16[16,32,128]{2,1,0:T(8,128)(2,1)}, u32[]{:S(2)}, u32[]{:S(2)}) collective-permute-start(bf16[16,32,128]{2,1,0:T(8,128)(2,1)} %get-tuple-element.70), channel_id=1, source_target_pairs={{0,4},{1,5},{2,6},{3,7},{4,0},{5,1},{6,2},{7,3},{8,12},{9,13},{10,... | collective-permute-start | bytes 393224 | tf_op jit(solution)/shard_map/ppermute | solution.py:521
  176.4 32.2 %collective-permute-start.19 = (bf16[16,32,128]{2,1,0:T(8,128)(2,1)}, bf16[16,32,128]{2,1,0:T(8,128)(2,1)}, u32[]{:S(2)}, u32[]{:S(2)}) collective-permute-start(bf16[16,32,128]{2,1,0:T(8,128)(2,1)} %get-tuple-element.71), channel_id=1, source_target_pairs={{0,6},{1,7},{2,0},{3,1},{4,2},{5,3},{6,4},{7,5},{8,14},{9,15},{10,... | collective-permute-start | bytes 393224 | tf_op jit(solution)/shard_map/ppermute | solution.py:521
  190.1 23.2 %collective-permute-start.10 = (bf16[16,32,128]{2,1,0:T(8,128)(2,1)}, bf16[16,32,128]{2,1,0:T(8,128)(2,1)}, u32[]{:S(2)}, u32[]{:S(2)}) collective-permute-start(bf16[16,32,128]{2,1,0:T(8,128)(2,1)} %get-tuple-element.59), channel_id=1, source_target_pairs={{0,4},{1,5},{2,6},{3,7},{4,0},{5,1},{6,2},{7,3},{8,12},{9,13},{10,... | collective-permute-start | bytes 393224 | tf_op jit(solution)/shard_map/ppermute | solution.py:521
  192.4 23.4 %collective-permute-start.11 = (bf16[16,32,128]{2,1,0:T(8,128)(2,1)}, bf16[16,32,128]{2,1,0:T(8,128)(2,1)}, u32[]{:S(2)}, u32[]{:S(2)}) collective-permute-start(bf16[16,32,128]{2,1,0:T(8,128)(2,1)} %get-tuple-element.60), channel_id=1, source_target_pairs={{0,6},{1,7},{2,0},{3,1},{4,2},{5,3},{6,4},{7,5},{8,14},{9,15},{10,... | collective-permute-start | bytes 393224 | tf_op jit(solution)/shard_map/ppermute | solution.py:521
  194.9 21.0 %collective-permute-start.9 = (bf16[16,32,128]{2,1,0:T(8,128)(2,1)}, bf16[16,32,128]{2,1,0:T(8,128)(2,1)}, u32[]{:S(2)}, u32[]{:S(2)}) collective-permute-start(bf16[16,32,128]{2,1,0:T(8,128)(2,1)} %get-tuple-element.58), channel_id=1, source_target_pairs={{0,2},{1,3},{2,4},{3,5},{4,6},{5,7},{6,0},{7,1},{8,10},{9,11},{10,... | collective-permute-start | bytes 393224 | tf_op jit(solution)/shard_map/ppermute | solution.py:521
  208.5 12.1 %collective-permute-start.25 = (bf16[16,32,128]{2,1,0:T(8,128)(2,1)}, bf16[16,32,128]{2,1,0:T(8,128)(2,1)}, u32[]{:S(2)}, u32[]{:S(2)}) collective-permute-start(bf16[16,32,128]{2,1,0:T(8,128)(2,1)} %get-tuple-element.80), channel_id=1, source_target_pairs={{0,2},{1,3},{2,4},{3,5},{4,6},{5,7},{6,0},{7,1},{8,10},{9,11},{10,... | collective-permute-start | bytes 393224 | tf_op jit(solution)/shard_map/ppermute | solution.py:521
  208.6 12.0 %collective-permute-start.26 = (bf16[16,32,128]{2,1,0:T(8,128)(2,1)}, bf16[16,32,128]{2,1,0:T(8,128)(2,1)}, u32[]{:S(2)}, u32[]{:S(2)}) collective-permute-start(bf16[16,32,128]{2,1,0:T(8,128)(2,1)} %get-tuple-element.81), channel_id=1, source_target_pairs={{0,4},{1,5},{2,6},{3,7},{4,0},{5,1},{6,2},{7,3},{8,12},{9,13},{10,... | collective-permute-start | bytes 393224 | tf_op jit(solution)/shard_map/ppermute | solution.py:521
  213.3 7.4 %collective-permute-start.27 = (bf16[16,32,128]{2,1,0:T(8,128)(2,1)}, bf16[16,32,128]{2,1,0:T(8,128)(2,1)}, u32[]{:S(2)}, u32[]{:S(2)}) collective-permute-start(bf16[16,32,128]{2,1,0:T(8,128)(2,1)} %get-tuple-element.82), channel_id=1, source_target_pairs={{0,6},{1,7},{2,0},{3,1},{4,2},{5,3},{6,4},{7,5},{8,14},{9,15},{10,... | collective-permute-start | bytes 393224 | tf_op jit(solution)/shard_map/ppermute | solution.py:521

commit v5 on v4

--- a/solution.py
+++ b/solution.py
@@ -84,54 +84,59 @@
                 packed[2 * pair + side, pl.ds(first + half * 8, 8)] = both[side]
 
 
-def near_kernel(place_ref, near_ref, key_ref, value_ref, weight, packed, sem):
-    fetch_weight(0, place_ref[1], key_ref, value_ref, weight, sem)
-    pack_rows(near_ref, weight, packed, 0)
-
-
-def project_near(place, near, w_key, w_value):
-    rows, width = near.shape
+def first_kernel(feat_ref, key_ref, value_ref, *refs):
+    out_ref, feats, weights, made, sems, done = refs
+    halves = [slice(half * 512, half * 512 + 512) for half in range(2)]
+    fetches = [
+        pltpu.make_async_copy(key_ref.at[:, :COLS], weights.at[0], sems.at[0]),
+        pltpu.make_async_copy(feat_ref.at[halves[0]], feats.at[halves[0]], sems.at[1]),
+        pltpu.make_async_copy(feat_ref.at[halves[1]], feats.at[halves[1]], sems.at[2]),
+        pltpu.make_async_copy(value_ref.at[:, :COLS], weights.at[1], sems.at[3]),
+    ]
+    for copy in fetches:
+        copy.start()
+    copies = []
+    fetches[0].wait()
+    for kind in range(2):
+        if kind == 1:
+            fetches[3].wait()
+        for half, at in enumerate(halves):
+            if kind == 0:
+                fetches[1 + half].wait()
+            rows = jnp.dot(feats[at, :], weights[kind], preferred_element_type=F32)
+            for pair in range(2):
+                both = pack_pair(rows[:, pair * LANES : (pair + 1) * LANES])
+                for side in range(2):
+                    dest = 2 * (2 * pair + side) + kind
+                    made[dest, half * 8 : half * 8 + 8] = both[side]
+        for z in range(CHIPS):
+            dest = 2 * z + kind
+            copies.append(pltpu.make_async_copy(made.at[dest], out_ref.at[dest], done.at[dest]))
+            copies[-1].start()
+    for copy in copies:
+        copy.wait()
+
+
+def project_first(features, w_key, w_value):
+    rows, width = features.shape
     return pl.pallas_call(
-        near_kernel,
-        in_specs=[SMEM, VMEM, HBM, HBM],
-        out_specs=[VMEM] * 2,
-        out_shape=[
-            jax.ShapeDtypeStruct((width, COLS), BF16),
-            jax.ShapeDtypeStruct((CHIPS, OWN) + TILE, BF16),
+        first_kernel,
+        in_specs=[HBM] * 3,
+        out_specs=HBM,
+        out_shape=jax.ShapeDtypeStruct((2 * CHIPS, OWN) + TILE, BF16),
+        scratch_shapes=[
+            pltpu.VMEM((rows, width), BF16),
+            pltpu.VMEM((2, width, COLS), BF16),
+            pltpu.VMEM((2 * CHIPS, OWN) + TILE, BF16),
+            pltpu.SemaphoreType.DMA((4,)),
+            pltpu.SemaphoreType.DMA((2 * CHIPS,)),
         ],
-        scratch_shapes=[pltpu.SemaphoreType.DMA],
         compiler_params=params(0),
         cost_estimate=pl.CostEstimate(
-            flops=2 * rows * width * COLS, bytes_accessed=3 << 20, transcendentals=0
+            flops=4 * rows * width * COLS, bytes_accessed=4 << 20, transcendentals=0
         ),
-        name="near_keys_values",
-    )(place, near, w_key, w_value)
-
-
-def far_kernel(place_ref, far_ref, weight, near_packed, *refs):
-    outs, (packed,) = refs[:CHIPS], refs[CHIPS:]
-    z, core = place_ref[0], place_ref[1]
-    pack_rows(far_ref, weight, packed, 0)
-    for step in range(CHIPS):
-        dest = lax.rem(z + step, CHIPS)
-        outs[step][pl.ds(core * OWN, OWN)] = near_packed[dest]
-        outs[step][pl.ds((1 - core) * OWN, OWN)] = packed[dest]
-
-
-def project_far(place, far, weight, near_packed):
-    rows, width = far.shape
-    return pl.pallas_call(
-        far_kernel,
-        in_specs=[SMEM] + [VMEM] * 3,
-        out_specs=[VMEM] * CHIPS,
-        out_shape=[jax.ShapeDtypeStruct((2 * OWN,) + TILE, BF16)] * CHIPS,
-        scratch_shapes=[pltpu.VMEM((CHIPS, OWN) + TILE, BF16)],
-        compiler_params=params(0),
-        cost_estimate=pl.CostEstimate(
-            flops=2 * rows * width * COLS, bytes_accessed=3 << 20, transcendentals=0
-        ),
-        name="far_keys_values",
-    )(place, far, weight, near_packed)
+        name="first_keys_values",
+    )(features, w_key, w_value)
 
 
 def keys_values_kernel(chunk, place_ref, near_ref, far_ref, key_ref, value_ref, *refs):
@@ -198,25 +203,22 @@
     )(place, features, w_query)
 
 
-def collect_kernel(list_ref, place_ref, *refs):
-    parts, (out_ref, own_ref, swap_ref, held, picked, sems) = refs[:CHIPS], refs[CHIPS:]
+def collect_kernel(count, list_ref, place_ref, *refs):
+    parts, (out_ref, own_ref, swap_ref, *scratch) = refs[:count], refs[count:]
     z, core = place_ref[0], place_ref[1]
-    for step in range(CHIPS):
-        source = lax.rem(z + CHIPS - step, CHIPS)
-        held[pl.ds(source * 2 * OWN, 2 * OWN)] = parts[step][...]
-    quarter = picked.shape[0] // CAP // 4
-
-    def body(step, carry):
-        for extra in range(CAP):
-            picked[step * CAP + extra] = held[list_ref[0, step, extra]]
-        return carry
-
+    held, picked, arrive, sems = scratch
+    if count == 1:
+        copies = [pltpu.make_async_copy(parts[0], held, arrive.at[0])]
+    else:
+        copies = []
+        for step in range(CHIPS):
+            at = pl.ds(lax.rem(z + CHIPS - step, CHIPS) * 2 * OWN, 2 * OWN)
+            copies.append(pltpu.make_async_copy(parts[step], held.at[at], arrive.at[step]))
+    for copy in copies:
+        copy.start()
+    for copy in copies:
+        copy.wait()
     copies = []
-    for part in range(4):
-        lax.fori_loop(part * quarter, (part + 1) * quarter, body, 0)
-        at = pl.ds(part * quarter * CAP, quarter * CAP)
-        copies.append(pltpu.make_async_copy(picked.at[at], out_ref.at[at], sems.at[part]))
-        copies[-1].start()
     for source in range(CHIPS):
         for which, target in enumerate((own_ref, swap_ref)):
             side = core if which == 0 else 1 - core
@@ -227,6 +229,18 @@
                 )
             )
             copies[-1].start()
+    quarter = picked.shape[0] // CAP // 4
+
+    def body(step, carry):
+        for extra in range(CAP):
+            picked[step * CAP + extra] = held[list_ref[0, step, extra]]
+        return carry
+
+    for part in range(4):
+        lax.fori_loop(part * quarter, (part + 1) * quarter, body, 0)
+        at = pl.ds(part * quarter * CAP, quarter * CAP)
+        copies.append(pltpu.make_async_copy(picked.at[at], out_ref.at[at], sems.at[part]))
+        copies[-1].start()
     for copy in copies:
         copy.wait()
 
@@ -235,13 +249,14 @@
     slots = send_list.shape[1] * send_list.shape[2]
     own = jax.ShapeDtypeStruct((CHIPS, OWN) + TILE, BF16)
     return pl.pallas_call(
-        collect_kernel,
-        in_specs=[SMEM, SMEM] + [VMEM] * CHIPS,
+        functools.partial(collect_kernel, len(parts)),
+        in_specs=[SMEM, SMEM] + [HBM] * len(parts),
         out_specs=[HBM] * 3,
         out_shape=[jax.ShapeDtypeStruct((slots,) + TILE, BF16), own, own],
         scratch_shapes=[
             pltpu.VMEM((CHIPS * 2 * OWN,) + TILE, BF16),
             pltpu.VMEM((slots,) + TILE, BF16),
+            pltpu.SemaphoreType.DMA((CHIPS,)),
             pltpu.SemaphoreType.DMA((4 + 2 * CHIPS,)),
         ],
         compiler_params=params(0),
@@ -253,8 +268,16 @@
 def attend_kernel(chunk, owner_ref, slot_ref, count_ref, place_ref, *refs):
     parts, (own_ref, swap_ref, mine_ref, other_ref) = refs[:CHIPS], refs[CHIPS : CHIPS + 4]
     outs = refs[CHIPS + 4 : 2 * CHIPS + 4]
-    queries, made, keys, values, own_keys, own_values, sems = refs[2 * CHIPS + 4 :]
+    queries, made, keys, values, own_keys, own_values, asked, sems, done = refs[2 * CHIPS + 4 :]
     z, core = place_ref[0], place_ref[1]
+
+    asking = []
+    for step in range(CHIPS):
+        source = lax.rem(z + CHIPS - step, CHIPS)
+        asking.append(
+            pltpu.make_async_copy(parts[step].at[chunk], queries.at[source], asked.at[step])
+        )
+        asking[-1].start()
 
     def place_in(near, near_own, far, far_own):
         copies = [
@@ -276,8 +299,8 @@
     def _():
         place_in(values, own_values, keys, own_keys)
 
-    for step in range(CHIPS):
-        queries[lax.rem(z + CHIPS - step, CHIPS)] = parts[step][chunk]
+    for copy in asking:
+        copy.wait()
 
     low = low_lanes(HALF)
     lane = lax.broadcasted_iota(jnp.int32, (1, LANES), 1)
@@ -286,7 +309,8 @@
     group = 8
 
     def attend_group(at, carry):
-        source, first = at // 2, (at % 2) * group
+        ahead = lax.rem(at // 2 + 1, CHIPS)
+        source, first = lax.rem(z + ahead, CHIPS), (at % 2) * group
         blocks = [source * 2 * OWN + core * OWN + first + k for k in range(group)]
         slots = [
             [owner_ref[entry, block] * CAP + slot_ref[entry, block] for entry in range(MAXK)]
@@ -360,11 +384,18 @@
             crossed = jnp.where(low, summed[k][HALF : 2 * HALF], summed[k][2 * HALF : 3 * HALF])
             result = (straight + pltpu.roll(crossed, HDIM, 1)) * share
             made[source, first + k] = result.astype(BF16)
+        for step in range(CHIPS):
+
+            @pl.when(jnp.logical_and(at % 2 == 1, ahead == step))
+            def _():
+                pltpu.make_async_copy(made.at[source], outs[step], done.at[step]).start()
+
         return carry
 
     lax.fori_loop(0, CHIPS * OWN // group, attend_group, 0)
     for step in range(CHIPS):
-        outs[step][...] = made[lax.rem(z + step, CHIPS)]
+        source = lax.rem(z + step, CHIPS)
+        pltpu.make_async_copy(made.at[source], outs[step], done.at[step]).wait()
 
 
 def attend(tables, place, queries, own, swapped, mine, other, chunk):
@@ -372,8 +403,8 @@
     blocks = pltpu.VMEM((CHIPS, OWN) + TILE, BF16)
     return pl.pallas_call(
         functools.partial(attend_kernel, chunk),
-        in_specs=[SMEM] * 4 + [VMEM] * CHIPS + [HBM] * 4,
-        out_specs=[VMEM] * CHIPS,
+        in_specs=[SMEM] * 4 + [HBM] * (CHIPS + 4),
+        out_specs=[HBM] * CHIPS,
         out_shape=[jax.ShapeDtypeStruct((OWN,) + TILE, BF16)] * CHIPS,
         scratch_shapes=[
             blocks,
@@ -382,7 +413,9 @@
             pltpu.VMEM((slots,) + TILE, BF16),
             blocks,
             blocks,
+            pltpu.SemaphoreType.DMA((CHIPS,)),
             pltpu.SemaphoreType.DMA((4,)),
+            pltpu.SemaphoreType.DMA((CHIPS,)),
         ],
         compiler_params=params(0),
         cost_estimate=pl.CostEstimate(
@@ -404,71 +437,82 @@
     return jnp.dot(jnp.concatenate(pieces, axis=1), weight, preferred_element_type=F32)
 
 
-def gather_parts(place_ref, parts, held):
-    z = place_ref[0]
+def gather_parts(place_ref, parts, held, sems):
+    copies = []
     for step in range(CHIPS):
-        held[lax.rem(z + CHIPS - step, CHIPS)] = parts[step][...]
+        source = lax.rem(place_ref[0] + CHIPS - step, CHIPS)
+        copies.append(pltpu.make_async_copy(parts[step], held.at[source], sems.at[step]))
+        copies[-1].start()
+    return copies
 
 
 def mix_kernel(place_ref, feat_ref, *refs):
-    parts, (weight_ref, out_ref, held, made, sems) = refs[: 2 * CHIPS], refs[2 * CHIPS :]
+    parts, (weight_ref, out_ref, held, weight, made, arrive, sems) = refs[:CHIPS], refs[CHIPS:]
+    rows = feat_ref.shape[0] // 2
+    fetch = pltpu.make_async_copy(weight_ref.at[:COLS], weight, sems.at[0])
+    fetch.start()
+    for copy in gather_parts(place_ref, parts, held, arrive):
+        copy.wait()
+    fetch.wait()
     copies = []
-    rows = feat_ref.shape[0] // 2
-    for chunk in range(2):
-        gather_parts(place_ref, parts[chunk * CHIPS : (chunk + 1) * CHIPS], held.at[chunk])
     for half in range(2):
         at = slice(half * rows, (half + 1) * rows)
-        mixed = feat_ref[at, :].astype(F32)
-        for chunk in range(2):
-            weight = weight_ref[chunk * COLS : (chunk + 1) * COLS, :]
-            mixed = mixed + mixed_rows(held.at[chunk], half, weight)
-        made[at, :] = mixed
-        copies.append(pltpu.make_async_copy(made.at[at], out_ref.at[at], sems.at[half]))
+        made[at, :] = feat_ref[at, :].astype(F32) + mixed_rows(held, half, weight[...])
+        copies.append(pltpu.make_async_copy(made.at[at], out_ref.at[at], sems.at[1 + half]))
         copies[-1].start()
     for copy in copies:
         copy.wait()
 
 
-def mix(place, features, backs, w_out):
+def mix(place, features, back, w_out):
     rows, width = features.shape
     return pl.pallas_call(
         mix_kernel,
-        in_specs=[SMEM, VMEM] + [VMEM] * (2 * CHIPS + 1),
+        in_specs=[SMEM, VMEM] + [HBM] * (CHIPS + 1),
         out_specs=HBM,
         out_shape=jax.ShapeDtypeStruct((rows, width), F32),
         scratch_shapes=[
-            pltpu.VMEM((2, CHIPS, OWN) + TILE, BF16),
+            pltpu.VMEM((CHIPS, OWN) + TILE, BF16),
+            pltpu.VMEM((COLS, width), BF16),
             pltpu.VMEM((rows, width), F32),
-            pltpu.SemaphoreType.DMA((2,)),
+            pltpu.SemaphoreType.DMA((CHIPS,)),
+            pltpu.SemaphoreType.DMA((3,)),
         ],
         compiler_params=params(0),
         cost_estimate=pl.CostEstimate(
-            flops=4 * rows * COLS * width, bytes_accessed=7 << 20, transcendentals=0
+            flops=2 * rows * COLS * width, bytes_accessed=6 << 20, transcendentals=0
         ),
         name="mix",
-    )(place, features, *[part for back in backs for part in back], w_out)
+    )(place, features, *back, w_out)
 
 
 def finish_kernel(place_ref, mixed_ref, *refs):
-    parts, refs = refs[:CHIPS], refs[CHIPS:]
+    late = CHUNKS - 1
+    parts, refs = refs[: late * CHIPS], refs[late * CHIPS :]
     out_w_ref, up_ref, down_ref, gain_a_ref, gain_f_ref, result_ref, *scratch = refs
-    held, early, out_w, up, down, sems = scratch
+    held, early, out_w, up, down, made, arrive, sems = scratch
     rows = mixed_ref.shape[0] // 2
     halves = [slice(half * rows, (half + 1) * rows) for half in range(2)]
     copies = [
-        pltpu.make_async_copy(out_w_ref.at[(CHUNKS - 1) * COLS :], out_w, sems.at[0]),
+        pltpu.make_async_copy(out_w_ref.at[COLS:], out_w, sems.at[0]),
         pltpu.make_async_copy(mixed_ref.at[halves[0]], early.at[halves[0]], sems.at[1]),
         pltpu.make_async_copy(mixed_ref.at[halves[1]], early.at[halves[1]], sems.at[2]),
         pltpu.make_async_copy(up_ref, up, sems.at[3]),
         pltpu.make_async_copy(down_ref, down, sems.at[4]),
     ]
+    arriving = []
+    for which in range(late):
+        some = parts[which * CHIPS : (which + 1) * CHIPS]
+        arriving += gather_parts(place_ref, some, held.at[which], arrive.at[which])
     for copy in copies:
         copy.start()
-    gather_parts(place_ref, parts, held)
+    for copy in arriving:
+        copy.wait()
     copies[0].wait()
     firsts = []
     for half, at in enumerate(halves):
-        added = mixed_rows(held, half, out_w[...])
+        added = mixed_rows(held.at[0], half, out_w[:COLS, :])
+        added = added + mixed_rows(held.at[1], half, out_w[COLS:, :])
         copies[1 + half].wait()
         firsts.append(normed(early[at, :] + added, gain_a_ref[...]).astype(BF16))
     for half, at in enumerate(halves):
@@ -479,30 +523,36 @@
         if half == 0:
             copies[4].wait()
         total = first.astype(F32) + jnp.dot(hidden, down[...], preferred_element_type=F32)
-        result_ref[at, :] = normed(total, gain_f_ref[...]).astype(BF16)
-
-
-def finish(place, mixed, back, w_out, w_up, w_down, gain_attn, gain_ffn):
+        made[at, :] = normed(total, gain_f_ref[...]).astype(BF16)
+        copies.append(pltpu.make_async_copy(made.at[at], result_ref.at[at], sems.at[5 + half]))
+        copies[-1].start()
+    for copy in copies[5:]:
+        copy.wait()
+
+
+def finish(place, mixed, backs, w_out, w_up, w_down, gain_attn, gain_ffn):
     rows, width = mixed.shape
     return pl.pallas_call(
         finish_kernel,
-        in_specs=[SMEM, HBM] + [VMEM] * CHIPS + [HBM, HBM, HBM, VMEM, VMEM],
-        out_specs=VMEM,
+        in_specs=[SMEM] + [HBM] * (2 * CHIPS + 4) + [VMEM, VMEM],
+        out_specs=HBM,
         out_shape=jax.ShapeDtypeStruct((rows, width), BF16),
         scratch_shapes=[
-            pltpu.VMEM((CHIPS, OWN) + TILE, BF16),
+            pltpu.VMEM((CHUNKS - 1, CHIPS, OWN) + TILE, BF16),
             pltpu.VMEM((rows, width), F32),
-            pltpu.VMEM((COLS, width), BF16),
+            pltpu.VMEM((2 * COLS, width), BF16),
             pltpu.VMEM(w_up.shape, BF16),
             pltpu.VMEM(w_down.shape, BF16),
-            pltpu.SemaphoreType.DMA((5,)),
+            pltpu.VMEM((rows, width), BF16),
+            pltpu.SemaphoreType.DMA((CHUNKS - 1, CHIPS)),
+            pltpu.SemaphoreType.DMA((7,)),
         ],
         compiler_params=params(0),
         name="finish",
     )(
         place,
         mixed,
-        *back,
+        *[part for back in backs for part in back],
         w_out,
         w_up,
         w_down,
@@ -533,14 +583,15 @@
     groups = send_list.shape[1]
     owners, slots = edge_owner.T, edge_slot.T
     far = swap(features)
-    weight, near_packed = project_near(place, features, w_key, w_value)
     collected = []
     for c in range(CHUNKS):
         if c == 0:
-            parts = project_far(place, far, weight, near_packed)
+            whole = project_first(features, w_key, w_value)
+            whole = lax.all_to_all(whole, "head", split_axis=0, concat_axis=0, tiled=True)
+            parts = [whole.reshape((-1,) + TILE)]
         else:
             parts = project_keys_values(place, features, far, w_key, w_value, c)
-        parts = along_z(parts)
+            parts = along_z(parts)
         collected.append(collect(send_list, place, parts))
     queries = along_z(project_queries(place, features, w_query))
     mines = []
@@ -557,8 +608,8 @@
             tables, place, queries, collected[c][1], swapped, mines[c], other, c
         )
         backs.append(along_z(done))
-    mixed = mix(place, features, backs[:2], w_out)
-    return finish(place, mixed, backs[2], w_out, w_up, w_down, gain_attn, gain_ffn)
+    mixed = mix(place, features, backs[0], w_out)
+    return finish(place, mixed, backs[1:], w_out, w_up, w_down, gain_attn, gain_ffn)
 
 
 def solution(mesh):

time: 235 us -> 238 us (1.013)
  waiting for transfers between devices: 79.4 us -> 87.8 us
  starting transfers between devices: 60.7 us -> 55.5 us
    all_to_all x0 -> x1, waiting for transfers between devices: none -> 15.4 us  [per_device(): lax.all_to_all(whole, 'head', split_axis=0, concat_axis=0, tiled=True)]
    ppermute x21 -> x18, starting transfers between devices: 37.8 us -> 27.2 us  [along_z(): lax.ppermute(parts[step], 'head', [(i, (i + 2 * step) % (2 * CHIPS)) for...]
    ppermute x21 -> x18, waiting for transfers between devices: 49.1 us -> 41.9 us  [along_z(): lax.ppermute(parts[step], 'head', [(i, (i + 2 * step) % (2 * CHIPS)) for...]
    all_to_all x0 -> x1, starting transfers between devices: none -> 5.33 us  [per_device(): lax.all_to_all(whole, 'head', split_axis=0, concat_axis=0, tiled=True)]
    pallas_call x7 -> x6, Pallas kernels: 32.7 us -> 33.6 us  [the longest x1 13.2 us: finish(): pl.pallas_call(finish_kernel, in_specs=[SMEM] + [HBM] * (2 * CHIPS + 4) +...]
  transfers between devices with their start and end apart: 31 -> 29, of which waited for: 14 -> 12; matrix products, arithmetic and copies ran while one was open for 1% -> 1% of each run, Pallas kernels for 30% -> 28%
where the time goes in v5:
time: 238 us; the launch traced here: 234 us
  waiting for transfers between devices  87.8 us (37%)
  Pallas kernels  87.6 us (37%)
  starting transfers between devices  55.5 us (23%)
  local copies, waits for them, and re-layouts  2.55 us (1%)
    ppermute x18, waiting for transfers between devices, along_z(): lax.ppermute(parts[step], 'head', [(i, (i + 2 * step) % (2 * CHIPS)) for...  41.9 us
    pallas_call x3, Pallas kernels, attend(): pl.pallas_call(functools.partial(attend_kernel, chunk), in_specs=[SMEM] *...  39.3 us
    ppermute x18, starting transfers between devices, along_z(): lax.ppermute(parts[step], 'head', [(i, (i + 2 * step) % (2 * CHIPS)) for...  27.2 us
    all_to_all x3, waiting for transfers between devices, per_device(): got = lax.all_to_all(sent, 'node', split_axis=0, concat_axis=0, tiled=True)  26.3 us
    all_to_all x3, starting transfers between devices, per_device(): got = lax.all_to_all(sent, 'node', split_axis=0, concat_axis=0, tiled=True)  22.3 us
    all_to_all x1, waiting for transfers between devices, per_device(): lax.all_to_all(whole, 'head', split_axis=0, concat_axis=0, tiled=True)  15.4 us
    pallas_call x1, Pallas kernels, finish(): pl.pallas_call(finish_kernel, in_specs=[SMEM] + [HBM] * (2 * CHIPS + 4) +...  13.2 us
    pallas_call x3, Pallas kernels, collect(): pl.pallas_call(functools.partial(collect_kernel, len(parts)), in_specs=[S...  11.5 us
  transfers between devices with their start and end apart: 29, of which 12 were waited for; matrix products, arithmetic and copies ran while one was open for 1% of the time, Pallas kernels for 28%

profile of v5, /device:TPU:20, one launch (start us, length us, event | category | flops | bytes accessed | tf_op | source)
XLA Modules:
  0.0 234.4 jit_solution(2876043524542168497)
XLA Ops:
  0.0 4.1 %first_keys_values.1 = bf16[8,16,32,128]{3,2,1,0:T(8,128)(2,1)} custom-call(bf16[1024,768]{1,0:T(8,128)(2,1)} %near_ref.3, bf16[768,768]{1,0:T(8,128)(2,1)} %key_ref.5, bf16[768,768]{1,0:T(8,128)(2,1)} %value_ref.5), custom_call_target="tpu_custom_call" | custom-call | flops 805306368 | bytes 4194304 | tf_op jit(solution)/shard_map/first_keys_values/pallas_call | solution.py:122
  4.1 5.3 %all-to-all-start = ((bf16[8,16,32,128]{3,2,1,0:T(8,128)(2,1)}), bf16[8,16,32,128]{3,2,1,0:T(8,128)(2,1)}, u32[]{:S(2)}, u32[]{:S(2)}) async-start(bf16[8,16,32,128]{3,2,1,0:T(8,128)(2,1)} %first_keys_values.1), calls=%async_computation | async-start | bytes 2097152 | tf_op jit(solution)/shard_map/all_to_all | solution.py:590
  9.4 0.6 pad_add_fusion.place_ref
  10.0 15.4 %all-to-all-done = bf16[8,16,32,128]{3,2,1,0:T(8,128)(2,1)} async-done(((bf16[8,16,32,128]{3,2,1,0:T(8,128)(2,1)}), bf16[8,16,32,128]{3,2,1,0:T(8,128)(2,1)}, u32[]{:S(2)}, u32[]{:S(2)}) %all-to-all-start) | async-done | bytes 1048608 | tf_op jit(solution)/shard_map/all_to_all | solution.py:590
  25.4 3.8 %collect.3 = (bf16[256,32,128]{2,1,0:T(8,128)(2,1)}, bf16[4,16,32,128]{3,2,1,0:T(8,128)(2,1)}, bf16[4,16,32,128]{3,2,1,0:T(8,128)(2,1)}) custom-call(s32[1,16,16]{2,1,0:T(8,128)} %list_ref.5, s32[2]{0:T(128)} %pad_add_fusion.place_ref, bf16[128,32,128]{2,1,0:T(8,128)(2,1)} %bitcast.4.refs_0_), custom_call_target="tpu_custom_call" | custom-call | bytes 5242880 | tf_op jit(solution)/shard_map/collect/pallas_call | solution.py:251
  29.3 7.4 %all-to-all-start.1 = ((bf16[16,16,32,128]{3,2,1,0:T(8,128)(2,1)}), bf16[16,16,32,128]{3,2,1,0:T(8,128)(2,1)}, u32[]{:S(2)}, u32[]{:S(2)}) async-start(bf16[16,16,32,128]{3,2,1,0:T(8,128)(2,1)} %bitcast.12), calls=%async_computation.1 | async-start | bytes 4194304 | tf_op jit(solution)/shard_map/all_to_all | solution.py:600
  36.8 3.5 %collective-permute-done.8.far_ref = bf16[1024,768]{1,0:T(8,128)(2,1)} collective-permute-done((bf16[1024,768]{1,0:T(8,128)(2,1)S(1)}, bf16[1024,768]{1,0:T(8,128)(2,1)}, u32[]{:S(2)}, u32[]{:S(2)}) %collective-permute-start.8) | collective-permute-done | bytes 1572896 | tf_op jit(solution)/shard_map/ppermute | solution.py:565
  40.3 5.0 %keys_values.3 = (bf16[32,32,128]{2,1,0:T(8,128)(2,1)}, bf16[32,32,128]{2,1,0:T(8,128)(2,1)}, bf16[32,32,128]{2,1,0:T(8,128)(2,1)}, bf16[32,32,128]{2,1,0:T(8,128)(2,1)}) custom-call(s32[2]{0:T(128)} %pad_add_fusion.place_ref, bf16[1024,768]{1,0:T(8,128)(2,1)} %near_ref.3, bf16[1024,768]{1,0:T(8,128)(2,1)} %collective-permute-done.8.far_ref, ...), custom_call_target="tpu_custom_call" | custom-call | flops 805306368 | bytes 5242880 | tf_op jit(solution)/shard_map/keys_values/pallas_call | solution.py:154
  45.3 0.6 collective-permute-start.17
  45.9 2.1 collective-permute-start.18
  48.0 0.7 collective-permute-start.19
  48.7 12.2 %collective-permute-done.17.refs_1_ = bf16[32,32,128]{2,1,0:T(8,128)(2,1)} collective-permute-done((bf16[32,32,128]{2,1,0:T(8,128)(2,1)}, bf16[32,32,128]{2,1,0:T(8,128)(2,1)}, u32[]{:S(2)}, u32[]{:S(2)}) %collective-permute-start.17) | collective-permute-done | bytes 262176 | tf_op jit(solution)/shard_map/ppermute | solution.py:571
  60.8 0.6 collective-permute-done.19.refs_3_
  61.5 3.8 %collect.5 = (bf16[256,32,128]{2,1,0:T(8,128)(2,1)}, bf16[4,16,32,128]{3,2,1,0:T(8,128)(2,1)}, bf16[4,16,32,128]{3,2,1,0:T(8,128)(2,1)}) custom-call(s32[1,16,16]{2,1,0:T(8,128)} %list_ref.5, s32[2]{0:T(128)} %pad_add_fusion.place_ref, bf16[32,32,128]{2,1,0:T(8,128)(2,1)} %get-tuple-element.60.refs_0_, bf16[32,32,128]{2,1,0:T(8,128)(2,1)} %collective-permute-done.17.refs_1_, ...), custom_call_target="tpu_custom_call" | custom-call | bytes 5242880 | tf_op jit(solution)/shard_map/collect/pallas_call | solution.py:251
  65.3 7.2 %all-to-all-start.3 = ((bf16[16,16,32,128]{3,2,1,0:T(8,128)(2,1)}), bf16[16,16,32,128]{3,2,1,0:T(8,128)(2,1)}, u32[]{:S(2)}, u32[]{:S(2)}) async-start(bf16[16,16,32,128]{3,2,1,0:T(8,128)(2,1)} %bitcast.11), calls=%async_computation.3 | async-start | bytes 4194304 | tf_op jit(solution)/shard_map/all_to_all | solution.py:600
  72.5 5.0 %keys_values.2 = (bf16[32,32,128]{2,1,0:T(8,128)(2,1)}, bf16[32,32,128]{2,1,0:T(8,128)(2,1)}, bf16[32,32,128]{2,1,0:T(8,128)(2,1)}, bf16[32,32,128]{2,1,0:T(8,128)(2,1)}) custom-call(s32[2]{0:T(128)} %pad_add_fusion.place_ref, bf16[1024,768]{1,0:T(8,128)(2,1)} %near_ref.3, bf16[1024,768]{1,0:T(8,128)(2,1)} %collective-permute-done.8.far_ref, ...), custom_call_target="tpu_custom_call" | custom-call | flops 805306368 | bytes 5242880 | tf_op jit(solution)/shard_map/keys_values/pallas_call | solution.py:154
  77.5 1.1 collective-permute-start.10
  78.6 2.0 collective-permute-start.11
  80.6 0.3 collective-permute-start.9
  80.9 7.7 %collective-permute-done.10.refs_2_ = bf16[32,32,128]{2,1,0:T(8,128)(2,1)} collective-permute-done((bf16[32,32,128]{2,1,0:T(8,128)(2,1)}, bf16[32,32,128]{2,1,0:T(8,128)(2,1)}, u32[]{:S(2)}, u32[]{:S(2)}) %collective-permute-start.10) | collective-permute-done | bytes 262176 | tf_op jit(solution)/shard_map/ppermute | solution.py:571
  88.6 3.7 %collective-permute-done.11.refs_3_ = bf16[32,32,128]{2,1,0:T(8,128)(2,1)} collective-permute-done((bf16[32,32,128]{2,1,0:T(8,128)(2,1)}, bf16[32,32,128]{2,1,0:T(8,128)(2,1)}, u32[]{:S(2)}, u32[]{:S(2)}) %collective-permute-start.11) | collective-permute-done | bytes 262176 | tf_op jit(solution)/shard_map/ppermute | solution.py:571
  92.3 3.9 %collect.4 = (bf16[256,32,128]{2,1,0:T(8,128)(2,1)}, bf16[4,16,32,128]{3,2,1,0:T(8,128)(2,1)}, bf16[4,16,32,128]{3,2,1,0:T(8,128)(2,1)}) custom-call(s32[1,16,16]{2,1,0:T(8,128)} %list_ref.5, s32[2]{0:T(128)} %pad_add_fusion.place_ref, bf16[32,32,128]{2,1,0:T(8,128)(2,1)} %get-tuple-element.49.refs_0_, bf16[32,32,128]{2,1,0:T(8,128)(2,1)} %collective-permute-done.9.refs_1_, ...), custom_call_target="tpu_custom_call" | custom-call | bytes 5242880 | tf_op jit(solution)/shard_map/collect/pallas_call | solution.py:251
  96.2 2.1 all-to-all-done.3
  98.3 7.6 %all-to-all-start.2 = ((bf16[16,16,32,128]{3,2,1,0:T(8,128)(2,1)}), bf16[16,16,32,128]{3,2,1,0:T(8,128)(2,1)}, u32[]{:S(2)}, u32[]{:S(2)}) async-start(bf16[16,16,32,128]{3,2,1,0:T(8,128)(2,1)} %bitcast.13), calls=%async_computation.2 | async-start | bytes 4194304 | tf_op jit(solution)/shard_map/all_to_all | solution.py:600
  105.9 0.5 collective-permute-start.21
  106.4 24.2 %all-to-all-done.2 = bf16[16,16,32,128]{3,2,1,0:T(8,128)(2,1)} async-done(((bf16[16,16,32,128]{3,2,1,0:T(8,128)(2,1)}), bf16[16,16,32,128]{3,2,1,0:T(8,128)(2,1)}, u32[]{:S(2)}, u32[]{:S(2)}) %all-to-all-start.2) | async-done | bytes 2097184 | tf_op jit(solution)/shard_map/all_to_all | solution.py:600
  130.7 4.7 %queries.1 = (bf16[3,16,32,128]{3,2,1,0:T(8,128)(2,1)}, bf16[3,16,32,128]{3,2,1,0:T(8,128)(2,1)}, bf16[3,16,32,128]{3,2,1,0:T(8,128)(2,1)}, bf16[3,16,32,128]{3,2,1,0:T(8,128)(2,1)}) custom-call(s32[2]{0:T(128)} %pad_add_fusion.place_ref, bf16[1024,768]{1,0:T(8,128)(2,1)} %near_ref.3, bf16[768,768]{1,0:T(8,128)(2,1)} %query_ref.1), custom_call_target="tpu_custom_call" | custom-call | flops 1207959552 | bytes 5242880 | tf_op jit(solution)/shard_map/queries/pallas_call | solution.py:192
  135.4 2.2 collective-permute-start
  137.6 3.1 %collective-permute-start.1 = (bf16[3,16,32,128]{3,2,1,0:T(8,128)(2,1)}, bf16[3,16,32,128]{3,2,1,0:T(8,128)(2,1)}, u32[]{:S(2)}, u32[]{:S(2)}) collective-permute-start(bf16[3,16,32,128]{3,2,1,0:T(8,128)(2,1)} %get-tuple-element.40), channel_id=1, source_target_pairs={{0,4},{1,5},{2,6},{3,7},{4,0},{5,1},{6,2},{7,3},{8,12},{9,13},{10,... | collective-permute-start | bytes 1179656 | tf_op jit(solution)/shard_map/ppermute | solution.py:571
  140.7 8.6 %collective-permute-done.refs_1_ = bf16[3,16,32,128]{3,2,1,0:T(8,128)(2,1)} collective-permute-done((bf16[3,16,32,128]{3,2,1,0:T(8,128)(2,1)}, bf16[3,16,32,128]{3,2,1,0:T(8,128)(2,1)}, u32[]{:S(2)}, u32[]{:S(2)}) %collective-permute-start) | collective-permute-done | bytes 393248 | tf_op jit(solution)/shard_map/ppermute | solution.py:571
  149.3 2.2 collective-permute-start.2
  151.5 7.4 %collective-permute-done.1.refs_2_ = bf16[3,16,32,128]{3,2,1,0:T(8,128)(2,1)} collective-permute-done((bf16[3,16,32,128]{3,2,1,0:T(8,128)(2,1)}, bf16[3,16,32,128]{3,2,1,0:T(8,128)(2,1)}, u32[]{:S(2)}, u32[]{:S(2)}) %collective-permute-start.1) | collective-permute-done | bytes 393248 | tf_op jit(solution)/shard_map/ppermute | solution.py:571
  158.9 1.6 collective-permute-done.2.refs_3_
  160.6 0.6 collective-permute-done.3.refs_5_
  161.2 0.1 collective-permute-start.12
  161.3 13.1 %attend.3 = (bf16[16,32,128]{2,1,0:T(8,128)(2,1)}, bf16[16,32,128]{2,1,0:T(8,128)(2,1)}, bf16[16,32,128]{2,1,0:T(8,128)(2,1)}, bf16[16,32,128]{2,1,0:T(8,128)(2,1)}) custom-call(s32[8,128]{1,0:T(8,128)} %bitcast.14, s32[8,128]{1,0:T(8,128)} %bitcast.17, s32[128]{0:T(128)} %count_ref.5, s32[2]{0:T(128)} %pad_add_fusion.place_ref, ...), custom_call_target="tpu_custom_call" | custom-call | flops 1610612736 | bytes 8388608 | tf_op jit(solution)/shard_map/attend/pallas_call | solution.py:404
  174.5 3.9 %collective-permute-start.6 = (bf16[16,32,128]{2,1,0:T(8,128)(2,1)}, bf16[16,32,128]{2,1,0:T(8,128)(2,1)}, u32[]{:S(2)}, u32[]{:S(2)}) collective-permute-start(bf16[16,32,128]{2,1,0:T(8,128)(2,1)} %get-tuple-element.47), channel_id=1, source_target_pairs={{0,4},{1,5},{2,6},{3,7},{4,0},{5,1},{6,2},{7,3},{8,12},{9,13},{10,... | collective-permute-start | bytes 393224 | tf_op jit(solution)/shard_map/ppermute | solution.py:571
  178.4 13.1 %attend.5 = (bf16[16,32,128]{2,1,0:T(8,128)(2,1)}, bf16[16,32,128]{2,1,0:T(8,128)(2,1)}, bf16[16,32,128]{2,1,0:T(8,128)(2,1)}, bf16[16,32,128]{2,1,0:T(8,128)(2,1)}) custom-call(s32[8,128]{1,0:T(8,128)} %bitcast.15, s32[8,128]{1,0:T(8,128)} %bitcast.18, s32[128]{0:T(128)} %count_ref.5, s32[2]{0:T(128)} %pad_add_fusion.place_ref, ...), custom_call_target="tpu_custom_call" | custom-call | flops 1610612736 | bytes 8388608 | tf_op jit(solution)/shard_map/attend/pallas_call | solution.py:404
  191.5 2.1 collective-permute-start.22
  193.6 0.3 collective-permute-start.23
  194.0 13.1 %attend.4 = (bf16[16,32,128]{2,1,0:T(8,128)(2,1)}, bf16[16,32,128]{2,1,0:T(8,128)(2,1)}, bf16[16,32,128]{2,1,0:T(8,128)(2,1)}, bf16[16,32,128]{2,1,0:T(8,128)(2,1)}) custom-call(s32[8,128]{1,0:T(8,128)} %bitcast.16, s32[8,128]{1,0:T(8,128)} %bitcast.19, s32[128]{0:T(128)} %count_ref.5, s32[2]{0:T(128)} %pad_add_fusion.place_ref, ...), custom_call_target="tpu_custom_call" | custom-call | flops 1610612736 | bytes 8388608 | tf_op jit(solution)/shard_map/attend/pallas_call | solution.py:404
  207.1 2.6 %collective-permute-start.24 = (bf16[16,32,128]{2,1,0:T(8,128)(2,1)}, bf16[16,32,128]{2,1,0:T(8,128)(2,1)}, u32[]{:S(2)}, u32[]{:S(2)}) collective-permute-start(bf16[16,32,128]{2,1,0:T(8,128)(2,1)} %get-tuple-element.70), channel_id=1, source_target_pairs={{0,6},{1,7},{2,0},{3,1},{4,2},{5,3},{6,4},{7,5},{8,14},{9,15},{10,... | collective-permute-start | bytes 393224 | tf_op jit(solution)/shard_map/ppermute | solution.py:571
  209.7 2.7 %collective-permute-start.15 = (bf16[16,32,128]{2,1,0:T(8,128)(2,1)}, bf16[16,32,128]{2,1,0:T(8,128)(2,1)}, u32[]{:S(2)}, u32[]{:S(2)}) collective-permute-start(bf16[16,32,128]{2,1,0:T(8,128)(2,1)} %get-tuple-element.58), channel_id=1, source_target_pairs={{0,4},{1,5},{2,6},{3,7},{4,0},{5,1},{6,2},{7,3},{8,12},{9,13},{10,... | collective-permute-start | bytes 393224 | tf_op jit(solution)/shard_map/ppermute | solution.py:571
  212.4 1.2 collective-permute-start.16
  213.6 1.3 reshape.34.refs_11_
  214.9 1.3 reshape.35.refs_12_
  216.2 4.8 %mix.1.mixed_ref = f32[1024,768]{1,0:T(8,128)} custom-call(s32[2]{0:T(128)} %pad_add_fusion.place_ref, bf16[1024,768]{1,0:T(8,128)(2,1)} %near_ref.3, bf16[16,32,128]{2,1,0:T(8,128)(2,1)} %get-tuple-element.45.refs_0_, bf16[16,32,128]{2,1,0:T(8,128)(2,1)} %collective-permute-done.5.refs_1_, bf16[16,32,128]{2,1,0:T(8,128)(2,1)} %collective-permute-done.6.refs_2_, ...), custom_call_target="tpu_custom_call" | custom-call | flops 402653184 | bytes 6291456 | tf_op jit(solution)/shard_map/mix/pallas_call | solution.py:469
  221.0 13.2 %finish.1 = bf16[1024,768]{1,0:T(8,128)(2,1)} custom-call(s32[2]{0:T(128)} %pad_add_fusion.place_ref, f32[1024,768]{1,0:T(8,128)} %mix.1.mixed_ref, bf16[16,32,128]{2,1,0:T(8,128)(2,1)} %get-tuple-element.56.refs_0_, bf16[16,32,128]{2,1,0:T(8,128)(2,1)} %collective-permute-done.14.refs_1_, bf16[16,32,128]{2,1,0:T(8,128)(2,1)} %collective-permute-done.15.refs_2_, ...), custom_call_target="tpu_custom_call" | custom-call | tf_op jit(solution)/shard_map/finish/pallas_call | solution.py:535
  (27 shorter events, 0.2 us)
Async XLA Ops:
  4.1 21.4 %all-to-all-start = ((bf16[8,16,32,128]{3,2,1,0:T(8,128)(2,1)}), bf16[8,16,32,128]{3,2,1,0:T(8,128)(2,1)}, u32[]{:S(2)}, u32[]{:S(2)}) async-start(bf16[8,16,32,128]{3,2,1,0:T(8,128)(2,1)} %first_keys_values.1), calls=%async_computation | async-start | bytes 2097152 | tf_op jit(solution)/shard_map/all_to_all | solution.py:590
  29.3 7.4 %copy-start = (bf16[1024,768]{1,0:T(8,128)(2,1)S(1)}, bf16[1024,768]{1,0:T(8,128)(2,1)}, u32[]{:S(2)}) copy-start(bf16[1024,768]{1,0:T(8,128)(2,1)} %near_ref.3) | copy-start | bytes 4718596
  29.3 36.0 %all-to-all-start.1 = ((bf16[16,16,32,128]{3,2,1,0:T(8,128)(2,1)}), bf16[16,16,32,128]{3,2,1,0:T(8,128)(2,1)}, u32[]{:S(2)}, u32[]{:S(2)}) async-start(bf16[16,16,32,128]{3,2,1,0:T(8,128)(2,1)} %bitcast.12), calls=%async_computation.1 | async-start | bytes 4194304 | tf_op jit(solution)/shard_map/all_to_all | solution.py:600
  36.7 3.6 %collective-permute-start.8 = (bf16[1024,768]{1,0:T(8,128)(2,1)S(1)}, bf16[1024,768]{1,0:T(8,128)(2,1)}, u32[]{:S(2)}, u32[]{:S(2)}) collective-permute-start(bf16[1024,768]{1,0:T(8,128)(2,1)S(1)} %copy-done), channel_id=1, source_target_pairs={{0,1},{1,0},{2,3},{3,2},{4,5},{5,4},{6,7},{7,6},{8,9},{9,8},{10,11... | collective-permute-start | bytes 4718600 | tf_op jit(solution)/shard_map/ppermute | solution.py:565
  45.3 15.6 %collective-permute-start.17 = (bf16[32,32,128]{2,1,0:T(8,128)(2,1)}, bf16[32,32,128]{2,1,0:T(8,128)(2,1)}, u32[]{:S(2)}, u32[]{:S(2)}) collective-permute-start(bf16[32,32,128]{2,1,0:T(8,128)(2,1)} %get-tuple-element.61), channel_id=1, source_target_pairs={{0,2},{1,3},{2,4},{3,5},{4,6},{5,7},{6,0},{7,1},{8,10},{9,11},{10,... | collective-permute-start | bytes 786440 | tf_op jit(solution)/shard_map/ppermute | solution.py:571
  45.9 14.9 %collective-permute-start.18 = (bf16[32,32,128]{2,1,0:T(8,128)(2,1)}, bf16[32,32,128]{2,1,0:T(8,128)(2,1)}, u32[]{:S(2)}, u32[]{:S(2)}) collective-permute-start(bf16[32,32,128]{2,1,0:T(8,128)(2,1)} %get-tuple-element.62), channel_id=1, source_target_pairs={{0,4},{1,5},{2,6},{3,7},{4,0},{5,1},{6,2},{7,3},{8,12},{9,13},{10,... | collective-permute-start | bytes 786440 | tf_op jit(solution)/shard_map/ppermute | solution.py:571
  48.0 13.5 %collective-permute-start.19 = (bf16[32,32,128]{2,1,0:T(8,128)(2,1)}, bf16[32,32,128]{2,1,0:T(8,128)(2,1)}, u32[]{:S(2)}, u32[]{:S(2)}) collective-permute-start(bf16[32,32,128]{2,1,0:T(8,128)(2,1)} %get-tuple-element.63), channel_id=1, source_target_pairs={{0,6},{1,7},{2,0},{3,1},{4,2},{5,3},{6,4},{7,5},{8,14},{9,15},{10,... | collective-permute-start | bytes 786440 | tf_op jit(solution)/shard_map/ppermute | solution.py:571
  65.3 33.0 %all-to-all-start.3 = ((bf16[16,16,32,128]{3,2,1,0:T(8,128)(2,1)}), bf16[16,16,32,128]{3,2,1,0:T(8,128)(2,1)}, u32[]{:S(2)}, u32[]{:S(2)}) async-start(bf16[16,16,32,128]{3,2,1,0:T(8,128)(2,1)} %bitcast.11), calls=%async_computation.3 | async-start | bytes 4194304 | tf_op jit(solution)/shard_map/all_to_all | solution.py:600
  77.5 11.1 %collective-permute-start.10 = (bf16[32,32,128]{2,1,0:T(8,128)(2,1)}, bf16[32,32,128]{2,1,0:T(8,128)(2,1)}, u32[]{:S(2)}, u32[]{:S(2)}) collective-permute-start(bf16[32,32,128]{2,1,0:T(8,128)(2,1)} %get-tuple-element.51), channel_id=1, source_target_pairs={{0,4},{1,5},{2,6},{3,7},{4,0},{5,1},{6,2},{7,3},{8,12},{9,13},{10,... | collective-permute-start | bytes 786440 | tf_op jit(solution)/shard_map/ppermute | solution.py:571
  78.6 13.7 %collective-permute-start.11 = (bf16[32,32,128]{2,1,0:T(8,128)(2,1)}, bf16[32,32,128]{2,1,0:T(8,128)(2,1)}, u32[]{:S(2)}, u32[]{:S(2)}) collective-permute-start(bf16[32,32,128]{2,1,0:T(8,128)(2,1)} %get-tuple-element.52), channel_id=1, source_target_pairs={{0,6},{1,7},{2,0},{3,1},{4,2},{5,3},{6,4},{7,5},{8,14},{9,15},{10,... | collective-permute-start | bytes 786440 | tf_op jit(solution)/shard_map/ppermute | solution.py:571
  80.6 11.7 %collective-permute-start.9 = (bf16[32,32,128]{2,1,0:T(8,128)(2,1)}, bf16[32,32,128]{2,1,0:T(8,128)(2,1)}, u32[]{:S(2)}, u32[]{:S(2)}) collective-permute-start(bf16[32,32,128]{2,1,0:T(8,128)(2,1)} %get-tuple-element.50), channel_id=1, source_target_pairs={{0,2},{1,3},{2,4},{3,5},{4,6},{5,7},{6,0},{7,1},{8,10},{9,11},{10,... | collective-permute-start | bytes 786440 | tf_op jit(solution)/shard_map/ppermute | solution.py:571
  98.3 32.4 %all-to-all-start.2 = ((bf16[16,16,32,128]{3,2,1,0:T(8,128)(2,1)}), bf16[16,16,32,128]{3,2,1,0:T(8,128)(2,1)}, u32[]{:S(2)}, u32[]{:S(2)}) async-start(bf16[16,16,32,128]{3,2,1,0:T(8,128)(2,1)} %bitcast.13), calls=%async_computation.2 | async-start | bytes 4194304 | tf_op jit(solution)/shard_map/all_to_all | solution.py:600
  105.9 55.4 %collective-permute-start.4 = (bf16[256,32,128]{2,1,0:T(8,128)(2,1)}, bf16[256,32,128]{2,1,0:T(8,128)(2,1)}, u32[]{:S(2)}, u32[]{:S(2)}) collective-permute-start(bf16[256,32,128]{2,1,0:T(8,128)(2,1)} %bitcast.6.refs_6_), channel_id=1, source_target_pairs={{0,1},{1,0},{2,3},{3,2},{4,5},{5,4},{6,7},{7,6},{8,9},{9,8},{10,11... | collective-permute-start | bytes 6291464 | tf_op jit(solution)/shard_map/ppermute | solution.py:565
  105.9 72.5 %collective-permute-start.21 = (bf16[256,32,128]{2,1,0:T(8,128)(2,1)}, bf16[256,32,128]{2,1,0:T(8,128)(2,1)}, u32[]{:S(2)}, u32[]{:S(2)}) collective-permute-start(bf16[256,32,128]{2,1,0:T(8,128)(2,1)} %bitcast.10.refs_6_), channel_id=1, source_target_pairs={{0,1},{1,0},{2,3},{3,2},{4,5},{5,4},{6,7},{7,6},{8,9},{9,8},{10,11... | collective-permute-start | bytes 6291464 | tf_op jit(solution)/shard_map/ppermute | solution.py:565
  130.6 63.0 %collective-permute-start.13 = (bf16[256,32,128]{2,1,0:T(8,128)(2,1)}, bf16[256,32,128]{2,1,0:T(8,128)(2,1)}, u32[]{:S(2)}, u32[]{:S(2)}) collective-permute-start(bf16[256,32,128]{2,1,0:T(8,128)(2,1)} %bitcast.8.refs_6_), channel_id=1, source_target_pairs={{0,1},{1,0},{2,3},{3,2},{4,5},{5,4},{6,7},{7,6},{8,9},{9,8},{10,11... | collective-permute-start | bytes 6291464 | tf_op jit(solution)/shard_map/ppermute | solution.py:565
  135.4 13.9 %collective-permute-start = (bf16[3,16,32,128]{3,2,1,0:T(8,128)(2,1)}, bf16[3,16,32,128]{3,2,1,0:T(8,128)(2,1)}, u32[]{:S(2)}, u32[]{:S(2)}) collective-permute-start(bf16[3,16,32,128]{3,2,1,0:T(8,128)(2,1)} %get-tuple-element.39), channel_id=1, source_target_pairs={{0,2},{1,3},{2,4},{3,5},{4,6},{5,7},{6,0},{7,1},{8,10},{9,11},{10,... | collective-permute-start | bytes 1179656 | tf_op jit(solution)/shard_map/ppermute | solution.py:571
  137.6 21.3 %collective-permute-start.1 = (bf16[3,16,32,128]{3,2,1,0:T(8,128)(2,1)}, bf16[3,16,32,128]{3,2,1,0:T(8,128)(2,1)}, u32[]{:S(2)}, u32[]{:S(2)}) collective-permute-start(bf16[3,16,32,128]{3,2,1,0:T(8,128)(2,1)} %get-tuple-element.40), channel_id=1, source_target_pairs={{0,4},{1,5},{2,6},{3,7},{4,0},{5,1},{6,2},{7,3},{8,12},{9,13},{10,... | collective-permute-start | bytes 1179656 | tf_op jit(solution)/shard_map/ppermute | solution.py:571
  149.3 11.3 %collective-permute-start.2 = (bf16[3,16,32,128]{3,2,1,0:T(8,128)(2,1)}, bf16[3,16,32,128]{3,2,1,0:T(8,128)(2,1)}, u32[]{:S(2)}, u32[]{:S(2)}) collective-permute-start(bf16[3,16,32,128]{3,2,1,0:T(8,128)(2,1)} %get-tuple-element.41), channel_id=1, source_target_pairs={{0,6},{1,7},{2,0},{3,1},{4,2},{5,3},{6,4},{7,5},{8,14},{9,15},{10,... | collective-permute-start | bytes 1179656 | tf_op jit(solution)/shard_map/ppermute | solution.py:571
  158.9 2.3 collective-permute-start.3
  160.6 13.9 %collective-permute-start.20 = (bf16[4,16,32,128]{3,2,1,0:T(8,128)(2,1)}, bf16[4,16,32,128]{3,2,1,0:T(8,128)(2,1)}, u32[]{:S(2)}, u32[]{:S(2)}) collective-permute-start(bf16[4,16,32,128]{3,2,1,0:T(8,128)(2,1)} %get-tuple-element.65), channel_id=1, source_target_pairs={{0,1},{1,0},{2,3},{3,2},{4,5},{5,4},{6,7},{7,6},{8,9},{9,8},{10,11... | collective-permute-start | bytes 1572872 | tf_op jit(solution)/shard_map/ppermute | solution.py:565
  161.2 30.4 %collective-permute-start.12 = (bf16[4,16,32,128]{3,2,1,0:T(8,128)(2,1)}, bf16[4,16,32,128]{3,2,1,0:T(8,128)(2,1)}, u32[]{:S(2)}, u32[]{:S(2)}) collective-permute-start(bf16[4,16,32,128]{3,2,1,0:T(8,128)(2,1)} %get-tuple-element.54), channel_id=1, source_target_pairs={{0,1},{1,0},{2,3},{3,2},{4,5},{5,4},{6,7},{7,6},{8,9},{9,8},{10,11... | collective-permute-start | bytes 1572872 | tf_op jit(solution)/shard_map/ppermute | solution.py:565
  174.4 32.7 %collective-permute-start.5 = (bf16[16,32,128]{2,1,0:T(8,128)(2,1)}, bf16[16,32,128]{2,1,0:T(8,128)(2,1)}, u32[]{:S(2)}, u32[]{:S(2)}) collective-permute-start(bf16[16,32,128]{2,1,0:T(8,128)(2,1)} %get-tuple-element.46), channel_id=1, source_target_pairs={{0,2},{1,3},{2,4},{3,5},{4,6},{5,7},{6,0},{7,1},{8,10},{9,11},{10,... | collective-permute-start | bytes 393224 | tf_op jit(solution)/shard_map/ppermute | solution.py:571
  174.5 35.2 %collective-permute-start.6 = (bf16[16,32,128]{2,1,0:T(8,128)(2,1)}, bf16[16,32,128]{2,1,0:T(8,128)(2,1)}, u32[]{:S(2)}, u32[]{:S(2)}) collective-permute-start(bf16[16,32,128]{2,1,0:T(8,128)(2,1)} %get-tuple-element.47), channel_id=1, source_target_pairs={{0,4},{1,5},{2,6},{3,7},{4,0},{5,1},{6,2},{7,3},{8,12},{9,13},{10,... | collective-permute-start | bytes 393224 | tf_op jit(solution)/shard_map/ppermute | solution.py:571
  178.4 31.3 %collective-permute-start.7 = (bf16[16,32,128]{2,1,0:T(8,128)(2,1)}, bf16[16,32,128]{2,1,0:T(8,128)(2,1)}, u32[]{:S(2)}, u32[]{:S(2)}) collective-permute-start(bf16[16,32,128]{2,1,0:T(8,128)(2,1)} %get-tuple-element.48), channel_id=1, source_target_pairs={{0,6},{1,7},{2,0},{3,1},{4,2},{5,3},{6,4},{7,5},{8,14},{9,15},{10,... | collective-permute-start | bytes 393224 | tf_op jit(solution)/shard_map/ppermute | solution.py:571
  191.5 20.9 %collective-permute-start.22 = (bf16[16,32,128]{2,1,0:T(8,128)(2,1)}, bf16[16,32,128]{2,1,0:T(8,128)(2,1)}, u32[]{:S(2)}, u32[]{:S(2)}) collective-permute-start(bf16[16,32,128]{2,1,0:T(8,128)(2,1)} %get-tuple-element.68), channel_id=1, source_target_pairs={{0,2},{1,3},{2,4},{3,5},{4,6},{5,7},{6,0},{7,1},{8,10},{9,11},{10,... | collective-permute-start | bytes 393224 | tf_op jit(solution)/shard_map/ppermute | solution.py:571
  193.6 27.3 %collective-permute-start.23 = (bf16[16,32,128]{2,1,0:T(8,128)(2,1)}, bf16[16,32,128]{2,1,0:T(8,128)(2,1)}, u32[]{:S(2)}, u32[]{:S(2)}) collective-permute-start(bf16[16,32,128]{2,1,0:T(8,128)(2,1)} %get-tuple-element.69), channel_id=1, source_target_pairs={{0,4},{1,5},{2,6},{3,7},{4,0},{5,1},{6,2},{7,3},{8,12},{9,13},{10,... | collective-permute-start | bytes 393224 | tf_op jit(solution)/shard_map/ppermute | solution.py:571
  207.1 13.9 %collective-permute-start.24 = (bf16[16,32,128]{2,1,0:T(8,128)(2,1)}, bf16[16,32,128]{2,1,0:T(8,128)(2,1)}, u32[]{:S(2)}, u32[]{:S(2)}) collective-permute-start(bf16[16,32,128]{2,1,0:T(8,128)(2,1)} %get-tuple-element.70), channel_id=1, source_target_pairs={{0,6},{1,7},{2,0},{3,1},{4,2},{5,3},{6,4},{7,5},{8,14},{9,15},{10,... | collective-permute-start | bytes 393224 | tf_op jit(solution)/shard_map/ppermute | solution.py:571
  209.7 11.3 %collective-permute-start.14 = (bf16[16,32,128]{2,1,0:T(8,128)(2,1)}, bf16[16,32,128]{2,1,0:T(8,128)(2,1)}, u32[]{:S(2)}, u32[]{:S(2)}) collective-permute-start(bf16[16,32,128]{2,1,0:T(8,128)(2,1)} %get-tuple-element.57), channel_id=1, source_target_pairs={{0,2},{1,3},{2,4},{3,5},{4,6},{5,7},{6,0},{7,1},{8,10},{9,11},{10,... | collective-permute-start | bytes 393224 | tf_op jit(solution)/shard_map/ppermute | solution.py:571
  209.7 11.3 %collective-permute-start.15 = (bf16[16,32,128]{2,1,0:T(8,128)(2,1)}, bf16[16,32,128]{2,1,0:T(8,128)(2,1)}, u32[]{:S(2)}, u32[]{:S(2)}) collective-permute-start(bf16[16,32,128]{2,1,0:T(8,128)(2,1)} %get-tuple-element.58), channel_id=1, source_target_pairs={{0,4},{1,5},{2,6},{3,7},{4,0},{5,1},{6,2},{7,3},{8,12},{9,13},{10,... | collective-permute-start | bytes 393224 | tf_op jit(solution)/shard_map/ppermute | solution.py:571
  212.4 8.6 %collective-permute-start.16 = (bf16[16,32,128]{2,1,0:T(8,128)(2,1)}, bf16[16,32,128]{2,1,0:T(8,128)(2,1)}, u32[]{:S(2)}, u32[]{:S(2)}) collective-permute-start(bf16[16,32,128]{2,1,0:T(8,128)(2,1)} %get-tuple-element.59), channel_id=1, source_target_pairs={{0,6},{1,7},{2,0},{3,1},{4,2},{5,3},{6,4},{7,5},{8,14},{9,15},{10,... | collective-permute-start | bytes 393224 | tf_op jit(solution)/shard_map/ppermute | solution.py:571

commit v6 on v5

--- a/solution.py
+++ b/solution.py
@@ -206,19 +206,26 @@
 def collect_kernel(count, list_ref, place_ref, *refs):
     parts, (out_ref, own_ref, swap_ref, *scratch) = refs[:count], refs[count:]
     z, core = place_ref[0], place_ref[1]
-    held, picked, arrive, sems = scratch
     if count == 1:
-        copies = [pltpu.make_async_copy(parts[0], held, arrive.at[0])]
+        held, (picked, sems) = parts[0], scratch
     else:
-        copies = []
+        held, picked, sems = scratch
         for step in range(CHIPS):
-            at = pl.ds(lax.rem(z + CHIPS - step, CHIPS) * 2 * OWN, 2 * OWN)
-            copies.append(pltpu.make_async_copy(parts[step], held.at[at], arrive.at[step]))
-    for copy in copies:
-        copy.start()
-    for copy in copies:
-        copy.wait()
+            source = lax.rem(z + CHIPS - step, CHIPS)
+            held[pl.ds(source * 2 * OWN, 2 * OWN)] = parts[step][...]
+    quarter = picked.shape[0] // CAP // 4
+
+    def body(step, carry):
+        for extra in range(CAP):
+            picked[step * CAP + extra] = held[list_ref[0, step, extra]]
+        return carry
+
     copies = []
+    for part in range(4):
+        lax.fori_loop(part * quarter, (part + 1) * quarter, body, 0)
+        at = pl.ds(part * quarter * CAP, quarter * CAP)
+        copies.append(pltpu.make_async_copy(picked.at[at], out_ref.at[at], sems.at[part]))
+        copies[-1].start()
     for source in range(CHIPS):
         for which, target in enumerate((own_ref, swap_ref)):
             side = core if which == 0 else 1 - core
@@ -229,18 +236,6 @@
                 )
             )
             copies[-1].start()
-    quarter = picked.shape[0] // CAP // 4
-
-    def body(step, carry):
-        for extra in range(CAP):
-            picked[step * CAP + extra] = held[list_ref[0, step, extra]]
-        return carry
-
-    for part in range(4):
-        lax.fori_loop(part * quarter, (part + 1) * quarter, body, 0)
-        at = pl.ds(part * quarter * CAP, quarter * CAP)
-        copies.append(pltpu.make_async_copy(picked.at[at], out_ref.at[at], sems.at[part]))
-        copies[-1].start()
     for copy in copies:
         copy.wait()
 
@@ -250,15 +245,11 @@
     own = jax.ShapeDtypeStruct((CHIPS, OWN) + TILE, BF16)
     return pl.pallas_call(
         functools.partial(collect_kernel, len(parts)),
-        in_specs=[SMEM, SMEM] + [HBM] * len(parts),
+        in_specs=[SMEM, SMEM] + [VMEM] * len(parts),
         out_specs=[HBM] * 3,
         out_shape=[jax.ShapeDtypeStruct((slots,) + TILE, BF16), own, own],
-        scratch_shapes=[
-            pltpu.VMEM((CHIPS * 2 * OWN,) + TILE, BF16),
-            pltpu.VMEM((slots,) + TILE, BF16),
-            pltpu.SemaphoreType.DMA((CHIPS,)),
-            pltpu.SemaphoreType.DMA((4 + 2 * CHIPS,)),
-        ],
+        scratch_shapes=[pltpu.VMEM((CHIPS * 2 * OWN,) + TILE, BF16)] * (len(parts) > 1)
+        + [pltpu.VMEM((slots,) + TILE, BF16), pltpu.SemaphoreType.DMA((4 + 2 * CHIPS,))],
         compiler_params=params(0),
         cost_estimate=pl.CostEstimate(flops=0, bytes_accessed=5 << 20, transcendentals=0),
         name="collect",
@@ -446,64 +437,39 @@
     return copies
 
 
-def mix_kernel(place_ref, feat_ref, *refs):
-    parts, (weight_ref, out_ref, held, weight, made, arrive, sems) = refs[:CHIPS], refs[CHIPS:]
+def gains_kernel(attn_ref, ffn_ref, out_ref):
+    out_ref[0, :] = attn_ref[...]
+    out_ref[1, :] = ffn_ref[...]
+
+
+def stack_gains(gain_attn, gain_ffn):
+    return pl.pallas_call(
+        gains_kernel,
+        in_specs=[VMEM, VMEM],
+        out_specs=VMEM,
+        out_shape=jax.ShapeDtypeStruct((2,) + gain_attn.shape, F32),
+        compiler_params=params(0),
+        name="gains",
+    )(gain_attn, gain_ffn)
+
+
+def finish_kernel(place_ref, feat_ref, *refs):
+    parts, refs = refs[: CHUNKS * CHIPS], refs[CHUNKS * CHIPS :]
+    out_w_ref, up_ref, down_ref, gain_ref, result_ref, *scratch = refs
+    held, feats, out_w, up, down, made, arrive, sems = scratch
     rows = feat_ref.shape[0] // 2
-    fetch = pltpu.make_async_copy(weight_ref.at[:COLS], weight, sems.at[0])
-    fetch.start()
-    for copy in gather_parts(place_ref, parts, held, arrive):
-        copy.wait()
-    fetch.wait()
-    copies = []
-    for half in range(2):
-        at = slice(half * rows, (half + 1) * rows)
-        made[at, :] = feat_ref[at, :].astype(F32) + mixed_rows(held, half, weight[...])
-        copies.append(pltpu.make_async_copy(made.at[at], out_ref.at[at], sems.at[1 + half]))
-        copies[-1].start()
-    for copy in copies:
-        copy.wait()
-
-
-def mix(place, features, back, w_out):
-    rows, width = features.shape
-    return pl.pallas_call(
-        mix_kernel,
-        in_specs=[SMEM, VMEM] + [HBM] * (CHIPS + 1),
-        out_specs=HBM,
-        out_shape=jax.ShapeDtypeStruct((rows, width), F32),
-        scratch_shapes=[
-            pltpu.VMEM((CHIPS, OWN) + TILE, BF16),
-            pltpu.VMEM((COLS, width), BF16),
-            pltpu.VMEM((rows, width), F32),
-            pltpu.SemaphoreType.DMA((CHIPS,)),
-            pltpu.SemaphoreType.DMA((3,)),
-        ],
-        compiler_params=params(0),
-        cost_estimate=pl.CostEstimate(
-            flops=2 * rows * COLS * width, bytes_accessed=6 << 20, transcendentals=0
-        ),
-        name="mix",
-    )(place, features, *back, w_out)
-
-
-def finish_kernel(place_ref, mixed_ref, *refs):
-    late = CHUNKS - 1
-    parts, refs = refs[: late * CHIPS], refs[late * CHIPS :]
-    out_w_ref, up_ref, down_ref, gain_a_ref, gain_f_ref, result_ref, *scratch = refs
-    held, early, out_w, up, down, made, arrive, sems = scratch
-    rows = mixed_ref.shape[0] // 2
     halves = [slice(half * rows, (half + 1) * rows) for half in range(2)]
+    arriving = []
+    for which in range(CHUNKS):
+        some = parts[which * CHIPS : (which + 1) * CHIPS]
+        arriving += gather_parts(place_ref, some, held.at[which], arrive.at[which])
     copies = [
-        pltpu.make_async_copy(out_w_ref.at[COLS:], out_w, sems.at[0]),
-        pltpu.make_async_copy(mixed_ref.at[halves[0]], early.at[halves[0]], sems.at[1]),
-        pltpu.make_async_copy(mixed_ref.at[halves[1]], early.at[halves[1]], sems.at[2]),
+        pltpu.make_async_copy(out_w_ref, out_w, sems.at[0]),
+        pltpu.make_async_copy(feat_ref.at[halves[0]], feats.at[halves[0]], sems.at[1]),
+        pltpu.make_async_copy(feat_ref.at[halves[1]], feats.at[halves[1]], sems.at[2]),
         pltpu.make_async_copy(up_ref, up, sems.at[3]),
         pltpu.make_async_copy(down_ref, down, sems.at[4]),
     ]
-    arriving = []
-    for which in range(late):
-        some = parts[which * CHIPS : (which + 1) * CHIPS]
-        arriving += gather_parts(place_ref, some, held.at[which], arrive.at[which])
     for copy in copies:
         copy.start()
     for copy in arriving:
@@ -512,9 +478,12 @@
     firsts = []
     for half, at in enumerate(halves):
         added = mixed_rows(held.at[0], half, out_w[:COLS, :])
-        added = added + mixed_rows(held.at[1], half, out_w[COLS:, :])
+        for which in range(1, CHUNKS):
+            weight = out_w[which * COLS : (which + 1) * COLS, :]
+            added = added + mixed_rows(held.at[which], half, weight)
         copies[1 + half].wait()
-        firsts.append(normed(early[at, :] + added, gain_a_ref[...]).astype(BF16))
+        mixed = feats[at, :].astype(F32) + added
+        firsts.append(normed(mixed, gain_ref[0:1, :]).astype(BF16))
     for half, at in enumerate(halves):
         first = firsts[half]
         if half == 0:
@@ -523,42 +492,33 @@
         if half == 0:
             copies[4].wait()
         total = first.astype(F32) + jnp.dot(hidden, down[...], preferred_element_type=F32)
-        made[at, :] = normed(total, gain_f_ref[...]).astype(BF16)
+        made[at, :] = normed(total, gain_ref[1:2, :]).astype(BF16)
         copies.append(pltpu.make_async_copy(made.at[at], result_ref.at[at], sems.at[5 + half]))
         copies[-1].start()
     for copy in copies[5:]:
         copy.wait()
 
 
-def finish(place, mixed, backs, w_out, w_up, w_down, gain_attn, gain_ffn):
-    rows, width = mixed.shape
+def finish(place, features, backs, w_out, w_up, w_down, gains):
+    rows, width = features.shape
     return pl.pallas_call(
         finish_kernel,
-        in_specs=[SMEM] + [HBM] * (2 * CHIPS + 4) + [VMEM, VMEM],
+        in_specs=[SMEM] + [HBM] * (CHUNKS * CHIPS + 4) + [VMEM],
         out_specs=HBM,
         out_shape=jax.ShapeDtypeStruct((rows, width), BF16),
         scratch_shapes=[
-            pltpu.VMEM((CHUNKS - 1, CHIPS, OWN) + TILE, BF16),
-            pltpu.VMEM((rows, width), F32),
-            pltpu.VMEM((2 * COLS, width), BF16),
+            pltpu.VMEM((CHUNKS, CHIPS, OWN) + TILE, BF16),
+            pltpu.VMEM((rows, width), BF16),
+            pltpu.VMEM(w_out.shape, BF16),
             pltpu.VMEM(w_up.shape, BF16),
             pltpu.VMEM(w_down.shape, BF16),
             pltpu.VMEM((rows, width), BF16),
-            pltpu.SemaphoreType.DMA((CHUNKS - 1, CHIPS)),
+            pltpu.SemaphoreType.DMA((CHUNKS, CHIPS)),
             pltpu.SemaphoreType.DMA((7,)),
         ],
         compiler_params=params(0),
         name="finish",
-    )(
-        place,
-        mixed,
-        *[part for back in backs for part in back],
-        w_out,
-        w_up,
-        w_down,
-        gain_attn.reshape(1, width),
-        gain_ffn.reshape(1, width),
-    )
+    )(place, features, *[part for back in backs for part in back], w_out, w_up, w_down, gains)
 
 
 def swap(array):
@@ -608,8 +568,8 @@
             tables, place, queries, collected[c][1], swapped, mines[c], other, c
         )
         backs.append(along_z(done))
-    mixed = mix(place, features, backs[0], w_out)
-    return finish(place, mixed, backs[1:], w_out, w_up, w_down, gain_attn, gain_ffn)
+    gains = stack_gains(gain_attn, gain_ffn)
+    return finish(place, features, backs, w_out, w_up, w_down, gains)
 
 
 def solution(mesh):

time: 238 us -> 236 us (level)
  waiting for transfers between devices: 87.8 us -> 92.6 us
  Pallas kernels: 87.6 us -> 83.3 us
  local copies, waits for them, and re-layouts: 2.55 us -> 0.01 us
    ppermute x18, waiting for transfers between devices: 41.9 us -> 46.1 us  [along_z(): lax.ppermute(parts[step], 'head', [(i, (i + 2 * step) % (2 * CHIPS)) for...]
    reshape x2 -> x0, local copies, waits for them, and re-layouts: 2.54 us -> none  [the longest x1 1.28 us: finish(): gain_attn.reshape(1, width)]
  transfers between devices with their start and end apart: 29 -> 29, of which waited for: 12 -> 14; matrix products, arithmetic and copies ran while one was open for 1% -> 0% of each run, Pallas kernels for 28% -> 27%
where the time goes in v6:
time: 236 us; the launch traced here: 232 us
  waiting for transfers between devices  92.6 us (39%)
  Pallas kernels  83.3 us (35%)
  starting transfers between devices  55.5 us (24%)
    ppermute x18, waiting for transfers between devices, along_z(): lax.ppermute(parts[step], 'head', [(i, (i + 2 * step) % (2 * CHIPS)) for...  46.1 us
    pallas_call x3, Pallas kernels, attend(): pl.pallas_call(functools.partial(attend_kernel, chunk), in_specs=[SMEM] *...  39.3 us
    ppermute x18, starting transfers between devices, along_z(): lax.ppermute(parts[step], 'head', [(i, (i + 2 * step) % (2 * CHIPS)) for...  27.2 us
    all_to_all x3, waiting for transfers between devices, per_device(): got = lax.all_to_all(sent, 'node', split_axis=0, concat_axis=0, tiled=True)  27 us
    all_to_all x3, starting transfers between devices, per_device(): got = lax.all_to_all(sent, 'node', split_axis=0, concat_axis=0, tiled=True)  22.2 us
    all_to_all x1, waiting for transfers between devices, per_device(): lax.all_to_all(whole, 'head', split_axis=0, concat_axis=0, tiled=True)  15.4 us
    pallas_call x1, Pallas kernels, finish(): pl.pallas_call(finish_kernel, in_specs=[SMEM] + [HBM] * (CHUNKS * CHIPS +...  14.4 us
    pallas_call x2, Pallas kernels, project_keys_values(): pl.pallas_call(functools.partial(keys_values_kernel, chunk), in_specs=[SM...  9.99 us
  transfers between devices with their start and end apart: 29, of which 14 were waited for; matrix products, arithmetic and copies ran while one was open for 0% of the time, Pallas kernels for 27%

profile of v6, /device:TPU:20, one launch (start us, length us, event | category | flops | bytes accessed | tf_op | source)
XLA Modules:
  0.0 232.3 jit_solution(689230995084955397)
XLA Ops:
  0.0 4.1 %first_keys_values.1 = bf16[8,16,32,128]{3,2,1,0:T(8,128)(2,1)} custom-call(bf16[1024,768]{1,0:T(8,128)(2,1)} %feat_ref.5, bf16[768,768]{1,0:T(8,128)(2,1)} %key_ref.5, bf16[768,768]{1,0:T(8,128)(2,1)} %value_ref.5), custom_call_target="tpu_custom_call" | custom-call | flops 805306368 | bytes 4194304 | tf_op jit(solution)/shard_map/first_keys_values/pallas_call | solution.py:122
  4.1 5.3 %all-to-all-start = ((bf16[8,16,32,128]{3,2,1,0:T(8,128)(2,1)}), bf16[8,16,32,128]{3,2,1,0:T(8,128)(2,1)}, u32[]{:S(2)}, u32[]{:S(2)}) async-start(bf16[8,16,32,128]{3,2,1,0:T(8,128)(2,1)} %first_keys_values.1), calls=%async_computation | async-start | bytes 2097152 | tf_op jit(solution)/shard_map/all_to_all | solution.py:550
  9.4 0.6 pad_add_fusion.place_ref
  10.0 15.4 %all-to-all-done = bf16[8,16,32,128]{3,2,1,0:T(8,128)(2,1)} async-done(((bf16[8,16,32,128]{3,2,1,0:T(8,128)(2,1)}), bf16[8,16,32,128]{3,2,1,0:T(8,128)(2,1)}, u32[]{:S(2)}, u32[]{:S(2)}) %all-to-all-start) | async-done | bytes 1048608 | tf_op jit(solution)/shard_map/all_to_all | solution.py:550
  25.4 3.1 %collect.3 = (bf16[256,32,128]{2,1,0:T(8,128)(2,1)}, bf16[4,16,32,128]{3,2,1,0:T(8,128)(2,1)}, bf16[4,16,32,128]{3,2,1,0:T(8,128)(2,1)}) custom-call(s32[1,16,16]{2,1,0:T(8,128)} %list_ref.5, s32[2]{0:T(128)} %pad_add_fusion.place_ref, bf16[128,32,128]{2,1,0:T(8,128)(2,1)} %bitcast.4.refs_0_), custom_call_target="tpu_custom_call" | custom-call | bytes 5242880 | tf_op jit(solution)/shard_map/collect/pallas_call | solution.py:246
  28.5 7.4 %all-to-all-start.1 = ((bf16[16,16,32,128]{3,2,1,0:T(8,128)(2,1)}), bf16[16,16,32,128]{3,2,1,0:T(8,128)(2,1)}, u32[]{:S(2)}, u32[]{:S(2)}) async-start(bf16[16,16,32,128]{3,2,1,0:T(8,128)(2,1)} %bitcast.12), calls=%async_computation.1 | async-start | bytes 4194304 | tf_op jit(solution)/shard_map/all_to_all | solution.py:560
  36.0 3.5 %collective-permute-done.8.far_ref = bf16[1024,768]{1,0:T(8,128)(2,1)} collective-permute-done((bf16[1024,768]{1,0:T(8,128)(2,1)S(1)}, bf16[1024,768]{1,0:T(8,128)(2,1)}, u32[]{:S(2)}, u32[]{:S(2)}) %collective-permute-start.8) | collective-permute-done | bytes 1572896 | tf_op jit(solution)/shard_map/ppermute | solution.py:525
  39.5 5.0 %keys_values.3 = (bf16[32,32,128]{2,1,0:T(8,128)(2,1)}, bf16[32,32,128]{2,1,0:T(8,128)(2,1)}, bf16[32,32,128]{2,1,0:T(8,128)(2,1)}, bf16[32,32,128]{2,1,0:T(8,128)(2,1)}) custom-call(s32[2]{0:T(128)} %pad_add_fusion.place_ref, bf16[1024,768]{1,0:T(8,128)(2,1)} %feat_ref.5, bf16[1024,768]{1,0:T(8,128)(2,1)} %collective-permute-done.8.far_ref, ...), custom_call_target="tpu_custom_call" | custom-call | flops 805306368 | bytes 5242880 | tf_op jit(solution)/shard_map/keys_values/pallas_call | solution.py:154
  44.5 0.6 collective-permute-start.17
  45.2 2.1 collective-permute-start.18
  47.2 0.7 collective-permute-start.19
  47.9 12.2 %collective-permute-done.17.refs_1_ = bf16[32,32,128]{2,1,0:T(8,128)(2,1)} collective-permute-done((bf16[32,32,128]{2,1,0:T(8,128)(2,1)}, bf16[32,32,128]{2,1,0:T(8,128)(2,1)}, u32[]{:S(2)}, u32[]{:S(2)}) %collective-permute-start.17) | collective-permute-done | bytes 262176 | tf_op jit(solution)/shard_map/ppermute | solution.py:531
  60.1 0.6 collective-permute-done.19.refs_3_
  60.7 3.2 %collect.5 = (bf16[256,32,128]{2,1,0:T(8,128)(2,1)}, bf16[4,16,32,128]{3,2,1,0:T(8,128)(2,1)}, bf16[4,16,32,128]{3,2,1,0:T(8,128)(2,1)}) custom-call(s32[1,16,16]{2,1,0:T(8,128)} %list_ref.5, s32[2]{0:T(128)} %pad_add_fusion.place_ref, bf16[32,32,128]{2,1,0:T(8,128)(2,1)} %get-tuple-element.60.refs_0_, bf16[32,32,128]{2,1,0:T(8,128)(2,1)} %collective-permute-done.17.refs_1_, ...), custom_call_target="tpu_custom_call" | custom-call | bytes 5242880 | tf_op jit(solution)/shard_map/collect/pallas_call | solution.py:246
  63.9 7.2 %all-to-all-start.3 = ((bf16[16,16,32,128]{3,2,1,0:T(8,128)(2,1)}), bf16[16,16,32,128]{3,2,1,0:T(8,128)(2,1)}, u32[]{:S(2)}, u32[]{:S(2)}) async-start(bf16[16,16,32,128]{3,2,1,0:T(8,128)(2,1)} %bitcast.11), calls=%async_computation.3 | async-start | bytes 4194304 | tf_op jit(solution)/shard_map/all_to_all | solution.py:560
  71.1 5.0 %keys_values.2 = (bf16[32,32,128]{2,1,0:T(8,128)(2,1)}, bf16[32,32,128]{2,1,0:T(8,128)(2,1)}, bf16[32,32,128]{2,1,0:T(8,128)(2,1)}, bf16[32,32,128]{2,1,0:T(8,128)(2,1)}) custom-call(s32[2]{0:T(128)} %pad_add_fusion.place_ref, bf16[1024,768]{1,0:T(8,128)(2,1)} %feat_ref.5, bf16[1024,768]{1,0:T(8,128)(2,1)} %collective-permute-done.8.far_ref, ...), custom_call_target="tpu_custom_call" | custom-call | flops 805306368 | bytes 5242880 | tf_op jit(solution)/shard_map/keys_values/pallas_call | solution.py:154
  76.2 1.1 collective-permute-start.10
  77.2 2.0 collective-permute-start.11
  79.2 0.3 collective-permute-start.9
  79.5 7.7 %collective-permute-done.10.refs_2_ = bf16[32,32,128]{2,1,0:T(8,128)(2,1)} collective-permute-done((bf16[32,32,128]{2,1,0:T(8,128)(2,1)}, bf16[32,32,128]{2,1,0:T(8,128)(2,1)}, u32[]{:S(2)}, u32[]{:S(2)}) %collective-permute-start.10) | collective-permute-done | bytes 262176 | tf_op jit(solution)/shard_map/ppermute | solution.py:531
  87.2 3.7 %collective-permute-done.11.refs_3_ = bf16[32,32,128]{2,1,0:T(8,128)(2,1)} collective-permute-done((bf16[32,32,128]{2,1,0:T(8,128)(2,1)}, bf16[32,32,128]{2,1,0:T(8,128)(2,1)}, u32[]{:S(2)}, u32[]{:S(2)}) %collective-permute-start.11) | collective-permute-done | bytes 262176 | tf_op jit(solution)/shard_map/ppermute | solution.py:531
  90.9 3.2 %collect.4 = (bf16[256,32,128]{2,1,0:T(8,128)(2,1)}, bf16[4,16,32,128]{3,2,1,0:T(8,128)(2,1)}, bf16[4,16,32,128]{3,2,1,0:T(8,128)(2,1)}) custom-call(s32[1,16,16]{2,1,0:T(8,128)} %list_ref.5, s32[2]{0:T(128)} %pad_add_fusion.place_ref, bf16[32,32,128]{2,1,0:T(8,128)(2,1)} %get-tuple-element.49.refs_0_, bf16[32,32,128]{2,1,0:T(8,128)(2,1)} %collective-permute-done.9.refs_1_, ...), custom_call_target="tpu_custom_call" | custom-call | bytes 5242880 | tf_op jit(solution)/shard_map/collect/pallas_call | solution.py:246
  94.2 2.7 %all-to-all-done.3 = bf16[16,16,32,128]{3,2,1,0:T(8,128)(2,1)} async-done(((bf16[16,16,32,128]{3,2,1,0:T(8,128)(2,1)}), bf16[16,16,32,128]{3,2,1,0:T(8,128)(2,1)}, u32[]{:S(2)}, u32[]{:S(2)}) %all-to-all-start.3) | async-done | bytes 2097184 | tf_op jit(solution)/shard_map/all_to_all | solution.py:560
  96.9 7.6 %all-to-all-start.2 = ((bf16[16,16,32,128]{3,2,1,0:T(8,128)(2,1)}), bf16[16,16,32,128]{3,2,1,0:T(8,128)(2,1)}, u32[]{:S(2)}, u32[]{:S(2)}) async-start(bf16[16,16,32,128]{3,2,1,0:T(8,128)(2,1)} %bitcast.13), calls=%async_computation.2 | async-start | bytes 4194304 | tf_op jit(solution)/shard_map/all_to_all | solution.py:560
  104.5 0.5 collective-permute-start.21
  105.0 24.2 %all-to-all-done.2 = bf16[16,16,32,128]{3,2,1,0:T(8,128)(2,1)} async-done(((bf16[16,16,32,128]{3,2,1,0:T(8,128)(2,1)}), bf16[16,16,32,128]{3,2,1,0:T(8,128)(2,1)}, u32[]{:S(2)}, u32[]{:S(2)}) %all-to-all-start.2) | async-done | bytes 2097184 | tf_op jit(solution)/shard_map/all_to_all | solution.py:560
  129.3 4.7 %queries.1 = (bf16[3,16,32,128]{3,2,1,0:T(8,128)(2,1)}, bf16[3,16,32,128]{3,2,1,0:T(8,128)(2,1)}, bf16[3,16,32,128]{3,2,1,0:T(8,128)(2,1)}, bf16[3,16,32,128]{3,2,1,0:T(8,128)(2,1)}) custom-call(s32[2]{0:T(128)} %pad_add_fusion.place_ref, bf16[1024,768]{1,0:T(8,128)(2,1)} %feat_ref.5, bf16[768,768]{1,0:T(8,128)(2,1)} %query_ref.1), custom_call_target="tpu_custom_call" | custom-call | flops 1207959552 | bytes 5242880 | tf_op jit(solution)/shard_map/queries/pallas_call | solution.py:192
  134.0 2.2 collective-permute-start
  136.2 3.1 %collective-permute-start.1 = (bf16[3,16,32,128]{3,2,1,0:T(8,128)(2,1)}, bf16[3,16,32,128]{3,2,1,0:T(8,128)(2,1)}, u32[]{:S(2)}, u32[]{:S(2)}) collective-permute-start(bf16[3,16,32,128]{3,2,1,0:T(8,128)(2,1)} %get-tuple-element.40), channel_id=1, source_target_pairs={{0,4},{1,5},{2,6},{3,7},{4,0},{5,1},{6,2},{7,3},{8,12},{9,13},{10,... | collective-permute-start | bytes 1179656 | tf_op jit(solution)/shard_map/ppermute | solution.py:531
  139.3 8.6 %collective-permute-done.refs_1_ = bf16[3,16,32,128]{3,2,1,0:T(8,128)(2,1)} collective-permute-done((bf16[3,16,32,128]{3,2,1,0:T(8,128)(2,1)}, bf16[3,16,32,128]{3,2,1,0:T(8,128)(2,1)}, u32[]{:S(2)}, u32[]{:S(2)}) %collective-permute-start) | collective-permute-done | bytes 393248 | tf_op jit(solution)/shard_map/ppermute | solution.py:531
  147.9 2.2 collective-permute-start.2
  150.1 7.4 %collective-permute-done.1.refs_2_ = bf16[3,16,32,128]{3,2,1,0:T(8,128)(2,1)} collective-permute-done((bf16[3,16,32,128]{3,2,1,0:T(8,128)(2,1)}, bf16[3,16,32,128]{3,2,1,0:T(8,128)(2,1)}, u32[]{:S(2)}, u32[]{:S(2)}) %collective-permute-start.1) | collective-permute-done | bytes 393248 | tf_op jit(solution)/shard_map/ppermute | solution.py:531
  157.5 1.6 collective-permute-done.2.refs_3_
  159.2 0.6 collective-permute-done.3.refs_5_
  159.8 0.1 collective-permute-start.12
  159.9 13.1 %attend.3 = (bf16[16,32,128]{2,1,0:T(8,128)(2,1)}, bf16[16,32,128]{2,1,0:T(8,128)(2,1)}, bf16[16,32,128]{2,1,0:T(8,128)(2,1)}, bf16[16,32,128]{2,1,0:T(8,128)(2,1)}) custom-call(s32[8,128]{1,0:T(8,128)} %bitcast.14, s32[8,128]{1,0:T(8,128)} %bitcast.17, s32[128]{0:T(128)} %count_ref.5, s32[2]{0:T(128)} %pad_add_fusion.place_ref, ...), custom_call_target="tpu_custom_call" | custom-call | flops 1610612736 | bytes 8388608 | tf_op jit(solution)/shard_map/attend/pallas_call | solution.py:395
  173.1 3.9 %collective-permute-start.6 = (bf16[16,32,128]{2,1,0:T(8,128)(2,1)}, bf16[16,32,128]{2,1,0:T(8,128)(2,1)}, u32[]{:S(2)}, u32[]{:S(2)}) collective-permute-start(bf16[16,32,128]{2,1,0:T(8,128)(2,1)} %get-tuple-element.47), channel_id=1, source_target_pairs={{0,4},{1,5},{2,6},{3,7},{4,0},{5,1},{6,2},{7,3},{8,12},{9,13},{10,... | collective-permute-start | bytes 393224 | tf_op jit(solution)/shard_map/ppermute | solution.py:531
  177.0 13.1 %attend.5 = (bf16[16,32,128]{2,1,0:T(8,128)(2,1)}, bf16[16,32,128]{2,1,0:T(8,128)(2,1)}, bf16[16,32,128]{2,1,0:T(8,128)(2,1)}, bf16[16,32,128]{2,1,0:T(8,128)(2,1)}) custom-call(s32[8,128]{1,0:T(8,128)} %bitcast.15, s32[8,128]{1,0:T(8,128)} %bitcast.18, s32[128]{0:T(128)} %count_ref.5, s32[2]{0:T(128)} %pad_add_fusion.place_ref, ...), custom_call_target="tpu_custom_call" | custom-call | flops 1610612736 | bytes 8388608 | tf_op jit(solution)/shard_map/attend/pallas_call | solution.py:395
  190.1 2.1 collective-permute-start.22
  192.2 0.3 collective-permute-start.23
  192.6 13.1 %attend.4 = (bf16[16,32,128]{2,1,0:T(8,128)(2,1)}, bf16[16,32,128]{2,1,0:T(8,128)(2,1)}, bf16[16,32,128]{2,1,0:T(8,128)(2,1)}, bf16[16,32,128]{2,1,0:T(8,128)(2,1)}) custom-call(s32[8,128]{1,0:T(8,128)} %bitcast.16, s32[8,128]{1,0:T(8,128)} %bitcast.19, s32[128]{0:T(128)} %count_ref.5, s32[2]{0:T(128)} %pad_add_fusion.place_ref, ...), custom_call_target="tpu_custom_call" | custom-call | flops 1610612736 | bytes 8388608 | tf_op jit(solution)/shard_map/attend/pallas_call | solution.py:395
  205.7 2.6 %collective-permute-start.24 = (bf16[16,32,128]{2,1,0:T(8,128)(2,1)}, bf16[16,32,128]{2,1,0:T(8,128)(2,1)}, u32[]{:S(2)}, u32[]{:S(2)}) collective-permute-start(bf16[16,32,128]{2,1,0:T(8,128)(2,1)} %get-tuple-element.70), channel_id=1, source_target_pairs={{0,6},{1,7},{2,0},{3,1},{4,2},{5,3},{6,4},{7,5},{8,14},{9,15},{10,... | collective-permute-start | bytes 393224 | tf_op jit(solution)/shard_map/ppermute | solution.py:531
  208.3 2.7 %collective-permute-start.15 = (bf16[16,32,128]{2,1,0:T(8,128)(2,1)}, bf16[16,32,128]{2,1,0:T(8,128)(2,1)}, u32[]{:S(2)}, u32[]{:S(2)}) collective-permute-start(bf16[16,32,128]{2,1,0:T(8,128)(2,1)} %get-tuple-element.58), channel_id=1, source_target_pairs={{0,4},{1,5},{2,6},{3,7},{4,0},{5,1},{6,2},{7,3},{8,12},{9,13},{10,... | collective-permute-start | bytes 393224 | tf_op jit(solution)/shard_map/ppermute | solution.py:531
  211.0 1.2 collective-permute-start.16
  212.2 1.3 gains.1.refs_15_
  213.5 3.6 %collective-permute-done.14.refs_5_ = bf16[16,32,128]{2,1,0:T(8,128)(2,1)} collective-permute-done((bf16[16,32,128]{2,1,0:T(8,128)(2,1)}, bf16[16,32,128]{2,1,0:T(8,128)(2,1)}, u32[]{:S(2)}, u32[]{:S(2)}) %collective-permute-start.14) | collective-permute-done | bytes 131104 | tf_op jit(solution)/shard_map/ppermute | solution.py:531
  217.1 0.6 collective-permute-done.16.refs_7_
  217.7 14.4 %finish.1 = bf16[1024,768]{1,0:T(8,128)(2,1)} custom-call(s32[2]{0:T(128)} %pad_add_fusion.place_ref, bf16[1024,768]{1,0:T(8,128)(2,1)} %feat_ref.5, bf16[16,32,128]{2,1,0:T(8,128)(2,1)} %get-tuple-element.45.refs_0_, bf16[16,32,128]{2,1,0:T(8,128)(2,1)} %collective-permute-done.5.refs_1_, bf16[16,32,128]{2,1,0:T(8,128)(2,1)} %collective-permute-done.6.refs_2_, ...), custom_call_target="tpu_custom_call" | custom-call | tf_op jit(solution)/shard_map/finish/pallas_call | solution.py:504
  (25 shorter events, 0.2 us)
Async XLA Ops:
  4.1 21.4 %all-to-all-start = ((bf16[8,16,32,128]{3,2,1,0:T(8,128)(2,1)}), bf16[8,16,32,128]{3,2,1,0:T(8,128)(2,1)}, u32[]{:S(2)}, u32[]{:S(2)}) async-start(bf16[8,16,32,128]{3,2,1,0:T(8,128)(2,1)} %first_keys_values.1), calls=%async_computation | async-start | bytes 2097152 | tf_op jit(solution)/shard_map/all_to_all | solution.py:550
  28.5 7.4 %copy-start = (bf16[1024,768]{1,0:T(8,128)(2,1)S(1)}, bf16[1024,768]{1,0:T(8,128)(2,1)}, u32[]{:S(2)}) copy-start(bf16[1024,768]{1,0:T(8,128)(2,1)} %feat_ref.5) | copy-start | bytes 4718596
  28.5 35.3 %all-to-all-start.1 = ((bf16[16,16,32,128]{3,2,1,0:T(8,128)(2,1)}), bf16[16,16,32,128]{3,2,1,0:T(8,128)(2,1)}, u32[]{:S(2)}, u32[]{:S(2)}) async-start(bf16[16,16,32,128]{3,2,1,0:T(8,128)(2,1)} %bitcast.12), calls=%async_computation.1 | async-start | bytes 4194304 | tf_op jit(solution)/shard_map/all_to_all | solution.py:560
  35.9 3.6 %collective-permute-start.8 = (bf16[1024,768]{1,0:T(8,128)(2,1)S(1)}, bf16[1024,768]{1,0:T(8,128)(2,1)}, u32[]{:S(2)}, u32[]{:S(2)}) collective-permute-start(bf16[1024,768]{1,0:T(8,128)(2,1)S(1)} %copy-done), channel_id=1, source_target_pairs={{0,1},{1,0},{2,3},{3,2},{4,5},{5,4},{6,7},{7,6},{8,9},{9,8},{10,11... | collective-permute-start | bytes 4718600 | tf_op jit(solution)/shard_map/ppermute | solution.py:525
  44.5 15.6 %collective-permute-start.17 = (bf16[32,32,128]{2,1,0:T(8,128)(2,1)}, bf16[32,32,128]{2,1,0:T(8,128)(2,1)}, u32[]{:S(2)}, u32[]{:S(2)}) collective-permute-start(bf16[32,32,128]{2,1,0:T(8,128)(2,1)} %get-tuple-element.61), channel_id=1, source_target_pairs={{0,2},{1,3},{2,4},{3,5},{4,6},{5,7},{6,0},{7,1},{8,10},{9,11},{10,... | collective-permute-start | bytes 786440 | tf_op jit(solution)/shard_map/ppermute | solution.py:531
  45.2 14.9 %collective-permute-start.18 = (bf16[32,32,128]{2,1,0:T(8,128)(2,1)}, bf16[32,32,128]{2,1,0:T(8,128)(2,1)}, u32[]{:S(2)}, u32[]{:S(2)}) collective-permute-start(bf16[32,32,128]{2,1,0:T(8,128)(2,1)} %get-tuple-element.62), channel_id=1, source_target_pairs={{0,4},{1,5},{2,6},{3,7},{4,0},{5,1},{6,2},{7,3},{8,12},{9,13},{10,... | collective-permute-start | bytes 786440 | tf_op jit(solution)/shard_map/ppermute | solution.py:531
  47.2 13.5 %collective-permute-start.19 = (bf16[32,32,128]{2,1,0:T(8,128)(2,1)}, bf16[32,32,128]{2,1,0:T(8,128)(2,1)}, u32[]{:S(2)}, u32[]{:S(2)}) collective-permute-start(bf16[32,32,128]{2,1,0:T(8,128)(2,1)} %get-tuple-element.63), channel_id=1, source_target_pairs={{0,6},{1,7},{2,0},{3,1},{4,2},{5,3},{6,4},{7,5},{8,14},{9,15},{10,... | collective-permute-start | bytes 786440 | tf_op jit(solution)/shard_map/ppermute | solution.py:531
  63.9 33.0 %all-to-all-start.3 = ((bf16[16,16,32,128]{3,2,1,0:T(8,128)(2,1)}), bf16[16,16,32,128]{3,2,1,0:T(8,128)(2,1)}, u32[]{:S(2)}, u32[]{:S(2)}) async-start(bf16[16,16,32,128]{3,2,1,0:T(8,128)(2,1)} %bitcast.11), calls=%async_computation.3 | async-start | bytes 4194304 | tf_op jit(solution)/shard_map/all_to_all | solution.py:560
  76.2 11.1 %collective-permute-start.10 = (bf16[32,32,128]{2,1,0:T(8,128)(2,1)}, bf16[32,32,128]{2,1,0:T(8,128)(2,1)}, u32[]{:S(2)}, u32[]{:S(2)}) collective-permute-start(bf16[32,32,128]{2,1,0:T(8,128)(2,1)} %get-tuple-element.51), channel_id=1, source_target_pairs={{0,4},{1,5},{2,6},{3,7},{4,0},{5,1},{6,2},{7,3},{8,12},{9,13},{10,... | collective-permute-start | bytes 786440 | tf_op jit(solution)/shard_map/ppermute | solution.py:531
  77.2 13.7 %collective-permute-start.11 = (bf16[32,32,128]{2,1,0:T(8,128)(2,1)}, bf16[32,32,128]{2,1,0:T(8,128)(2,1)}, u32[]{:S(2)}, u32[]{:S(2)}) collective-permute-start(bf16[32,32,128]{2,1,0:T(8,128)(2,1)} %get-tuple-element.52), channel_id=1, source_target_pairs={{0,6},{1,7},{2,0},{3,1},{4,2},{5,3},{6,4},{7,5},{8,14},{9,15},{10,... | collective-permute-start | bytes 786440 | tf_op jit(solution)/shard_map/ppermute | solution.py:531
  79.2 11.7 %collective-permute-start.9 = (bf16[32,32,128]{2,1,0:T(8,128)(2,1)}, bf16[32,32,128]{2,1,0:T(8,128)(2,1)}, u32[]{:S(2)}, u32[]{:S(2)}) collective-permute-start(bf16[32,32,128]{2,1,0:T(8,128)(2,1)} %get-tuple-element.50), channel_id=1, source_target_pairs={{0,2},{1,3},{2,4},{3,5},{4,6},{5,7},{6,0},{7,1},{8,10},{9,11},{10,... | collective-permute-start | bytes 786440 | tf_op jit(solution)/shard_map/ppermute | solution.py:531
  96.9 32.4 %all-to-all-start.2 = ((bf16[16,16,32,128]{3,2,1,0:T(8,128)(2,1)}), bf16[16,16,32,128]{3,2,1,0:T(8,128)(2,1)}, u32[]{:S(2)}, u32[]{:S(2)}) async-start(bf16[16,16,32,128]{3,2,1,0:T(8,128)(2,1)} %bitcast.13), calls=%async_computation.2 | async-start | bytes 4194304 | tf_op jit(solution)/shard_map/all_to_all | solution.py:560
  104.5 55.4 %collective-permute-start.4 = (bf16[256,32,128]{2,1,0:T(8,128)(2,1)}, bf16[256,32,128]{2,1,0:T(8,128)(2,1)}, u32[]{:S(2)}, u32[]{:S(2)}) collective-permute-start(bf16[256,32,128]{2,1,0:T(8,128)(2,1)} %bitcast.6.refs_6_), channel_id=1, source_target_pairs={{0,1},{1,0},{2,3},{3,2},{4,5},{5,4},{6,7},{7,6},{8,9},{9,8},{10,11... | collective-permute-start | bytes 6291464 | tf_op jit(solution)/shard_map/ppermute | solution.py:525
  104.5 72.5 %collective-permute-start.21 = (bf16[256,32,128]{2,1,0:T(8,128)(2,1)}, bf16[256,32,128]{2,1,0:T(8,128)(2,1)}, u32[]{:S(2)}, u32[]{:S(2)}) collective-permute-start(bf16[256,32,128]{2,1,0:T(8,128)(2,1)} %bitcast.10.refs_6_), channel_id=1, source_target_pairs={{0,1},{1,0},{2,3},{3,2},{4,5},{5,4},{6,7},{7,6},{8,9},{9,8},{10,11... | collective-permute-start | bytes 6291464 | tf_op jit(solution)/shard_map/ppermute | solution.py:525
  129.3 63.0 %collective-permute-start.13 = (bf16[256,32,128]{2,1,0:T(8,128)(2,1)}, bf16[256,32,128]{2,1,0:T(8,128)(2,1)}, u32[]{:S(2)}, u32[]{:S(2)}) collective-permute-start(bf16[256,32,128]{2,1,0:T(8,128)(2,1)} %bitcast.8.refs_6_), channel_id=1, source_target_pairs={{0,1},{1,0},{2,3},{3,2},{4,5},{5,4},{6,7},{7,6},{8,9},{9,8},{10,11... | collective-permute-start | bytes 6291464 | tf_op jit(solution)/shard_map/ppermute | solution.py:525
  134.0 13.9 %collective-permute-start = (bf16[3,16,32,128]{3,2,1,0:T(8,128)(2,1)}, bf16[3,16,32,128]{3,2,1,0:T(8,128)(2,1)}, u32[]{:S(2)}, u32[]{:S(2)}) collective-permute-start(bf16[3,16,32,128]{3,2,1,0:T(8,128)(2,1)} %get-tuple-element.39), channel_id=1, source_target_pairs={{0,2},{1,3},{2,4},{3,5},{4,6},{5,7},{6,0},{7,1},{8,10},{9,11},{10,... | collective-permute-start | bytes 1179656 | tf_op jit(solution)/shard_map/ppermute | solution.py:531
  136.2 21.3 %collective-permute-start.1 = (bf16[3,16,32,128]{3,2,1,0:T(8,128)(2,1)}, bf16[3,16,32,128]{3,2,1,0:T(8,128)(2,1)}, u32[]{:S(2)}, u32[]{:S(2)}) collective-permute-start(bf16[3,16,32,128]{3,2,1,0:T(8,128)(2,1)} %get-tuple-element.40), channel_id=1, source_target_pairs={{0,4},{1,5},{2,6},{3,7},{4,0},{5,1},{6,2},{7,3},{8,12},{9,13},{10,... | collective-permute-start | bytes 1179656 | tf_op jit(solution)/shard_map/ppermute | solution.py:531
  147.9 11.3 %collective-permute-start.2 = (bf16[3,16,32,128]{3,2,1,0:T(8,128)(2,1)}, bf16[3,16,32,128]{3,2,1,0:T(8,128)(2,1)}, u32[]{:S(2)}, u32[]{:S(2)}) collective-permute-start(bf16[3,16,32,128]{3,2,1,0:T(8,128)(2,1)} %get-tuple-element.41), channel_id=1, source_target_pairs={{0,6},{1,7},{2,0},{3,1},{4,2},{5,3},{6,4},{7,5},{8,14},{9,15},{10,... | collective-permute-start | bytes 1179656 | tf_op jit(solution)/shard_map/ppermute | solution.py:531
  157.5 2.3 collective-permute-start.3
  159.2 13.9 %collective-permute-start.20 = (bf16[4,16,32,128]{3,2,1,0:T(8,128)(2,1)}, bf16[4,16,32,128]{3,2,1,0:T(8,128)(2,1)}, u32[]{:S(2)}, u32[]{:S(2)}) collective-permute-start(bf16[4,16,32,128]{3,2,1,0:T(8,128)(2,1)} %get-tuple-element.65), channel_id=1, source_target_pairs={{0,1},{1,0},{2,3},{3,2},{4,5},{5,4},{6,7},{7,6},{8,9},{9,8},{10,11... | collective-permute-start | bytes 1572872 | tf_op jit(solution)/shard_map/ppermute | solution.py:525
  159.8 30.4 %collective-permute-start.12 = (bf16[4,16,32,128]{3,2,1,0:T(8,128)(2,1)}, bf16[4,16,32,128]{3,2,1,0:T(8,128)(2,1)}, u32[]{:S(2)}, u32[]{:S(2)}) collective-permute-start(bf16[4,16,32,128]{3,2,1,0:T(8,128)(2,1)} %get-tuple-element.54), channel_id=1, source_target_pairs={{0,1},{1,0},{2,3},{3,2},{4,5},{5,4},{6,7},{7,6},{8,9},{9,8},{10,11... | collective-permute-start | bytes 1572872 | tf_op jit(solution)/shard_map/ppermute | solution.py:525
  173.0 32.7 %collective-permute-start.5 = (bf16[16,32,128]{2,1,0:T(8,128)(2,1)}, bf16[16,32,128]{2,1,0:T(8,128)(2,1)}, u32[]{:S(2)}, u32[]{:S(2)}) collective-permute-start(bf16[16,32,128]{2,1,0:T(8,128)(2,1)} %get-tuple-element.46), channel_id=1, source_target_pairs={{0,2},{1,3},{2,4},{3,5},{4,6},{5,7},{6,0},{7,1},{8,10},{9,11},{10,... | collective-permute-start | bytes 393224 | tf_op jit(solution)/shard_map/ppermute | solution.py:531
  173.1 35.2 %collective-permute-start.6 = (bf16[16,32,128]{2,1,0:T(8,128)(2,1)}, bf16[16,32,128]{2,1,0:T(8,128)(2,1)}, u32[]{:S(2)}, u32[]{:S(2)}) collective-permute-start(bf16[16,32,128]{2,1,0:T(8,128)(2,1)} %get-tuple-element.47), channel_id=1, source_target_pairs={{0,4},{1,5},{2,6},{3,7},{4,0},{5,1},{6,2},{7,3},{8,12},{9,13},{10,... | collective-permute-start | bytes 393224 | tf_op jit(solution)/shard_map/ppermute | solution.py:531
  177.0 31.3 %collective-permute-start.7 = (bf16[16,32,128]{2,1,0:T(8,128)(2,1)}, bf16[16,32,128]{2,1,0:T(8,128)(2,1)}, u32[]{:S(2)}, u32[]{:S(2)}) collective-permute-start(bf16[16,32,128]{2,1,0:T(8,128)(2,1)} %get-tuple-element.48), channel_id=1, source_target_pairs={{0,6},{1,7},{2,0},{3,1},{4,2},{5,3},{6,4},{7,5},{8,14},{9,15},{10,... | collective-permute-start | bytes 393224 | tf_op jit(solution)/shard_map/ppermute | solution.py:531
  190.1 20.8 %collective-permute-start.22 = (bf16[16,32,128]{2,1,0:T(8,128)(2,1)}, bf16[16,32,128]{2,1,0:T(8,128)(2,1)}, u32[]{:S(2)}, u32[]{:S(2)}) collective-permute-start(bf16[16,32,128]{2,1,0:T(8,128)(2,1)} %get-tuple-element.68), channel_id=1, source_target_pairs={{0,2},{1,3},{2,4},{3,5},{4,6},{5,7},{6,0},{7,1},{8,10},{9,11},{10,... | collective-permute-start | bytes 393224 | tf_op jit(solution)/shard_map/ppermute | solution.py:531
  192.2 21.3 %collective-permute-start.23 = (bf16[16,32,128]{2,1,0:T(8,128)(2,1)}, bf16[16,32,128]{2,1,0:T(8,128)(2,1)}, u32[]{:S(2)}, u32[]{:S(2)}) collective-permute-start(bf16[16,32,128]{2,1,0:T(8,128)(2,1)} %get-tuple-element.69), channel_id=1, source_target_pairs={{0,4},{1,5},{2,6},{3,7},{4,0},{5,1},{6,2},{7,3},{8,12},{9,13},{10,... | collective-permute-start | bytes 393224 | tf_op jit(solution)/shard_map/ppermute | solution.py:531
  205.7 7.8 %collective-permute-start.24 = (bf16[16,32,128]{2,1,0:T(8,128)(2,1)}, bf16[16,32,128]{2,1,0:T(8,128)(2,1)}, u32[]{:S(2)}, u32[]{:S(2)}) collective-permute-start(bf16[16,32,128]{2,1,0:T(8,128)(2,1)} %get-tuple-element.70), channel_id=1, source_target_pairs={{0,6},{1,7},{2,0},{3,1},{4,2},{5,3},{6,4},{7,5},{8,14},{9,15},{10,... | collective-permute-start | bytes 393224 | tf_op jit(solution)/shard_map/ppermute | solution.py:531
  208.3 8.8 %collective-permute-start.14 = (bf16[16,32,128]{2,1,0:T(8,128)(2,1)}, bf16[16,32,128]{2,1,0:T(8,128)(2,1)}, u32[]{:S(2)}, u32[]{:S(2)}) collective-permute-start(bf16[16,32,128]{2,1,0:T(8,128)(2,1)} %get-tuple-element.57), channel_id=1, source_target_pairs={{0,2},{1,3},{2,4},{3,5},{4,6},{5,7},{6,0},{7,1},{8,10},{9,11},{10,... | collective-permute-start | bytes 393224 | tf_op jit(solution)/shard_map/ppermute | solution.py:531
  208.3 8.8 %collective-permute-start.15 = (bf16[16,32,128]{2,1,0:T(8,128)(2,1)}, bf16[16,32,128]{2,1,0:T(8,128)(2,1)}, u32[]{:S(2)}, u32[]{:S(2)}) collective-permute-start(bf16[16,32,128]{2,1,0:T(8,128)(2,1)} %get-tuple-element.58), channel_id=1, source_target_pairs={{0,4},{1,5},{2,6},{3,7},{4,0},{5,1},{6,2},{7,3},{8,12},{9,13},{10,... | collective-permute-start | bytes 393224 | tf_op jit(solution)/shard_map/ppermute | solution.py:531
  211.0 6.7 %collective-permute-start.16 = (bf16[16,32,128]{2,1,0:T(8,128)(2,1)}, bf16[16,32,128]{2,1,0:T(8,128)(2,1)}, u32[]{:S(2)}, u32[]{:S(2)}) collective-permute-start(bf16[16,32,128]{2,1,0:T(8,128)(2,1)} %get-tuple-element.59), channel_id=1, source_target_pairs={{0,6},{1,7},{2,0},{3,1},{4,2},{5,3},{6,4},{7,5},{8,14},{9,15},{10,... | collective-permute-start | bytes 393224 | tf_op jit(solution)/shard_map/ppermute | solution.py:531

commit v7 on v6

--- a/solution.py
+++ b/solution.py
@@ -256,10 +256,11 @@
     )(send_list, place, *parts)
 
 
-def attend_kernel(chunk, owner_ref, slot_ref, count_ref, place_ref, *refs):
+def attend_kernel(chunk, carried, owner_ref, slot_ref, count_ref, place_ref, *refs):
     parts, (own_ref, swap_ref, mine_ref, other_ref) = refs[:CHIPS], refs[CHIPS : CHIPS + 4]
-    outs = refs[CHIPS + 4 : 2 * CHIPS + 4]
-    queries, made, keys, values, own_keys, own_values, asked, sems, done = refs[2 * CHIPS + 4 :]
+    befores, refs = refs[CHIPS + 4 : CHIPS + 4 + carried], refs[CHIPS + 4 + carried :]
+    outs, refs = refs[:CHIPS], refs[CHIPS:]
+    queries, made, keys, values, own_keys, own_values, asked, sems, done = refs[:9]
     z, core = place_ref[0], place_ref[1]
 
     asking = []
@@ -292,6 +293,16 @@
 
     for copy in asking:
         copy.wait()
+    targets = outs
+    if carried:
+        before, taken, passed = refs[9:]
+        taking = []
+        for step in range(CHIPS):
+            taking.append(
+                pltpu.make_async_copy(befores[step], before.at[step], taken.at[step])
+            )
+            taking[-1].start()
+        targets = [out.at[1] for out in outs]
 
     low = low_lanes(HALF)
     lane = lax.broadcasted_iota(jnp.int32, (1, LANES), 1)
@@ -379,24 +390,34 @@
 
             @pl.when(jnp.logical_and(at % 2 == 1, ahead == step))
             def _():
-                pltpu.make_async_copy(made.at[source], outs[step], done.at[step]).start()
+                pltpu.make_async_copy(made.at[source], targets[step], done.at[step]).start()
 
         return carry
 
     lax.fori_loop(0, CHIPS * OWN // group, attend_group, 0)
+    if carried:
+        passing = []
+        for step in range(CHIPS):
+            taking[step].wait()
+            passing.append(
+                pltpu.make_async_copy(before.at[step], outs[step].at[0], passed.at[step])
+            )
+            passing[-1].start()
+        for copy in passing:
+            copy.wait()
     for step in range(CHIPS):
         source = lax.rem(z + step, CHIPS)
-        pltpu.make_async_copy(made.at[source], outs[step], done.at[step]).wait()
-
-
-def attend(tables, place, queries, own, swapped, mine, other, chunk):
+        pltpu.make_async_copy(made.at[source], targets[step], done.at[step]).wait()
+
+
+def attend(tables, place, queries, own, swapped, mine, other, chunk, before=()):
     slots = mine.shape[0]
     blocks = pltpu.VMEM((CHIPS, OWN) + TILE, BF16)
     return pl.pallas_call(
-        functools.partial(attend_kernel, chunk),
-        in_specs=[SMEM] * 4 + [HBM] * (CHIPS + 4),
+        functools.partial(attend_kernel, chunk, len(before)),
+        in_specs=[SMEM] * 4 + [HBM] * (CHIPS + 4 + len(before)),
         out_specs=[HBM] * CHIPS,
-        out_shape=[jax.ShapeDtypeStruct((OWN,) + TILE, BF16)] * CHIPS,
+        out_shape=[jax.ShapeDtypeStruct((2,) * (len(before) > 0) + (OWN,) + TILE, BF16)] * CHIPS,
         scratch_shapes=[
             blocks,
             blocks,
@@ -407,13 +428,15 @@
             pltpu.SemaphoreType.DMA((CHIPS,)),
             pltpu.SemaphoreType.DMA((4,)),
             pltpu.SemaphoreType.DMA((CHIPS,)),
-        ],
+        ]
+        + [blocks, pltpu.SemaphoreType.DMA((CHIPS,)), pltpu.SemaphoreType.DMA((CHIPS,))]
+        * (len(before) > 0),
         compiler_params=params(0),
         cost_estimate=pl.CostEstimate(
             flops=64 * 4 * 128 * 128 * 384, bytes_accessed=8 << 20, transcendentals=64 * 128 * 384
         ),
         name="attend",
-    )(*tables, place, *queries, own, swapped, mine, other)
+    )(*tables, place, *queries, own, swapped, mine, other, *before)
 
 
 def normed(values, gain):
@@ -454,14 +477,17 @@
 
 
 def finish_kernel(place_ref, feat_ref, *refs):
-    parts, refs = refs[: CHUNKS * CHIPS], refs[CHUNKS * CHIPS :]
+    parts, refs = refs[: 2 * CHIPS], refs[2 * CHIPS :]
     out_w_ref, up_ref, down_ref, gain_ref, result_ref, *scratch = refs
     held, feats, out_w, up, down, made, arrive, sems = scratch
     rows = feat_ref.shape[0] // 2
     halves = [slice(half * rows, (half + 1) * rows) for half in range(2)]
     arriving = []
     for which in range(CHUNKS):
-        some = parts[which * CHIPS : (which + 1) * CHIPS]
+        if which < CHUNKS - 1:
+            some = [part.at[which] for part in parts[:CHIPS]]
+        else:
+            some = parts[CHIPS:]
         arriving += gather_parts(place_ref, some, held.at[which], arrive.at[which])
     copies = [
         pltpu.make_async_copy(out_w_ref, out_w, sems.at[0]),
@@ -484,8 +510,10 @@
         copies[1 + half].wait()
         mixed = feats[at, :].astype(F32) + added
         firsts.append(normed(mixed, gain_ref[0:1, :]).astype(BF16))
-    for half, at in enumerate(halves):
-        first = firsts[half]
+    rows = rows // 2
+    firsts = [first[at : at + rows] for first in firsts for at in (0, rows)]
+    for half, first in enumerate(firsts):
+        at = slice(half * rows, (half + 1) * rows)
         if half == 0:
             copies[3].wait()
         hidden = jnp.maximum(jnp.dot(first, up[...], preferred_element_type=F32), 0.0).astype(BF16)
@@ -503,7 +531,7 @@
     rows, width = features.shape
     return pl.pallas_call(
         finish_kernel,
-        in_specs=[SMEM] + [HBM] * (CHUNKS * CHIPS + 4) + [VMEM],
+        in_specs=[SMEM] + [HBM] * (2 * CHIPS + 4) + [VMEM],
         out_specs=HBM,
         out_shape=jax.ShapeDtypeStruct((rows, width), BF16),
         scratch_shapes=[
@@ -514,7 +542,7 @@
             pltpu.VMEM(w_down.shape, BF16),
             pltpu.VMEM((rows, width), BF16),
             pltpu.SemaphoreType.DMA((CHUNKS, CHIPS)),
-            pltpu.SemaphoreType.DMA((7,)),
+            pltpu.SemaphoreType.DMA((9,)),
         ],
         compiler_params=params(0),
         name="finish",
@@ -564,10 +592,10 @@
         swapped = swap(collected[c][2])
         other = swap(mines[c])
         tables = (owners, slots, edge_count)
-        done = attend(
-            tables, place, queries, collected[c][1], swapped, mines[c], other, c
-        )
-        backs.append(along_z(done))
+        before = done if c == 1 else ()
+        done = attend(tables, place, queries, collected[c][1], swapped, mines[c], other, c, before)
+        if c > 0:
+            backs.append(along_z(done))
     gains = stack_gains(gain_attn, gain_ffn)
     return finish(place, features, backs, w_out, w_up, w_down, gains)
 

time: 236 us -> 240 us (1.017)
  waiting for transfers between devices: 92.6 us -> 99.6 us
  starting transfers between devices: 55.5 us -> 52.7 us
    ppermute x18 -> x15, waiting for transfers between devices: 46.1 us -> 53.6 us  [along_z(): lax.ppermute(parts[step], 'head', [(i, (i + 2 * step) % (2 * CHIPS)) for...]
    ppermute x18 -> x15, starting transfers between devices: 27.2 us -> 24.3 us  [along_z(): lax.ppermute(parts[step], 'head', [(i, (i + 2 * step) % (2 * CHIPS)) for...]
  transfers between devices with their start and end apart: 29 -> 26, of which waited for: 14 -> 14; matrix products, arithmetic and copies ran while one was open for 0% -> 0% of each run, Pallas kernels for 27% -> 26%
where the time goes in v7:
time: 240 us; the launch traced here: 236 us
  waiting for transfers between devices  99.6 us (42%)
  Pallas kernels  82.6 us (34%)
  starting transfers between devices  52.7 us (22%)
    ppermute x15, waiting for transfers between devices, along_z(): lax.ppermute(parts[step], 'head', [(i, (i + 2 * step) % (2 * CHIPS)) for...  53.6 us
    pallas_call x3, Pallas kernels, attend(): pl.pallas_call(functools.partial(attend_kernel, chunk, len(before)), in_s...  39.7 us
    all_to_all x3, waiting for transfers between devices, per_device(): got = lax.all_to_all(sent, 'node', split_axis=0, concat_axis=0, tiled=True)  26.6 us
    ppermute x15, starting transfers between devices, along_z(): lax.ppermute(parts[step], 'head', [(i, (i + 2 * step) % (2 * CHIPS)) for...  24.3 us
    all_to_all x3, starting transfers between devices, per_device(): got = lax.all_to_all(sent, 'node', split_axis=0, concat_axis=0, tiled=True)  22.3 us
    all_to_all x1, waiting for transfers between devices, per_device(): lax.all_to_all(whole, 'head', split_axis=0, concat_axis=0, tiled=True)  15.4 us
    pallas_call x1, Pallas kernels, finish(): pl.pallas_call(finish_kernel, in_specs=[SMEM] + [HBM] * (2 * CHIPS + 4) +...  13.7 us
    pallas_call x2, Pallas kernels, project_keys_values(): pl.pallas_call(functools.partial(keys_values_kernel, chunk), in_specs=[SM...  9.88 us
  transfers between devices with their start and end apart: 26, of which 14 were waited for; matrix products, arithmetic and copies ran while one was open for 0% of the time, Pallas kernels for 26%

profile of v7, /device:TPU:20, one launch (start us, length us, event | category | flops | bytes accessed | tf_op | source)
XLA Modules:
  0.0 235.9 jit_solution(13877875032475474055)
XLA Ops:
  0.0 4.1 %first_keys_values.1 = bf16[8,16,32,128]{3,2,1,0:T(8,128)(2,1)} custom-call(bf16[1024,768]{1,0:T(8,128)(2,1)} %feat_ref.5, bf16[768,768]{1,0:T(8,128)(2,1)} %key_ref.5, bf16[768,768]{1,0:T(8,128)(2,1)} %value_ref.5), custom_call_target="tpu_custom_call" | custom-call | flops 805306368 | bytes 4194304 | tf_op jit(solution)/shard_map/first_keys_values/pallas_call | solution.py:122
  4.1 5.3 %all-to-all-start.1 = ((bf16[8,16,32,128]{3,2,1,0:T(8,128)(2,1)}), bf16[8,16,32,128]{3,2,1,0:T(8,128)(2,1)}, u32[]{:S(2)}, u32[]{:S(2)}) async-start(bf16[8,16,32,128]{3,2,1,0:T(8,128)(2,1)} %first_keys_values.1), calls=%async_computation.1 | async-start | bytes 2097152 | tf_op jit(solution)/shard_map/all_to_all | solution.py:578
  9.4 0.6 pad_add_fusion.place_ref
  10.0 15.4 %all-to-all-done.1 = bf16[8,16,32,128]{3,2,1,0:T(8,128)(2,1)} async-done(((bf16[8,16,32,128]{3,2,1,0:T(8,128)(2,1)}), bf16[8,16,32,128]{3,2,1,0:T(8,128)(2,1)}, u32[]{:S(2)}, u32[]{:S(2)}) %all-to-all-start.1) | async-done | bytes 1048608 | tf_op jit(solution)/shard_map/all_to_all | solution.py:578
  25.4 3.1 %collect.4 = (bf16[256,32,128]{2,1,0:T(8,128)(2,1)}, bf16[4,16,32,128]{3,2,1,0:T(8,128)(2,1)}, bf16[4,16,32,128]{3,2,1,0:T(8,128)(2,1)}) custom-call(s32[1,16,16]{2,1,0:T(8,128)} %list_ref.5, s32[2]{0:T(128)} %pad_add_fusion.place_ref, bf16[128,32,128]{2,1,0:T(8,128)(2,1)} %bitcast.6.refs_0_), custom_call_target="tpu_custom_call" | custom-call | bytes 5242880 | tf_op jit(solution)/shard_map/collect/pallas_call | solution.py:246
  28.5 0.0 copy-start
  28.5 7.4 %all-to-all-start.2 = ((bf16[16,16,32,128]{3,2,1,0:T(8,128)(2,1)}), bf16[16,16,32,128]{3,2,1,0:T(8,128)(2,1)}, u32[]{:S(2)}, u32[]{:S(2)}) async-start(bf16[16,16,32,128]{3,2,1,0:T(8,128)(2,1)} %bitcast.12), calls=%async_computation.2 | async-start | bytes 4194304 | tf_op jit(solution)/shard_map/all_to_all | solution.py:588
  35.9 0.1 collective-permute-start.3
  36.0 3.5 %collective-permute-done.3.far_ref = bf16[1024,768]{1,0:T(8,128)(2,1)} collective-permute-done((bf16[1024,768]{1,0:T(8,128)(2,1)S(1)}, bf16[1024,768]{1,0:T(8,128)(2,1)}, u32[]{:S(2)}, u32[]{:S(2)}) %collective-permute-start.3) | collective-permute-done | bytes 1572896 | tf_op jit(solution)/shard_map/ppermute | solution.py:553
  39.5 4.9 %keys_values.3 = (bf16[32,32,128]{2,1,0:T(8,128)(2,1)}, bf16[32,32,128]{2,1,0:T(8,128)(2,1)}, bf16[32,32,128]{2,1,0:T(8,128)(2,1)}, bf16[32,32,128]{2,1,0:T(8,128)(2,1)}) custom-call(s32[2]{0:T(128)} %pad_add_fusion.place_ref, bf16[1024,768]{1,0:T(8,128)(2,1)} %feat_ref.5, bf16[1024,768]{1,0:T(8,128)(2,1)} %collective-permute-done.3.far_ref, ...), custom_call_target="tpu_custom_call" | custom-call | flops 805306368 | bytes 5242880 | tf_op jit(solution)/shard_map/keys_values/pallas_call | solution.py:154
  44.5 0.6 collective-permute-start.14
  45.1 2.1 collective-permute-start.15
  47.2 0.7 collective-permute-start.16
  47.9 12.2 %collective-permute-done.14.refs_1_ = bf16[32,32,128]{2,1,0:T(8,128)(2,1)} collective-permute-done((bf16[32,32,128]{2,1,0:T(8,128)(2,1)}, bf16[32,32,128]{2,1,0:T(8,128)(2,1)}, u32[]{:S(2)}, u32[]{:S(2)}) %collective-permute-start.14) | collective-permute-done | bytes 262176 | tf_op jit(solution)/shard_map/ppermute | solution.py:559
  60.0 0.6 collective-permute-done.16.refs_3_
  60.7 3.1 %collect.5 = (bf16[256,32,128]{2,1,0:T(8,128)(2,1)}, bf16[4,16,32,128]{3,2,1,0:T(8,128)(2,1)}, bf16[4,16,32,128]{3,2,1,0:T(8,128)(2,1)}) custom-call(s32[1,16,16]{2,1,0:T(8,128)} %list_ref.5, s32[2]{0:T(128)} %pad_add_fusion.place_ref, bf16[32,32,128]{2,1,0:T(8,128)(2,1)} %get-tuple-element.60.refs_0_, bf16[32,32,128]{2,1,0:T(8,128)(2,1)} %collective-permute-done.14.refs_1_, ...), custom_call_target="tpu_custom_call" | custom-call | bytes 5242880 | tf_op jit(solution)/shard_map/collect/pallas_call | solution.py:246
  63.8 7.2 %all-to-all-start.3 = ((bf16[16,16,32,128]{3,2,1,0:T(8,128)(2,1)}), bf16[16,16,32,128]{3,2,1,0:T(8,128)(2,1)}, u32[]{:S(2)}, u32[]{:S(2)}) async-start(bf16[16,16,32,128]{3,2,1,0:T(8,128)(2,1)} %bitcast.11), calls=%async_computation.3 | async-start | bytes 4194304 | tf_op jit(solution)/shard_map/all_to_all | solution.py:588
  71.0 4.9 %keys_values.2 = (bf16[32,32,128]{2,1,0:T(8,128)(2,1)}, bf16[32,32,128]{2,1,0:T(8,128)(2,1)}, bf16[32,32,128]{2,1,0:T(8,128)(2,1)}, bf16[32,32,128]{2,1,0:T(8,128)(2,1)}) custom-call(s32[2]{0:T(128)} %pad_add_fusion.place_ref, bf16[1024,768]{1,0:T(8,128)(2,1)} %feat_ref.5, bf16[1024,768]{1,0:T(8,128)(2,1)} %collective-permute-done.3.far_ref, ...), custom_call_target="tpu_custom_call" | custom-call | flops 805306368 | bytes 5242880 | tf_op jit(solution)/shard_map/keys_values/pallas_call | solution.py:154
  76.0 0.4 collective-permute-start.4
  76.4 3.6 %collective-permute-start.5 = (bf16[32,32,128]{2,1,0:T(8,128)(2,1)}, bf16[32,32,128]{2,1,0:T(8,128)(2,1)}, u32[]{:S(2)}, u32[]{:S(2)}) collective-permute-start(bf16[32,32,128]{2,1,0:T(8,128)(2,1)} %get-tuple-element.44), channel_id=1, source_target_pairs={{0,4},{1,5},{2,6},{3,7},{4,0},{5,1},{6,2},{7,3},{8,12},{9,13},{10,... | collective-permute-start | bytes 786440 | tf_op jit(solution)/shard_map/ppermute | solution.py:559
  79.9 5.1 %collective-permute-done.4.refs_1_ = bf16[32,32,128]{2,1,0:T(8,128)(2,1)} collective-permute-done((bf16[32,32,128]{2,1,0:T(8,128)(2,1)}, bf16[32,32,128]{2,1,0:T(8,128)(2,1)}, u32[]{:S(2)}, u32[]{:S(2)}) %collective-permute-start.4) | collective-permute-done | bytes 262176 | tf_op jit(solution)/shard_map/ppermute | solution.py:559
  85.0 6.3 %collective-permute-done.5.refs_2_ = bf16[32,32,128]{2,1,0:T(8,128)(2,1)} collective-permute-done((bf16[32,32,128]{2,1,0:T(8,128)(2,1)}, bf16[32,32,128]{2,1,0:T(8,128)(2,1)}, u32[]{:S(2)}, u32[]{:S(2)}) %collective-permute-start.5) | collective-permute-done | bytes 262176 | tf_op jit(solution)/shard_map/ppermute | solution.py:559
  91.3 3.1 %collect.3 = (bf16[256,32,128]{2,1,0:T(8,128)(2,1)}, bf16[4,16,32,128]{3,2,1,0:T(8,128)(2,1)}, bf16[4,16,32,128]{3,2,1,0:T(8,128)(2,1)}) custom-call(s32[1,16,16]{2,1,0:T(8,128)} %list_ref.5, s32[2]{0:T(128)} %pad_add_fusion.place_ref, bf16[32,32,128]{2,1,0:T(8,128)(2,1)} %get-tuple-element.42.refs_0_, bf16[32,32,128]{2,1,0:T(8,128)(2,1)} %collective-permute-done.4.refs_1_, ...), custom_call_target="tpu_custom_call" | custom-call | bytes 5242880 | tf_op jit(solution)/shard_map/collect/pallas_call | solution.py:246
  94.4 2.3 all-to-all-done.3
  96.7 7.6 %all-to-all-start = ((bf16[16,16,32,128]{3,2,1,0:T(8,128)(2,1)}), bf16[16,16,32,128]{3,2,1,0:T(8,128)(2,1)}, u32[]{:S(2)}, u32[]{:S(2)}) async-start(bf16[16,16,32,128]{3,2,1,0:T(8,128)(2,1)} %bitcast.13), calls=%async_computation | async-start | bytes 4194304 | tf_op jit(solution)/shard_map/all_to_all | solution.py:588
  104.4 0.5 collective-permute-start.18
  104.9 24.2 %all-to-all-done = bf16[16,16,32,128]{3,2,1,0:T(8,128)(2,1)} async-done(((bf16[16,16,32,128]{3,2,1,0:T(8,128)(2,1)}), bf16[16,16,32,128]{3,2,1,0:T(8,128)(2,1)}, u32[]{:S(2)}, u32[]{:S(2)}) %all-to-all-start) | async-done | bytes 2097184 | tf_op jit(solution)/shard_map/all_to_all | solution.py:588
  129.1 4.7 %queries.1 = (bf16[3,16,32,128]{3,2,1,0:T(8,128)(2,1)}, bf16[3,16,32,128]{3,2,1,0:T(8,128)(2,1)}, bf16[3,16,32,128]{3,2,1,0:T(8,128)(2,1)}, bf16[3,16,32,128]{3,2,1,0:T(8,128)(2,1)}) custom-call(s32[2]{0:T(128)} %pad_add_fusion.place_ref, bf16[1024,768]{1,0:T(8,128)(2,1)} %feat_ref.5, bf16[768,768]{1,0:T(8,128)(2,1)} %query_ref.1), custom_call_target="tpu_custom_call" | custom-call | flops 1207959552 | bytes 5242880 | tf_op jit(solution)/shard_map/queries/pallas_call | solution.py:192
  133.9 2.2 collective-permute-start
  136.1 3.1 %collective-permute-start.1 = (bf16[3,16,32,128]{3,2,1,0:T(8,128)(2,1)}, bf16[3,16,32,128]{3,2,1,0:T(8,128)(2,1)}, u32[]{:S(2)}, u32[]{:S(2)}) collective-permute-start(bf16[3,16,32,128]{3,2,1,0:T(8,128)(2,1)} %get-tuple-element.40), channel_id=1, source_target_pairs={{0,4},{1,5},{2,6},{3,7},{4,0},{5,1},{6,2},{7,3},{8,12},{9,13},{10,... | collective-permute-start | bytes 1179656 | tf_op jit(solution)/shard_map/ppermute | solution.py:559
  139.1 8.6 %collective-permute-done.refs_1_ = bf16[3,16,32,128]{3,2,1,0:T(8,128)(2,1)} collective-permute-done((bf16[3,16,32,128]{3,2,1,0:T(8,128)(2,1)}, bf16[3,16,32,128]{3,2,1,0:T(8,128)(2,1)}, u32[]{:S(2)}, u32[]{:S(2)}) %collective-permute-start) | collective-permute-done | bytes 393248 | tf_op jit(solution)/shard_map/ppermute | solution.py:559
  147.8 2.2 collective-permute-start.2
  150.0 7.4 %collective-permute-done.1.refs_2_ = bf16[3,16,32,128]{3,2,1,0:T(8,128)(2,1)} collective-permute-done((bf16[3,16,32,128]{3,2,1,0:T(8,128)(2,1)}, bf16[3,16,32,128]{3,2,1,0:T(8,128)(2,1)}, u32[]{:S(2)}, u32[]{:S(2)}) %collective-permute-start.1) | collective-permute-done | bytes 393248 | tf_op jit(solution)/shard_map/ppermute | solution.py:559
  157.4 1.7 collective-permute-done.2.refs_3_
  159.0 0.6 collective-permute-done.9.refs_5_
  159.6 0.1 collective-permute-start.7
  159.8 13.2 %attend.3 = (bf16[16,32,128]{2,1,0:T(8,128)(2,1)}, bf16[16,32,128]{2,1,0:T(8,128)(2,1)}, bf16[16,32,128]{2,1,0:T(8,128)(2,1)}, bf16[16,32,128]{2,1,0:T(8,128)(2,1)}) custom-call(s32[8,128]{1,0:T(8,128)} %bitcast.14, s32[8,128]{1,0:T(8,128)} %bitcast.17, s32[128]{0:T(128)} %count_ref.5, s32[2]{0:T(128)} %pad_add_fusion.place_ref, ...), custom_call_target="tpu_custom_call" | custom-call | flops 1610612736 | bytes 8388608 | tf_op jit(solution)/shard_map/attend/pallas_call | solution.py:416
  173.0 13.1 %attend.5 = (bf16[16,32,128]{2,1,0:T(8,128)(2,1)}, bf16[16,32,128]{2,1,0:T(8,128)(2,1)}, bf16[16,32,128]{2,1,0:T(8,128)(2,1)}, bf16[16,32,128]{2,1,0:T(8,128)(2,1)}) custom-call(s32[8,128]{1,0:T(8,128)} %bitcast.15, s32[8,128]{1,0:T(8,128)} %bitcast.18, s32[128]{0:T(128)} %count_ref.5, s32[2]{0:T(128)} %pad_add_fusion.place_ref, ...), custom_call_target="tpu_custom_call" | custom-call | flops 1610612736 | bytes 8388608 | tf_op jit(solution)/shard_map/attend/pallas_call | solution.py:416
  186.1 0.1 collective-permute-start.19
  186.2 13.4 %attend.4 = (bf16[2,16,32,128]{3,2,1,0:T(8,128)(2,1)}, bf16[2,16,32,128]{3,2,1,0:T(8,128)(2,1)}, bf16[2,16,32,128]{3,2,1,0:T(8,128)(2,1)}, bf16[2,16,32,128]{3,2,1,0:T(8,128)(2,1)}) custom-call(s32[8,128]{1,0:T(8,128)} %bitcast.16, s32[8,128]{1,0:T(8,128)} %bitcast.19, s32[128]{0:T(128)} %count_ref.5, s32[2]{0:T(128)} %pad_add_fusion.place_ref, ...), custom_call_target="tpu_custom_call" | custom-call | flops 1610612736 | bytes 8388608 | tf_op jit(solution)/shard_map/attend/pallas_call | solution.py:416
  199.6 1.0 collective-permute-start.11
  200.6 3.8 %collective-permute-start.12 = (bf16[2,16,32,128]{3,2,1,0:T(8,128)(2,1)}, bf16[2,16,32,128]{3,2,1,0:T(8,128)(2,1)}, u32[]{:S(2)}, u32[]{:S(2)}) collective-permute-start(bf16[2,16,32,128]{3,2,1,0:T(8,128)(2,1)} %get-tuple-element.58), channel_id=1, source_target_pairs={{0,4},{1,5},{2,6},{3,7},{4,0},{5,1},{6,2},{7,3},{8,12},{9,13},{10,... | collective-permute-start | bytes 786440 | tf_op jit(solution)/shard_map/ppermute | solution.py:559
  204.3 1.9 collective-permute-start.13
  206.2 2.8 %collective-permute-start.21 = (bf16[16,32,128]{2,1,0:T(8,128)(2,1)}, bf16[16,32,128]{2,1,0:T(8,128)(2,1)}, u32[]{:S(2)}, u32[]{:S(2)}) collective-permute-start(bf16[16,32,128]{2,1,0:T(8,128)(2,1)} %get-tuple-element.70), channel_id=1, source_target_pairs={{0,6},{1,7},{2,0},{3,1},{4,2},{5,3},{6,4},{7,5},{8,14},{9,15},{10,... | collective-permute-start | bytes 393224 | tf_op jit(solution)/shard_map/ppermute | solution.py:559
  209.0 1.3 gains.1.refs_11_
  210.3 9.3 %collective-permute-done.20.refs_6_ = bf16[16,32,128]{2,1,0:T(8,128)(2,1)} collective-permute-done((bf16[16,32,128]{2,1,0:T(8,128)(2,1)}, bf16[16,32,128]{2,1,0:T(8,128)(2,1)}, u32[]{:S(2)}, u32[]{:S(2)}) %collective-permute-start.20) | collective-permute-done | bytes 131104 | tf_op jit(solution)/shard_map/ppermute | solution.py:559
  219.6 2.4 %collective-permute-done.21.refs_7_ = bf16[16,32,128]{2,1,0:T(8,128)(2,1)} collective-permute-done((bf16[16,32,128]{2,1,0:T(8,128)(2,1)}, bf16[16,32,128]{2,1,0:T(8,128)(2,1)}, u32[]{:S(2)}, u32[]{:S(2)}) %collective-permute-start.21) | collective-permute-done | bytes 131104 | tf_op jit(solution)/shard_map/ppermute | solution.py:559
  222.0 13.7 %finish.1 = bf16[1024,768]{1,0:T(8,128)(2,1)} custom-call(s32[2]{0:T(128)} %pad_add_fusion.place_ref, bf16[1024,768]{1,0:T(8,128)(2,1)} %feat_ref.5, bf16[2,16,32,128]{3,2,1,0:T(8,128)(2,1)} %get-tuple-element.56.refs_0_, bf16[2,16,32,128]{3,2,1,0:T(8,128)(2,1)} %collective-permute-done.11.refs_1_, bf16[2,16,32,128]{3,2,1,0:T(8,128)(2,1)} %collective-permute-done.12.refs_2_, ...), custom_call_target="tpu_custom_call" | custom-call | tf_op jit(solution)/shard_map/finish/pallas_call | solution.py:532
  (19 shorter events, 0.0 us)
Async XLA Ops:
  4.1 21.4 %all-to-all-start.1 = ((bf16[8,16,32,128]{3,2,1,0:T(8,128)(2,1)}), bf16[8,16,32,128]{3,2,1,0:T(8,128)(2,1)}, u32[]{:S(2)}, u32[]{:S(2)}) async-start(bf16[8,16,32,128]{3,2,1,0:T(8,128)(2,1)} %first_keys_values.1), calls=%async_computation.1 | async-start | bytes 2097152 | tf_op jit(solution)/shard_map/all_to_all | solution.py:578
  28.5 7.4 %copy-start = (bf16[1024,768]{1,0:T(8,128)(2,1)S(1)}, bf16[1024,768]{1,0:T(8,128)(2,1)}, u32[]{:S(2)}) copy-start(bf16[1024,768]{1,0:T(8,128)(2,1)} %feat_ref.5) | copy-start | bytes 4718596
  28.5 35.2 %all-to-all-start.2 = ((bf16[16,16,32,128]{3,2,1,0:T(8,128)(2,1)}), bf16[16,16,32,128]{3,2,1,0:T(8,128)(2,1)}, u32[]{:S(2)}, u32[]{:S(2)}) async-start(bf16[16,16,32,128]{3,2,1,0:T(8,128)(2,1)} %bitcast.12), calls=%async_computation.2 | async-start | bytes 4194304 | tf_op jit(solution)/shard_map/all_to_all | solution.py:588
  35.9 3.6 %collective-permute-start.3 = (bf16[1024,768]{1,0:T(8,128)(2,1)S(1)}, bf16[1024,768]{1,0:T(8,128)(2,1)}, u32[]{:S(2)}, u32[]{:S(2)}) collective-permute-start(bf16[1024,768]{1,0:T(8,128)(2,1)S(1)} %copy-done), channel_id=1, source_target_pairs={{0,1},{1,0},{2,3},{3,2},{4,5},{5,4},{6,7},{7,6},{8,9},{9,8},{10,11... | collective-permute-start | bytes 4718600 | tf_op jit(solution)/shard_map/ppermute | solution.py:553
  44.5 15.6 %collective-permute-start.14 = (bf16[32,32,128]{2,1,0:T(8,128)(2,1)}, bf16[32,32,128]{2,1,0:T(8,128)(2,1)}, u32[]{:S(2)}, u32[]{:S(2)}) collective-permute-start(bf16[32,32,128]{2,1,0:T(8,128)(2,1)} %get-tuple-element.61), channel_id=1, source_target_pairs={{0,2},{1,3},{2,4},{3,5},{4,6},{5,7},{6,0},{7,1},{8,10},{9,11},{10,... | collective-permute-start | bytes 786440 | tf_op jit(solution)/shard_map/ppermute | solution.py:559
  45.1 14.9 %collective-permute-start.15 = (bf16[32,32,128]{2,1,0:T(8,128)(2,1)}, bf16[32,32,128]{2,1,0:T(8,128)(2,1)}, u32[]{:S(2)}, u32[]{:S(2)}) collective-permute-start(bf16[32,32,128]{2,1,0:T(8,128)(2,1)} %get-tuple-element.62), channel_id=1, source_target_pairs={{0,4},{1,5},{2,6},{3,7},{4,0},{5,1},{6,2},{7,3},{8,12},{9,13},{10,... | collective-permute-start | bytes 786440 | tf_op jit(solution)/shard_map/ppermute | solution.py:559
  47.2 13.5 %collective-permute-start.16 = (bf16[32,32,128]{2,1,0:T(8,128)(2,1)}, bf16[32,32,128]{2,1,0:T(8,128)(2,1)}, u32[]{:S(2)}, u32[]{:S(2)}) collective-permute-start(bf16[32,32,128]{2,1,0:T(8,128)(2,1)} %get-tuple-element.63), channel_id=1, source_target_pairs={{0,6},{1,7},{2,0},{3,1},{4,2},{5,3},{6,4},{7,5},{8,14},{9,15},{10,... | collective-permute-start | bytes 786440 | tf_op jit(solution)/shard_map/ppermute | solution.py:559
  63.8 33.0 %all-to-all-start.3 = ((bf16[16,16,32,128]{3,2,1,0:T(8,128)(2,1)}), bf16[16,16,32,128]{3,2,1,0:T(8,128)(2,1)}, u32[]{:S(2)}, u32[]{:S(2)}) async-start(bf16[16,16,32,128]{3,2,1,0:T(8,128)(2,1)} %bitcast.11), calls=%async_computation.3 | async-start | bytes 4194304 | tf_op jit(solution)/shard_map/all_to_all | solution.py:588
  76.0 9.1 %collective-permute-start.4 = (bf16[32,32,128]{2,1,0:T(8,128)(2,1)}, bf16[32,32,128]{2,1,0:T(8,128)(2,1)}, u32[]{:S(2)}, u32[]{:S(2)}) collective-permute-start(bf16[32,32,128]{2,1,0:T(8,128)(2,1)} %get-tuple-element.43), channel_id=1, source_target_pairs={{0,2},{1,3},{2,4},{3,5},{4,6},{5,7},{6,0},{7,1},{8,10},{9,11},{10,... | collective-permute-start | bytes 786440 | tf_op jit(solution)/shard_map/ppermute | solution.py:559
  76.4 14.9 %collective-permute-start.5 = (bf16[32,32,128]{2,1,0:T(8,128)(2,1)}, bf16[32,32,128]{2,1,0:T(8,128)(2,1)}, u32[]{:S(2)}, u32[]{:S(2)}) collective-permute-start(bf16[32,32,128]{2,1,0:T(8,128)(2,1)} %get-tuple-element.44), channel_id=1, source_target_pairs={{0,4},{1,5},{2,6},{3,7},{4,0},{5,1},{6,2},{7,3},{8,12},{9,13},{10,... | collective-permute-start | bytes 786440 | tf_op jit(solution)/shard_map/ppermute | solution.py:559
  79.9 11.4 %collective-permute-start.6 = (bf16[32,32,128]{2,1,0:T(8,128)(2,1)}, bf16[32,32,128]{2,1,0:T(8,128)(2,1)}, u32[]{:S(2)}, u32[]{:S(2)}) collective-permute-start(bf16[32,32,128]{2,1,0:T(8,128)(2,1)} %get-tuple-element.45), channel_id=1, source_target_pairs={{0,6},{1,7},{2,0},{3,1},{4,2},{5,3},{6,4},{7,5},{8,14},{9,15},{10,... | collective-permute-start | bytes 786440 | tf_op jit(solution)/shard_map/ppermute | solution.py:559
  96.7 32.4 %all-to-all-start = ((bf16[16,16,32,128]{3,2,1,0:T(8,128)(2,1)}), bf16[16,16,32,128]{3,2,1,0:T(8,128)(2,1)}, u32[]{:S(2)}, u32[]{:S(2)}) async-start(bf16[16,16,32,128]{3,2,1,0:T(8,128)(2,1)} %bitcast.13), calls=%async_computation | async-start | bytes 4194304 | tf_op jit(solution)/shard_map/all_to_all | solution.py:588
  104.4 55.4 %collective-permute-start.10 = (bf16[256,32,128]{2,1,0:T(8,128)(2,1)}, bf16[256,32,128]{2,1,0:T(8,128)(2,1)}, u32[]{:S(2)}, u32[]{:S(2)}) collective-permute-start(bf16[256,32,128]{2,1,0:T(8,128)(2,1)} %bitcast.8.refs_6_), channel_id=1, source_target_pairs={{0,1},{1,0},{2,3},{3,2},{4,5},{5,4},{6,7},{7,6},{8,9},{9,8},{10,11... | collective-permute-start | bytes 6291464 | tf_op jit(solution)/shard_map/ppermute | solution.py:553
  104.4 68.6 %collective-permute-start.18 = (bf16[256,32,128]{2,1,0:T(8,128)(2,1)}, bf16[256,32,128]{2,1,0:T(8,128)(2,1)}, u32[]{:S(2)}, u32[]{:S(2)}) collective-permute-start(bf16[256,32,128]{2,1,0:T(8,128)(2,1)} %bitcast.10.refs_6_), channel_id=1, source_target_pairs={{0,1},{1,0},{2,3},{3,2},{4,5},{5,4},{6,7},{7,6},{8,9},{9,8},{10,11... | collective-permute-start | bytes 6291464 | tf_op jit(solution)/shard_map/ppermute | solution.py:553
  129.1 57.1 %collective-permute-start.8 = (bf16[256,32,128]{2,1,0:T(8,128)(2,1)}, bf16[256,32,128]{2,1,0:T(8,128)(2,1)}, u32[]{:S(2)}, u32[]{:S(2)}) collective-permute-start(bf16[256,32,128]{2,1,0:T(8,128)(2,1)} %bitcast.5.refs_6_), channel_id=1, source_target_pairs={{0,1},{1,0},{2,3},{3,2},{4,5},{5,4},{6,7},{7,6},{8,9},{9,8},{10,11... | collective-permute-start | bytes 6291464 | tf_op jit(solution)/shard_map/ppermute | solution.py:553
  133.9 13.9 %collective-permute-start = (bf16[3,16,32,128]{3,2,1,0:T(8,128)(2,1)}, bf16[3,16,32,128]{3,2,1,0:T(8,128)(2,1)}, u32[]{:S(2)}, u32[]{:S(2)}) collective-permute-start(bf16[3,16,32,128]{3,2,1,0:T(8,128)(2,1)} %get-tuple-element.39), channel_id=1, source_target_pairs={{0,2},{1,3},{2,4},{3,5},{4,6},{5,7},{6,0},{7,1},{8,10},{9,11},{10,... | collective-permute-start | bytes 1179656 | tf_op jit(solution)/shard_map/ppermute | solution.py:559
  136.1 21.3 %collective-permute-start.1 = (bf16[3,16,32,128]{3,2,1,0:T(8,128)(2,1)}, bf16[3,16,32,128]{3,2,1,0:T(8,128)(2,1)}, u32[]{:S(2)}, u32[]{:S(2)}) collective-permute-start(bf16[3,16,32,128]{3,2,1,0:T(8,128)(2,1)} %get-tuple-element.40), channel_id=1, source_target_pairs={{0,4},{1,5},{2,6},{3,7},{4,0},{5,1},{6,2},{7,3},{8,12},{9,13},{10,... | collective-permute-start | bytes 1179656 | tf_op jit(solution)/shard_map/ppermute | solution.py:559
  147.8 11.3 %collective-permute-start.2 = (bf16[3,16,32,128]{3,2,1,0:T(8,128)(2,1)}, bf16[3,16,32,128]{3,2,1,0:T(8,128)(2,1)}, u32[]{:S(2)}, u32[]{:S(2)}) collective-permute-start(bf16[3,16,32,128]{3,2,1,0:T(8,128)(2,1)} %get-tuple-element.41), channel_id=1, source_target_pairs={{0,6},{1,7},{2,0},{3,1},{4,2},{5,3},{6,4},{7,5},{8,14},{9,15},{10,... | collective-permute-start | bytes 1179656 | tf_op jit(solution)/shard_map/ppermute | solution.py:559
  157.4 2.3 collective-permute-start.9
  159.0 13.9 %collective-permute-start.17 = (bf16[4,16,32,128]{3,2,1,0:T(8,128)(2,1)}, bf16[4,16,32,128]{3,2,1,0:T(8,128)(2,1)}, u32[]{:S(2)}, u32[]{:S(2)}) collective-permute-start(bf16[4,16,32,128]{3,2,1,0:T(8,128)(2,1)} %get-tuple-element.65), channel_id=1, source_target_pairs={{0,1},{1,0},{2,3},{3,2},{4,5},{5,4},{6,7},{7,6},{8,9},{9,8},{10,11... | collective-permute-start | bytes 1572872 | tf_op jit(solution)/shard_map/ppermute | solution.py:553
  159.6 26.6 %collective-permute-start.7 = (bf16[4,16,32,128]{3,2,1,0:T(8,128)(2,1)}, bf16[4,16,32,128]{3,2,1,0:T(8,128)(2,1)}, u32[]{:S(2)}, u32[]{:S(2)}) collective-permute-start(bf16[4,16,32,128]{3,2,1,0:T(8,128)(2,1)} %get-tuple-element.47), channel_id=1, source_target_pairs={{0,1},{1,0},{2,3},{3,2},{4,5},{5,4},{6,7},{7,6},{8,9},{9,8},{10,11... | collective-permute-start | bytes 1572872 | tf_op jit(solution)/shard_map/ppermute | solution.py:553
  186.1 20.1 %collective-permute-start.19 = (bf16[16,32,128]{2,1,0:T(8,128)(2,1)}, bf16[16,32,128]{2,1,0:T(8,128)(2,1)}, u32[]{:S(2)}, u32[]{:S(2)}) collective-permute-start(bf16[16,32,128]{2,1,0:T(8,128)(2,1)} %get-tuple-element.68), channel_id=1, source_target_pairs={{0,2},{1,3},{2,4},{3,5},{4,6},{5,7},{6,0},{7,1},{8,10},{9,11},{10,... | collective-permute-start | bytes 393224 | tf_op jit(solution)/shard_map/ppermute | solution.py:559
  199.6 22.4 %collective-permute-start.11 = (bf16[2,16,32,128]{3,2,1,0:T(8,128)(2,1)}, bf16[2,16,32,128]{3,2,1,0:T(8,128)(2,1)}, u32[]{:S(2)}, u32[]{:S(2)}) collective-permute-start(bf16[2,16,32,128]{3,2,1,0:T(8,128)(2,1)} %get-tuple-element.57), channel_id=1, source_target_pairs={{0,2},{1,3},{2,4},{3,5},{4,6},{5,7},{6,0},{7,1},{8,10},{9,11},{10,... | collective-permute-start | bytes 786440 | tf_op jit(solution)/shard_map/ppermute | solution.py:559
  200.6 21.5 %collective-permute-start.12 = (bf16[2,16,32,128]{3,2,1,0:T(8,128)(2,1)}, bf16[2,16,32,128]{3,2,1,0:T(8,128)(2,1)}, u32[]{:S(2)}, u32[]{:S(2)}) collective-permute-start(bf16[2,16,32,128]{3,2,1,0:T(8,128)(2,1)} %get-tuple-element.58), channel_id=1, source_target_pairs={{0,4},{1,5},{2,6},{3,7},{4,0},{5,1},{6,2},{7,3},{8,12},{9,13},{10,... | collective-permute-start | bytes 786440 | tf_op jit(solution)/shard_map/ppermute | solution.py:559
  204.3 17.7 %collective-permute-start.13 = (bf16[2,16,32,128]{3,2,1,0:T(8,128)(2,1)}, bf16[2,16,32,128]{3,2,1,0:T(8,128)(2,1)}, u32[]{:S(2)}, u32[]{:S(2)}) collective-permute-start(bf16[2,16,32,128]{3,2,1,0:T(8,128)(2,1)} %get-tuple-element.59), channel_id=1, source_target_pairs={{0,6},{1,7},{2,0},{3,1},{4,2},{5,3},{6,4},{7,5},{8,14},{9,15},{10,... | collective-permute-start | bytes 786440 | tf_op jit(solution)/shard_map/ppermute | solution.py:559
  206.2 13.4 %collective-permute-start.20 = (bf16[16,32,128]{2,1,0:T(8,128)(2,1)}, bf16[16,32,128]{2,1,0:T(8,128)(2,1)}, u32[]{:S(2)}, u32[]{:S(2)}) collective-permute-start(bf16[16,32,128]{2,1,0:T(8,128)(2,1)} %get-tuple-element.69), channel_id=1, source_target_pairs={{0,4},{1,5},{2,6},{3,7},{4,0},{5,1},{6,2},{7,3},{8,12},{9,13},{10,... | collective-permute-start | bytes 393224 | tf_op jit(solution)/shard_map/ppermute | solution.py:559
  206.2 15.8 %collective-permute-start.21 = (bf16[16,32,128]{2,1,0:T(8,128)(2,1)}, bf16[16,32,128]{2,1,0:T(8,128)(2,1)}, u32[]{:S(2)}, u32[]{:S(2)}) collective-permute-start(bf16[16,32,128]{2,1,0:T(8,128)(2,1)} %get-tuple-element.70), channel_id=1, source_target_pairs={{0,6},{1,7},{2,0},{3,1},{4,2},{5,3},{6,4},{7,5},{8,14},{9,15},{10,... | collective-permute-start | bytes 393224 | tf_op jit(solution)/shard_map/ppermute | solution.py:559

commit v8 on v7

--- a/solution.py
+++ b/solution.py
@@ -476,23 +476,71 @@
     )(gain_attn, gain_ffn)
 
 
-def finish_kernel(place_ref, feat_ref, *refs):
-    parts, refs = refs[: 2 * CHIPS], refs[2 * CHIPS :]
+def mix_kernel(place_ref, feat_ref, *refs):
+    parts, (weight_ref, out_ref, *scratch) = refs[:CHIPS], refs[CHIPS:]
+    held, feats, weight, made, arrive, sems = scratch
+    rows = feat_ref.shape[0] // 2
+    arriving = []
+    for which in range(CHUNKS - 1):
+        some = [part.at[which] for part in parts]
+        arriving += gather_parts(place_ref, some, held.at[which], arrive.at[which])
+    fetches = [
+        pltpu.make_async_copy(weight_ref.at[: (CHUNKS - 1) * COLS], weight, sems.at[0]),
+        pltpu.make_async_copy(feat_ref, feats, sems.at[1]),
+    ]
+    for copy in fetches:
+        copy.start()
+    for copy in arriving + fetches:
+        copy.wait()
+    copies = []
+    for half in range(2):
+        at = slice(half * rows, (half + 1) * rows)
+        mixed = feats[at, :].astype(F32)
+        for which in range(CHUNKS - 1):
+            part = weight[which * COLS : (which + 1) * COLS, :]
+            mixed = mixed + mixed_rows(held.at[which], half, part)
+        made[at, :] = mixed
+        copies.append(pltpu.make_async_copy(made.at[at], out_ref.at[at], sems.at[2 + half]))
+        copies[-1].start()
+    for copy in copies:
+        copy.wait()
+
+
+def mix(place, features, back, w_out):
+    rows, width = features.shape
+    early = (CHUNKS - 1) * COLS
+    return pl.pallas_call(
+        mix_kernel,
+        in_specs=[SMEM] + [HBM] * (CHIPS + 2),
+        out_specs=HBM,
+        out_shape=jax.ShapeDtypeStruct((rows, width), F32),
+        scratch_shapes=[
+            pltpu.VMEM((CHUNKS - 1, CHIPS, OWN) + TILE, BF16),
+            pltpu.VMEM((rows, width), BF16),
+            pltpu.VMEM((early, width), BF16),
+            pltpu.VMEM((rows, width), F32),
+            pltpu.SemaphoreType.DMA((CHUNKS - 1, CHIPS)),
+            pltpu.SemaphoreType.DMA((4,)),
+        ],
+        compiler_params=params(0),
+        cost_estimate=pl.CostEstimate(
+            flops=2 * rows * early * width, bytes_accessed=7 << 20, transcendentals=0
+        ),
+        name="mix",
+    )(place, features, *back, w_out)
+
+
+def finish_kernel(place_ref, mixed_ref, *refs):
+    parts, refs = refs[:CHIPS], refs[CHIPS:]
     out_w_ref, up_ref, down_ref, gain_ref, result_ref, *scratch = refs
-    held, feats, out_w, up, down, made, arrive, sems = scratch
-    rows = feat_ref.shape[0] // 2
+    held, early, out_w, up, down, made, arrive, sems = scratch
+    rows = mixed_ref.shape[0] // 2
     halves = [slice(half * rows, (half + 1) * rows) for half in range(2)]
-    arriving = []
-    for which in range(CHUNKS):
-        if which < CHUNKS - 1:
-            some = [part.at[which] for part in parts[:CHIPS]]
-        else:
-            some = parts[CHIPS:]
-        arriving += gather_parts(place_ref, some, held.at[which], arrive.at[which])
+    arriving = gather_parts(place_ref, parts, held, arrive)
     copies = [
-        pltpu.make_async_copy(out_w_ref, out_w, sems.at[0]),
-        pltpu.make_async_copy(feat_ref.at[halves[0]], feats.at[halves[0]], sems.at[1]),
-        pltpu.make_async_copy(feat_ref.at[halves[1]], feats.at[halves[1]], sems.at[2]),
+        pltpu.make_async_copy(out_w_ref.at[(CHUNKS - 1) * COLS :], out_w, sems.at[0]),
+        pltpu.make_async_copy(mixed_ref.at[halves[0]], early.at[halves[0]], sems.at[1]),
+        pltpu.make_async_copy(mixed_ref.at[halves[1]], early.at[halves[1]], sems.at[2]),
         pltpu.make_async_copy(up_ref, up, sems.at[3]),
         pltpu.make_async_copy(down_ref, down, sems.at[4]),
     ]
@@ -503,13 +551,9 @@
     copies[0].wait()
     firsts = []
     for half, at in enumerate(halves):
-        added = mixed_rows(held.at[0], half, out_w[:COLS, :])
-        for which in range(1, CHUNKS):
-            weight = out_w[which * COLS : (which + 1) * COLS, :]
-            added = added + mixed_rows(held.at[which], half, weight)
+        added = mixed_rows(held, half, out_w[...])
         copies[1 + half].wait()
-        mixed = feats[at, :].astype(F32) + added
-        firsts.append(normed(mixed, gain_ref[0:1, :]).astype(BF16))
+        firsts.append(normed(early[at, :] + added, gain_ref[0:1, :]).astype(BF16))
     rows = rows // 2
     firsts = [first[at : at + rows] for first in firsts for at in (0, rows)]
     for half, first in enumerate(firsts):
@@ -527,26 +571,26 @@
         copy.wait()
 
 
-def finish(place, features, backs, w_out, w_up, w_down, gains):
-    rows, width = features.shape
+def finish(place, mixed, back, w_out, w_up, w_down, gains):
+    rows, width = mixed.shape
     return pl.pallas_call(
         finish_kernel,
-        in_specs=[SMEM] + [HBM] * (2 * CHIPS + 4) + [VMEM],
+        in_specs=[SMEM] + [HBM] * (CHIPS + 4) + [VMEM],
         out_specs=HBM,
         out_shape=jax.ShapeDtypeStruct((rows, width), BF16),
         scratch_shapes=[
-            pltpu.VMEM((CHUNKS, CHIPS, OWN) + TILE, BF16),
-            pltpu.VMEM((rows, width), BF16),
-            pltpu.VMEM(w_out.shape, BF16),
+            pltpu.VMEM((CHIPS, OWN) + TILE, BF16),
+            pltpu.VMEM((rows, width), F32),
+            pltpu.VMEM((COLS, width), BF16),
             pltpu.VMEM(w_up.shape, BF16),
             pltpu.VMEM(w_down.shape, BF16),
             pltpu.VMEM((rows, width), BF16),
-            pltpu.SemaphoreType.DMA((CHUNKS, CHIPS)),
+            pltpu.SemaphoreType.DMA((CHIPS,)),
             pltpu.SemaphoreType.DMA((9,)),
         ],
         compiler_params=params(0),
         name="finish",
-    )(place, features, *[part for back in backs for part in back], w_out, w_up, w_down, gains)
+    )(place, mixed, *back, w_out, w_up, w_down, gains)
 
 
 def swap(array):
@@ -597,7 +641,8 @@
         if c > 0:
             backs.append(along_z(done))
     gains = stack_gains(gain_attn, gain_ffn)
-    return finish(place, features, backs, w_out, w_up, w_down, gains)
+    mixed = mix(place, features, backs[0], w_out)
+    return finish(place, mixed, backs[1], w_out, w_up, w_down, gains)
 
 
 def solution(mesh):

time: 240 us -> 231 us (0.963)
  waiting for transfers between devices: 99.6 us -> 87.8 us
  Pallas kernels: 82.6 us -> 86.8 us
    ppermute x15, waiting for transfers between devices: 53.6 us -> 41.9 us  [along_z(): lax.ppermute(parts[step], 'head', [(i, (i + 2 * step) % (2 * CHIPS)) for...]
    pallas_call x1 -> x2, Pallas kernels: 13.7 us -> 17.7 us  [the longest x1 12.5 us: finish(): pl.pallas_call(finish_kernel, in_specs=[SMEM] + [HBM] * (CHIPS + 4) + [VM...]
  transfers between devices with their start and end apart: 26 -> 26, of which waited for: 14 -> 12; matrix products, arithmetic and copies ran while one was open for 0% -> 0% of each run, Pallas kernels for 26% -> 29%
where the time goes in v8:
time: 231 us; the launch traced here: 228 us
  waiting for transfers between devices  87.8 us (38%)
  Pallas kernels  86.8 us (38%)
  starting transfers between devices  52.1 us (23%)
    ppermute x15, waiting for transfers between devices, along_z(): lax.ppermute(parts[step], 'head', [(i, (i + 2 * step) % (2 * CHIPS)) for...  41.9 us
    pallas_call x3, Pallas kernels, attend(): pl.pallas_call(functools.partial(attend_kernel, chunk, len(before)), in_s...  39.7 us
    all_to_all x3, waiting for transfers between devices, per_device(): got = lax.all_to_all(sent, 'node', split_axis=0, concat_axis=0, tiled=True)  26.4 us
    ppermute x15, starting transfers between devices, along_z(): lax.ppermute(parts[step], 'head', [(i, (i + 2 * step) % (2 * CHIPS)) for...  23.8 us
    all_to_all x3, starting transfers between devices, per_device(): got = lax.all_to_all(sent, 'node', split_axis=0, concat_axis=0, tiled=True)  22.2 us
    all_to_all x1, waiting for transfers between devices, per_device(): lax.all_to_all(whole, 'head', split_axis=0, concat_axis=0, tiled=True)  15.4 us
    pallas_call x1, Pallas kernels, finish(): pl.pallas_call(finish_kernel, in_specs=[SMEM] + [HBM] * (CHIPS + 4) + [VM...  12.5 us
    pallas_call x2, Pallas kernels, project_keys_values(): pl.pallas_call(functools.partial(keys_values_kernel, chunk), in_specs=[SM...  9.92 us
  transfers between devices with their start and end apart: 26, of which 12 were waited for; matrix products, arithmetic and copies ran while one was open for 0% of the time, Pallas kernels for 29%

profile of v8, /device:TPU:20, one launch (start us, length us, event | category | flops | bytes accessed | tf_op | source)
XLA Modules:
  0.0 227.6 jit_solution(11093407528921358178)
XLA Ops:
  0.0 4.1 %first_keys_values.1 = bf16[8,16,32,128]{3,2,1,0:T(8,128)(2,1)} custom-call(bf16[1024,768]{1,0:T(8,128)(2,1)} %near_ref.3, bf16[768,768]{1,0:T(8,128)(2,1)} %key_ref.5, bf16[768,768]{1,0:T(8,128)(2,1)} %value_ref.5), custom_call_target="tpu_custom_call" | custom-call | flops 805306368 | bytes 4194304 | tf_op jit(solution)/shard_map/first_keys_values/pallas_call | solution.py:122
  4.1 5.3 %all-to-all-start.1 = ((bf16[8,16,32,128]{3,2,1,0:T(8,128)(2,1)}), bf16[8,16,32,128]{3,2,1,0:T(8,128)(2,1)}, u32[]{:S(2)}, u32[]{:S(2)}) async-start(bf16[8,16,32,128]{3,2,1,0:T(8,128)(2,1)} %first_keys_values.1), calls=%async_computation.1 | async-start | bytes 2097152 | tf_op jit(solution)/shard_map/all_to_all | solution.py:622
  9.4 0.6 pad_add_fusion.place_ref
  10.0 15.4 %all-to-all-done.1 = bf16[8,16,32,128]{3,2,1,0:T(8,128)(2,1)} async-done(((bf16[8,16,32,128]{3,2,1,0:T(8,128)(2,1)}), bf16[8,16,32,128]{3,2,1,0:T(8,128)(2,1)}, u32[]{:S(2)}, u32[]{:S(2)}) %all-to-all-start.1) | async-done | bytes 1048608 | tf_op jit(solution)/shard_map/all_to_all | solution.py:622
  25.4 3.1 %collect.4 = (bf16[256,32,128]{2,1,0:T(8,128)(2,1)}, bf16[4,16,32,128]{3,2,1,0:T(8,128)(2,1)}, bf16[4,16,32,128]{3,2,1,0:T(8,128)(2,1)}) custom-call(s32[1,16,16]{2,1,0:T(8,128)} %list_ref.5, s32[2]{0:T(128)} %pad_add_fusion.place_ref, bf16[128,32,128]{2,1,0:T(8,128)(2,1)} %bitcast.6.refs_0_), custom_call_target="tpu_custom_call" | custom-call | bytes 5242880 | tf_op jit(solution)/shard_map/collect/pallas_call | solution.py:246
  28.5 0.0 copy-start
  28.5 7.4 %all-to-all-start.2 = ((bf16[16,16,32,128]{3,2,1,0:T(8,128)(2,1)}), bf16[16,16,32,128]{3,2,1,0:T(8,128)(2,1)}, u32[]{:S(2)}, u32[]{:S(2)}) async-start(bf16[16,16,32,128]{3,2,1,0:T(8,128)(2,1)} %bitcast.12), calls=%async_computation.2 | async-start | bytes 4194304 | tf_op jit(solution)/shard_map/all_to_all | solution.py:632
  35.9 0.1 collective-permute-start.3
  36.0 3.5 %collective-permute-done.3.far_ref = bf16[1024,768]{1,0:T(8,128)(2,1)} collective-permute-done((bf16[1024,768]{1,0:T(8,128)(2,1)S(1)}, bf16[1024,768]{1,0:T(8,128)(2,1)}, u32[]{:S(2)}, u32[]{:S(2)}) %collective-permute-start.3) | collective-permute-done | bytes 1572896 | tf_op jit(solution)/shard_map/ppermute | solution.py:597
  39.5 4.9 %keys_values.2 = (bf16[32,32,128]{2,1,0:T(8,128)(2,1)}, bf16[32,32,128]{2,1,0:T(8,128)(2,1)}, bf16[32,32,128]{2,1,0:T(8,128)(2,1)}, bf16[32,32,128]{2,1,0:T(8,128)(2,1)}) custom-call(s32[2]{0:T(128)} %pad_add_fusion.place_ref, bf16[1024,768]{1,0:T(8,128)(2,1)} %near_ref.3, bf16[1024,768]{1,0:T(8,128)(2,1)} %collective-permute-done.3.far_ref, ...), custom_call_target="tpu_custom_call" | custom-call | flops 805306368 | bytes 5242880 | tf_op jit(solution)/shard_map/keys_values/pallas_call | solution.py:154
  44.5 0.6 collective-permute-start.4
  45.1 2.1 collective-permute-start.5
  47.2 0.7 collective-permute-start.6
  47.9 12.2 %collective-permute-done.4.refs_1_ = bf16[32,32,128]{2,1,0:T(8,128)(2,1)} collective-permute-done((bf16[32,32,128]{2,1,0:T(8,128)(2,1)}, bf16[32,32,128]{2,1,0:T(8,128)(2,1)}, u32[]{:S(2)}, u32[]{:S(2)}) %collective-permute-start.4) | collective-permute-done | bytes 262176 | tf_op jit(solution)/shard_map/ppermute | solution.py:603
  60.0 0.0 collective-permute-done.5.refs_2_
  60.0 0.6 collective-permute-done.6.refs_3_
  60.6 3.1 %collect.3 = (bf16[256,32,128]{2,1,0:T(8,128)(2,1)}, bf16[4,16,32,128]{3,2,1,0:T(8,128)(2,1)}, bf16[4,16,32,128]{3,2,1,0:T(8,128)(2,1)}) custom-call(s32[1,16,16]{2,1,0:T(8,128)} %list_ref.5, s32[2]{0:T(128)} %pad_add_fusion.place_ref, bf16[32,32,128]{2,1,0:T(8,128)(2,1)} %get-tuple-element.42.refs_0_, bf16[32,32,128]{2,1,0:T(8,128)(2,1)} %collective-permute-done.4.refs_1_, ...), custom_call_target="tpu_custom_call" | custom-call | bytes 5242880 | tf_op jit(solution)/shard_map/collect/pallas_call | solution.py:246
  63.8 7.2 %all-to-all-start = ((bf16[16,16,32,128]{3,2,1,0:T(8,128)(2,1)}), bf16[16,16,32,128]{3,2,1,0:T(8,128)(2,1)}, u32[]{:S(2)}, u32[]{:S(2)}) async-start(bf16[16,16,32,128]{3,2,1,0:T(8,128)(2,1)} %bitcast.11), calls=%async_computation | async-start | bytes 4194304 | tf_op jit(solution)/shard_map/all_to_all | solution.py:632
  71.0 5.0 %keys_values.3 = (bf16[32,32,128]{2,1,0:T(8,128)(2,1)}, bf16[32,32,128]{2,1,0:T(8,128)(2,1)}, bf16[32,32,128]{2,1,0:T(8,128)(2,1)}, bf16[32,32,128]{2,1,0:T(8,128)(2,1)}) custom-call(s32[2]{0:T(128)} %pad_add_fusion.place_ref, bf16[1024,768]{1,0:T(8,128)(2,1)} %near_ref.3, bf16[1024,768]{1,0:T(8,128)(2,1)} %collective-permute-done.3.far_ref, ...), custom_call_target="tpu_custom_call" | custom-call | flops 805306368 | bytes 5242880 | tf_op jit(solution)/shard_map/keys_values/pallas_call | solution.py:154
  76.0 0.4 collective-permute-start.14
  76.4 3.6 %collective-permute-start.15 = (bf16[32,32,128]{2,1,0:T(8,128)(2,1)}, bf16[32,32,128]{2,1,0:T(8,128)(2,1)}, u32[]{:S(2)}, u32[]{:S(2)}) collective-permute-start(bf16[32,32,128]{2,1,0:T(8,128)(2,1)} %get-tuple-element.62), channel_id=1, source_target_pairs={{0,4},{1,5},{2,6},{3,7},{4,0},{5,1},{6,2},{7,3},{8,12},{9,13},{10,... | collective-permute-start | bytes 786440 | tf_op jit(solution)/shard_map/ppermute | solution.py:603
  80.0 5.1 %collective-permute-done.14.refs_1_ = bf16[32,32,128]{2,1,0:T(8,128)(2,1)} collective-permute-done((bf16[32,32,128]{2,1,0:T(8,128)(2,1)}, bf16[32,32,128]{2,1,0:T(8,128)(2,1)}, u32[]{:S(2)}, u32[]{:S(2)}) %collective-permute-start.14) | collective-permute-done | bytes 262176 | tf_op jit(solution)/shard_map/ppermute | solution.py:603
  85.1 6.3 %collective-permute-done.15.refs_2_ = bf16[32,32,128]{2,1,0:T(8,128)(2,1)} collective-permute-done((bf16[32,32,128]{2,1,0:T(8,128)(2,1)}, bf16[32,32,128]{2,1,0:T(8,128)(2,1)}, u32[]{:S(2)}, u32[]{:S(2)}) %collective-permute-start.15) | collective-permute-done | bytes 262176 | tf_op jit(solution)/shard_map/ppermute | solution.py:603
  91.3 3.2 %collect.5 = (bf16[256,32,128]{2,1,0:T(8,128)(2,1)}, bf16[4,16,32,128]{3,2,1,0:T(8,128)(2,1)}, bf16[4,16,32,128]{3,2,1,0:T(8,128)(2,1)}) custom-call(s32[1,16,16]{2,1,0:T(8,128)} %list_ref.5, s32[2]{0:T(128)} %pad_add_fusion.place_ref, bf16[32,32,128]{2,1,0:T(8,128)(2,1)} %get-tuple-element.60.refs_0_, bf16[32,32,128]{2,1,0:T(8,128)(2,1)} %collective-permute-done.14.refs_1_, ...), custom_call_target="tpu_custom_call" | custom-call | bytes 5242880 | tf_op jit(solution)/shard_map/collect/pallas_call | solution.py:246
  94.6 2.2 all-to-all-done
  96.7 7.6 %all-to-all-start.3 = ((bf16[16,16,32,128]{3,2,1,0:T(8,128)(2,1)}), bf16[16,16,32,128]{3,2,1,0:T(8,128)(2,1)}, u32[]{:S(2)}, u32[]{:S(2)}) async-start(bf16[16,16,32,128]{3,2,1,0:T(8,128)(2,1)} %bitcast.13), calls=%async_computation.3 | async-start | bytes 4194304 | tf_op jit(solution)/shard_map/all_to_all | solution.py:632
  104.4 0.5 collective-permute-start.8
  104.9 24.2 %all-to-all-done.3 = bf16[16,16,32,128]{3,2,1,0:T(8,128)(2,1)} async-done(((bf16[16,16,32,128]{3,2,1,0:T(8,128)(2,1)}), bf16[16,16,32,128]{3,2,1,0:T(8,128)(2,1)}, u32[]{:S(2)}, u32[]{:S(2)}) %all-to-all-start.3) | async-done | bytes 2097184 | tf_op jit(solution)/shard_map/all_to_all | solution.py:632
  129.1 4.7 %queries.1 = (bf16[3,16,32,128]{3,2,1,0:T(8,128)(2,1)}, bf16[3,16,32,128]{3,2,1,0:T(8,128)(2,1)}, bf16[3,16,32,128]{3,2,1,0:T(8,128)(2,1)}, bf16[3,16,32,128]{3,2,1,0:T(8,128)(2,1)}) custom-call(s32[2]{0:T(128)} %pad_add_fusion.place_ref, bf16[1024,768]{1,0:T(8,128)(2,1)} %near_ref.3, bf16[768,768]{1,0:T(8,128)(2,1)} %query_ref.1), custom_call_target="tpu_custom_call" | custom-call | flops 1207959552 | bytes 5242880 | tf_op jit(solution)/shard_map/queries/pallas_call | solution.py:192
  133.9 2.2 collective-permute-start
  136.1 3.1 %collective-permute-start.1 = (bf16[3,16,32,128]{3,2,1,0:T(8,128)(2,1)}, bf16[3,16,32,128]{3,2,1,0:T(8,128)(2,1)}, u32[]{:S(2)}, u32[]{:S(2)}) collective-permute-start(bf16[3,16,32,128]{3,2,1,0:T(8,128)(2,1)} %get-tuple-element.40), channel_id=1, source_target_pairs={{0,4},{1,5},{2,6},{3,7},{4,0},{5,1},{6,2},{7,3},{8,12},{9,13},{10,... | collective-permute-start | bytes 1179656 | tf_op jit(solution)/shard_map/ppermute | solution.py:603
  139.1 8.6 %collective-permute-done.refs_1_ = bf16[3,16,32,128]{3,2,1,0:T(8,128)(2,1)} collective-permute-done((bf16[3,16,32,128]{3,2,1,0:T(8,128)(2,1)}, bf16[3,16,32,128]{3,2,1,0:T(8,128)(2,1)}, u32[]{:S(2)}, u32[]{:S(2)}) %collective-permute-start) | collective-permute-done | bytes 393248 | tf_op jit(solution)/shard_map/ppermute | solution.py:603
  147.8 2.2 collective-permute-start.2
  150.0 7.4 %collective-permute-done.1.refs_2_ = bf16[3,16,32,128]{3,2,1,0:T(8,128)(2,1)} collective-permute-done((bf16[3,16,32,128]{3,2,1,0:T(8,128)(2,1)}, bf16[3,16,32,128]{3,2,1,0:T(8,128)(2,1)}, u32[]{:S(2)}, u32[]{:S(2)}) %collective-permute-start.1) | collective-permute-done | bytes 393248 | tf_op jit(solution)/shard_map/ppermute | solution.py:603
  157.4 1.7 collective-permute-done.2.refs_3_
  159.0 0.6 collective-permute-done.9.refs_5_
  159.6 0.1 collective-permute-start.17
  159.8 13.2 %attend.3 = (bf16[16,32,128]{2,1,0:T(8,128)(2,1)}, bf16[16,32,128]{2,1,0:T(8,128)(2,1)}, bf16[16,32,128]{2,1,0:T(8,128)(2,1)}, bf16[16,32,128]{2,1,0:T(8,128)(2,1)}) custom-call(s32[8,128]{1,0:T(8,128)} %bitcast.14, s32[8,128]{1,0:T(8,128)} %bitcast.17, s32[128]{0:T(128)} %count_ref.5, s32[2]{0:T(128)} %pad_add_fusion.place_ref, ...), custom_call_target="tpu_custom_call" | custom-call | flops 1610612736 | bytes 8388608 | tf_op jit(solution)/shard_map/attend/pallas_call | solution.py:416
  173.0 13.4 %attend.4 = (bf16[2,16,32,128]{3,2,1,0:T(8,128)(2,1)}, bf16[2,16,32,128]{3,2,1,0:T(8,128)(2,1)}, bf16[2,16,32,128]{3,2,1,0:T(8,128)(2,1)}, bf16[2,16,32,128]{3,2,1,0:T(8,128)(2,1)}) custom-call(s32[8,128]{1,0:T(8,128)} %bitcast.15, s32[8,128]{1,0:T(8,128)} %bitcast.18, s32[128]{0:T(128)} %count_ref.5, s32[2]{0:T(128)} %pad_add_fusion.place_ref, ...), custom_call_target="tpu_custom_call" | custom-call | flops 1610612736 | bytes 8388608 | tf_op jit(solution)/shard_map/attend/pallas_call | solution.py:416
  186.4 0.1 collective-permute-start.11
  186.5 3.9 %collective-permute-start.12 = (bf16[2,16,32,128]{3,2,1,0:T(8,128)(2,1)}, bf16[2,16,32,128]{3,2,1,0:T(8,128)(2,1)}, u32[]{:S(2)}, u32[]{:S(2)}) collective-permute-start(bf16[2,16,32,128]{3,2,1,0:T(8,128)(2,1)} %get-tuple-element.58), channel_id=1, source_target_pairs={{0,4},{1,5},{2,6},{3,7},{4,0},{5,1},{6,2},{7,3},{8,12},{9,13},{10,... | collective-permute-start | bytes 786440 | tf_op jit(solution)/shard_map/ppermute | solution.py:603
  190.4 13.1 %attend.5 = (bf16[16,32,128]{2,1,0:T(8,128)(2,1)}, bf16[16,32,128]{2,1,0:T(8,128)(2,1)}, bf16[16,32,128]{2,1,0:T(8,128)(2,1)}, bf16[16,32,128]{2,1,0:T(8,128)(2,1)}) custom-call(s32[8,128]{1,0:T(8,128)} %bitcast.16, s32[8,128]{1,0:T(8,128)} %bitcast.19, s32[128]{0:T(128)} %count_ref.5, s32[2]{0:T(128)} %pad_add_fusion.place_ref, ...), custom_call_target="tpu_custom_call" | custom-call | flops 1610612736 | bytes 8388608 | tf_op jit(solution)/shard_map/attend/pallas_call | solution.py:416
  203.5 2.1 collective-permute-start.19
  205.6 0.3 collective-permute-start.20
  205.9 2.5 %collective-permute-start.21 = (bf16[16,32,128]{2,1,0:T(8,128)(2,1)}, bf16[16,32,128]{2,1,0:T(8,128)(2,1)}, u32[]{:S(2)}, u32[]{:S(2)}) collective-permute-start(bf16[16,32,128]{2,1,0:T(8,128)(2,1)} %get-tuple-element.70), channel_id=1, source_target_pairs={{0,6},{1,7},{2,0},{3,1},{4,2},{5,3},{6,4},{7,5},{8,14},{9,15},{10,... | collective-permute-start | bytes 393224 | tf_op jit(solution)/shard_map/ppermute | solution.py:603
  208.5 1.3 gains.1.refs_7_
  209.8 5.1 %mix.1.mixed_ref = f32[1024,768]{1,0:T(8,128)} custom-call(s32[2]{0:T(128)} %pad_add_fusion.place_ref, bf16[1024,768]{1,0:T(8,128)(2,1)} %near_ref.3, bf16[2,16,32,128]{3,2,1,0:T(8,128)(2,1)} %get-tuple-element.56.refs_0_, bf16[2,16,32,128]{3,2,1,0:T(8,128)(2,1)} %collective-permute-done.11.refs_1_, ...), custom_call_target="tpu_custom_call" | custom-call | flops 805306368 | bytes 7340032 | tf_op jit(solution)/shard_map/mix/pallas_call | solution.py:512
  214.9 12.5 %finish.1 = bf16[1024,768]{1,0:T(8,128)(2,1)} custom-call(s32[2]{0:T(128)} %pad_add_fusion.place_ref, f32[1024,768]{1,0:T(8,128)} %mix.1.mixed_ref, bf16[16,32,128]{2,1,0:T(8,128)(2,1)} %get-tuple-element.67.refs_0_, bf16[16,32,128]{2,1,0:T(8,128)(2,1)} %collective-permute-done.19.refs_1_, bf16[16,32,128]{2,1,0:T(8,128)(2,1)} %collective-permute-done.20.refs_2_, ...), custom_call_target="tpu_custom_call" | custom-call | tf_op jit(solution)/shard_map/finish/pallas_call | solution.py:576
  (20 shorter events, 0.1 us)
Async XLA Ops:
  4.1 21.4 %all-to-all-start.1 = ((bf16[8,16,32,128]{3,2,1,0:T(8,128)(2,1)}), bf16[8,16,32,128]{3,2,1,0:T(8,128)(2,1)}, u32[]{:S(2)}, u32[]{:S(2)}) async-start(bf16[8,16,32,128]{3,2,1,0:T(8,128)(2,1)} %first_keys_values.1), calls=%async_computation.1 | async-start | bytes 2097152 | tf_op jit(solution)/shard_map/all_to_all | solution.py:622
  28.5 7.4 %copy-start = (bf16[1024,768]{1,0:T(8,128)(2,1)S(1)}, bf16[1024,768]{1,0:T(8,128)(2,1)}, u32[]{:S(2)}) copy-start(bf16[1024,768]{1,0:T(8,128)(2,1)} %near_ref.3) | copy-start | bytes 4718596
  28.5 35.2 %all-to-all-start.2 = ((bf16[16,16,32,128]{3,2,1,0:T(8,128)(2,1)}), bf16[16,16,32,128]{3,2,1,0:T(8,128)(2,1)}, u32[]{:S(2)}, u32[]{:S(2)}) async-start(bf16[16,16,32,128]{3,2,1,0:T(8,128)(2,1)} %bitcast.12), calls=%async_computation.2 | async-start | bytes 4194304 | tf_op jit(solution)/shard_map/all_to_all | solution.py:632
  35.9 3.6 %collective-permute-start.3 = (bf16[1024,768]{1,0:T(8,128)(2,1)S(1)}, bf16[1024,768]{1,0:T(8,128)(2,1)}, u32[]{:S(2)}, u32[]{:S(2)}) collective-permute-start(bf16[1024,768]{1,0:T(8,128)(2,1)S(1)} %copy-done), channel_id=1, source_target_pairs={{0,1},{1,0},{2,3},{3,2},{4,5},{5,4},{6,7},{7,6},{8,9},{9,8},{10,11... | collective-permute-start | bytes 4718600 | tf_op jit(solution)/shard_map/ppermute | solution.py:597
  44.5 15.6 %collective-permute-start.4 = (bf16[32,32,128]{2,1,0:T(8,128)(2,1)}, bf16[32,32,128]{2,1,0:T(8,128)(2,1)}, u32[]{:S(2)}, u32[]{:S(2)}) collective-permute-start(bf16[32,32,128]{2,1,0:T(8,128)(2,1)} %get-tuple-element.43), channel_id=1, source_target_pairs={{0,2},{1,3},{2,4},{3,5},{4,6},{5,7},{6,0},{7,1},{8,10},{9,11},{10,... | collective-permute-start | bytes 786440 | tf_op jit(solution)/shard_map/ppermute | solution.py:603
  45.1 14.9 %collective-permute-start.5 = (bf16[32,32,128]{2,1,0:T(8,128)(2,1)}, bf16[32,32,128]{2,1,0:T(8,128)(2,1)}, u32[]{:S(2)}, u32[]{:S(2)}) collective-permute-start(bf16[32,32,128]{2,1,0:T(8,128)(2,1)} %get-tuple-element.44), channel_id=1, source_target_pairs={{0,4},{1,5},{2,6},{3,7},{4,0},{5,1},{6,2},{7,3},{8,12},{9,13},{10,... | collective-permute-start | bytes 786440 | tf_op jit(solution)/shard_map/ppermute | solution.py:603
  47.2 13.5 %collective-permute-start.6 = (bf16[32,32,128]{2,1,0:T(8,128)(2,1)}, bf16[32,32,128]{2,1,0:T(8,128)(2,1)}, u32[]{:S(2)}, u32[]{:S(2)}) collective-permute-start(bf16[32,32,128]{2,1,0:T(8,128)(2,1)} %get-tuple-element.45), channel_id=1, source_target_pairs={{0,6},{1,7},{2,0},{3,1},{4,2},{5,3},{6,4},{7,5},{8,14},{9,15},{10,... | collective-permute-start | bytes 786440 | tf_op jit(solution)/shard_map/ppermute | solution.py:603
  63.8 33.0 %all-to-all-start = ((bf16[16,16,32,128]{3,2,1,0:T(8,128)(2,1)}), bf16[16,16,32,128]{3,2,1,0:T(8,128)(2,1)}, u32[]{:S(2)}, u32[]{:S(2)}) async-start(bf16[16,16,32,128]{3,2,1,0:T(8,128)(2,1)} %bitcast.11), calls=%async_computation | async-start | bytes 4194304 | tf_op jit(solution)/shard_map/all_to_all | solution.py:632
  76.0 9.1 %collective-permute-start.14 = (bf16[32,32,128]{2,1,0:T(8,128)(2,1)}, bf16[32,32,128]{2,1,0:T(8,128)(2,1)}, u32[]{:S(2)}, u32[]{:S(2)}) collective-permute-start(bf16[32,32,128]{2,1,0:T(8,128)(2,1)} %get-tuple-element.61), channel_id=1, source_target_pairs={{0,2},{1,3},{2,4},{3,5},{4,6},{5,7},{6,0},{7,1},{8,10},{9,11},{10,... | collective-permute-start | bytes 786440 | tf_op jit(solution)/shard_map/ppermute | solution.py:603
  76.4 14.9 %collective-permute-start.15 = (bf16[32,32,128]{2,1,0:T(8,128)(2,1)}, bf16[32,32,128]{2,1,0:T(8,128)(2,1)}, u32[]{:S(2)}, u32[]{:S(2)}) collective-permute-start(bf16[32,32,128]{2,1,0:T(8,128)(2,1)} %get-tuple-element.62), channel_id=1, source_target_pairs={{0,4},{1,5},{2,6},{3,7},{4,0},{5,1},{6,2},{7,3},{8,12},{9,13},{10,... | collective-permute-start | bytes 786440 | tf_op jit(solution)/shard_map/ppermute | solution.py:603
  80.0 11.4 %collective-permute-start.16 = (bf16[32,32,128]{2,1,0:T(8,128)(2,1)}, bf16[32,32,128]{2,1,0:T(8,128)(2,1)}, u32[]{:S(2)}, u32[]{:S(2)}) collective-permute-start(bf16[32,32,128]{2,1,0:T(8,128)(2,1)} %get-tuple-element.63), channel_id=1, source_target_pairs={{0,6},{1,7},{2,0},{3,1},{4,2},{5,3},{6,4},{7,5},{8,14},{9,15},{10,... | collective-permute-start | bytes 786440 | tf_op jit(solution)/shard_map/ppermute | solution.py:603
  96.7 32.4 %all-to-all-start.3 = ((bf16[16,16,32,128]{3,2,1,0:T(8,128)(2,1)}), bf16[16,16,32,128]{3,2,1,0:T(8,128)(2,1)}, u32[]{:S(2)}, u32[]{:S(2)}) async-start(bf16[16,16,32,128]{3,2,1,0:T(8,128)(2,1)} %bitcast.13), calls=%async_computation.3 | async-start | bytes 4194304 | tf_op jit(solution)/shard_map/all_to_all | solution.py:632
  104.4 55.4 %collective-permute-start.10 = (bf16[256,32,128]{2,1,0:T(8,128)(2,1)}, bf16[256,32,128]{2,1,0:T(8,128)(2,1)}, u32[]{:S(2)}, u32[]{:S(2)}) collective-permute-start(bf16[256,32,128]{2,1,0:T(8,128)(2,1)} %bitcast.8.refs_6_), channel_id=1, source_target_pairs={{0,1},{1,0},{2,3},{3,2},{4,5},{5,4},{6,7},{7,6},{8,9},{9,8},{10,11... | collective-permute-start | bytes 6291464 | tf_op jit(solution)/shard_map/ppermute | solution.py:597
  104.4 68.6 %collective-permute-start.8 = (bf16[256,32,128]{2,1,0:T(8,128)(2,1)}, bf16[256,32,128]{2,1,0:T(8,128)(2,1)}, u32[]{:S(2)}, u32[]{:S(2)}) collective-permute-start(bf16[256,32,128]{2,1,0:T(8,128)(2,1)} %bitcast.5.refs_6_), channel_id=1, source_target_pairs={{0,1},{1,0},{2,3},{3,2},{4,5},{5,4},{6,7},{7,6},{8,9},{9,8},{10,11... | collective-permute-start | bytes 6291464 | tf_op jit(solution)/shard_map/ppermute | solution.py:597
  129.1 61.3 %collective-permute-start.18 = (bf16[256,32,128]{2,1,0:T(8,128)(2,1)}, bf16[256,32,128]{2,1,0:T(8,128)(2,1)}, u32[]{:S(2)}, u32[]{:S(2)}) collective-permute-start(bf16[256,32,128]{2,1,0:T(8,128)(2,1)} %bitcast.10.refs_6_), channel_id=1, source_target_pairs={{0,1},{1,0},{2,3},{3,2},{4,5},{5,4},{6,7},{7,6},{8,9},{9,8},{10,11... | collective-permute-start | bytes 6291464 | tf_op jit(solution)/shard_map/ppermute | solution.py:597
  133.9 13.9 %collective-permute-start = (bf16[3,16,32,128]{3,2,1,0:T(8,128)(2,1)}, bf16[3,16,32,128]{3,2,1,0:T(8,128)(2,1)}, u32[]{:S(2)}, u32[]{:S(2)}) collective-permute-start(bf16[3,16,32,128]{3,2,1,0:T(8,128)(2,1)} %get-tuple-element.39), channel_id=1, source_target_pairs={{0,2},{1,3},{2,4},{3,5},{4,6},{5,7},{6,0},{7,1},{8,10},{9,11},{10,... | collective-permute-start | bytes 1179656 | tf_op jit(solution)/shard_map/ppermute | solution.py:603
  136.1 21.3 %collective-permute-start.1 = (bf16[3,16,32,128]{3,2,1,0:T(8,128)(2,1)}, bf16[3,16,32,128]{3,2,1,0:T(8,128)(2,1)}, u32[]{:S(2)}, u32[]{:S(2)}) collective-permute-start(bf16[3,16,32,128]{3,2,1,0:T(8,128)(2,1)} %get-tuple-element.40), channel_id=1, source_target_pairs={{0,4},{1,5},{2,6},{3,7},{4,0},{5,1},{6,2},{7,3},{8,12},{9,13},{10,... | collective-permute-start | bytes 1179656 | tf_op jit(solution)/shard_map/ppermute | solution.py:603
  147.8 11.3 %collective-permute-start.2 = (bf16[3,16,32,128]{3,2,1,0:T(8,128)(2,1)}, bf16[3,16,32,128]{3,2,1,0:T(8,128)(2,1)}, u32[]{:S(2)}, u32[]{:S(2)}) collective-permute-start(bf16[3,16,32,128]{3,2,1,0:T(8,128)(2,1)} %get-tuple-element.41), channel_id=1, source_target_pairs={{0,6},{1,7},{2,0},{3,1},{4,2},{5,3},{6,4},{7,5},{8,14},{9,15},{10,... | collective-permute-start | bytes 1179656 | tf_op jit(solution)/shard_map/ppermute | solution.py:603
  157.4 2.3 collective-permute-start.9
  159.0 13.9 %collective-permute-start.7 = (bf16[4,16,32,128]{3,2,1,0:T(8,128)(2,1)}, bf16[4,16,32,128]{3,2,1,0:T(8,128)(2,1)}, u32[]{:S(2)}, u32[]{:S(2)}) collective-permute-start(bf16[4,16,32,128]{3,2,1,0:T(8,128)(2,1)} %get-tuple-element.47), channel_id=1, source_target_pairs={{0,1},{1,0},{2,3},{3,2},{4,5},{5,4},{6,7},{7,6},{8,9},{9,8},{10,11... | collective-permute-start | bytes 1572872 | tf_op jit(solution)/shard_map/ppermute | solution.py:597
  159.6 30.8 %collective-permute-start.17 = (bf16[4,16,32,128]{3,2,1,0:T(8,128)(2,1)}, bf16[4,16,32,128]{3,2,1,0:T(8,128)(2,1)}, u32[]{:S(2)}, u32[]{:S(2)}) collective-permute-start(bf16[4,16,32,128]{3,2,1,0:T(8,128)(2,1)} %get-tuple-element.65), channel_id=1, source_target_pairs={{0,1},{1,0},{2,3},{3,2},{4,5},{5,4},{6,7},{7,6},{8,9},{9,8},{10,11... | collective-permute-start | bytes 1572872 | tf_op jit(solution)/shard_map/ppermute | solution.py:597
  186.4 19.5 %collective-permute-start.11 = (bf16[2,16,32,128]{3,2,1,0:T(8,128)(2,1)}, bf16[2,16,32,128]{3,2,1,0:T(8,128)(2,1)}, u32[]{:S(2)}, u32[]{:S(2)}) collective-permute-start(bf16[2,16,32,128]{3,2,1,0:T(8,128)(2,1)} %get-tuple-element.57), channel_id=1, source_target_pairs={{0,2},{1,3},{2,4},{3,5},{4,6},{5,7},{6,0},{7,1},{8,10},{9,11},{10,... | collective-permute-start | bytes 786440 | tf_op jit(solution)/shard_map/ppermute | solution.py:603
  186.5 23.3 %collective-permute-start.12 = (bf16[2,16,32,128]{3,2,1,0:T(8,128)(2,1)}, bf16[2,16,32,128]{3,2,1,0:T(8,128)(2,1)}, u32[]{:S(2)}, u32[]{:S(2)}) collective-permute-start(bf16[2,16,32,128]{3,2,1,0:T(8,128)(2,1)} %get-tuple-element.58), channel_id=1, source_target_pairs={{0,4},{1,5},{2,6},{3,7},{4,0},{5,1},{6,2},{7,3},{8,12},{9,13},{10,... | collective-permute-start | bytes 786440 | tf_op jit(solution)/shard_map/ppermute | solution.py:603
  190.4 19.4 %collective-permute-start.13 = (bf16[2,16,32,128]{3,2,1,0:T(8,128)(2,1)}, bf16[2,16,32,128]{3,2,1,0:T(8,128)(2,1)}, u32[]{:S(2)}, u32[]{:S(2)}) collective-permute-start(bf16[2,16,32,128]{3,2,1,0:T(8,128)(2,1)} %get-tuple-element.59), channel_id=1, source_target_pairs={{0,6},{1,7},{2,0},{3,1},{4,2},{5,3},{6,4},{7,5},{8,14},{9,15},{10,... | collective-permute-start | bytes 786440 | tf_op jit(solution)/shard_map/ppermute | solution.py:603
  203.5 11.4 %collective-permute-start.19 = (bf16[16,32,128]{2,1,0:T(8,128)(2,1)}, bf16[16,32,128]{2,1,0:T(8,128)(2,1)}, u32[]{:S(2)}, u32[]{:S(2)}) collective-permute-start(bf16[16,32,128]{2,1,0:T(8,128)(2,1)} %get-tuple-element.68), channel_id=1, source_target_pairs={{0,2},{1,3},{2,4},{3,5},{4,6},{5,7},{6,0},{7,1},{8,10},{9,11},{10,... | collective-permute-start | bytes 393224 | tf_op jit(solution)/shard_map/ppermute | solution.py:603
  205.6 9.3 %collective-permute-start.20 = (bf16[16,32,128]{2,1,0:T(8,128)(2,1)}, bf16[16,32,128]{2,1,0:T(8,128)(2,1)}, u32[]{:S(2)}, u32[]{:S(2)}) collective-permute-start(bf16[16,32,128]{2,1,0:T(8,128)(2,1)} %get-tuple-element.69), channel_id=1, source_target_pairs={{0,4},{1,5},{2,6},{3,7},{4,0},{5,1},{6,2},{7,3},{8,12},{9,13},{10,... | collective-permute-start | bytes 393224 | tf_op jit(solution)/shard_map/ppermute | solution.py:603
  205.9 9.0 %collective-permute-start.21 = (bf16[16,32,128]{2,1,0:T(8,128)(2,1)}, bf16[16,32,128]{2,1,0:T(8,128)(2,1)}, u32[]{:S(2)}, u32[]{:S(2)}) collective-permute-start(bf16[16,32,128]{2,1,0:T(8,128)(2,1)} %get-tuple-element.70), channel_id=1, source_target_pairs={{0,6},{1,7},{2,0},{3,1},{4,2},{5,3},{6,4},{7,5},{8,14},{9,15},{10,... | collective-permute-start | bytes 393224 | tf_op jit(solution)/shard_map/ppermute | solution.py:603

commit v9 on v8

--- a/solution.py
+++ b/solution.py
@@ -308,11 +308,11 @@
     lane = lax.broadcasted_iota(jnp.int32, (1, LANES), 1)
     dims = (((1,), (1,)), ((), ()))
     rows = 2 * BLOCK
-    group = 8
+    group = OWN
 
     def attend_group(at, carry):
-        ahead = lax.rem(at // 2 + 1, CHIPS)
-        source, first = lax.rem(z + ahead, CHIPS), (at % 2) * group
+        ahead = lax.rem(at + 1, CHIPS)
+        source, first = lax.rem(z + ahead, CHIPS), 0
         blocks = [source * 2 * OWN + core * OWN + first + k for k in range(group)]
         slots = [
             [owner_ref[entry, block] * CAP + slot_ref[entry, block] for entry in range(MAXK)]
@@ -388,7 +388,7 @@
             made[source, first + k] = result.astype(BF16)
         for step in range(CHIPS):
 
-            @pl.when(jnp.logical_and(at % 2 == 1, ahead == step))
+            @pl.when(ahead == step)
             def _():
                 pltpu.make_async_copy(made.at[source], targets[step], done.at[step]).start()
 

time: 231 us -> 227 us (0.983)
  Pallas kernels: 86.8 us -> 82.1 us
    pallas_call x3, Pallas kernels: 39.7 us -> 35 us  [attend(): pl.pallas_call(functools.partial(attend_kernel, chunk, len(before)), in_s...]
  transfers between devices with their start and end apart: 26 -> 26, of which waited for: 12 -> 12; matrix products, arithmetic and copies ran while one was open for 0% -> 0% of each run, Pallas kernels for 29% -> 28%
where the time goes in v9:
time: 227 us; the launch traced here: 223 us
  waiting for transfers between devices  87.8 us (39%)
  Pallas kernels  82.1 us (36%)
  starting transfers between devices  52.1 us (23%)
    ppermute x15, waiting for transfers between devices, along_z(): lax.ppermute(parts[step], 'head', [(i, (i + 2 * step) % (2 * CHIPS)) for...  41.9 us
    pallas_call x3, Pallas kernels, attend(): pl.pallas_call(functools.partial(attend_kernel, chunk, len(before)), in_s...  35 us
    all_to_all x3, waiting for transfers between devices, per_device(): got = lax.all_to_all(sent, 'node', split_axis=0, concat_axis=0, tiled=True)  26.4 us
    ppermute x15, starting transfers between devices, along_z(): lax.ppermute(parts[step], 'head', [(i, (i + 2 * step) % (2 * CHIPS)) for...  23.8 us
    all_to_all x3, starting transfers between devices, per_device(): got = lax.all_to_all(sent, 'node', split_axis=0, concat_axis=0, tiled=True)  22.2 us
    all_to_all x1, waiting for transfers between devices, per_device(): lax.all_to_all(whole, 'head', split_axis=0, concat_axis=0, tiled=True)  15.4 us
    pallas_call x1, Pallas kernels, finish(): pl.pallas_call(finish_kernel, in_specs=[SMEM] + [HBM] * (CHIPS + 4) + [VM...  12.5 us
    pallas_call x2, Pallas kernels, project_keys_values(): pl.pallas_call(functools.partial(keys_values_kernel, chunk), in_specs=[SM...  9.92 us
  transfers between devices with their start and end apart: 26, of which 12 were waited for; matrix products, arithmetic and copies ran while one was open for 0% of the time, Pallas kernels for 28%

profile of v9, /device:TPU:20, one launch (start us, length us, event | category | flops | bytes accessed | tf_op | source)
XLA Modules:
  0.0 223.0 jit_solution(14631801676959722004)
XLA Ops:
  0.0 4.1 %first_keys_values.1 = bf16[8,16,32,128]{3,2,1,0:T(8,128)(2,1)} custom-call(bf16[1024,768]{1,0:T(8,128)(2,1)} %near_ref.3, bf16[768,768]{1,0:T(8,128)(2,1)} %key_ref.5, bf16[768,768]{1,0:T(8,128)(2,1)} %value_ref.5), custom_call_target="tpu_custom_call" | custom-call | flops 805306368 | bytes 4194304 | tf_op jit(solution)/shard_map/first_keys_values/pallas_call | solution.py:122
  4.1 5.3 %all-to-all-start.1 = ((bf16[8,16,32,128]{3,2,1,0:T(8,128)(2,1)}), bf16[8,16,32,128]{3,2,1,0:T(8,128)(2,1)}, u32[]{:S(2)}, u32[]{:S(2)}) async-start(bf16[8,16,32,128]{3,2,1,0:T(8,128)(2,1)} %first_keys_values.1), calls=%async_computation.1 | async-start | bytes 2097152 | tf_op jit(solution)/shard_map/all_to_all | solution.py:622
  9.4 0.6 pad_add_fusion.place_ref
  10.0 15.4 %all-to-all-done.1 = bf16[8,16,32,128]{3,2,1,0:T(8,128)(2,1)} async-done(((bf16[8,16,32,128]{3,2,1,0:T(8,128)(2,1)}), bf16[8,16,32,128]{3,2,1,0:T(8,128)(2,1)}, u32[]{:S(2)}, u32[]{:S(2)}) %all-to-all-start.1) | async-done | bytes 1048608 | tf_op jit(solution)/shard_map/all_to_all | solution.py:622
  25.4 3.1 %collect.4 = (bf16[256,32,128]{2,1,0:T(8,128)(2,1)}, bf16[4,16,32,128]{3,2,1,0:T(8,128)(2,1)}, bf16[4,16,32,128]{3,2,1,0:T(8,128)(2,1)}) custom-call(s32[1,16,16]{2,1,0:T(8,128)} %list_ref.5, s32[2]{0:T(128)} %pad_add_fusion.place_ref, bf16[128,32,128]{2,1,0:T(8,128)(2,1)} %bitcast.6.refs_0_), custom_call_target="tpu_custom_call" | custom-call | bytes 5242880 | tf_op jit(solution)/shard_map/collect/pallas_call | solution.py:246
  28.5 0.0 copy-start
  28.5 7.4 %all-to-all-start.2 = ((bf16[16,16,32,128]{3,2,1,0:T(8,128)(2,1)}), bf16[16,16,32,128]{3,2,1,0:T(8,128)(2,1)}, u32[]{:S(2)}, u32[]{:S(2)}) async-start(bf16[16,16,32,128]{3,2,1,0:T(8,128)(2,1)} %bitcast.12), calls=%async_computation.2 | async-start | bytes 4194304 | tf_op jit(solution)/shard_map/all_to_all | solution.py:632
  35.9 0.1 collective-permute-start.3
  36.0 3.5 %collective-permute-done.3.far_ref = bf16[1024,768]{1,0:T(8,128)(2,1)} collective-permute-done((bf16[1024,768]{1,0:T(8,128)(2,1)S(1)}, bf16[1024,768]{1,0:T(8,128)(2,1)}, u32[]{:S(2)}, u32[]{:S(2)}) %collective-permute-start.3) | collective-permute-done | bytes 1572896 | tf_op jit(solution)/shard_map/ppermute | solution.py:597
  39.5 4.9 %keys_values.2 = (bf16[32,32,128]{2,1,0:T(8,128)(2,1)}, bf16[32,32,128]{2,1,0:T(8,128)(2,1)}, bf16[32,32,128]{2,1,0:T(8,128)(2,1)}, bf16[32,32,128]{2,1,0:T(8,128)(2,1)}) custom-call(s32[2]{0:T(128)} %pad_add_fusion.place_ref, bf16[1024,768]{1,0:T(8,128)(2,1)} %near_ref.3, bf16[1024,768]{1,0:T(8,128)(2,1)} %collective-permute-done.3.far_ref, ...), custom_call_target="tpu_custom_call" | custom-call | flops 805306368 | bytes 5242880 | tf_op jit(solution)/shard_map/keys_values/pallas_call | solution.py:154
  44.5 0.6 collective-permute-start.4
  45.1 2.1 collective-permute-start.5
  47.2 0.7 collective-permute-start.6
  47.9 12.2 %collective-permute-done.4.refs_1_ = bf16[32,32,128]{2,1,0:T(8,128)(2,1)} collective-permute-done((bf16[32,32,128]{2,1,0:T(8,128)(2,1)}, bf16[32,32,128]{2,1,0:T(8,128)(2,1)}, u32[]{:S(2)}, u32[]{:S(2)}) %collective-permute-start.4) | collective-permute-done | bytes 262176 | tf_op jit(solution)/shard_map/ppermute | solution.py:603
  60.0 0.0 collective-permute-done.5.refs_2_
  60.0 0.6 collective-permute-done.6.refs_3_
  60.6 3.1 %collect.3 = (bf16[256,32,128]{2,1,0:T(8,128)(2,1)}, bf16[4,16,32,128]{3,2,1,0:T(8,128)(2,1)}, bf16[4,16,32,128]{3,2,1,0:T(8,128)(2,1)}) custom-call(s32[1,16,16]{2,1,0:T(8,128)} %list_ref.5, s32[2]{0:T(128)} %pad_add_fusion.place_ref, bf16[32,32,128]{2,1,0:T(8,128)(2,1)} %get-tuple-element.42.refs_0_, bf16[32,32,128]{2,1,0:T(8,128)(2,1)} %collective-permute-done.4.refs_1_, ...), custom_call_target="tpu_custom_call" | custom-call | bytes 5242880 | tf_op jit(solution)/shard_map/collect/pallas_call | solution.py:246
  63.8 7.2 %all-to-all-start = ((bf16[16,16,32,128]{3,2,1,0:T(8,128)(2,1)}), bf16[16,16,32,128]{3,2,1,0:T(8,128)(2,1)}, u32[]{:S(2)}, u32[]{:S(2)}) async-start(bf16[16,16,32,128]{3,2,1,0:T(8,128)(2,1)} %bitcast.11), calls=%async_computation | async-start | bytes 4194304 | tf_op jit(solution)/shard_map/all_to_all | solution.py:632
  71.0 5.0 %keys_values.3 = (bf16[32,32,128]{2,1,0:T(8,128)(2,1)}, bf16[32,32,128]{2,1,0:T(8,128)(2,1)}, bf16[32,32,128]{2,1,0:T(8,128)(2,1)}, bf16[32,32,128]{2,1,0:T(8,128)(2,1)}) custom-call(s32[2]{0:T(128)} %pad_add_fusion.place_ref, bf16[1024,768]{1,0:T(8,128)(2,1)} %near_ref.3, bf16[1024,768]{1,0:T(8,128)(2,1)} %collective-permute-done.3.far_ref, ...), custom_call_target="tpu_custom_call" | custom-call | flops 805306368 | bytes 5242880 | tf_op jit(solution)/shard_map/keys_values/pallas_call | solution.py:154
  76.0 0.4 collective-permute-start.14
  76.4 3.6 %collective-permute-start.15 = (bf16[32,32,128]{2,1,0:T(8,128)(2,1)}, bf16[32,32,128]{2,1,0:T(8,128)(2,1)}, u32[]{:S(2)}, u32[]{:S(2)}) collective-permute-start(bf16[32,32,128]{2,1,0:T(8,128)(2,1)} %get-tuple-element.62), channel_id=1, source_target_pairs={{0,4},{1,5},{2,6},{3,7},{4,0},{5,1},{6,2},{7,3},{8,12},{9,13},{10,... | collective-permute-start | bytes 786440 | tf_op jit(solution)/shard_map/ppermute | solution.py:603
  80.0 5.1 %collective-permute-done.14.refs_1_ = bf16[32,32,128]{2,1,0:T(8,128)(2,1)} collective-permute-done((bf16[32,32,128]{2,1,0:T(8,128)(2,1)}, bf16[32,32,128]{2,1,0:T(8,128)(2,1)}, u32[]{:S(2)}, u32[]{:S(2)}) %collective-permute-start.14) | collective-permute-done | bytes 262176 | tf_op jit(solution)/shard_map/ppermute | solution.py:603
  85.1 6.3 %collective-permute-done.15.refs_2_ = bf16[32,32,128]{2,1,0:T(8,128)(2,1)} collective-permute-done((bf16[32,32,128]{2,1,0:T(8,128)(2,1)}, bf16[32,32,128]{2,1,0:T(8,128)(2,1)}, u32[]{:S(2)}, u32[]{:S(2)}) %collective-permute-start.15) | collective-permute-done | bytes 262176 | tf_op jit(solution)/shard_map/ppermute | solution.py:603
  91.3 3.2 %collect.5 = (bf16[256,32,128]{2,1,0:T(8,128)(2,1)}, bf16[4,16,32,128]{3,2,1,0:T(8,128)(2,1)}, bf16[4,16,32,128]{3,2,1,0:T(8,128)(2,1)}) custom-call(s32[1,16,16]{2,1,0:T(8,128)} %list_ref.5, s32[2]{0:T(128)} %pad_add_fusion.place_ref, bf16[32,32,128]{2,1,0:T(8,128)(2,1)} %get-tuple-element.60.refs_0_, bf16[32,32,128]{2,1,0:T(8,128)(2,1)} %collective-permute-done.14.refs_1_, ...), custom_call_target="tpu_custom_call" | custom-call | bytes 5242880 | tf_op jit(solution)/shard_map/collect/pallas_call | solution.py:246
  94.6 2.2 all-to-all-done
  96.7 7.6 %all-to-all-start.3 = ((bf16[16,16,32,128]{3,2,1,0:T(8,128)(2,1)}), bf16[16,16,32,128]{3,2,1,0:T(8,128)(2,1)}, u32[]{:S(2)}, u32[]{:S(2)}) async-start(bf16[16,16,32,128]{3,2,1,0:T(8,128)(2,1)} %bitcast.13), calls=%async_computation.3 | async-start | bytes 4194304 | tf_op jit(solution)/shard_map/all_to_all | solution.py:632
  104.4 0.5 collective-permute-start.8
  104.9 24.2 %all-to-all-done.3 = bf16[16,16,32,128]{3,2,1,0:T(8,128)(2,1)} async-done(((bf16[16,16,32,128]{3,2,1,0:T(8,128)(2,1)}), bf16[16,16,32,128]{3,2,1,0:T(8,128)(2,1)}, u32[]{:S(2)}, u32[]{:S(2)}) %all-to-all-start.3) | async-done | bytes 2097184 | tf_op jit(solution)/shard_map/all_to_all | solution.py:632
  129.1 4.7 %queries.1 = (bf16[3,16,32,128]{3,2,1,0:T(8,128)(2,1)}, bf16[3,16,32,128]{3,2,1,0:T(8,128)(2,1)}, bf16[3,16,32,128]{3,2,1,0:T(8,128)(2,1)}, bf16[3,16,32,128]{3,2,1,0:T(8,128)(2,1)}) custom-call(s32[2]{0:T(128)} %pad_add_fusion.place_ref, bf16[1024,768]{1,0:T(8,128)(2,1)} %near_ref.3, bf16[768,768]{1,0:T(8,128)(2,1)} %query_ref.1), custom_call_target="tpu_custom_call" | custom-call | flops 1207959552 | bytes 5242880 | tf_op jit(solution)/shard_map/queries/pallas_call | solution.py:192
  133.9 2.2 collective-permute-start
  136.1 3.1 %collective-permute-start.1 = (bf16[3,16,32,128]{3,2,1,0:T(8,128)(2,1)}, bf16[3,16,32,128]{3,2,1,0:T(8,128)(2,1)}, u32[]{:S(2)}, u32[]{:S(2)}) collective-permute-start(bf16[3,16,32,128]{3,2,1,0:T(8,128)(2,1)} %get-tuple-element.40), channel_id=1, source_target_pairs={{0,4},{1,5},{2,6},{3,7},{4,0},{5,1},{6,2},{7,3},{8,12},{9,13},{10,... | collective-permute-start | bytes 1179656 | tf_op jit(solution)/shard_map/ppermute | solution.py:603
  139.1 8.6 %collective-permute-done.refs_1_ = bf16[3,16,32,128]{3,2,1,0:T(8,128)(2,1)} collective-permute-done((bf16[3,16,32,128]{3,2,1,0:T(8,128)(2,1)}, bf16[3,16,32,128]{3,2,1,0:T(8,128)(2,1)}, u32[]{:S(2)}, u32[]{:S(2)}) %collective-permute-start) | collective-permute-done | bytes 393248 | tf_op jit(solution)/shard_map/ppermute | solution.py:603
  147.8 2.2 collective-permute-start.2
  150.0 7.4 %collective-permute-done.1.refs_2_ = bf16[3,16,32,128]{3,2,1,0:T(8,128)(2,1)} collective-permute-done((bf16[3,16,32,128]{3,2,1,0:T(8,128)(2,1)}, bf16[3,16,32,128]{3,2,1,0:T(8,128)(2,1)}, u32[]{:S(2)}, u32[]{:S(2)}) %collective-permute-start.1) | collective-permute-done | bytes 393248 | tf_op jit(solution)/shard_map/ppermute | solution.py:603
  157.4 1.7 collective-permute-done.2.refs_3_
  159.0 0.6 collective-permute-done.9.refs_5_
  159.6 0.1 collective-permute-start.17
  159.8 11.6 %attend.3 = (bf16[16,32,128]{2,1,0:T(8,128)(2,1)}, bf16[16,32,128]{2,1,0:T(8,128)(2,1)}, bf16[16,32,128]{2,1,0:T(8,128)(2,1)}, bf16[16,32,128]{2,1,0:T(8,128)(2,1)}) custom-call(s32[8,128]{1,0:T(8,128)} %bitcast.14, s32[8,128]{1,0:T(8,128)} %bitcast.17, s32[128]{0:T(128)} %count_ref.5, s32[2]{0:T(128)} %pad_add_fusion.place_ref, ...), custom_call_target="tpu_custom_call" | custom-call | flops 1610612736 | bytes 8388608 | tf_op jit(solution)/shard_map/attend/pallas_call | solution.py:416
  171.4 11.9 %attend.4 = (bf16[2,16,32,128]{3,2,1,0:T(8,128)(2,1)}, bf16[2,16,32,128]{3,2,1,0:T(8,128)(2,1)}, bf16[2,16,32,128]{3,2,1,0:T(8,128)(2,1)}, bf16[2,16,32,128]{3,2,1,0:T(8,128)(2,1)}) custom-call(s32[8,128]{1,0:T(8,128)} %bitcast.15, s32[8,128]{1,0:T(8,128)} %bitcast.18, s32[128]{0:T(128)} %count_ref.5, s32[2]{0:T(128)} %pad_add_fusion.place_ref, ...), custom_call_target="tpu_custom_call" | custom-call | flops 1610612736 | bytes 8388608 | tf_op jit(solution)/shard_map/attend/pallas_call | solution.py:416
  183.3 0.1 collective-permute-start.11
  183.4 3.9 %collective-permute-start.12 = (bf16[2,16,32,128]{3,2,1,0:T(8,128)(2,1)}, bf16[2,16,32,128]{3,2,1,0:T(8,128)(2,1)}, u32[]{:S(2)}, u32[]{:S(2)}) collective-permute-start(bf16[2,16,32,128]{3,2,1,0:T(8,128)(2,1)} %get-tuple-element.58), channel_id=1, source_target_pairs={{0,4},{1,5},{2,6},{3,7},{4,0},{5,1},{6,2},{7,3},{8,12},{9,13},{10,... | collective-permute-start | bytes 786440 | tf_op jit(solution)/shard_map/ppermute | solution.py:603
  187.3 11.5 %attend.5 = (bf16[16,32,128]{2,1,0:T(8,128)(2,1)}, bf16[16,32,128]{2,1,0:T(8,128)(2,1)}, bf16[16,32,128]{2,1,0:T(8,128)(2,1)}, bf16[16,32,128]{2,1,0:T(8,128)(2,1)}) custom-call(s32[8,128]{1,0:T(8,128)} %bitcast.16, s32[8,128]{1,0:T(8,128)} %bitcast.19, s32[128]{0:T(128)} %count_ref.5, s32[2]{0:T(128)} %pad_add_fusion.place_ref, ...), custom_call_target="tpu_custom_call" | custom-call | flops 1610612736 | bytes 8388608 | tf_op jit(solution)/shard_map/attend/pallas_call | solution.py:416
  198.8 2.1 collective-permute-start.19
  200.9 0.3 collective-permute-start.20
  201.2 2.5 %collective-permute-start.21 = (bf16[16,32,128]{2,1,0:T(8,128)(2,1)}, bf16[16,32,128]{2,1,0:T(8,128)(2,1)}, u32[]{:S(2)}, u32[]{:S(2)}) collective-permute-start(bf16[16,32,128]{2,1,0:T(8,128)(2,1)} %get-tuple-element.70), channel_id=1, source_target_pairs={{0,6},{1,7},{2,0},{3,1},{4,2},{5,3},{6,4},{7,5},{8,14},{9,15},{10,... | collective-permute-start | bytes 393224 | tf_op jit(solution)/shard_map/ppermute | solution.py:603
  203.8 1.3 gains.1.refs_7_
  205.1 5.1 %mix.1.mixed_ref = f32[1024,768]{1,0:T(8,128)} custom-call(s32[2]{0:T(128)} %pad_add_fusion.place_ref, bf16[1024,768]{1,0:T(8,128)(2,1)} %near_ref.3, bf16[2,16,32,128]{3,2,1,0:T(8,128)(2,1)} %get-tuple-element.56.refs_0_, bf16[2,16,32,128]{3,2,1,0:T(8,128)(2,1)} %collective-permute-done.11.refs_1_, ...), custom_call_target="tpu_custom_call" | custom-call | flops 805306368 | bytes 7340032 | tf_op jit(solution)/shard_map/mix/pallas_call | solution.py:512
  210.2 12.5 %finish.1 = bf16[1024,768]{1,0:T(8,128)(2,1)} custom-call(s32[2]{0:T(128)} %pad_add_fusion.place_ref, f32[1024,768]{1,0:T(8,128)} %mix.1.mixed_ref, bf16[16,32,128]{2,1,0:T(8,128)(2,1)} %get-tuple-element.67.refs_0_, bf16[16,32,128]{2,1,0:T(8,128)(2,1)} %collective-permute-done.19.refs_1_, bf16[16,32,128]{2,1,0:T(8,128)(2,1)} %collective-permute-done.20.refs_2_, ...), custom_call_target="tpu_custom_call" | custom-call | tf_op jit(solution)/shard_map/finish/pallas_call | solution.py:576
  (20 shorter events, 0.1 us)
Async XLA Ops:
  4.1 21.4 %all-to-all-start.1 = ((bf16[8,16,32,128]{3,2,1,0:T(8,128)(2,1)}), bf16[8,16,32,128]{3,2,1,0:T(8,128)(2,1)}, u32[]{:S(2)}, u32[]{:S(2)}) async-start(bf16[8,16,32,128]{3,2,1,0:T(8,128)(2,1)} %first_keys_values.1), calls=%async_computation.1 | async-start | bytes 2097152 | tf_op jit(solution)/shard_map/all_to_all | solution.py:622
  28.5 7.4 %copy-start = (bf16[1024,768]{1,0:T(8,128)(2,1)S(1)}, bf16[1024,768]{1,0:T(8,128)(2,1)}, u32[]{:S(2)}) copy-start(bf16[1024,768]{1,0:T(8,128)(2,1)} %near_ref.3) | copy-start | bytes 4718596
  28.5 35.2 %all-to-all-start.2 = ((bf16[16,16,32,128]{3,2,1,0:T(8,128)(2,1)}), bf16[16,16,32,128]{3,2,1,0:T(8,128)(2,1)}, u32[]{:S(2)}, u32[]{:S(2)}) async-start(bf16[16,16,32,128]{3,2,1,0:T(8,128)(2,1)} %bitcast.12), calls=%async_computation.2 | async-start | bytes 4194304 | tf_op jit(solution)/shard_map/all_to_all | solution.py:632
  35.9 3.6 %collective-permute-start.3 = (bf16[1024,768]{1,0:T(8,128)(2,1)S(1)}, bf16[1024,768]{1,0:T(8,128)(2,1)}, u32[]{:S(2)}, u32[]{:S(2)}) collective-permute-start(bf16[1024,768]{1,0:T(8,128)(2,1)S(1)} %copy-done), channel_id=1, source_target_pairs={{0,1},{1,0},{2,3},{3,2},{4,5},{5,4},{6,7},{7,6},{8,9},{9,8},{10,11... | collective-permute-start | bytes 4718600 | tf_op jit(solution)/shard_map/ppermute | solution.py:597
  44.5 15.6 %collective-permute-start.4 = (bf16[32,32,128]{2,1,0:T(8,128)(2,1)}, bf16[32,32,128]{2,1,0:T(8,128)(2,1)}, u32[]{:S(2)}, u32[]{:S(2)}) collective-permute-start(bf16[32,32,128]{2,1,0:T(8,128)(2,1)} %get-tuple-element.43), channel_id=1, source_target_pairs={{0,2},{1,3},{2,4},{3,5},{4,6},{5,7},{6,0},{7,1},{8,10},{9,11},{10,... | collective-permute-start | bytes 786440 | tf_op jit(solution)/shard_map/ppermute | solution.py:603
  45.1 14.9 %collective-permute-start.5 = (bf16[32,32,128]{2,1,0:T(8,128)(2,1)}, bf16[32,32,128]{2,1,0:T(8,128)(2,1)}, u32[]{:S(2)}, u32[]{:S(2)}) collective-permute-start(bf16[32,32,128]{2,1,0:T(8,128)(2,1)} %get-tuple-element.44), channel_id=1, source_target_pairs={{0,4},{1,5},{2,6},{3,7},{4,0},{5,1},{6,2},{7,3},{8,12},{9,13},{10,... | collective-permute-start | bytes 786440 | tf_op jit(solution)/shard_map/ppermute | solution.py:603
  47.2 13.5 %collective-permute-start.6 = (bf16[32,32,128]{2,1,0:T(8,128)(2,1)}, bf16[32,32,128]{2,1,0:T(8,128)(2,1)}, u32[]{:S(2)}, u32[]{:S(2)}) collective-permute-start(bf16[32,32,128]{2,1,0:T(8,128)(2,1)} %get-tuple-element.45), channel_id=1, source_target_pairs={{0,6},{1,7},{2,0},{3,1},{4,2},{5,3},{6,4},{7,5},{8,14},{9,15},{10,... | collective-permute-start | bytes 786440 | tf_op jit(solution)/shard_map/ppermute | solution.py:603
  63.8 33.0 %all-to-all-start = ((bf16[16,16,32,128]{3,2,1,0:T(8,128)(2,1)}), bf16[16,16,32,128]{3,2,1,0:T(8,128)(2,1)}, u32[]{:S(2)}, u32[]{:S(2)}) async-start(bf16[16,16,32,128]{3,2,1,0:T(8,128)(2,1)} %bitcast.11), calls=%async_computation | async-start | bytes 4194304 | tf_op jit(solution)/shard_map/all_to_all | solution.py:632
  76.0 9.1 %collective-permute-start.14 = (bf16[32,32,128]{2,1,0:T(8,128)(2,1)}, bf16[32,32,128]{2,1,0:T(8,128)(2,1)}, u32[]{:S(2)}, u32[]{:S(2)}) collective-permute-start(bf16[32,32,128]{2,1,0:T(8,128)(2,1)} %get-tuple-element.61), channel_id=1, source_target_pairs={{0,2},{1,3},{2,4},{3,5},{4,6},{5,7},{6,0},{7,1},{8,10},{9,11},{10,... | collective-permute-start | bytes 786440 | tf_op jit(solution)/shard_map/ppermute | solution.py:603
  76.4 14.9 %collective-permute-start.15 = (bf16[32,32,128]{2,1,0:T(8,128)(2,1)}, bf16[32,32,128]{2,1,0:T(8,128)(2,1)}, u32[]{:S(2)}, u32[]{:S(2)}) collective-permute-start(bf16[32,32,128]{2,1,0:T(8,128)(2,1)} %get-tuple-element.62), channel_id=1, source_target_pairs={{0,4},{1,5},{2,6},{3,7},{4,0},{5,1},{6,2},{7,3},{8,12},{9,13},{10,... | collective-permute-start | bytes 786440 | tf_op jit(solution)/shard_map/ppermute | solution.py:603
  80.0 11.4 %collective-permute-start.16 = (bf16[32,32,128]{2,1,0:T(8,128)(2,1)}, bf16[32,32,128]{2,1,0:T(8,128)(2,1)}, u32[]{:S(2)}, u32[]{:S(2)}) collective-permute-start(bf16[32,32,128]{2,1,0:T(8,128)(2,1)} %get-tuple-element.63), channel_id=1, source_target_pairs={{0,6},{1,7},{2,0},{3,1},{4,2},{5,3},{6,4},{7,5},{8,14},{9,15},{10,... | collective-permute-start | bytes 786440 | tf_op jit(solution)/shard_map/ppermute | solution.py:603
  96.7 32.4 %all-to-all-start.3 = ((bf16[16,16,32,128]{3,2,1,0:T(8,128)(2,1)}), bf16[16,16,32,128]{3,2,1,0:T(8,128)(2,1)}, u32[]{:S(2)}, u32[]{:S(2)}) async-start(bf16[16,16,32,128]{3,2,1,0:T(8,128)(2,1)} %bitcast.13), calls=%async_computation.3 | async-start | bytes 4194304 | tf_op jit(solution)/shard_map/all_to_all | solution.py:632
  104.4 55.4 %collective-permute-start.10 = (bf16[256,32,128]{2,1,0:T(8,128)(2,1)}, bf16[256,32,128]{2,1,0:T(8,128)(2,1)}, u32[]{:S(2)}, u32[]{:S(2)}) collective-permute-start(bf16[256,32,128]{2,1,0:T(8,128)(2,1)} %bitcast.8.refs_6_), channel_id=1, source_target_pairs={{0,1},{1,0},{2,3},{3,2},{4,5},{5,4},{6,7},{7,6},{8,9},{9,8},{10,11... | collective-permute-start | bytes 6291464 | tf_op jit(solution)/shard_map/ppermute | solution.py:597
  104.4 67.0 %collective-permute-start.8 = (bf16[256,32,128]{2,1,0:T(8,128)(2,1)}, bf16[256,32,128]{2,1,0:T(8,128)(2,1)}, u32[]{:S(2)}, u32[]{:S(2)}) collective-permute-start(bf16[256,32,128]{2,1,0:T(8,128)(2,1)} %bitcast.5.refs_6_), channel_id=1, source_target_pairs={{0,1},{1,0},{2,3},{3,2},{4,5},{5,4},{6,7},{7,6},{8,9},{9,8},{10,11... | collective-permute-start | bytes 6291464 | tf_op jit(solution)/shard_map/ppermute | solution.py:597
  129.1 58.2 %collective-permute-start.18 = (bf16[256,32,128]{2,1,0:T(8,128)(2,1)}, bf16[256,32,128]{2,1,0:T(8,128)(2,1)}, u32[]{:S(2)}, u32[]{:S(2)}) collective-permute-start(bf16[256,32,128]{2,1,0:T(8,128)(2,1)} %bitcast.10.refs_6_), channel_id=1, source_target_pairs={{0,1},{1,0},{2,3},{3,2},{4,5},{5,4},{6,7},{7,6},{8,9},{9,8},{10,11... | collective-permute-start | bytes 6291464 | tf_op jit(solution)/shard_map/ppermute | solution.py:597
  133.9 13.9 %collective-permute-start = (bf16[3,16,32,128]{3,2,1,0:T(8,128)(2,1)}, bf16[3,16,32,128]{3,2,1,0:T(8,128)(2,1)}, u32[]{:S(2)}, u32[]{:S(2)}) collective-permute-start(bf16[3,16,32,128]{3,2,1,0:T(8,128)(2,1)} %get-tuple-element.39), channel_id=1, source_target_pairs={{0,2},{1,3},{2,4},{3,5},{4,6},{5,7},{6,0},{7,1},{8,10},{9,11},{10,... | collective-permute-start | bytes 1179656 | tf_op jit(solution)/shard_map/ppermute | solution.py:603
  136.1 21.3 %collective-permute-start.1 = (bf16[3,16,32,128]{3,2,1,0:T(8,128)(2,1)}, bf16[3,16,32,128]{3,2,1,0:T(8,128)(2,1)}, u32[]{:S(2)}, u32[]{:S(2)}) collective-permute-start(bf16[3,16,32,128]{3,2,1,0:T(8,128)(2,1)} %get-tuple-element.40), channel_id=1, source_target_pairs={{0,4},{1,5},{2,6},{3,7},{4,0},{5,1},{6,2},{7,3},{8,12},{9,13},{10,... | collective-permute-start | bytes 1179656 | tf_op jit(solution)/shard_map/ppermute | solution.py:603
  147.8 11.3 %collective-permute-start.2 = (bf16[3,16,32,128]{3,2,1,0:T(8,128)(2,1)}, bf16[3,16,32,128]{3,2,1,0:T(8,128)(2,1)}, u32[]{:S(2)}, u32[]{:S(2)}) collective-permute-start(bf16[3,16,32,128]{3,2,1,0:T(8,128)(2,1)} %get-tuple-element.41), channel_id=1, source_target_pairs={{0,6},{1,7},{2,0},{3,1},{4,2},{5,3},{6,4},{7,5},{8,14},{9,15},{10,... | collective-permute-start | bytes 1179656 | tf_op jit(solution)/shard_map/ppermute | solution.py:603
  157.4 2.3 %collective-permute-start.9 = (bf16[4,16,32,128]{3,2,1,0:T(8,128)(2,1)}, bf16[4,16,32,128]{3,2,1,0:T(8,128)(2,1)}, u32[]{:S(2)}, u32[]{:S(2)}) collective-permute-start(bf16[4,16,32,128]{3,2,1,0:T(8,128)(2,1)} %get-tuple-element.50), channel_id=1, source_target_pairs={{0,1},{1,0},{2,3},{3,2},{4,5},{5,4},{6,7},{7,6},{8,9},{9,8},{10,11... | collective-permute-start | bytes 1572872 | tf_op jit(solution)/shard_map/ppermute | solution.py:597
  159.0 12.3 %collective-permute-start.7 = (bf16[4,16,32,128]{3,2,1,0:T(8,128)(2,1)}, bf16[4,16,32,128]{3,2,1,0:T(8,128)(2,1)}, u32[]{:S(2)}, u32[]{:S(2)}) collective-permute-start(bf16[4,16,32,128]{3,2,1,0:T(8,128)(2,1)} %get-tuple-element.47), channel_id=1, source_target_pairs={{0,1},{1,0},{2,3},{3,2},{4,5},{5,4},{6,7},{7,6},{8,9},{9,8},{10,11... | collective-permute-start | bytes 1572872 | tf_op jit(solution)/shard_map/ppermute | solution.py:597
  159.6 27.7 %collective-permute-start.17 = (bf16[4,16,32,128]{3,2,1,0:T(8,128)(2,1)}, bf16[4,16,32,128]{3,2,1,0:T(8,128)(2,1)}, u32[]{:S(2)}, u32[]{:S(2)}) collective-permute-start(bf16[4,16,32,128]{3,2,1,0:T(8,128)(2,1)} %get-tuple-element.65), channel_id=1, source_target_pairs={{0,1},{1,0},{2,3},{3,2},{4,5},{5,4},{6,7},{7,6},{8,9},{9,8},{10,11... | collective-permute-start | bytes 1572872 | tf_op jit(solution)/shard_map/ppermute | solution.py:597
  183.3 17.9 %collective-permute-start.11 = (bf16[2,16,32,128]{3,2,1,0:T(8,128)(2,1)}, bf16[2,16,32,128]{3,2,1,0:T(8,128)(2,1)}, u32[]{:S(2)}, u32[]{:S(2)}) collective-permute-start(bf16[2,16,32,128]{3,2,1,0:T(8,128)(2,1)} %get-tuple-element.57), channel_id=1, source_target_pairs={{0,2},{1,3},{2,4},{3,5},{4,6},{5,7},{6,0},{7,1},{8,10},{9,11},{10,... | collective-permute-start | bytes 786440 | tf_op jit(solution)/shard_map/ppermute | solution.py:603
  183.4 21.7 %collective-permute-start.12 = (bf16[2,16,32,128]{3,2,1,0:T(8,128)(2,1)}, bf16[2,16,32,128]{3,2,1,0:T(8,128)(2,1)}, u32[]{:S(2)}, u32[]{:S(2)}) collective-permute-start(bf16[2,16,32,128]{3,2,1,0:T(8,128)(2,1)} %get-tuple-element.58), channel_id=1, source_target_pairs={{0,4},{1,5},{2,6},{3,7},{4,0},{5,1},{6,2},{7,3},{8,12},{9,13},{10,... | collective-permute-start | bytes 786440 | tf_op jit(solution)/shard_map/ppermute | solution.py:603
  187.3 17.8 %collective-permute-start.13 = (bf16[2,16,32,128]{3,2,1,0:T(8,128)(2,1)}, bf16[2,16,32,128]{3,2,1,0:T(8,128)(2,1)}, u32[]{:S(2)}, u32[]{:S(2)}) collective-permute-start(bf16[2,16,32,128]{3,2,1,0:T(8,128)(2,1)} %get-tuple-element.59), channel_id=1, source_target_pairs={{0,6},{1,7},{2,0},{3,1},{4,2},{5,3},{6,4},{7,5},{8,14},{9,15},{10,... | collective-permute-start | bytes 786440 | tf_op jit(solution)/shard_map/ppermute | solution.py:603
  198.8 11.4 %collective-permute-start.19 = (bf16[16,32,128]{2,1,0:T(8,128)(2,1)}, bf16[16,32,128]{2,1,0:T(8,128)(2,1)}, u32[]{:S(2)}, u32[]{:S(2)}) collective-permute-start(bf16[16,32,128]{2,1,0:T(8,128)(2,1)} %get-tuple-element.68), channel_id=1, source_target_pairs={{0,2},{1,3},{2,4},{3,5},{4,6},{5,7},{6,0},{7,1},{8,10},{9,11},{10,... | collective-permute-start | bytes 393224 | tf_op jit(solution)/shard_map/ppermute | solution.py:603
  200.9 9.3 %collective-permute-start.20 = (bf16[16,32,128]{2,1,0:T(8,128)(2,1)}, bf16[16,32,128]{2,1,0:T(8,128)(2,1)}, u32[]{:S(2)}, u32[]{:S(2)}) collective-permute-start(bf16[16,32,128]{2,1,0:T(8,128)(2,1)} %get-tuple-element.69), channel_id=1, source_target_pairs={{0,4},{1,5},{2,6},{3,7},{4,0},{5,1},{6,2},{7,3},{8,12},{9,13},{10,... | collective-permute-start | bytes 393224 | tf_op jit(solution)/shard_map/ppermute | solution.py:603
  201.2 9.0 %collective-permute-start.21 = (bf16[16,32,128]{2,1,0:T(8,128)(2,1)}, bf16[16,32,128]{2,1,0:T(8,128)(2,1)}, u32[]{:S(2)}, u32[]{:S(2)}) collective-permute-start(bf16[16,32,128]{2,1,0:T(8,128)(2,1)} %get-tuple-element.70), channel_id=1, source_target_pairs={{0,6},{1,7},{2,0},{3,1},{4,2},{5,3},{6,4},{7,5},{8,14},{9,15},{10,... | collective-permute-start | bytes 393224 | tf_op jit(solution)/shard_map/ppermute | solution.py:603

commit v10 on v9

--- a/solution.py
+++ b/solution.py
@@ -544,29 +544,35 @@
         pltpu.make_async_copy(up_ref, up, sems.at[3]),
         pltpu.make_async_copy(down_ref, down, sems.at[4]),
     ]
-    for copy in copies:
-        copy.start()
+    for which in (0, 1, 3, 4, 2):
+        copies[which].start()
     for copy in arriving:
         copy.wait()
     copies[0].wait()
-    firsts = []
+    rows = rows // 2
     for half, at in enumerate(halves):
         added = mixed_rows(held, half, out_w[...])
         copies[1 + half].wait()
-        firsts.append(normed(early[at, :] + added, gain_ref[0:1, :]).astype(BF16))
-    rows = rows // 2
-    firsts = [first[at : at + rows] for first in firsts for at in (0, rows)]
-    for half, first in enumerate(firsts):
-        at = slice(half * rows, (half + 1) * rows)
-        if half == 0:
-            copies[3].wait()
-        hidden = jnp.maximum(jnp.dot(first, up[...], preferred_element_type=F32), 0.0).astype(BF16)
-        if half == 0:
-            copies[4].wait()
-        total = first.astype(F32) + jnp.dot(hidden, down[...], preferred_element_type=F32)
-        made[at, :] = normed(total, gain_ref[1:2, :]).astype(BF16)
-        copies.append(pltpu.make_async_copy(made.at[at], result_ref.at[at], sems.at[5 + half]))
-        copies[-1].start()
+        whole = normed(early[at, :] + added, gain_ref[0:1, :]).astype(BF16)
+        for part in range(2):
+            first = whole[part * rows : (part + 1) * rows]
+            row = (half * 2 + part) * rows
+            if half + part == 0:
+                copies[3].wait()
+            hidden = jnp.dot(first, up[...], preferred_element_type=F32)
+            hidden = jnp.maximum(hidden, 0.0).astype(BF16)
+            if half + part == 0:
+                copies[4].wait()
+            total = first.astype(F32) + jnp.dot(hidden, down[...], preferred_element_type=F32)
+            made[row : row + rows, :] = normed(total, gain_ref[1:2, :]).astype(BF16)
+            copies.append(
+                pltpu.make_async_copy(
+                    made.at[row : row + rows],
+                    result_ref.at[row : row + rows],
+                    sems.at[5 + half * 2 + part],
+                )
+            )
+            copies[-1].start()
     for copy in copies[5:]:
         copy.wait()
 

time: 227 us -> 227 us (level)
  no operation moved by 1% of the time
where the time goes in v10:
time: 227 us; the launch traced here: 223 us
  waiting for transfers between devices  87.8 us (39%)
  Pallas kernels  81.8 us (36%)
  starting transfers between devices  52.1 us (23%)
    ppermute x15, waiting for transfers between devices, along_z(): lax.ppermute(parts[step], 'head', [(i, (i + 2 * step) % (2 * CHIPS)) for...  41.9 us
    pallas_call x3, Pallas kernels, attend(): pl.pallas_call(functools.partial(attend_kernel, chunk, len(before)), in_s...  35 us
    all_to_all x3, waiting for transfers between devices, per_device(): got = lax.all_to_all(sent, 'node', split_axis=0, concat_axis=0, tiled=True)  26.4 us
    ppermute x15, starting transfers between devices, along_z(): lax.ppermute(parts[step], 'head', [(i, (i + 2 * step) % (2 * CHIPS)) for...  23.8 us
    all_to_all x3, starting transfers between devices, per_device(): got = lax.all_to_all(sent, 'node', split_axis=0, concat_axis=0, tiled=True)  22.2 us
    all_to_all x1, waiting for transfers between devices, per_device(): lax.all_to_all(whole, 'head', split_axis=0, concat_axis=0, tiled=True)  15.4 us
    pallas_call x1, Pallas kernels, finish(): pl.pallas_call(finish_kernel, in_specs=[SMEM] + [HBM] * (CHIPS + 4) + [VM...  12.3 us
    pallas_call x2, Pallas kernels, project_keys_values(): pl.pallas_call(functools.partial(keys_values_kernel, chunk), in_specs=[SM...  9.92 us
  transfers between devices with their start and end apart: 26, of which 12 were waited for; matrix products, arithmetic and copies ran while one was open for 0% of the time, Pallas kernels for 28%

profile of v10, /device:TPU:20, one launch (start us, length us, event | category | flops | bytes accessed | tf_op | source)
XLA Modules:
  0.0 222.7 jit_solution(11019596459316070714)
XLA Ops:
  0.0 4.1 %first_keys_values.1 = bf16[8,16,32,128]{3,2,1,0:T(8,128)(2,1)} custom-call(bf16[1024,768]{1,0:T(8,128)(2,1)} %near_ref.3, bf16[768,768]{1,0:T(8,128)(2,1)} %key_ref.5, bf16[768,768]{1,0:T(8,128)(2,1)} %value_ref.5), custom_call_target="tpu_custom_call" | custom-call | flops 805306368 | bytes 4194304 | tf_op jit(solution)/shard_map/first_keys_values/pallas_call | solution.py:122
  4.1 5.3 %all-to-all-start.1 = ((bf16[8,16,32,128]{3,2,1,0:T(8,128)(2,1)}), bf16[8,16,32,128]{3,2,1,0:T(8,128)(2,1)}, u32[]{:S(2)}, u32[]{:S(2)}) async-start(bf16[8,16,32,128]{3,2,1,0:T(8,128)(2,1)} %first_keys_values.1), calls=%async_computation.1 | async-start | bytes 2097152 | tf_op jit(solution)/shard_map/all_to_all | solution.py:628
  9.4 0.6 pad_add_fusion.place_ref
  10.0 15.4 %all-to-all-done.1 = bf16[8,16,32,128]{3,2,1,0:T(8,128)(2,1)} async-done(((bf16[8,16,32,128]{3,2,1,0:T(8,128)(2,1)}), bf16[8,16,32,128]{3,2,1,0:T(8,128)(2,1)}, u32[]{:S(2)}, u32[]{:S(2)}) %all-to-all-start.1) | async-done | bytes 1048608 | tf_op jit(solution)/shard_map/all_to_all | solution.py:628
  25.4 3.1 %collect.4 = (bf16[256,32,128]{2,1,0:T(8,128)(2,1)}, bf16[4,16,32,128]{3,2,1,0:T(8,128)(2,1)}, bf16[4,16,32,128]{3,2,1,0:T(8,128)(2,1)}) custom-call(s32[1,16,16]{2,1,0:T(8,128)} %list_ref.5, s32[2]{0:T(128)} %pad_add_fusion.place_ref, bf16[128,32,128]{2,1,0:T(8,128)(2,1)} %bitcast.6.refs_0_), custom_call_target="tpu_custom_call" | custom-call | bytes 5242880 | tf_op jit(solution)/shard_map/collect/pallas_call | solution.py:246
  28.5 0.0 copy-start
  28.5 7.4 %all-to-all-start.2 = ((bf16[16,16,32,128]{3,2,1,0:T(8,128)(2,1)}), bf16[16,16,32,128]{3,2,1,0:T(8,128)(2,1)}, u32[]{:S(2)}, u32[]{:S(2)}) async-start(bf16[16,16,32,128]{3,2,1,0:T(8,128)(2,1)} %bitcast.12), calls=%async_computation.2 | async-start | bytes 4194304 | tf_op jit(solution)/shard_map/all_to_all | solution.py:638
  35.9 0.1 collective-permute-start.3
  36.0 3.5 %collective-permute-done.3.far_ref = bf16[1024,768]{1,0:T(8,128)(2,1)} collective-permute-done((bf16[1024,768]{1,0:T(8,128)(2,1)S(1)}, bf16[1024,768]{1,0:T(8,128)(2,1)}, u32[]{:S(2)}, u32[]{:S(2)}) %collective-permute-start.3) | collective-permute-done | bytes 1572896 | tf_op jit(solution)/shard_map/ppermute | solution.py:603
  39.5 4.9 %keys_values.2 = (bf16[32,32,128]{2,1,0:T(8,128)(2,1)}, bf16[32,32,128]{2,1,0:T(8,128)(2,1)}, bf16[32,32,128]{2,1,0:T(8,128)(2,1)}, bf16[32,32,128]{2,1,0:T(8,128)(2,1)}) custom-call(s32[2]{0:T(128)} %pad_add_fusion.place_ref, bf16[1024,768]{1,0:T(8,128)(2,1)} %near_ref.3, bf16[1024,768]{1,0:T(8,128)(2,1)} %collective-permute-done.3.far_ref, ...), custom_call_target="tpu_custom_call" | custom-call | flops 805306368 | bytes 5242880 | tf_op jit(solution)/shard_map/keys_values/pallas_call | solution.py:154
  44.5 0.6 collective-permute-start.4
  45.1 2.1 collective-permute-start.5
  47.2 0.7 collective-permute-start.6
  47.9 12.2 %collective-permute-done.4.refs_1_ = bf16[32,32,128]{2,1,0:T(8,128)(2,1)} collective-permute-done((bf16[32,32,128]{2,1,0:T(8,128)(2,1)}, bf16[32,32,128]{2,1,0:T(8,128)(2,1)}, u32[]{:S(2)}, u32[]{:S(2)}) %collective-permute-start.4) | collective-permute-done | bytes 262176 | tf_op jit(solution)/shard_map/ppermute | solution.py:609
  60.0 0.0 collective-permute-done.5.refs_2_
  60.0 0.6 collective-permute-done.6.refs_3_
  60.6 3.1 %collect.3 = (bf16[256,32,128]{2,1,0:T(8,128)(2,1)}, bf16[4,16,32,128]{3,2,1,0:T(8,128)(2,1)}, bf16[4,16,32,128]{3,2,1,0:T(8,128)(2,1)}) custom-call(s32[1,16,16]{2,1,0:T(8,128)} %list_ref.5, s32[2]{0:T(128)} %pad_add_fusion.place_ref, bf16[32,32,128]{2,1,0:T(8,128)(2,1)} %get-tuple-element.42.refs_0_, bf16[32,32,128]{2,1,0:T(8,128)(2,1)} %collective-permute-done.4.refs_1_, ...), custom_call_target="tpu_custom_call" | custom-call | bytes 5242880 | tf_op jit(solution)/shard_map/collect/pallas_call | solution.py:246
  63.8 7.2 %all-to-all-start = ((bf16[16,16,32,128]{3,2,1,0:T(8,128)(2,1)}), bf16[16,16,32,128]{3,2,1,0:T(8,128)(2,1)}, u32[]{:S(2)}, u32[]{:S(2)}) async-start(bf16[16,16,32,128]{3,2,1,0:T(8,128)(2,1)} %bitcast.11), calls=%async_computation | async-start | bytes 4194304 | tf_op jit(solution)/shard_map/all_to_all | solution.py:638
  71.0 5.0 %keys_values.3 = (bf16[32,32,128]{2,1,0:T(8,128)(2,1)}, bf16[32,32,128]{2,1,0:T(8,128)(2,1)}, bf16[32,32,128]{2,1,0:T(8,128)(2,1)}, bf16[32,32,128]{2,1,0:T(8,128)(2,1)}) custom-call(s32[2]{0:T(128)} %pad_add_fusion.place_ref, bf16[1024,768]{1,0:T(8,128)(2,1)} %near_ref.3, bf16[1024,768]{1,0:T(8,128)(2,1)} %collective-permute-done.3.far_ref, ...), custom_call_target="tpu_custom_call" | custom-call | flops 805306368 | bytes 5242880 | tf_op jit(solution)/shard_map/keys_values/pallas_call | solution.py:154
  76.0 0.4 collective-permute-start.14
  76.4 3.6 %collective-permute-start.15 = (bf16[32,32,128]{2,1,0:T(8,128)(2,1)}, bf16[32,32,128]{2,1,0:T(8,128)(2,1)}, u32[]{:S(2)}, u32[]{:S(2)}) collective-permute-start(bf16[32,32,128]{2,1,0:T(8,128)(2,1)} %get-tuple-element.62), channel_id=1, source_target_pairs={{0,4},{1,5},{2,6},{3,7},{4,0},{5,1},{6,2},{7,3},{8,12},{9,13},{10,... | collective-permute-start | bytes 786440 | tf_op jit(solution)/shard_map/ppermute | solution.py:609
  80.0 5.1 %collective-permute-done.14.refs_1_ = bf16[32,32,128]{2,1,0:T(8,128)(2,1)} collective-permute-done((bf16[32,32,128]{2,1,0:T(8,128)(2,1)}, bf16[32,32,128]{2,1,0:T(8,128)(2,1)}, u32[]{:S(2)}, u32[]{:S(2)}) %collective-permute-start.14) | collective-permute-done | bytes 262176 | tf_op jit(solution)/shard_map/ppermute | solution.py:609
  85.1 6.3 %collective-permute-done.15.refs_2_ = bf16[32,32,128]{2,1,0:T(8,128)(2,1)} collective-permute-done((bf16[32,32,128]{2,1,0:T(8,128)(2,1)}, bf16[32,32,128]{2,1,0:T(8,128)(2,1)}, u32[]{:S(2)}, u32[]{:S(2)}) %collective-permute-start.15) | collective-permute-done | bytes 262176 | tf_op jit(solution)/shard_map/ppermute | solution.py:609
  91.3 3.2 %collect.5 = (bf16[256,32,128]{2,1,0:T(8,128)(2,1)}, bf16[4,16,32,128]{3,2,1,0:T(8,128)(2,1)}, bf16[4,16,32,128]{3,2,1,0:T(8,128)(2,1)}) custom-call(s32[1,16,16]{2,1,0:T(8,128)} %list_ref.5, s32[2]{0:T(128)} %pad_add_fusion.place_ref, bf16[32,32,128]{2,1,0:T(8,128)(2,1)} %get-tuple-element.60.refs_0_, bf16[32,32,128]{2,1,0:T(8,128)(2,1)} %collective-permute-done.14.refs_1_, ...), custom_call_target="tpu_custom_call" | custom-call | bytes 5242880 | tf_op jit(solution)/shard_map/collect/pallas_call | solution.py:246
  94.6 2.2 all-to-all-done
  96.7 7.6 %all-to-all-start.3 = ((bf16[16,16,32,128]{3,2,1,0:T(8,128)(2,1)}), bf16[16,16,32,128]{3,2,1,0:T(8,128)(2,1)}, u32[]{:S(2)}, u32[]{:S(2)}) async-start(bf16[16,16,32,128]{3,2,1,0:T(8,128)(2,1)} %bitcast.13), calls=%async_computation.3 | async-start | bytes 4194304 | tf_op jit(solution)/shard_map/all_to_all | solution.py:638
  104.4 0.5 collective-permute-start.8
  104.9 24.2 %all-to-all-done.3 = bf16[16,16,32,128]{3,2,1,0:T(8,128)(2,1)} async-done(((bf16[16,16,32,128]{3,2,1,0:T(8,128)(2,1)}), bf16[16,16,32,128]{3,2,1,0:T(8,128)(2,1)}, u32[]{:S(2)}, u32[]{:S(2)}) %all-to-all-start.3) | async-done | bytes 2097184 | tf_op jit(solution)/shard_map/all_to_all | solution.py:638
  129.1 4.7 %queries.1 = (bf16[3,16,32,128]{3,2,1,0:T(8,128)(2,1)}, bf16[3,16,32,128]{3,2,1,0:T(8,128)(2,1)}, bf16[3,16,32,128]{3,2,1,0:T(8,128)(2,1)}, bf16[3,16,32,128]{3,2,1,0:T(8,128)(2,1)}) custom-call(s32[2]{0:T(128)} %pad_add_fusion.place_ref, bf16[1024,768]{1,0:T(8,128)(2,1)} %near_ref.3, bf16[768,768]{1,0:T(8,128)(2,1)} %query_ref.1), custom_call_target="tpu_custom_call" | custom-call | flops 1207959552 | bytes 5242880 | tf_op jit(solution)/shard_map/queries/pallas_call | solution.py:192
  133.9 2.2 collective-permute-start
  136.1 3.1 %collective-permute-start.1 = (bf16[3,16,32,128]{3,2,1,0:T(8,128)(2,1)}, bf16[3,16,32,128]{3,2,1,0:T(8,128)(2,1)}, u32[]{:S(2)}, u32[]{:S(2)}) collective-permute-start(bf16[3,16,32,128]{3,2,1,0:T(8,128)(2,1)} %get-tuple-element.40), channel_id=1, source_target_pairs={{0,4},{1,5},{2,6},{3,7},{4,0},{5,1},{6,2},{7,3},{8,12},{9,13},{10,... | collective-permute-start | bytes 1179656 | tf_op jit(solution)/shard_map/ppermute | solution.py:609
  139.1 8.6 %collective-permute-done.refs_1_ = bf16[3,16,32,128]{3,2,1,0:T(8,128)(2,1)} collective-permute-done((bf16[3,16,32,128]{3,2,1,0:T(8,128)(2,1)}, bf16[3,16,32,128]{3,2,1,0:T(8,128)(2,1)}, u32[]{:S(2)}, u32[]{:S(2)}) %collective-permute-start) | collective-permute-done | bytes 393248 | tf_op jit(solution)/shard_map/ppermute | solution.py:609
  147.8 2.2 collective-permute-start.2
  150.0 7.4 %collective-permute-done.1.refs_2_ = bf16[3,16,32,128]{3,2,1,0:T(8,128)(2,1)} collective-permute-done((bf16[3,16,32,128]{3,2,1,0:T(8,128)(2,1)}, bf16[3,16,32,128]{3,2,1,0:T(8,128)(2,1)}, u32[]{:S(2)}, u32[]{:S(2)}) %collective-permute-start.1) | collective-permute-done | bytes 393248 | tf_op jit(solution)/shard_map/ppermute | solution.py:609
  157.4 1.7 collective-permute-done.2.refs_3_
  159.0 0.6 collective-permute-done.9.refs_5_
  159.6 0.1 collective-permute-start.17
  159.8 11.6 %attend.3 = (bf16[16,32,128]{2,1,0:T(8,128)(2,1)}, bf16[16,32,128]{2,1,0:T(8,128)(2,1)}, bf16[16,32,128]{2,1,0:T(8,128)(2,1)}, bf16[16,32,128]{2,1,0:T(8,128)(2,1)}) custom-call(s32[8,128]{1,0:T(8,128)} %bitcast.14, s32[8,128]{1,0:T(8,128)} %bitcast.17, s32[128]{0:T(128)} %count_ref.5, s32[2]{0:T(128)} %pad_add_fusion.place_ref, ...), custom_call_target="tpu_custom_call" | custom-call | flops 1610612736 | bytes 8388608 | tf_op jit(solution)/shard_map/attend/pallas_call | solution.py:416
  171.4 11.9 %attend.4 = (bf16[2,16,32,128]{3,2,1,0:T(8,128)(2,1)}, bf16[2,16,32,128]{3,2,1,0:T(8,128)(2,1)}, bf16[2,16,32,128]{3,2,1,0:T(8,128)(2,1)}, bf16[2,16,32,128]{3,2,1,0:T(8,128)(2,1)}) custom-call(s32[8,128]{1,0:T(8,128)} %bitcast.15, s32[8,128]{1,0:T(8,128)} %bitcast.18, s32[128]{0:T(128)} %count_ref.5, s32[2]{0:T(128)} %pad_add_fusion.place_ref, ...), custom_call_target="tpu_custom_call" | custom-call | flops 1610612736 | bytes 8388608 | tf_op jit(solution)/shard_map/attend/pallas_call | solution.py:416
  183.3 0.1 collective-permute-start.11
  183.4 3.9 %collective-permute-start.12 = (bf16[2,16,32,128]{3,2,1,0:T(8,128)(2,1)}, bf16[2,16,32,128]{3,2,1,0:T(8,128)(2,1)}, u32[]{:S(2)}, u32[]{:S(2)}) collective-permute-start(bf16[2,16,32,128]{3,2,1,0:T(8,128)(2,1)} %get-tuple-element.58), channel_id=1, source_target_pairs={{0,4},{1,5},{2,6},{3,7},{4,0},{5,1},{6,2},{7,3},{8,12},{9,13},{10,... | collective-permute-start | bytes 786440 | tf_op jit(solution)/shard_map/ppermute | solution.py:609
  187.3 11.5 %attend.5 = (bf16[16,32,128]{2,1,0:T(8,128)(2,1)}, bf16[16,32,128]{2,1,0:T(8,128)(2,1)}, bf16[16,32,128]{2,1,0:T(8,128)(2,1)}, bf16[16,32,128]{2,1,0:T(8,128)(2,1)}) custom-call(s32[8,128]{1,0:T(8,128)} %bitcast.16, s32[8,128]{1,0:T(8,128)} %bitcast.19, s32[128]{0:T(128)} %count_ref.5, s32[2]{0:T(128)} %pad_add_fusion.place_ref, ...), custom_call_target="tpu_custom_call" | custom-call | flops 1610612736 | bytes 8388608 | tf_op jit(solution)/shard_map/attend/pallas_call | solution.py:416
  198.8 2.1 collective-permute-start.19
  200.9 0.3 collective-permute-start.20
  201.2 2.5 %collective-permute-start.21 = (bf16[16,32,128]{2,1,0:T(8,128)(2,1)}, bf16[16,32,128]{2,1,0:T(8,128)(2,1)}, u32[]{:S(2)}, u32[]{:S(2)}) collective-permute-start(bf16[16,32,128]{2,1,0:T(8,128)(2,1)} %get-tuple-element.70), channel_id=1, source_target_pairs={{0,6},{1,7},{2,0},{3,1},{4,2},{5,3},{6,4},{7,5},{8,14},{9,15},{10,... | collective-permute-start | bytes 393224 | tf_op jit(solution)/shard_map/ppermute | solution.py:609
  203.8 1.3 gains.1.refs_7_
  205.1 5.1 %mix.1.mixed_ref = f32[1024,768]{1,0:T(8,128)} custom-call(s32[2]{0:T(128)} %pad_add_fusion.place_ref, bf16[1024,768]{1,0:T(8,128)(2,1)} %near_ref.3, bf16[2,16,32,128]{3,2,1,0:T(8,128)(2,1)} %get-tuple-element.56.refs_0_, bf16[2,16,32,128]{3,2,1,0:T(8,128)(2,1)} %collective-permute-done.11.refs_1_, ...), custom_call_target="tpu_custom_call" | custom-call | flops 805306368 | bytes 7340032 | tf_op jit(solution)/shard_map/mix/pallas_call | solution.py:512
  210.2 12.3 %finish.1 = bf16[1024,768]{1,0:T(8,128)(2,1)} custom-call(s32[2]{0:T(128)} %pad_add_fusion.place_ref, f32[1024,768]{1,0:T(8,128)} %mix.1.mixed_ref, bf16[16,32,128]{2,1,0:T(8,128)(2,1)} %get-tuple-element.67.refs_0_, bf16[16,32,128]{2,1,0:T(8,128)(2,1)} %collective-permute-done.19.refs_1_, bf16[16,32,128]{2,1,0:T(8,128)(2,1)} %collective-permute-done.20.refs_2_, ...), custom_call_target="tpu_custom_call" | custom-call | tf_op jit(solution)/shard_map/finish/pallas_call | solution.py:582
  (20 shorter events, 0.1 us)
Async XLA Ops:
  4.1 21.4 %all-to-all-start.1 = ((bf16[8,16,32,128]{3,2,1,0:T(8,128)(2,1)}), bf16[8,16,32,128]{3,2,1,0:T(8,128)(2,1)}, u32[]{:S(2)}, u32[]{:S(2)}) async-start(bf16[8,16,32,128]{3,2,1,0:T(8,128)(2,1)} %first_keys_values.1), calls=%async_computation.1 | async-start | bytes 2097152 | tf_op jit(solution)/shard_map/all_to_all | solution.py:628
  28.5 7.4 %copy-start = (bf16[1024,768]{1,0:T(8,128)(2,1)S(1)}, bf16[1024,768]{1,0:T(8,128)(2,1)}, u32[]{:S(2)}) copy-start(bf16[1024,768]{1,0:T(8,128)(2,1)} %near_ref.3) | copy-start | bytes 4718596
  28.5 35.2 %all-to-all-start.2 = ((bf16[16,16,32,128]{3,2,1,0:T(8,128)(2,1)}), bf16[16,16,32,128]{3,2,1,0:T(8,128)(2,1)}, u32[]{:S(2)}, u32[]{:S(2)}) async-start(bf16[16,16,32,128]{3,2,1,0:T(8,128)(2,1)} %bitcast.12), calls=%async_computation.2 | async-start | bytes 4194304 | tf_op jit(solution)/shard_map/all_to_all | solution.py:638
  35.9 3.6 %collective-permute-start.3 = (bf16[1024,768]{1,0:T(8,128)(2,1)S(1)}, bf16[1024,768]{1,0:T(8,128)(2,1)}, u32[]{:S(2)}, u32[]{:S(2)}) collective-permute-start(bf16[1024,768]{1,0:T(8,128)(2,1)S(1)} %copy-done), channel_id=1, source_target_pairs={{0,1},{1,0},{2,3},{3,2},{4,5},{5,4},{6,7},{7,6},{8,9},{9,8},{10,11... | collective-permute-start | bytes 4718600 | tf_op jit(solution)/shard_map/ppermute | solution.py:603
  44.5 15.6 %collective-permute-start.4 = (bf16[32,32,128]{2,1,0:T(8,128)(2,1)}, bf16[32,32,128]{2,1,0:T(8,128)(2,1)}, u32[]{:S(2)}, u32[]{:S(2)}) collective-permute-start(bf16[32,32,128]{2,1,0:T(8,128)(2,1)} %get-tuple-element.43), channel_id=1, source_target_pairs={{0,2},{1,3},{2,4},{3,5},{4,6},{5,7},{6,0},{7,1},{8,10},{9,11},{10,... | collective-permute-start | bytes 786440 | tf_op jit(solution)/shard_map/ppermute | solution.py:609
  45.1 14.9 %collective-permute-start.5 = (bf16[32,32,128]{2,1,0:T(8,128)(2,1)}, bf16[32,32,128]{2,1,0:T(8,128)(2,1)}, u32[]{:S(2)}, u32[]{:S(2)}) collective-permute-start(bf16[32,32,128]{2,1,0:T(8,128)(2,1)} %get-tuple-element.44), channel_id=1, source_target_pairs={{0,4},{1,5},{2,6},{3,7},{4,0},{5,1},{6,2},{7,3},{8,12},{9,13},{10,... | collective-permute-start | bytes 786440 | tf_op jit(solution)/shard_map/ppermute | solution.py:609
  47.2 13.5 %collective-permute-start.6 = (bf16[32,32,128]{2,1,0:T(8,128)(2,1)}, bf16[32,32,128]{2,1,0:T(8,128)(2,1)}, u32[]{:S(2)}, u32[]{:S(2)}) collective-permute-start(bf16[32,32,128]{2,1,0:T(8,128)(2,1)} %get-tuple-element.45), channel_id=1, source_target_pairs={{0,6},{1,7},{2,0},{3,1},{4,2},{5,3},{6,4},{7,5},{8,14},{9,15},{10,... | collective-permute-start | bytes 786440 | tf_op jit(solution)/shard_map/ppermute | solution.py:609
  63.8 33.0 %all-to-all-start = ((bf16[16,16,32,128]{3,2,1,0:T(8,128)(2,1)}), bf16[16,16,32,128]{3,2,1,0:T(8,128)(2,1)}, u32[]{:S(2)}, u32[]{:S(2)}) async-start(bf16[16,16,32,128]{3,2,1,0:T(8,128)(2,1)} %bitcast.11), calls=%async_computation | async-start | bytes 4194304 | tf_op jit(solution)/shard_map/all_to_all | solution.py:638
  76.0 9.1 %collective-permute-start.14 = (bf16[32,32,128]{2,1,0:T(8,128)(2,1)}, bf16[32,32,128]{2,1,0:T(8,128)(2,1)}, u32[]{:S(2)}, u32[]{:S(2)}) collective-permute-start(bf16[32,32,128]{2,1,0:T(8,128)(2,1)} %get-tuple-element.61), channel_id=1, source_target_pairs={{0,2},{1,3},{2,4},{3,5},{4,6},{5,7},{6,0},{7,1},{8,10},{9,11},{10,... | collective-permute-start | bytes 786440 | tf_op jit(solution)/shard_map/ppermute | solution.py:609
  76.4 14.9 %collective-permute-start.15 = (bf16[32,32,128]{2,1,0:T(8,128)(2,1)}, bf16[32,32,128]{2,1,0:T(8,128)(2,1)}, u32[]{:S(2)}, u32[]{:S(2)}) collective-permute-start(bf16[32,32,128]{2,1,0:T(8,128)(2,1)} %get-tuple-element.62), channel_id=1, source_target_pairs={{0,4},{1,5},{2,6},{3,7},{4,0},{5,1},{6,2},{7,3},{8,12},{9,13},{10,... | collective-permute-start | bytes 786440 | tf_op jit(solution)/shard_map/ppermute | solution.py:609
  80.0 11.4 %collective-permute-start.16 = (bf16[32,32,128]{2,1,0:T(8,128)(2,1)}, bf16[32,32,128]{2,1,0:T(8,128)(2,1)}, u32[]{:S(2)}, u32[]{:S(2)}) collective-permute-start(bf16[32,32,128]{2,1,0:T(8,128)(2,1)} %get-tuple-element.63), channel_id=1, source_target_pairs={{0,6},{1,7},{2,0},{3,1},{4,2},{5,3},{6,4},{7,5},{8,14},{9,15},{10,... | collective-permute-start | bytes 786440 | tf_op jit(solution)/shard_map/ppermute | solution.py:609
  96.7 32.4 %all-to-all-start.3 = ((bf16[16,16,32,128]{3,2,1,0:T(8,128)(2,1)}), bf16[16,16,32,128]{3,2,1,0:T(8,128)(2,1)}, u32[]{:S(2)}, u32[]{:S(2)}) async-start(bf16[16,16,32,128]{3,2,1,0:T(8,128)(2,1)} %bitcast.13), calls=%async_computation.3 | async-start | bytes 4194304 | tf_op jit(solution)/shard_map/all_to_all | solution.py:638
  104.4 55.4 %collective-permute-start.10 = (bf16[256,32,128]{2,1,0:T(8,128)(2,1)}, bf16[256,32,128]{2,1,0:T(8,128)(2,1)}, u32[]{:S(2)}, u32[]{:S(2)}) collective-permute-start(bf16[256,32,128]{2,1,0:T(8,128)(2,1)} %bitcast.8.refs_6_), channel_id=1, source_target_pairs={{0,1},{1,0},{2,3},{3,2},{4,5},{5,4},{6,7},{7,6},{8,9},{9,8},{10,11... | collective-permute-start | bytes 6291464 | tf_op jit(solution)/shard_map/ppermute | solution.py:603
  104.4 67.0 %collective-permute-start.8 = (bf16[256,32,128]{2,1,0:T(8,128)(2,1)}, bf16[256,32,128]{2,1,0:T(8,128)(2,1)}, u32[]{:S(2)}, u32[]{:S(2)}) collective-permute-start(bf16[256,32,128]{2,1,0:T(8,128)(2,1)} %bitcast.5.refs_6_), channel_id=1, source_target_pairs={{0,1},{1,0},{2,3},{3,2},{4,5},{5,4},{6,7},{7,6},{8,9},{9,8},{10,11... | collective-permute-start | bytes 6291464 | tf_op jit(solution)/shard_map/ppermute | solution.py:603
  129.1 58.2 %collective-permute-start.18 = (bf16[256,32,128]{2,1,0:T(8,128)(2,1)}, bf16[256,32,128]{2,1,0:T(8,128)(2,1)}, u32[]{:S(2)}, u32[]{:S(2)}) collective-permute-start(bf16[256,32,128]{2,1,0:T(8,128)(2,1)} %bitcast.10.refs_6_), channel_id=1, source_target_pairs={{0,1},{1,0},{2,3},{3,2},{4,5},{5,4},{6,7},{7,6},{8,9},{9,8},{10,11... | collective-permute-start | bytes 6291464 | tf_op jit(solution)/shard_map/ppermute | solution.py:603
  133.9 13.9 %collective-permute-start = (bf16[3,16,32,128]{3,2,1,0:T(8,128)(2,1)}, bf16[3,16,32,128]{3,2,1,0:T(8,128)(2,1)}, u32[]{:S(2)}, u32[]{:S(2)}) collective-permute-start(bf16[3,16,32,128]{3,2,1,0:T(8,128)(2,1)} %get-tuple-element.39), channel_id=1, source_target_pairs={{0,2},{1,3},{2,4},{3,5},{4,6},{5,7},{6,0},{7,1},{8,10},{9,11},{10,... | collective-permute-start | bytes 1179656 | tf_op jit(solution)/shard_map/ppermute | solution.py:609
  136.1 21.3 %collective-permute-start.1 = (bf16[3,16,32,128]{3,2,1,0:T(8,128)(2,1)}, bf16[3,16,32,128]{3,2,1,0:T(8,128)(2,1)}, u32[]{:S(2)}, u32[]{:S(2)}) collective-permute-start(bf16[3,16,32,128]{3,2,1,0:T(8,128)(2,1)} %get-tuple-element.40), channel_id=1, source_target_pairs={{0,4},{1,5},{2,6},{3,7},{4,0},{5,1},{6,2},{7,3},{8,12},{9,13},{10,... | collective-permute-start | bytes 1179656 | tf_op jit(solution)/shard_map/ppermute | solution.py:609
  147.8 11.3 %collective-permute-start.2 = (bf16[3,16,32,128]{3,2,1,0:T(8,128)(2,1)}, bf16[3,16,32,128]{3,2,1,0:T(8,128)(2,1)}, u32[]{:S(2)}, u32[]{:S(2)}) collective-permute-start(bf16[3,16,32,128]{3,2,1,0:T(8,128)(2,1)} %get-tuple-element.41), channel_id=1, source_target_pairs={{0,6},{1,7},{2,0},{3,1},{4,2},{5,3},{6,4},{7,5},{8,14},{9,15},{10,... | collective-permute-start | bytes 1179656 | tf_op jit(solution)/shard_map/ppermute | solution.py:609
  157.4 2.3 %collective-permute-start.9 = (bf16[4,16,32,128]{3,2,1,0:T(8,128)(2,1)}, bf16[4,16,32,128]{3,2,1,0:T(8,128)(2,1)}, u32[]{:S(2)}, u32[]{:S(2)}) collective-permute-start(bf16[4,16,32,128]{3,2,1,0:T(8,128)(2,1)} %get-tuple-element.50), channel_id=1, source_target_pairs={{0,1},{1,0},{2,3},{3,2},{4,5},{5,4},{6,7},{7,6},{8,9},{9,8},{10,11... | collective-permute-start | bytes 1572872 | tf_op jit(solution)/shard_map/ppermute | solution.py:603
  159.0 12.3 %collective-permute-start.7 = (bf16[4,16,32,128]{3,2,1,0:T(8,128)(2,1)}, bf16[4,16,32,128]{3,2,1,0:T(8,128)(2,1)}, u32[]{:S(2)}, u32[]{:S(2)}) collective-permute-start(bf16[4,16,32,128]{3,2,1,0:T(8,128)(2,1)} %get-tuple-element.47), channel_id=1, source_target_pairs={{0,1},{1,0},{2,3},{3,2},{4,5},{5,4},{6,7},{7,6},{8,9},{9,8},{10,11... | collective-permute-start | bytes 1572872 | tf_op jit(solution)/shard_map/ppermute | solution.py:603
  159.6 27.7 %collective-permute-start.17 = (bf16[4,16,32,128]{3,2,1,0:T(8,128)(2,1)}, bf16[4,16,32,128]{3,2,1,0:T(8,128)(2,1)}, u32[]{:S(2)}, u32[]{:S(2)}) collective-permute-start(bf16[4,16,32,128]{3,2,1,0:T(8,128)(2,1)} %get-tuple-element.65), channel_id=1, source_target_pairs={{0,1},{1,0},{2,3},{3,2},{4,5},{5,4},{6,7},{7,6},{8,9},{9,8},{10,11... | collective-permute-start | bytes 1572872 | tf_op jit(solution)/shard_map/ppermute | solution.py:603
  183.3 17.9 %collective-permute-start.11 = (bf16[2,16,32,128]{3,2,1,0:T(8,128)(2,1)}, bf16[2,16,32,128]{3,2,1,0:T(8,128)(2,1)}, u32[]{:S(2)}, u32[]{:S(2)}) collective-permute-start(bf16[2,16,32,128]{3,2,1,0:T(8,128)(2,1)} %get-tuple-element.57), channel_id=1, source_target_pairs={{0,2},{1,3},{2,4},{3,5},{4,6},{5,7},{6,0},{7,1},{8,10},{9,11},{10,... | collective-permute-start | bytes 786440 | tf_op jit(solution)/shard_map/ppermute | solution.py:609
  183.4 21.7 %collective-permute-start.12 = (bf16[2,16,32,128]{3,2,1,0:T(8,128)(2,1)}, bf16[2,16,32,128]{3,2,1,0:T(8,128)(2,1)}, u32[]{:S(2)}, u32[]{:S(2)}) collective-permute-start(bf16[2,16,32,128]{3,2,1,0:T(8,128)(2,1)} %get-tuple-element.58), channel_id=1, source_target_pairs={{0,4},{1,5},{2,6},{3,7},{4,0},{5,1},{6,2},{7,3},{8,12},{9,13},{10,... | collective-permute-start | bytes 786440 | tf_op jit(solution)/shard_map/ppermute | solution.py:609
  187.3 17.8 %collective-permute-start.13 = (bf16[2,16,32,128]{3,2,1,0:T(8,128)(2,1)}, bf16[2,16,32,128]{3,2,1,0:T(8,128)(2,1)}, u32[]{:S(2)}, u32[]{:S(2)}) collective-permute-start(bf16[2,16,32,128]{3,2,1,0:T(8,128)(2,1)} %get-tuple-element.59), channel_id=1, source_target_pairs={{0,6},{1,7},{2,0},{3,1},{4,2},{5,3},{6,4},{7,5},{8,14},{9,15},{10,... | collective-permute-start | bytes 786440 | tf_op jit(solution)/shard_map/ppermute | solution.py:609
  198.8 11.4 %collective-permute-start.19 = (bf16[16,32,128]{2,1,0:T(8,128)(2,1)}, bf16[16,32,128]{2,1,0:T(8,128)(2,1)}, u32[]{:S(2)}, u32[]{:S(2)}) collective-permute-start(bf16[16,32,128]{2,1,0:T(8,128)(2,1)} %get-tuple-element.68), channel_id=1, source_target_pairs={{0,2},{1,3},{2,4},{3,5},{4,6},{5,7},{6,0},{7,1},{8,10},{9,11},{10,... | collective-permute-start | bytes 393224 | tf_op jit(solution)/shard_map/ppermute | solution.py:609
  200.9 9.3 %collective-permute-start.20 = (bf16[16,32,128]{2,1,0:T(8,128)(2,1)}, bf16[16,32,128]{2,1,0:T(8,128)(2,1)}, u32[]{:S(2)}, u32[]{:S(2)}) collective-permute-start(bf16[16,32,128]{2,1,0:T(8,128)(2,1)} %get-tuple-element.69), channel_id=1, source_target_pairs={{0,4},{1,5},{2,6},{3,7},{4,0},{5,1},{6,2},{7,3},{8,12},{9,13},{10,... | collective-permute-start | bytes 393224 | tf_op jit(solution)/shard_map/ppermute | solution.py:609
  201.2 9.0 %collective-permute-start.21 = (bf16[16,32,128]{2,1,0:T(8,128)(2,1)}, bf16[16,32,128]{2,1,0:T(8,128)(2,1)}, u32[]{:S(2)}, u32[]{:S(2)}) collective-permute-start(bf16[16,32,128]{2,1,0:T(8,128)(2,1)} %get-tuple-element.70), channel_id=1, source_target_pairs={{0,6},{1,7},{2,0},{3,1},{4,2},{5,3},{6,4},{7,5},{8,14},{9,15},{10,... | collective-permute-start | bytes 393224 | tf_op jit(solution)/shard_map/ppermute | solution.py:609
